TPU v7x, 256 devices: a whole 4x4x8 slice. The times are simulated.
256 devices in a mesh: blk: 64 (over z, x, core), ch: 4 (over y).
Axes of the slice: x: 4, y: 4, z: 8, core: 2. Of those that a mesh axis runs over, the one named last changes fastest.
Arguments:
- features: bfloat16 [128, 65536], P('ch', 'blk'), may hold values from -6 to 6
- weight: bfloat16 [27, 128, 128], P(None, 'ch'), may hold values from -0.1875 to 0.1875
- grad_out: bfloat16 [128, 65536], P('ch', 'blk'), may hold values from -6 to 6
- rulebook: int32 [27, 65536], P(None, 'blk'), may hold values from 0 to 1280, as said below
Outputs:
- output: bfloat16 [128, 65536], P('ch', 'blk')
- grad_features: bfloat16 [128, 65536], P('ch', 'blk')
- weight_grad: float32 [27, 128, 128], P(None, 'ch')
Inputs may be any that keep to these rules, and one draw needn't show every extreme that they name: `rulebook`: slots 0 to 127 of every block hold active voxels of its lowest layer, slots 128 to 255 active voxels of its highest layer, then come active inner voxels, then empty slots; at least 640 slots of a block are active and some block has all 1024. Offset k = 9 (dx + 1) + 3 (dy + 1) + (dz + 1), dz along the block order. An entry names the table column of the active neighbour at that offset, and the zero column 1280 for an inactive neighbour, one outside the image, and for every entry of an empty slot. If entry k of slot i names slot j, entry 26 - k of j names i.
All inputs are finite; a program needn't handle non-finite values.
Results may differ from a plain program's by a relative error of at most 0.001.
Values may be sent and summed in bfloat16 or wider, within the bound.
No kernel may reach another device: no remote copies, remote signals or barrier semaphores. Data moves between devices by JAX's collectives and lax.ppermute only.
A program may use at most 64 MiB of HBM per device.

v0:
```python
import math

import jax
import jax.numpy as jnp
from jax import lax
from jax.sharding import PartitionSpec as P

VOX = 1024
FACE = 128


def passed_along(value, axis, steps):
    count = lax.axis_size(axis)
    pairs = [(source, (source + steps) % count) for source in range(count)]
    return lax.ppermute(value, axis, pairs)


def split_faces(source):
    chan_count = source.shape[0]
    blocks = source.reshape(chan_count, source.shape[1] // VOX, VOX)
    lowest = blocks[:, :, :FACE].reshape(chan_count, -1)
    highest = blocks[:, :, FACE : 2 * FACE].reshape(chan_count, -1)
    return (lowest, highest)


def align(from_lower, from_upper):
    chan_count = from_lower.shape[0]
    lower_faces = from_lower.reshape(chan_count, -1, FACE)
    upper_faces = from_upper.reshape(chan_count, -1, FACE)
    blank_faces = jnp.zeros_like(lower_faces)
    position = lax.axis_index("blk")
    final_index = lax.axis_size("blk") - 1
    lower_faces = jnp.where(
        position == 0, jnp.concatenate([blank_faces, lower_faces[:, :-1]], axis=1), lower_faces
    )
    upper_faces = jnp.where(
        position == final_index,
        jnp.concatenate([upper_faces[:, 1:], blank_faces], axis=1),
        upper_faces,
    )
    return (lower_faces.reshape(chan_count, -1), upper_faces.reshape(chan_count, -1))


def extend(source, lower_faces, upper_faces):
    zero_column = jnp.zeros((source.shape[0], 1), source.dtype)
    return jnp.concatenate([source, lower_faces, upper_faces, zero_column], axis=1)


def densify(table, neighbours):
    table_rows = table.T
    picked_rows = jnp.take(table_rows, neighbours, axis=0)
    return picked_rows.reshape(neighbours.shape[0], -1)


def per_device(features, weight, grad_out, rulebook):
    quarter = features.shape[0]
    local_rows = features.shape[1]
    width = weight.shape[2]
    neighbours = rulebook.T
    lowest, highest = split_faces(features)
    from_lower = passed_along(highest, "blk", 1)
    from_upper = passed_along(lowest, "blk", -1)
    lower_faces, upper_faces = align(from_lower, from_upper)
    ext_inputs = extend(features, lower_faces, upper_faces)
    dense_inputs = densify(ext_inputs, neighbours)
    flat_weight = weight.reshape(27 * quarter, width)
    output = lax.psum_scatter(
        jnp.dot(dense_inputs, flat_weight, preferred_element_type=jnp.float32).T,
        "ch",
        scatter_dimension=0,
        tiled=True,
    )
    output = output.astype(jnp.bfloat16)
    grad_full = lax.all_gather(grad_out, "ch", axis=0, tiled=True)
    grad_lowest, grad_highest = split_faces(grad_full)
    grad_lower = passed_along(grad_highest, "blk", 1)
    grad_upper = passed_along(grad_lowest, "blk", -1)
    lower_grads, upper_grads = align(grad_lower, grad_upper)
    ext_grads = extend(grad_full, lower_grads, upper_grads)
    flipped = neighbours[:, ::-1]
    dense_grads = densify(ext_grads, flipped)
    back_weight = weight.transpose(0, 2, 1).reshape(27 * width, quarter)
    grad_inputs = jnp.dot(dense_grads, back_weight, preferred_element_type=jnp.float32).T
    local_terms = lax.dot_general(
        dense_inputs, grad_full.T, (((0,), (0,)), ((), ())), preferred_element_type=jnp.float32
    )
    local_terms = local_terms.reshape(27, quarter, width)
    norm_scale = 1.0 / math.sqrt(lax.axis_size("blk") * local_rows)
    weight_grad = lax.psum(local_terms, "blk") * norm_scale
    return (output, grad_inputs.astype(jnp.bfloat16), weight_grad)


def solution(mesh):
    placed = (P("ch", "blk"), P(None, "ch", None), P("ch", "blk"), P(None, "blk"))
    return jax.shard_map(
        per_device,
        mesh=mesh,
        in_specs=placed,
        out_specs=(P("ch", "blk"), P("ch", "blk"), P(None, "ch", None)),
        check_vma=False,
    )
```

profile of v0, /device:TPU:1, one launch (start us, length us, event | category | flops | bytes accessed | tf_op | source)
XLA Modules:
  0.0 368.4 jit_solution(6934085552225605736)
XLA Ops:
  8.1 11.6 %all_gather.3 = bf16[128,1024]{1,0:T(8,128)(2,1)S(1)} all-gather(bf16[32,1024]{1,0:T(8,128)(2,1)} %param.6), channel_id=1, replica_groups=mesh['blk'=64,'ch'=4] {'ch'}, dimensions={0}, use_global_device_ids=true | all-gather | bytes 327680 | tf_op jit(solution)/shard_map/all_gather | solution.py:74
  19.7 4.7 %collective-permute-start.3 = (bf16[128,128]{1,0:T(8,128)(2,1)S(1)}, bf16[128,128]{1,0:T(8,128)(2,1)S(1)}, u32[]{:S(2)}, u32[]{:S(2)}) collective-permute-start(bf16[128,128]{1,0:T(8,128)(2,1)S(1)} %get-tuple-element.16), channel_id=1, source_target_pairs={{0,252},{4,0},{8,4},{12,8},{16,12},{20,16},{24,20},{28,24},{32,28}... | collective-permute-start | bytes 98312 | tf_op jit(solution)/shard_map/ppermute | solution.py:15
  24.3 0.7 slice_bitcast_fusion.3
  25.0 3.6 collective-permute-start.1
  28.6 2.9 rev.3
  31.6 0.9 compare_select_fusion.1
  32.6 0.2 copy.44
  32.8 0.4 reshape.76
  33.4 0.4 reshape.68
  33.8 0.9 compare_and_fusion.1
  34.7 0.3 copy.43
  35.0 0.3 copy.37
  35.4 0.9 maximum_maximum_fusion
  36.2 0.2 copy.38
  36.5 96.4 %gather_fusion = bf16[27648,32]{1,0:T(8,128)(2,1)} fusion(bf16[1281,32]{1,0:T(8,128)(2,1)S(1)} %bitcast.48, s32[27648]{0:T(1024)S(1)} %broadcast_clamp_fusion.1), kind=kCustom, calls=%fused_computation | custom fusion | bytes 3649536 | tf_op jit(solution)/shard_map/jit(_take)/gather | solution.py:51
  132.9 5.4 %copy.40 = bf16[27648,32]{0,1:T(8,128)(2,1)S(1)} copy(bf16[27648,32]{1,0:T(8,128)(2,1)} %gather_fusion) | data formatting | bytes 3538944 | tf_op jit(solution)/shard_map/jit(_take)/gather | solution.py:51
  138.3 22.7 %reshape.67 = bf16[1024,27,32]{1,0,2:T(8,128)(2,1)} reshape(bf16[27648,32]{0,1:T(8,128)(2,1)S(1)} %copy.40) | data formatting | bytes 3538944 | tf_op jit(solution)/shard_map/jit(_take)/gather | solution.py:51
  161.0 7.7 %broadcast_select_fusion.1 = bf16[1024,27,32]{1,0,2:T(8,128)(2,1)} fusion(bf16[1024,27,32]{1,0,2:T(8,128)(2,1)} %reshape.67, pred[1024,27]{1,0:T(8,128)(4,1)S(1)} %copy.37), kind=kLoop, calls=%fused_computation.3 | loop fusion | flops 884736 | bytes 3566592 | tf_op jit(solution)/shard_map/jit(_take)/select_n | solution.py:51
  168.7 7.5 %copy.47 = bf16[1024,27,32]{0,2,1:T(8,128)(2,1)S(1)} copy(bf16[1024,27,32]{1,0,2:T(8,128)(2,1)} %broadcast_select_fusion.1) | data formatting | bytes 3538944 | tf_op jit(solution)/shard_map/jit(_take)/select_n | solution.py:51
  176.3 1.4 fusion.2
  177.7 0.2 reduce-scatter.4.cloned.1.call-start
  177.9 5.1 %convolution_bitcast_fusion = f32[128,1024]{0,1:T(8,128)S(1)} fusion(bf16[1024,27,32]{1,0,2:T(8,128)(2,1)} %broadcast_select_fusion.1, bf16[27,32,128]{2,1,0:T(8,128)(2,1)S(1)} %copy-done), kind=kOutput, calls=%fused_computation.8 | convolution fusion | flops 226492416 | bytes 2514944 | tf_op jit(solution)/shard_map/dot_general | solution.py:68
  183.1 1.0 copy.50
  184.2 0.2 copy.45
  184.5 96.4 %gather_fusion.1 = bf16[27648,128]{1,0:T(8,128)(2,1)} fusion(bf16[1281,128]{1,0:T(8,128)(2,1)S(1)} %copy.45, s32[27648]{0:T(1024)S(1)} %broadcast_clamp_fusion), kind=kCustom, calls=%fused_computation.1 | custom fusion | bytes 14266368 | tf_op jit(solution)/shard_map/jit(_take)/gather | solution.py:51
  280.8 11.9 %reshape.75 = bf16[1024,27,128]{2,1,0:T(8,128)(2,1)} reshape(bf16[27648,128]{1,0:T(8,128)(2,1)} %gather_fusion.1) | data formatting | bytes 14155776 | tf_op jit(solution)/shard_map/jit(_take)/gather | solution.py:51
  292.8 15.3 %broadcast_select_fusion = bf16[1024,27,128]{2,1,0:T(8,128)(2,1)S(1)} fusion(bf16[1024,27,128]{2,1,0:T(8,128)(2,1)} %reshape.75, pred[1024,27]{1,0:T(8,128)(4,1)S(1)} %copy.43), kind=kLoop, calls=%fused_computation.2 | loop fusion | flops 3538944 | bytes 14183424 | tf_op jit(solution)/shard_map/jit(_take)/select_n | solution.py:51
  308.1 4.3 %fusion.10 = bf16[32,1024]{1,0:T(8,128)(2,1)} fusion(bf16[1024,27,128]{2,1,0:T(8,128)(2,1)S(1)} %broadcast_select_fusion, bf16[27,32,128]{2,1,0:T(8,128)(2,1)S(1)} %copy-done), kind=kOutput, calls=%fused_computation.11 | convolution fusion | flops 226525184 | bytes 7364608 | tf_op jit(solution)/shard_map/dot_general | solution.py:83
  312.4 44.9 %all-reduce.2.cloned.1.call-done = f32[27,32,128]{2,1,0:T(8,128)} async-done(((f32[27,32,128]{2,1,0:T(8,128)}), f32[27,32,128]{2,1,0:T(8,128)}) %all-reduce.2.cloned.1.call-update) | async-done | bytes 442384 | tf_op jit(solution)/shard_map/psum | solution.py:89
  357.3 1.8 broadcast_multiply_fusion
  359.1 1.1 copy.51
  360.2 0.8 copy.48
  (24 shorter events, 0.5 us)
Async XLA Ops:
  8.0 169.9 %copy-start = (bf16[27,32,128]{2,1,0:T(8,128)(2,1)S(1)}, bf16[27,32,128]{2,1,0:T(8,128)(2,1)}, u32[]{:S(2)}) copy-start(bf16[27,32,128]{2,1,0:T(8,128)(2,1)} %param.5) | copy-start | bytes 663556
  8.0 349.3 %all-reduce.2.cloned.1.call-start = ((), (), s32[]{:S(2)}) async-start(), calls=%async_computation.1 | async-start | bytes 884736 | tf_op jit(solution)/shard_map/psum | solution.py:89
  19.7 164.4 %collective-permute-start.3 = (bf16[128,128]{1,0:T(8,128)(2,1)S(1)}, bf16[128,128]{1,0:T(8,128)(2,1)S(1)}, u32[]{:S(2)}, u32[]{:S(2)}) collective-permute-start(bf16[128,128]{1,0:T(8,128)(2,1)S(1)} %get-tuple-element.16), channel_id=1, source_target_pairs={{0,252},{4,0},{8,4},{12,8},{16,12},{20,16},{24,20},{28,24},{32,28}... | collective-permute-start | bytes 98312 | tf_op jit(solution)/shard_map/ppermute | solution.py:15
  24.3 159.8 %collective-permute-start.2 = (bf16[128,128]{1,0:T(8,128)(2,1)S(1)}, bf16[128,128]{1,0:T(8,128)(2,1)S(1)}, u32[]{:S(2)}, u32[]{:S(2)}) collective-permute-start(bf16[128,128]{1,0:T(8,128)(2,1)S(1)} %get-tuple-element.15), channel_id=1, source_target_pairs={{0,4},{4,8},{8,12},{12,16},{16,20},{20,24},{24,28},{28,32},{32,36}... | collective-permute-start | bytes 98312 | tf_op jit(solution)/shard_map/ppermute | solution.py:15
  25.0 10.3 %collective-permute-start.1 = (bf16[32,128]{1,0:T(8,128)(2,1)S(1)}, bf16[32,128]{1,0:T(8,128)(2,1)S(1)}, u32[]{:S(2)}, u32[]{:S(2)}) collective-permute-start(bf16[32,128]{1,0:T(8,128)(2,1)S(1)} %get-tuple-element.18), channel_id=1, source_target_pairs={{0,252},{4,0},{8,4},{12,8},{16,12},{20,16},{24,20},{28,24},{32,28}... | collective-permute-start | bytes 24584 | tf_op jit(solution)/shard_map/ppermute | solution.py:15
  28.6 6.7 %collective-permute-start = (bf16[32,128]{1,0:T(8,128)(2,1)S(1)}, bf16[32,128]{1,0:T(8,128)(2,1)S(1)}, u32[]{:S(2)}, u32[]{:S(2)}) collective-permute-start(bf16[32,128]{1,0:T(8,128)(2,1)S(1)} %get-tuple-element.17), channel_id=1, source_target_pairs={{0,4},{4,8},{8,12},{12,16},{16,20},{20,24},{24,28},{28,32},{32,36}... | collective-permute-start | bytes 24584 | tf_op jit(solution)/shard_map/ppermute | solution.py:15
  177.7 181.4 %reduce-scatter.4.cloned.1.call-start = ((), (), s32[]{:S(2)}) async-start(), calls=%async_computation.2 | async-start | bytes 655360
Sparse Core Ops, SparseCore 0:
  177.8 179.4 all-reduce.1
Sparse Core Ops, SparseCore 1:
  184.2 23.4 reduce-scatter.3
where the time goes:
time: 369 us; the launch traced here: 368 us
  local copies, waits for them, and re-layouts  249 us (67%)
  waiting for transfers between devices  44.9 us (12%)
  other arithmetic  27.8 us (8%)
  between operations  15.7 us (4%)
  blocking collectives  11.6 us (3%)
  matrix products  10.9 us (3%)
  starting transfers between devices  8.51 us (2%)
    gather x5, local copies, waits for them, and re-layouts, densify(): picked_rows = jnp.take(table_rows, neighbours, axis=0)  233 us
    psum x1, waiting for transfers between devices, per_device(): weight_grad = lax.psum(local_terms, 'blk') * norm_scale  44.9 us
    select_n x4, other arithmetic, densify(): picked_rows = jnp.take(table_rows, neighbours, axis=0)  24 us
    all_gather x1, blocking collectives, per_device(): grad_full = lax.all_gather(grad_out, 'ch', axis=0, tiled=True)  11.6 us
    ppermute x4, starting transfers between devices, passed_along(): return lax.ppermute(value, axis, pairs)  8.25 us
    select_n x3, local copies, waits for them, and re-layouts, densify(): picked_rows = jnp.take(table_rows, neighbours, axis=0)  7.95 us
  transfers between devices with their start and end apart: 6, of which 1 were waited for; matrix products, arithmetic and copies ran while one was open for 78% of the time, Pallas kernels for 0%

commit v1 on v0

v1 whole, which is shorter than its diff:
```python
import jax
import jax.numpy as jnp
from jax import lax
from jax.experimental import pallas as pl
from jax.experimental.pallas import tpu as pltpu
from jax.sharding import PartitionSpec as P

VOX = 1024
FACE = 128
LANES = 128
PART = 112
INNER = tuple(range(2, 8))
VMEM = pl.BlockSpec(memory_space=pltpu.VMEM)


def source_tiles(group, dz):
    if group == 0:
        return {-1: (8,), 0: (0,), 1: INNER}[dz]
    if group == 1:
        return {-1: INNER, 0: (1,), 1: (9,)}[dz]
    return {-1: (0,) + INNER, 0: INNER, 1: (1,) + INNER}[dz]


def picked(row, group, tiles, load):
    span = row[:, LANES * group : LANES * (group + 1)]
    index = jnp.broadcast_to(span, (32, LANES))
    lane = index & (LANES - 1)
    tile = index >> 7
    total = jnp.zeros((32, LANES), jnp.float32)
    for t in tiles:
        values = jnp.take_along_axis(load(t), lane, axis=1, mode="promise_in_bounds")
        total = jnp.where(tile == t, values, total)
    return total


def tile_span(t):
    return slice(LANES * t, LANES * (t + 1))


def gather_kernel(x_ref, rule_ref, dense_ref, table):
    table[...] = x_ref[...].astype(jnp.float32)

    def step(j, carry):
        for d in range(3):
            k = 3 * j + d
            row = rule_ref[pl.ds(k, 1), :]
            for group in range(8):
                tiles = source_tiles(group, d - 1)
                if tiles[0] >= 8:
                    continue
                got = picked(row, group, tiles, lambda t: table[:, tile_span(t)])
                rows = pl.ds(pl.multiple_of(32 * k, 32), 32)
                dense_ref[rows, tile_span(group)] = got.astype(jnp.bfloat16)
        return carry

    lax.fori_loop(0, 9, step, 0)


def weight_kernel(
    dense_in, rule_ref, lower_ref, upper_ref, g0, g1, g2, g3,
    dense_ref, grad_ref, low_ref, high_ref, keep_ref, send_ref, faces, terms,
):
    chan = lax.axis_index("ch")
    place = lax.axis_index("blk")
    for m, part in enumerate((g0, g1, g2, g3)):
        rows = pl.ds(pl.multiple_of(32 * (chan ^ m), 32), 32)
        grad_ref[rows, :] = part[...]
        low_ref[rows, :] = part[:, :FACE]
        high_ref[rows, :] = part[:, FACE : 2 * FACE]
    faces[:, :FACE] = lower_ref[...].astype(jnp.float32)
    faces[:, FACE:] = upper_ref[...].astype(jnp.float32)

    def step(j, carry):
        for group, d in ((0, 0), (1, 2)):
            k = 3 * j + d
            row = rule_ref[pl.ds(k, 1), :]
            got = picked(row, group, (8 + group,), lambda t: faces[:, tile_span(t - 8)])
            rows = pl.ds(pl.multiple_of(32 * k, 32), 32)
            dense_ref[rows, tile_span(group)] = got.astype(jnp.bfloat16)
        return carry

    lax.fori_loop(0, 9, step, 0)
    terms[:864, :] = lax.dot_general(
        dense_ref[...], grad_ref[...], (((1,), (1,)), ((), ())),
        preferred_element_type=jnp.float32,
    ) * (1.0 / 256.0)
    terms[864:, :] = jnp.zeros((32, LANES), jnp.float32)
    near = place & 7
    for q in range(4):
        for odd, target in ((0, keep_ref), (1, send_ref)):
            start = pl.multiple_of(PART * (near ^ (2 * q + odd)), 8)
            target[PART * q : PART * (q + 1), :] = terms[pl.ds(start, PART), :]


def forward_kernel(dense_ref, weight_ref, out_ref):
    out_ref[...] = lax.dot_general(
        weight_ref[...], dense_ref[...], (((0,), (0,)), ((), ())),
        preferred_element_type=jnp.float32,
    )


def back_kernel(grad_ref, lower_ref, upper_ref, weight_ref, rule_ref, out_ref, terms, total):
    weights = weight_ref[...]
    terms[:, :VOX] = jnp.dot(weights, grad_ref[...], preferred_element_type=jnp.float32)
    terms[:, VOX : VOX + FACE] = jnp.dot(
        weights, lower_ref[...], preferred_element_type=jnp.float32
    )
    terms[:, VOX + FACE :] = jnp.dot(
        weights, upper_ref[...], preferred_element_type=jnp.float32
    )
    total[...] = jnp.zeros_like(total)

    def step(j, carry):
        rules = [rule_ref[pl.ds(3 * j + d, 1), :] for d in range(3)]
        for group in range(8):
            running = total[:, tile_span(group)]
            for d in range(3):
                rows = pl.ds(pl.multiple_of(32 * (26 - 3 * j - d), 32), 32)
                running = running + picked(
                    rules[d], group, source_tiles(group, d - 1),
                    lambda t: terms[rows, tile_span(t)],
                )
            total[:, tile_span(group)] = running
        return carry

    lax.fori_loop(0, 9, step, 0)
    out_ref[...] = total[...].astype(jnp.bfloat16)


def split_sum_kernel(keep_ref, came_ref, *outs):
    for q, out in enumerate(outs):
        rows = slice(PART * q, PART * (q + 1))
        out[...] = keep_ref[rows, :] + came_ref[rows, :]


def sum_kernel(*refs):
    total = refs[0][...]
    for ref in refs[1:-1]:
        total = total + ref[...]
    refs[-1][...] = total


def join_kernel(*refs):
    for q, ref in enumerate(refs[:-1]):
        refs[-1][PART * q : PART * (q + 1), :] = ref[...]


def place_kernel(even_ref, odd_ref, out_ref, held):
    near = lax.axis_index("blk") & 7
    for q in range(4):
        rows = slice(PART * q, PART * (q + 1))
        held[2 * PART * q : 2 * PART * q + PART, :] = even_ref[rows, :]
        held[2 * PART * q + PART : 2 * PART * (q + 1), :] = odd_ref[rows, :]
    for p in range(8):
        count = min(PART, 864 - PART * p)
        start = pl.multiple_of(PART * (near ^ p), 8)
        out_ref[PART * p : PART * p + count, :] = held[pl.ds(start, count), :]


def call(kernel, outs, args, scratch=(), aliases=None, flops=0, name=None):
    moved = sum(a.size * a.dtype.itemsize for a in list(args) + jax.tree.leaves(outs))
    return pl.pallas_call(
        kernel,
        out_shape=outs,
        in_specs=[VMEM] * len(args),
        out_specs=jax.tree.map(lambda _: VMEM, outs),
        scratch_shapes=list(scratch),
        input_output_aliases=aliases or {},
        compiler_params=pltpu.CompilerParams(vmem_limit_bytes=40 << 20),
        cost_estimate=pl.CostEstimate(flops=flops, bytes_accessed=moved, transcendentals=0),
        name=name,
    )(*args)


def f32(*shape):
    return jax.ShapeDtypeStruct(shape, jnp.float32)


def bf16(*shape):
    return jax.ShapeDtypeStruct(shape, jnp.bfloat16)


def swap(value, mask):
    count = lax.axis_size("blk")
    return lax.ppermute(value, "blk", [(i, i ^ mask) for i in range(count)])


def shifted(value, steps):
    count = lax.axis_size("blk")
    return lax.ppermute(value, "blk", [(i, (i + steps) % count) for i in range(count)])


def per_device(features, weight, grad_out, rulebook):
    weights = weight.reshape(864, 128)
    from_lower = shifted(features[:, FACE : 2 * FACE], 1)
    from_upper = shifted(features[:, :FACE], -1)
    parts = [
        lax.ppermute(grad_out, "ch", [(i, i ^ m) for i in range(4)]) for m in (1, 2, 3)
    ]
    dense = call(
        gather_kernel, bf16(864, VOX), (features, rulebook),
        [pltpu.VMEM((32, VOX), jnp.float32)], flops=3 << 30, name="gather",
    )
    dense, grads, low, high, keep, send = call(
        weight_kernel,
        (bf16(864, VOX), bf16(128, VOX), bf16(128, FACE), bf16(128, FACE),
         f32(4 * PART, 128), f32(4 * PART, 128)),
        (dense, rulebook, from_lower, from_upper, grad_out, *parts),
        [pltpu.VMEM((32, 2 * FACE), jnp.float32), pltpu.VMEM((8 * PART, 128), jnp.float32)],
        aliases={0: 0}, flops=1 << 30, name="weight_terms",
    )
    came = swap(send, 1)
    partial = call(
        forward_kernel, f32(128, VOX), (dense, weights), flops=1 << 30, name="forward"
    )
    output = lax.psum_scatter(partial, "ch", scatter_dimension=0, tiled=True)
    pieces = call(split_sum_kernel, (f32(PART, 128),) * 4, (keep, came), name="sum_pair")
    others = [swap(pieces[q], 2 * q) for q in (1, 2, 3)]
    total = call(sum_kernel, f32(PART, 128), (pieces[0], *others), name="sum_four")
    for mask in (8, 16, 32):
        total = call(sum_kernel, f32(PART, 128), (total, swap(total, mask)), name="sum_two")
    even = call(
        join_kernel, f32(4 * PART, 128),
        (total, *[swap(total, 2 * q) for q in (1, 2, 3)]), name="join",
    )
    odd = swap(even, 1)
    weight_grad = call(
        place_kernel, f32(864, 128), (even, odd),
        [pltpu.VMEM((8 * PART, 128), jnp.float32)], name="place",
    )
    lower_grads = shifted(high, 1)
    upper_grads = shifted(low, -1)
    grad_features = call(
        back_kernel, bf16(32, VOX), (grads, lower_grads, upper_grads, weights, rulebook),
        [pltpu.VMEM((864, VOX + 2 * FACE), jnp.float32), pltpu.VMEM((32, VOX), jnp.float32)],
        flops=5 << 30, name="back",
    )
    return (
        output.astype(jnp.bfloat16),
        grad_features,
        weight_grad.reshape(27, 32, 128),
    )


def solution(mesh):
    placed = (P("ch", "blk"), P(None, "ch", None), P("ch", "blk"), P(None, "blk"))
    return jax.shard_map(
        per_device,
        mesh=mesh,
        in_specs=placed,
        out_specs=(P("ch", "blk"), P("ch", "blk"), P(None, "ch", None)),
        check_vma=False,
    )
```

time: 369 us -> 84.8 us (0.23)
  local copies, waits for them, and re-layouts: 249 us -> 2.47 us
  waiting for transfers between devices: 44.9 us -> 15.4 us
  other arithmetic: 27.8 us -> 1.54 us
  starting transfers between devices: 8.51 us -> 34.3 us
  Pallas kernels: 0 us -> 15.3 us
  blocking collectives: 11.6 us -> 0 us
  matrix products: 10.9 us -> 0 us
    gather x5 -> x0, local copies, waits for them, and re-layouts: 233 us -> none  [densify(): picked_rows = jnp.take(table_rows, neighbours, axis=0)]
    psum x1 -> x0, waiting for transfers between devices: 44.9 us -> none  [per_device(): weight_grad = lax.psum(local_terms, 'blk') * norm_scale]
    ppermute x4 -> x18, starting transfers between devices: 8.25 us -> 34.2 us  [the longest x11 21.8 us: swap(): return lax.ppermute(value, 'blk', [(i, i ^ mask) for i in range(count)])]
    select_n x8 -> x0, other arithmetic: 24 us -> none  [the longest x4 24 us: densify(): picked_rows = jnp.take(table_rows, neighbours, axis=0)]
    ppermute x4 -> x18, waiting for transfers between devices: 0.01 us -> 15.4 us  [the longest x11 15 us: swap(): return lax.ppermute(value, 'blk', [(i, i ^ mask) for i in range(count)])]
    pallas_call x0 -> x11, Pallas kernels: none -> 15.3 us  [call(): pl.pallas_call(kernel, out_shape=outs, in_specs=[VMEM] * len(args), out_s...]
    all_gather x1 -> x0, blocking collectives: 11.6 us -> none  [per_device(): grad_full = lax.all_gather(grad_out, 'ch', axis=0, tiled=True)]
    dot_general x3 -> x0, matrix products: 10.9 us -> none  [the longest x1 5.13 us: per_device(): jnp.dot(dense_inputs, flat_weight, preferred_element_type=jnp.float32)]
  transfers between devices with their start and end apart: 6 -> 19, of which waited for: 1 -> 7; matrix products, arithmetic and copies ran while one was open for 78% -> 1% of each run, Pallas kernels for 0% -> 15%
where the time goes in v1:
time: 84.8 us; the launch traced here: 83.2 us
  starting transfers between devices  34.3 us (40%)
  waiting for transfers between devices  15.4 us (18%)
  Pallas kernels  15.3 us (18%)
  between operations  14.2 us (17%)
  local copies, waits for them, and re-layouts  2.47 us (3%)
  other arithmetic  1.54 us (2%)
    ppermute x11, starting transfers between devices, swap(): return lax.ppermute(value, 'blk', [(i, i ^ mask) for i in range(count)])  21.8 us
    pallas_call x11, Pallas kernels, call(): pl.pallas_call(kernel, out_shape=outs, in_specs=[VMEM] * len(args), out_s...  15.3 us
    ppermute x11, waiting for transfers between devices, swap(): return lax.ppermute(value, 'blk', [(i, i ^ mask) for i in range(count)])  15 us
    ppermute x4, starting transfers between devices, shifted(): lax.ppermute(value, 'blk', [(i, (i + steps) % count) for i in range(count)])  7.78 us
    ppermute x3, starting transfers between devices, per_device(): lax.ppermute(grad_out, 'ch', [(i, i ^ m) for i in range(4)])  4.61 us
    unnamed x10, local copies, waits for them, and re-layouts  1.76 us
  transfers between devices with their start and end apart: 19, of which 7 were waited for; matrix products, arithmetic and copies ran while one was open for 1% of the time, Pallas kernels for 15%

profile of v1, /device:TPU:1, one launch (start us, length us, event | category | flops | bytes accessed | tf_op | source)
XLA Modules:
  0.0 83.2 jit_solution(14550360313176205013)
XLA Ops:
  7.2 0.0 reduce-scatter.2.cloned.1.call-start
  7.2 3.8 %collective-permute-start.3 = (bf16[32,1024]{1,0:T(8,128)(2,1)}, bf16[32,1024]{1,0:T(8,128)(2,1)S(1)}, u32[]{:S(2)}, u32[]{:S(2)}) collective-permute-start(bf16[32,1024]{1,0:T(8,128)(2,1)} %g0.1), channel_id=1, source_target_pairs={{0,2},{1,3},{2,0},{3,1},{4,6},{5,7},{6,4},{7,5},{8,10},{9,11},{10,... | collective-permute-start | bytes 196616 | tf_op jit(solution)/shard_map/ppermute | solution.py:198
  11.0 0.4 collective-permute-start.2
  11.4 0.4 collective-permute-start.4
  11.8 0.7 fusion
  12.5 2.8 %collective-permute-start.1 = (bf16[32,128]{1,0:T(8,128)(2,1)S(1)}, bf16[32,128]{1,0:T(8,128)(2,1)S(1)}, u32[]{:S(2)}, u32[]{:S(2)}) collective-permute-start(bf16[32,128]{1,0:T(8,128)(2,1)S(1)} %get-tuple-element.23), channel_id=1, source_target_pairs={{0,252},{4,0},{8,4},{12,8},{16,12},{20,16},{24,20},{28,24},{32,28}... | collective-permute-start | bytes 24584 | tf_op jit(solution)/shard_map/ppermute | solution.py:190
  15.4 0.8 %copy-done = bf16[32,1024]{1,0:T(8,128)(2,1)S(1)} copy-done((bf16[32,1024]{1,0:T(8,128)(2,1)S(1)}, bf16[32,1024]{1,0:T(8,128)(2,1)}, u32[]{:S(2)}) %copy-start) | copy-done | bytes 65560
  16.2 0.9 %copy-done.2 = s32[27,1024]{1,0:T(8,128)S(1)} copy-done((s32[27,1024]{1,0:T(8,128)S(1)}, s32[27,1024]{1,0:T(8,128)}, u32[]{:S(2)}) %copy-start.2) | copy-done | bytes 110616
  17.1 3.9 %gather.1.dense_in = bf16[864,1024]{1,0:T(8,128)(2,1)S(1)} custom-call(bf16[32,1024]{1,0:T(8,128)(2,1)S(1)} %copy-done, s32[27,1024]{1,0:T(8,128)S(1)} %copy-done.2), custom_call_target="tpu_custom_call" | custom-call | flops 3221225472 | bytes 1945600 | tf_op jit(solution)/shard_map/gather/pallas_call | solution.py:162
  21.0 0.4 collective-permute-done.lower_ref
  21.4 1.4 %weight_terms.1 = (bf16[864,1024]{1,0:T(8,128)(2,1)S(1)}, bf16[128,1024]{1,0:T(8,128)(2,1)S(1)}, bf16[128,128]{1,0:T(8,128)(2,1)S(1)}, bf16[128,128]{1,0:T(8,128...) custom-call(bf16[864,1024]{1,0:T(8,128)(2,1)S(1)} %gather.1.dense_in, ...), custom_call_target="tpu_custom_call", output_to_operand_aliasing={{0}: (0, {})} | custom-call | flops 1073741824 | bytes 4714496 | tf_op jit(solution)/shard_map/weight_terms/pallas_call | solution.py:162
  22.8 1.3 %forward.1 = f32[128,1024]{1,0:T(8,128)} custom-call(bf16[864,1024]{1,0:T(8,128)(2,1)S(1)} %get-tuple-element.13.dense_ref, bf16[864,128]{1,0:T(8,128)(2,1)S(1)} %bitcast.2), custom_call_target="tpu_custom_call" | custom-call | flops 1073741824 | bytes 2514944 | tf_op jit(solution)/shard_map/forward/pallas_call | solution.py:162
  24.2 5.8 %collective-permute-start.7 = (f32[448,128]{1,0:T(8,128)S(1)}, f32[448,128]{1,0:T(8,128)S(1)}, u32[]{:S(2)}, u32[]{:S(2)}) collective-permute-start(f32[448,128]{1,0:T(8,128)S(1)} %get-tuple-element.18), channel_id=1, source_target_pairs={{0,4},{4,0},{8,12},{12,8},{16,20},{20,16},{24,28},{28,24},{32,36},... | collective-permute-start | bytes 688136 | tf_op jit(solution)/shard_map/ppermute | solution.py:185
  30.0 1.1 %collective-permute-done.7.came_ref = f32[448,128]{1,0:T(8,128)S(1)} collective-permute-done((f32[448,128]{1,0:T(8,128)S(1)}, f32[448,128]{1,0:T(8,128)S(1)}, u32[]{:S(2)}, u32[]{:S(2)}) %collective-permute-start.7) | collective-permute-done | bytes 229408 | tf_op jit(solution)/shard_map/ppermute | solution.py:185
  31.1 0.1 collective-permute-start.8
  31.2 0.1 collective-permute-start.9
  31.3 3.7 %collective-permute-start.10 = (f32[112,128]{1,0:T(8,128)S(1)}, f32[112,128]{1,0:T(8,128)S(1)}, u32[]{:S(2)}, u32[]{:S(2)}) collective-permute-start(f32[112,128]{1,0:T(8,128)S(1)} %get-tuple-element.22), channel_id=1, source_target_pairs={{0,24},{4,28},{8,16},{12,20},{16,8},{20,12},{24,0},{28,4},{32,56},... | collective-permute-start | bytes 172040 | tf_op jit(solution)/shard_map/ppermute | solution.py:185
  35.1 0.8 collective-permute-done.9.refs_2_
  35.8 1.8 %collective-permute-done.10.refs_3_ = f32[112,128]{1,0:T(8,128)S(1)} collective-permute-done((f32[112,128]{1,0:T(8,128)S(1)}, f32[112,128]{1,0:T(8,128)S(1)}, u32[]{:S(2)}, u32[]{:S(2)}) %collective-permute-start.10) | collective-permute-done | bytes 57376 | tf_op jit(solution)/shard_map/ppermute | solution.py:185
  37.7 0.1 collective-permute-start.11
  37.8 3.4 %collective-permute-done.11.refs_1_ = f32[112,128]{1,0:T(8,128)S(1)} collective-permute-done((f32[112,128]{1,0:T(8,128)S(1)}, f32[112,128]{1,0:T(8,128)S(1)}, u32[]{:S(2)}, u32[]{:S(2)}) %collective-permute-start.11) | collective-permute-done | bytes 57376 | tf_op jit(solution)/shard_map/ppermute | solution.py:185
  41.2 0.9 %collective-permute-start.12 = (f32[112,128]{1,0:T(8,128)S(1)}, f32[112,128]{1,0:T(8,128)S(1)}, u32[]{:S(2)}, u32[]{:S(2)}) collective-permute-start(f32[112,128]{1,0:T(8,128)S(1)} %sum_two.3.refs_0_), channel_id=1, source_target_pairs={{0,64},{4,68},{8,72},{12,76},{16,80},{20,84},{24,88},{28,92},{32,9... | collective-permute-start | bytes 172040 | tf_op jit(solution)/shard_map/ppermute | solution.py:185
  42.0 3.7 %collective-permute-done.12.refs_1_ = f32[112,128]{1,0:T(8,128)S(1)} collective-permute-done((f32[112,128]{1,0:T(8,128)S(1)}, f32[112,128]{1,0:T(8,128)S(1)}, u32[]{:S(2)}, u32[]{:S(2)}) %collective-permute-start.12) | collective-permute-done | bytes 57376 | tf_op jit(solution)/shard_map/ppermute | solution.py:185
  45.8 2.8 %collective-permute-start.13 = (f32[112,128]{1,0:T(8,128)S(1)}, f32[112,128]{1,0:T(8,128)S(1)}, u32[]{:S(2)}, u32[]{:S(2)}) collective-permute-start(f32[112,128]{1,0:T(8,128)S(1)} %sum_two.4.refs_0_), channel_id=1, source_target_pairs={{0,128},{4,132},{8,136},{12,140},{16,144},{20,148},{24,152},{28,15... | collective-permute-start | bytes 172040 | tf_op jit(solution)/shard_map/ppermute | solution.py:185
  48.6 4.2 %collective-permute-done.13.refs_1_ = f32[112,128]{1,0:T(8,128)S(1)} collective-permute-done((f32[112,128]{1,0:T(8,128)S(1)}, f32[112,128]{1,0:T(8,128)S(1)}, u32[]{:S(2)}, u32[]{:S(2)}) %collective-permute-start.13) | collective-permute-done | bytes 57376 | tf_op jit(solution)/shard_map/ppermute | solution.py:185
  52.8 1.5 %collective-permute-start.16 = (f32[112,128]{1,0:T(8,128)S(1)}, f32[112,128]{1,0:T(8,128)S(1)}, u32[]{:S(2)}, u32[]{:S(2)}) collective-permute-start(f32[112,128]{1,0:T(8,128)S(1)} %sum_two.5.refs_0_), channel_id=1, source_target_pairs={{0,24},{4,28},{8,16},{12,20},{16,8},{20,12},{24,0},{28,4},{32,56},... | collective-permute-start | bytes 172040 | tf_op jit(solution)/shard_map/ppermute | solution.py:185
  54.3 1.8 %collective-permute-start.14 = (f32[112,128]{1,0:T(8,128)S(1)}, f32[112,128]{1,0:T(8,128)S(1)}, u32[]{:S(2)}, u32[]{:S(2)}) collective-permute-start(f32[112,128]{1,0:T(8,128)S(1)} %sum_two.5.refs_0_), channel_id=1, source_target_pairs={{0,8},{4,12},{8,0},{12,4},{16,24},{20,28},{24,16},{28,20},{32,40},... | collective-permute-start | bytes 172040 | tf_op jit(solution)/shard_map/ppermute | solution.py:185
  56.1 5.0 %collective-permute-start.5 = (bf16[128,128]{1,0:T(8,128)(2,1)S(1)}, bf16[128,128]{1,0:T(8,128)(2,1)S(1)}, u32[]{:S(2)}, u32[]{:S(2)}) collective-permute-start(bf16[128,128]{1,0:T(8,128)(2,1)S(1)} %get-tuple-element.15), channel_id=1, source_target_pairs={{0,4},{4,8},{8,12},{12,16},{16,20},{20,24},{24,28},{28,32},{32,36}... | collective-permute-start | bytes 98312 | tf_op jit(solution)/shard_map/ppermute | solution.py:190
  61.1 4.9 %collective-permute-start.17 = (f32[448,128]{1,0:T(8,128)S(1)}, f32[448,128]{1,0:T(8,128)S(1)}, u32[]{:S(2)}, u32[]{:S(2)}) collective-permute-start(f32[448,128]{1,0:T(8,128)S(1)} %join.1.even_ref), channel_id=1, source_target_pairs={{0,4},{4,0},{8,12},{12,8},{16,20},{20,16},{24,28},{28,24},{32,36},... | collective-permute-start | bytes 688136 | tf_op jit(solution)/shard_map/ppermute | solution.py:185
  66.1 7.9 %back.1 = bf16[32,1024]{1,0:T(8,128)(2,1)} custom-call(bf16[128,1024]{1,0:T(8,128)(2,1)S(1)} %get-tuple-element.14.grad_ref, bf16[128,128]{1,0:T(8,128)(2,1)S(1)} %collective-permute-done.5.lower_ref, bf16[128,128]{1,0:T(8,128)(2,1)S(1)} %collective-permute-done.6.upper_ref, bf16[864,128]{1,0:T(8,128)(2,1)S(1)} %bitcast.3, s32[27,1024]{1,0:T(8,128)S(1)} %copy-done.3), custom_call_target="tpu_custom_call" | custom-call | flops 5368709120 | bytes 724992 | tf_op jit(solution)/shard_map/back/pallas_call | solution.py:162
  74.0 0.8 place.1
  74.8 1.5 %convert_element_type.3 = bf16[32,1024]{1,0:T(8,128)(2,1)} convert(f32[32,1024]{1,0:T(8,128)} %reduce-scatter.2.cloned.1.call-done) | non-fusion elementwise | flops 32768 | bytes 196608 | tf_op jit(solution)/shard_map/convert_element_type | solution.py:239
  (30 shorter events, 0.2 us)
Async XLA Ops:
  7.2 67.6 %reduce-scatter.2.cloned.1.call-start = ((), (), s32[]{:S(2)}) async-start(), calls=%async_computation.1 | async-start | bytes 655360 | tf_op jit(solution)/shard_map/reduce_scatter | solution.py:216
  7.2 14.2 %collective-permute-start.3 = (bf16[32,1024]{1,0:T(8,128)(2,1)}, bf16[32,1024]{1,0:T(8,128)(2,1)S(1)}, u32[]{:S(2)}, u32[]{:S(2)}) collective-permute-start(bf16[32,1024]{1,0:T(8,128)(2,1)} %g0.1), channel_id=1, source_target_pairs={{0,2},{1,3},{2,0},{3,1},{4,6},{5,7},{6,4},{7,5},{8,10},{9,11},{10,... | collective-permute-start | bytes 196616 | tf_op jit(solution)/shard_map/ppermute | solution.py:198
  11.0 10.3 %collective-permute-start.2 = (bf16[32,1024]{1,0:T(8,128)(2,1)}, bf16[32,1024]{1,0:T(8,128)(2,1)S(1)}, u32[]{:S(2)}, u32[]{:S(2)}) collective-permute-start(bf16[32,1024]{1,0:T(8,128)(2,1)} %g0.1), channel_id=1, source_target_pairs={{0,1},{1,0},{2,3},{3,2},{4,5},{5,4},{6,7},{7,6},{8,9},{9,8},{10,11... | collective-permute-start | bytes 196616 | tf_op jit(solution)/shard_map/ppermute | solution.py:198
  11.4 9.9 %collective-permute-start.4 = (bf16[32,1024]{1,0:T(8,128)(2,1)}, bf16[32,1024]{1,0:T(8,128)(2,1)S(1)}, u32[]{:S(2)}, u32[]{:S(2)}) collective-permute-start(bf16[32,1024]{1,0:T(8,128)(2,1)} %g0.1), channel_id=1, source_target_pairs={{0,3},{1,2},{2,1},{3,0},{4,7},{5,6},{6,5},{7,4},{8,11},{9,10},{10,... | collective-permute-start | bytes 196616 | tf_op jit(solution)/shard_map/ppermute | solution.py:198
  12.5 8.4 %collective-permute-start.1 = (bf16[32,128]{1,0:T(8,128)(2,1)S(1)}, bf16[32,128]{1,0:T(8,128)(2,1)S(1)}, u32[]{:S(2)}, u32[]{:S(2)}) collective-permute-start(bf16[32,128]{1,0:T(8,128)(2,1)S(1)} %get-tuple-element.23), channel_id=1, source_target_pairs={{0,252},{4,0},{8,4},{12,8},{16,12},{20,16},{24,20},{28,24},{32,28}... | collective-permute-start | bytes 24584 | tf_op jit(solution)/shard_map/ppermute | solution.py:190
  15.3 6.0 %collective-permute-start = (bf16[32,128]{1,0:T(8,128)(2,1)S(1)}, bf16[32,128]{1,0:T(8,128)(2,1)S(1)}, u32[]{:S(2)}, u32[]{:S(2)}) collective-permute-start(bf16[32,128]{1,0:T(8,128)(2,1)S(1)} %get-tuple-element.24), channel_id=1, source_target_pairs={{0,4},{4,8},{8,12},{12,16},{16,20},{20,24},{24,28},{28,32},{32,36}... | collective-permute-start | bytes 24584 | tf_op jit(solution)/shard_map/ppermute | solution.py:190
  15.3 0.8 %copy-start = (bf16[32,1024]{1,0:T(8,128)(2,1)S(1)}, bf16[32,1024]{1,0:T(8,128)(2,1)}, u32[]{:S(2)}) copy-start(bf16[32,1024]{1,0:T(8,128)(2,1)} %x_ref.1) | copy-start | bytes 196612
  16.2 0.9 %copy-start.2 = (s32[27,1024]{1,0:T(8,128)S(1)}, s32[27,1024]{1,0:T(8,128)}, u32[]{:S(2)}) copy-start(s32[27,1024]{1,0:T(8,128)} %rule_ref.5) | copy-start | bytes 331780
  17.1 4.3 %copy-start.3 = (s32[27,1024]{1,0:T(8,128)S(1)}, s32[27,1024]{1,0:T(8,128)}, u32[]{:S(2)}) copy-start(s32[27,1024]{1,0:T(8,128)} %rule_ref.5) | copy-start | bytes 331780
  17.1 4.3 %copy-start.4 = (bf16[32,1024]{1,0:T(8,128)(2,1)S(1)}, bf16[32,1024]{1,0:T(8,128)(2,1)}, u32[]{:S(2)}) copy-start(bf16[32,1024]{1,0:T(8,128)(2,1)} %g0.1) | copy-start | bytes 196612
  21.0 1.9 %copy-start.1 = (bf16[27,32,128]{2,1,0:T(8,128)(2,1)S(1)}, bf16[27,32,128]{2,1,0:T(8,128)(2,1)}, u32[]{:S(2)}) copy-start(bf16[27,32,128]{2,1,0:T(8,128)(2,1)} %param.5) | copy-start | bytes 663556
  24.2 6.9 %collective-permute-start.7 = (f32[448,128]{1,0:T(8,128)S(1)}, f32[448,128]{1,0:T(8,128)S(1)}, u32[]{:S(2)}, u32[]{:S(2)}) collective-permute-start(f32[448,128]{1,0:T(8,128)S(1)} %get-tuple-element.18), channel_id=1, source_target_pairs={{0,4},{4,0},{8,12},{12,8},{16,20},{20,16},{24,28},{28,24},{32,36},... | collective-permute-start | bytes 688136 | tf_op jit(solution)/shard_map/ppermute | solution.py:185
  31.1 3.9 %collective-permute-start.8 = (f32[112,128]{1,0:T(8,128)S(1)}, f32[112,128]{1,0:T(8,128)S(1)}, u32[]{:S(2)}, u32[]{:S(2)}) collective-permute-start(f32[112,128]{1,0:T(8,128)S(1)} %get-tuple-element.20), channel_id=1, source_target_pairs={{0,8},{4,12},{8,0},{12,4},{16,24},{20,28},{24,16},{28,20},{32,40},... | collective-permute-start | bytes 172040 | tf_op jit(solution)/shard_map/ppermute | solution.py:185
  31.2 4.6 %collective-permute-start.9 = (f32[112,128]{1,0:T(8,128)S(1)}, f32[112,128]{1,0:T(8,128)S(1)}, u32[]{:S(2)}, u32[]{:S(2)}) collective-permute-start(f32[112,128]{1,0:T(8,128)S(1)} %get-tuple-element.21), channel_id=1, source_target_pairs={{0,16},{4,20},{8,24},{12,28},{16,0},{20,4},{24,8},{28,12},{32,48},... | collective-permute-start | bytes 172040 | tf_op jit(solution)/shard_map/ppermute | solution.py:185
  31.3 6.3 %collective-permute-start.10 = (f32[112,128]{1,0:T(8,128)S(1)}, f32[112,128]{1,0:T(8,128)S(1)}, u32[]{:S(2)}, u32[]{:S(2)}) collective-permute-start(f32[112,128]{1,0:T(8,128)S(1)} %get-tuple-element.22), channel_id=1, source_target_pairs={{0,24},{4,28},{8,16},{12,20},{16,8},{20,12},{24,0},{28,4},{32,56},... | collective-permute-start | bytes 172040 | tf_op jit(solution)/shard_map/ppermute | solution.py:185
  37.7 3.5 %collective-permute-start.11 = (f32[112,128]{1,0:T(8,128)S(1)}, f32[112,128]{1,0:T(8,128)S(1)}, u32[]{:S(2)}, u32[]{:S(2)}) collective-permute-start(f32[112,128]{1,0:T(8,128)S(1)} %sum_four.1.refs_0_), channel_id=1, source_target_pairs={{0,32},{4,36},{8,40},{12,44},{16,48},{20,52},{24,56},{28,60},{32,0... | collective-permute-start | bytes 172040 | tf_op jit(solution)/shard_map/ppermute | solution.py:185
  41.2 4.6 %collective-permute-start.12 = (f32[112,128]{1,0:T(8,128)S(1)}, f32[112,128]{1,0:T(8,128)S(1)}, u32[]{:S(2)}, u32[]{:S(2)}) collective-permute-start(f32[112,128]{1,0:T(8,128)S(1)} %sum_two.3.refs_0_), channel_id=1, source_target_pairs={{0,64},{4,68},{8,72},{12,76},{16,80},{20,84},{24,88},{28,92},{32,9... | collective-permute-start | bytes 172040 | tf_op jit(solution)/shard_map/ppermute | solution.py:185
  45.8 7.0 %collective-permute-start.13 = (f32[112,128]{1,0:T(8,128)S(1)}, f32[112,128]{1,0:T(8,128)S(1)}, u32[]{:S(2)}, u32[]{:S(2)}) collective-permute-start(f32[112,128]{1,0:T(8,128)S(1)} %sum_two.4.refs_0_), channel_id=1, source_target_pairs={{0,128},{4,132},{8,136},{12,140},{16,144},{20,148},{24,152},{28,15... | collective-permute-start | bytes 172040 | tf_op jit(solution)/shard_map/ppermute | solution.py:185
  52.8 8.3 %collective-permute-start.16 = (f32[112,128]{1,0:T(8,128)S(1)}, f32[112,128]{1,0:T(8,128)S(1)}, u32[]{:S(2)}, u32[]{:S(2)}) collective-permute-start(f32[112,128]{1,0:T(8,128)S(1)} %sum_two.5.refs_0_), channel_id=1, source_target_pairs={{0,24},{4,28},{8,16},{12,20},{16,8},{20,12},{24,0},{28,4},{32,56},... | collective-permute-start | bytes 172040 | tf_op jit(solution)/shard_map/ppermute | solution.py:185
  54.3 6.8 %collective-permute-start.15 = (f32[112,128]{1,0:T(8,128)S(1)}, f32[112,128]{1,0:T(8,128)S(1)}, u32[]{:S(2)}, u32[]{:S(2)}) collective-permute-start(f32[112,128]{1,0:T(8,128)S(1)} %sum_two.5.refs_0_), channel_id=1, source_target_pairs={{0,16},{4,20},{8,24},{12,28},{16,0},{20,4},{24,8},{28,12},{32,48},... | collective-permute-start | bytes 172040 | tf_op jit(solution)/shard_map/ppermute | solution.py:185
  54.3 6.8 %collective-permute-start.14 = (f32[112,128]{1,0:T(8,128)S(1)}, f32[112,128]{1,0:T(8,128)S(1)}, u32[]{:S(2)}, u32[]{:S(2)}) collective-permute-start(f32[112,128]{1,0:T(8,128)S(1)} %sum_two.5.refs_0_), channel_id=1, source_target_pairs={{0,8},{4,12},{8,0},{12,4},{16,24},{20,28},{24,16},{28,20},{32,40},... | collective-permute-start | bytes 172040 | tf_op jit(solution)/shard_map/ppermute | solution.py:185
  56.1 9.9 %collective-permute-start.5 = (bf16[128,128]{1,0:T(8,128)(2,1)S(1)}, bf16[128,128]{1,0:T(8,128)(2,1)S(1)}, u32[]{:S(2)}, u32[]{:S(2)}) collective-permute-start(bf16[128,128]{1,0:T(8,128)(2,1)S(1)} %get-tuple-element.15), channel_id=1, source_target_pairs={{0,4},{4,8},{8,12},{12,16},{16,20},{20,24},{24,28},{28,32},{32,36}... | collective-permute-start | bytes 98312 | tf_op jit(solution)/shard_map/ppermute | solution.py:190
  61.1 5.0 %collective-permute-start.6 = (bf16[128,128]{1,0:T(8,128)(2,1)S(1)}, bf16[128,128]{1,0:T(8,128)(2,1)S(1)}, u32[]{:S(2)}, u32[]{:S(2)}) collective-permute-start(bf16[128,128]{1,0:T(8,128)(2,1)S(1)} %get-tuple-element.16), channel_id=1, source_target_pairs={{0,252},{4,0},{8,4},{12,8},{16,12},{20,16},{24,20},{28,24},{32,28}... | collective-permute-start | bytes 98312 | tf_op jit(solution)/shard_map/ppermute | solution.py:190
  61.1 12.8 %collective-permute-start.17 = (f32[448,128]{1,0:T(8,128)S(1)}, f32[448,128]{1,0:T(8,128)S(1)}, u32[]{:S(2)}, u32[]{:S(2)}) collective-permute-start(f32[448,128]{1,0:T(8,128)S(1)} %join.1.even_ref), channel_id=1, source_target_pairs={{0,4},{4,0},{8,12},{12,8},{16,20},{20,16},{24,28},{28,24},{32,36},... | collective-permute-start | bytes 688136 | tf_op jit(solution)/shard_map/ppermute | solution.py:185
Sparse Core Ops, SparseCore 0:
  24.3 24.7 reduce-scatter.1

commit v2 on v1

--- a/solution.py
+++ b/solution.py
@@ -1,3 +1,5 @@
+import functools
+
 import jax
 import jax.numpy as jnp
 from jax import lax
@@ -58,17 +60,14 @@
 
 def weight_kernel(
     dense_in, rule_ref, lower_ref, upper_ref, g0, g1, g2, g3,
-    dense_ref, grad_ref, low_ref, high_ref, keep_ref, send_ref, faces, terms,
+    dense_ref, grad_ref, keep_ref, send_ref, faces, terms,
 ):
     chan = lax.axis_index("ch")
-    place = lax.axis_index("blk")
+    near = lax.axis_index("blk") & 7
     for m, part in enumerate((g0, g1, g2, g3)):
-        rows = pl.ds(pl.multiple_of(32 * (chan ^ m), 32), 32)
-        grad_ref[rows, :] = part[...]
-        low_ref[rows, :] = part[:, :FACE]
-        high_ref[rows, :] = part[:, FACE : 2 * FACE]
-    faces[:, :FACE] = lower_ref[...].astype(jnp.float32)
-    faces[:, FACE:] = upper_ref[...].astype(jnp.float32)
+        grad_ref[pl.ds(pl.multiple_of(32 * (chan ^ m), 32), 32), :] = part[...]
+    faces[:, :FACE] = lower_ref[:32, :].astype(jnp.float32)
+    faces[:, FACE:] = upper_ref[:32, :].astype(jnp.float32)
 
     def step(j, carry):
         for group, d in ((0, 0), (1, 2)):
@@ -85,46 +84,89 @@
         preferred_element_type=jnp.float32,
     ) * (1.0 / 256.0)
     terms[864:, :] = jnp.zeros((32, LANES), jnp.float32)
-    near = place & 7
     for q in range(4):
         for odd, target in ((0, keep_ref), (1, send_ref)):
             start = pl.multiple_of(PART * (near ^ (2 * q + odd)), 8)
             target[PART * q : PART * (q + 1), :] = terms[pl.ds(start, PART), :]
 
 
-def forward_kernel(dense_ref, weight_ref, out_ref):
-    out_ref[...] = lax.dot_general(
+def forward_kernel(dense_ref, weight_ref, lower_ref, upper_ref, own, s1, s2, s3, sums):
+    chan = lax.axis_index("ch")
+    sums[...] = lax.dot_general(
         weight_ref[...], dense_ref[...], (((0,), (0,)), ((), ())),
         preferred_element_type=jnp.float32,
     )
-
-
-def back_kernel(grad_ref, lower_ref, upper_ref, weight_ref, rule_ref, out_ref, terms, total):
-    weights = weight_ref[...]
-    terms[:, :VOX] = jnp.dot(weights, grad_ref[...], preferred_element_type=jnp.float32)
-    terms[:, VOX : VOX + FACE] = jnp.dot(
-        weights, lower_ref[...], preferred_element_type=jnp.float32
-    )
-    terms[:, VOX + FACE :] = jnp.dot(
-        weights, upper_ref[...], preferred_element_type=jnp.float32
-    )
-    total[...] = jnp.zeros_like(total)
+    for m, target in enumerate((own, s1, s2, s3)):
+        rows = pl.ds(pl.multiple_of(32 * (chan ^ m), 32), 32)
+        target[:, :VOX] = sums[rows, :]
+        if m:
+            target[:, VOX : VOX + FACE] = lower_ref[32:, :].astype(jnp.float32)
+            target[:, VOX + FACE :] = upper_ref[32:, :].astype(jnp.float32)
+
+
+def back_terms_kernel(weight_ref, grad_ref, terms_ref):
+    terms_ref[...] = jnp.dot(
+        weight_ref[...], grad_ref[...], preferred_element_type=jnp.float32
+    )
+
+
+def back_inner_kernel(groups, fresh, *refs):
+    terms, rule_ref = refs[0], refs[1]
+    out_ref = refs[-1]
+    for group in groups:
+        out_ref[:, tile_span(group)] = jnp.zeros((32, LANES), jnp.float32)
 
     def step(j, carry):
         rules = [rule_ref[pl.ds(3 * j + d, 1), :] for d in range(3)]
-        for group in range(8):
-            running = total[:, tile_span(group)]
+        for group in groups:
+            running = out_ref[:, tile_span(group)]
             for d in range(3):
                 rows = pl.ds(pl.multiple_of(32 * (26 - 3 * j - d), 32), 32)
                 running = running + picked(
                     rules[d], group, source_tiles(group, d - 1),
                     lambda t: terms[rows, tile_span(t)],
                 )
+            out_ref[:, tile_span(group)] = running
+        return carry
+
+    lax.fori_loop(0, 9, step, 0)
+
+
+def edge_kernel(
+    terms, rule_ref, weight_ref, lower_ref, upper_ref, inner, own, r1, r2, r3,
+    out_ref, grad_ref, faces, products, total,
+):
+    chan = lax.axis_index("ch")
+    summed = (own[...] + r1[:, :VOX]) + (r2[:, :VOX] + r3[:, :VOX])
+    out_ref[...] = summed.astype(jnp.bfloat16)
+    rows = pl.ds(pl.multiple_of(32 * chan, 32), 32)
+    faces[rows, :FACE] = lower_ref[32:, :]
+    faces[rows, FACE:] = upper_ref[32:, :]
+    for m, part in enumerate((r1, r2, r3)):
+        rows = pl.ds(pl.multiple_of(32 * (chan ^ (m + 1)), 32), 32)
+        faces[rows, :] = part[:, VOX:].astype(jnp.bfloat16)
+    products[...] = jnp.dot(
+        weight_ref[...], faces[...], preferred_element_type=jnp.float32
+    )
+    total[...] = jnp.zeros_like(total)
+
+    def step(j, carry):
+        rules = [rule_ref[pl.ds(3 * j + d, 1), :] for d in range(3)]
+        for group in range(2):
+            running = total[:, tile_span(group)]
+            for d in range(3):
+                rows = pl.ds(pl.multiple_of(32 * (26 - 3 * j - d), 32), 32)
+                running = running + picked(
+                    rules[d], group, source_tiles(group, d - 1),
+                    lambda t: products[rows, tile_span(t - 8)] if t >= 8
+                    else terms[rows, tile_span(t)],
+                )
             total[:, tile_span(group)] = running
         return carry
 
     lax.fori_loop(0, 9, step, 0)
-    out_ref[...] = total[...].astype(jnp.bfloat16)
+    grad_ref[:, : 2 * LANES] = total[...].astype(jnp.bfloat16)
+    grad_ref[:, 2 * LANES :] = inner[:, 2 * LANES :].astype(jnp.bfloat16)
 
 
 def split_sum_kernel(keep_ref, came_ref, *outs):
@@ -134,10 +176,10 @@
 
 
 def sum_kernel(*refs):
-    total = refs[0][...]
-    for ref in refs[1:-1]:
-        total = total + ref[...]
-    refs[-1][...] = total
+    values = [ref[...] for ref in refs[:-1]]
+    while len(values) > 1:
+        values = [values[i] + values[i + 1] for i in range(0, len(values), 2)]
+    refs[-1][...] = values[0]
 
 
 def join_kernel(*refs):
@@ -192,54 +234,69 @@
 
 def per_device(features, weight, grad_out, rulebook):
     weights = weight.reshape(864, 128)
-    from_lower = shifted(features[:, FACE : 2 * FACE], 1)
-    from_upper = shifted(features[:, :FACE], -1)
-    parts = [
-        lax.ppermute(grad_out, "ch", [(i, i ^ m) for i in range(4)]) for m in (1, 2, 3)
-    ]
+
+    def over_ch(value, mask):
+        return lax.ppermute(value, "ch", [(i, i ^ mask) for i in range(4)])
+
+    lowest = jnp.concatenate([features[:, :FACE], grad_out[:, :FACE]])
+    highest = jnp.concatenate([features[:, FACE : 2 * FACE], grad_out[:, FACE : 2 * FACE]])
+    parts = [over_ch(grad_out, m) for m in (1, 2, 3)]
+    from_lower = shifted(highest, 1)
+    from_upper = shifted(lowest, -1)
     dense = call(
         gather_kernel, bf16(864, VOX), (features, rulebook),
         [pltpu.VMEM((32, VOX), jnp.float32)], flops=3 << 30, name="gather",
     )
-    dense, grads, low, high, keep, send = call(
+    dense, grads, keep, send = call(
         weight_kernel,
-        (bf16(864, VOX), bf16(128, VOX), bf16(128, FACE), bf16(128, FACE),
-         f32(4 * PART, 128), f32(4 * PART, 128)),
+        (bf16(864, VOX), bf16(128, VOX), f32(4 * PART, 128), f32(4 * PART, 128)),
         (dense, rulebook, from_lower, from_upper, grad_out, *parts),
         [pltpu.VMEM((32, 2 * FACE), jnp.float32), pltpu.VMEM((8 * PART, 128), jnp.float32)],
         aliases={0: 0}, flops=1 << 30, name="weight_terms",
     )
     came = swap(send, 1)
-    partial = call(
-        forward_kernel, f32(128, VOX), (dense, weights), flops=1 << 30, name="forward"
-    )
-    output = lax.psum_scatter(partial, "ch", scatter_dimension=0, tiled=True)
+    own, *sends = call(
+        forward_kernel, (f32(32, VOX),) + (f32(32, VOX + 2 * FACE),) * 3,
+        (dense, weights, from_lower, from_upper),
+        [pltpu.VMEM((128, VOX), jnp.float32)], flops=1 << 30, name="forward",
+    )
     pieces = call(split_sum_kernel, (f32(PART, 128),) * 4, (keep, came), name="sum_pair")
     others = [swap(pieces[q], 2 * q) for q in (1, 2, 3)]
+    back = call(
+        back_terms_kernel, f32(864, VOX), (weights, grads), flops=1 << 30, name="back_terms"
+    )
     total = call(sum_kernel, f32(PART, 128), (pieces[0], *others), name="sum_four")
-    for mask in (8, 16, 32):
-        total = call(sum_kernel, f32(PART, 128), (total, swap(total, mask)), name="sum_two")
+    shares = [over_ch(sends[m - 1], m) for m in (1, 2, 3)]
+    total = call(sum_kernel, f32(PART, 128), (total, swap(total, 8)), name="sum_two")
+    inner = call(
+        functools.partial(back_inner_kernel, (2, 3, 4), True), f32(32, VOX),
+        (back, rulebook), flops=3 << 30, name="back_inner",
+    )
+    total = call(
+        sum_kernel, f32(PART, 128), (total, *[swap(total, m) for m in (16, 32, 48)]),
+        name="sum_four",
+    )
+    inner = call(
+        functools.partial(back_inner_kernel, (5, 6, 7), False), f32(32, VOX),
+        (back, rulebook, inner), aliases={2: 0}, flops=3 << 30, name="back_inner",
+    )
     even = call(
         join_kernel, f32(4 * PART, 128),
         (total, *[swap(total, 2 * q) for q in (1, 2, 3)]), name="join",
+    )
+    output, grad_features = call(
+        edge_kernel, (bf16(32, VOX), bf16(32, VOX)),
+        (back, rulebook, weights, from_lower, from_upper, inner, own, *shares),
+        [pltpu.VMEM((128, 2 * FACE), jnp.bfloat16), pltpu.VMEM((864, 2 * FACE), jnp.float32),
+         pltpu.VMEM((32, 2 * LANES), jnp.float32)],
+        flops=2 << 30, name="edge",
     )
     odd = swap(even, 1)
     weight_grad = call(
         place_kernel, f32(864, 128), (even, odd),
         [pltpu.VMEM((8 * PART, 128), jnp.float32)], name="place",
     )
-    lower_grads = shifted(high, 1)
-    upper_grads = shifted(low, -1)
-    grad_features = call(
-        back_kernel, bf16(32, VOX), (grads, lower_grads, upper_grads, weights, rulebook),
-        [pltpu.VMEM((864, VOX + 2 * FACE), jnp.float32), pltpu.VMEM((32, VOX), jnp.float32)],
-        flops=5 << 30, name="back",
-    )
-    return (
-        output.astype(jnp.bfloat16),
-        grad_features,
-        weight_grad.reshape(27, 32, 128),
-    )
+    return output, grad_features, weight_grad.reshape(27, 32, 128)
 
 
 def solution(mesh):

time: 84.8 us -> 65.9 us (0.78)
  between operations: 14.2 us -> 0.86 us
  waiting for transfers between devices: 15.4 us -> 8.51 us
  starting transfers between devices: 34.3 us -> 36.4 us
  other arithmetic: 1.54 us -> 0.01 us
    ppermute x11 -> x12, waiting for transfers between devices: 15 us -> 8.49 us  [swap(): return lax.ppermute(value, 'blk', [(i, i ^ mask) for i in range(count)])]
    ppermute x4 -> x2, starting transfers between devices: 7.78 us -> 3.24 us  [shifted(): lax.ppermute(value, 'blk', [(i, (i + steps) % count) for i in range(count)])]
    ppermute x3 -> x6, starting transfers between devices: 4.61 us -> 8.83 us  [over_ch(): return lax.ppermute(value, 'ch', [(i, i ^ mask) for i in range(4)])]
    ppermute x11 -> x12, starting transfers between devices: 21.8 us -> 24.3 us  [swap(): return lax.ppermute(value, 'blk', [(i, i ^ mask) for i in range(count)])]
    convert_element_type x1 -> x0, other arithmetic: 1.54 us -> none  [per_device(): output.astype(jnp.bfloat16)]
    pallas_call x11 -> x13, Pallas kernels: 15.3 us -> 16 us  [call(): pl.pallas_call(kernel, out_shape=outs, in_specs=[VMEM] * len(args), out_s...]
  transfers between devices with their start and end apart: 19 -> 20, of which waited for: 7 -> 5; matrix products, arithmetic and copies ran while one was open for 1% -> 2% of each run, Pallas kernels for 15% -> 21%
where the time goes in v2:
time: 65.9 us; the launch traced here: 65 us
  starting transfers between devices  36.4 us (55%)
  Pallas kernels  16 us (24%)
  waiting for transfers between devices  8.51 us (13%)
  local copies, waits for them, and re-layouts  3.24 us (5%)
  between operations  0.86 us (1%)
    ppermute x12, starting transfers between devices, swap(): return lax.ppermute(value, 'blk', [(i, i ^ mask) for i in range(count)])  24.3 us
    pallas_call x13, Pallas kernels, call(): pl.pallas_call(kernel, out_shape=outs, in_specs=[VMEM] * len(args), out_s...  16 us
    ppermute x6, starting transfers between devices, over_ch(): return lax.ppermute(value, 'ch', [(i, i ^ mask) for i in range(4)])  8.83 us
    ppermute x12, waiting for transfers between devices, swap(): return lax.ppermute(value, 'blk', [(i, i ^ mask) for i in range(count)])  8.49 us
    ppermute x2, starting transfers between devices, shifted(): lax.ppermute(value, 'blk', [(i, (i + steps) % count) for i in range(count)])  3.24 us
    unnamed x10, local copies, waits for them, and re-layouts  1.76 us
    slice x2, local copies, waits for them, and re-layouts, per_device(): lowest = jnp.concatenate([features[:, :FACE], grad_out[:, :FACE]])  1.48 us
  transfers between devices with their start and end apart: 20, of which 5 were waited for; matrix products, arithmetic and copies ran while one was open for 2% of the time, Pallas kernels for 21%

profile of v2, /device:TPU:1, one launch (start us, length us, event | category | flops | bytes accessed | tf_op | source)
XLA Modules:
  0.0 65.0 jit_solution(16845201437180961823)
XLA Ops:
  0.6 2.2 %collective-permute-start.2 = (bf16[32,1024]{1,0:T(8,128)(2,1)}, bf16[32,1024]{1,0:T(8,128)(2,1)S(1)}, u32[]{:S(2)}, u32[]{:S(2)}) collective-permute-start(bf16[32,1024]{1,0:T(8,128)(2,1)} %g0.1), channel_id=1, source_target_pairs={{0,1},{1,0},{2,3},{3,2},{4,5},{5,4},{6,7},{7,6},{8,9},{9,8},{10,11... | collective-permute-start | bytes 196616 | tf_op jit(solution)/shard_map/ppermute | solution.py:239
  2.8 2.6 %collective-permute-start.3 = (bf16[32,1024]{1,0:T(8,128)(2,1)}, bf16[32,1024]{1,0:T(8,128)(2,1)S(1)}, u32[]{:S(2)}, u32[]{:S(2)}) collective-permute-start(bf16[32,1024]{1,0:T(8,128)(2,1)} %g0.1), channel_id=1, source_target_pairs={{0,2},{1,3},{2,0},{3,1},{4,6},{5,7},{6,4},{7,5},{8,10},{9,11},{10,... | collective-permute-start | bytes 196616 | tf_op jit(solution)/shard_map/ppermute | solution.py:239
  5.5 0.8 %fusion.1 = (bf16[32,128]{1,0:T(8,128)(2,1)S(1)}, bf16[32,128]{1,0:T(8,128)(2,1)S(1)}) fusion(bf16[32,1024]{1,0:T(8,128)(2,1)} %g0.1), kind=kLoop, calls=%fused_computation.3 | loop fusion | bytes 32768 | tf_op jit(solution)/shard_map/slice | solution.py:241
  6.2 0.7 %fusion = (bf16[32,128]{1,0:T(8,128)(2,1)S(1)}, bf16[32,128]{1,0:T(8,128)(2,1)S(1)}) fusion(bf16[32,1024]{1,0:T(8,128)(2,1)} %x_ref.1), kind=kLoop, calls=%fused_computation.2 | loop fusion | bytes 32768 | tf_op jit(solution)/shard_map/slice | solution.py:241
  7.0 2.5 %collective-permute-start = (bf16[64,128]{1,0:T(8,128)(2,1)S(1)}, bf16[64,128]{1,0:T(8,128)(2,1)S(1)}, u32[]{:S(2)}, u32[]{:S(2)}) collective-permute-start(bf16[64,128]{1,0:T(8,128)(2,1)S(1)} %pad_maximum_fusion), channel_id=1, source_target_pairs={{0,4},{4,8},{8,12},{12,16},{16,20},{20,24},{24,28},{28,32},{32,36}... | collective-permute-start | bytes 49160 | tf_op jit(solution)/shard_map/ppermute | solution.py:232
  9.5 0.7 %collective-permute-start.1 = (bf16[64,128]{1,0:T(8,128)(2,1)S(1)}, bf16[64,128]{1,0:T(8,128)(2,1)S(1)}, u32[]{:S(2)}, u32[]{:S(2)}) collective-permute-start(bf16[64,128]{1,0:T(8,128)(2,1)S(1)} %pad_maximum_fusion.1), channel_id=1, source_target_pairs={{0,252},{4,0},{8,4},{12,8},{16,12},{20,16},{24,20},{28,24},{32,28}... | collective-permute-start | bytes 49160 | tf_op jit(solution)/shard_map/ppermute | solution.py:232
  10.2 0.8 %copy-done.1 = bf16[32,1024]{1,0:T(8,128)(2,1)S(1)} copy-done((bf16[32,1024]{1,0:T(8,128)(2,1)S(1)}, bf16[32,1024]{1,0:T(8,128)(2,1)}, u32[]{:S(2)}) %copy-start.1) | copy-done | bytes 65560
  11.0 0.9 %copy-done.3 = s32[27,1024]{1,0:T(8,128)S(1)} copy-done((s32[27,1024]{1,0:T(8,128)S(1)}, s32[27,1024]{1,0:T(8,128)}, u32[]{:S(2)}) %copy-start.3) | copy-done | bytes 110616
  11.9 3.9 %gather.1.dense_in = bf16[864,1024]{1,0:T(8,128)(2,1)S(1)} custom-call(bf16[32,1024]{1,0:T(8,128)(2,1)S(1)} %copy-done.1, s32[27,1024]{1,0:T(8,128)S(1)} %copy-done.3), custom_call_target="tpu_custom_call" | custom-call | flops 3221225472 | bytes 1945600 | tf_op jit(solution)/shard_map/gather/pallas_call | solution.py:204
  15.9 1.4 %weight_terms.1 = (bf16[864,1024]{1,0:T(8,128)(2,1)S(1)}, bf16[128,1024]{1,0:T(8,128)(2,1)S(1)}, f32[448,128]{1,0:T(8,128)S(1)}, f32[448,128]{1,0:T(8,128)S(1)}) custom-call(bf16[864,1024]{1,0:T(8,128)(2,1)S(1)} %gather.1.dense_in, s32[27,1024]{1,0:T(8,128)S(1)} %copy-done.4, ...), custom_call_target="tpu_custom_call", output_to_operand_aliasing={{0}: (0, {})} | custom-call | flops 1073741824 | bytes 4665344 | tf_op jit(solution)/shard_map/weight_terms/pallas_call | solution.py:204
  17.3 5.1 %collective-permute-start.8 = (f32[448,128]{1,0:T(8,128)S(1)}, f32[448,128]{1,0:T(8,128)S(1)}, u32[]{:S(2)}, u32[]{:S(2)}) collective-permute-start(f32[448,128]{1,0:T(8,128)S(1)} %get-tuple-element.26), channel_id=1, source_target_pairs={{0,4},{4,0},{8,12},{12,8},{16,20},{20,16},{24,28},{28,24},{32,36},... | collective-permute-start | bytes 688136 | tf_op jit(solution)/shard_map/ppermute | solution.py:227
  22.4 1.1 %collective-permute-done.8.came_ref = f32[448,128]{1,0:T(8,128)S(1)} collective-permute-done((f32[448,128]{1,0:T(8,128)S(1)}, f32[448,128]{1,0:T(8,128)S(1)}, u32[]{:S(2)}, u32[]{:S(2)}) %collective-permute-start.8) | collective-permute-done | bytes 229408 | tf_op jit(solution)/shard_map/ppermute | solution.py:227
  23.6 0.1 collective-permute-start.9
  23.8 3.7 %collective-permute-start.11 = (f32[112,128]{1,0:T(8,128)S(1)}, f32[112,128]{1,0:T(8,128)S(1)}, u32[]{:S(2)}, u32[]{:S(2)}) collective-permute-start(f32[112,128]{1,0:T(8,128)S(1)} %get-tuple-element.30), channel_id=1, source_target_pairs={{0,24},{4,28},{8,16},{12,20},{16,8},{20,12},{24,0},{28,4},{32,56},... | collective-permute-start | bytes 172040 | tf_op jit(solution)/shard_map/ppermute | solution.py:227
  27.5 0.8 %collective-permute-done.10.refs_2_ = f32[112,128]{1,0:T(8,128)S(1)} collective-permute-done((f32[112,128]{1,0:T(8,128)S(1)}, f32[112,128]{1,0:T(8,128)S(1)}, u32[]{:S(2)}, u32[]{:S(2)}) %collective-permute-start.10) | collective-permute-done | bytes 57376 | tf_op jit(solution)/shard_map/ppermute | solution.py:227
  28.3 1.8 %collective-permute-done.11.refs_3_ = f32[112,128]{1,0:T(8,128)S(1)} collective-permute-done((f32[112,128]{1,0:T(8,128)S(1)}, f32[112,128]{1,0:T(8,128)S(1)}, u32[]{:S(2)}, u32[]{:S(2)}) %collective-permute-start.11) | collective-permute-done | bytes 57376 | tf_op jit(solution)/shard_map/ppermute | solution.py:227
  30.1 0.1 collective-permute-start.12
  30.2 0.5 forward.1
  30.8 3.8 %collective-permute-start.6 = (f32[32,1280]{1,0:T(8,128)S(1)}, f32[32,1280]{1,0:T(8,128)S(1)}, u32[]{:S(2)}, u32[]{:S(2)}) collective-permute-start(f32[32,1280]{1,0:T(8,128)S(1)} %get-tuple-element.21), channel_id=1, source_target_pairs={{0,2},{1,3},{2,0},{3,1},{4,6},{5,7},{6,4},{7,5},{8,10},{9,11},{10,... | collective-permute-start | bytes 491528 | tf_op jit(solution)/shard_map/ppermute | solution.py:239
  34.6 3.6 %collective-permute-start.15 = (f32[112,128]{1,0:T(8,128)S(1)}, f32[112,128]{1,0:T(8,128)S(1)}, u32[]{:S(2)}, u32[]{:S(2)}) collective-permute-start(f32[112,128]{1,0:T(8,128)S(1)} %sum_two.1.refs_0_), channel_id=1, source_target_pairs={{0,192},{4,196},{8,200},{12,204},{16,208},{20,212},{24,216},{28,22... | collective-permute-start | bytes 172040 | tf_op jit(solution)/shard_map/ppermute | solution.py:227
  38.2 3.0 %collective-permute-start.14 = (f32[112,128]{1,0:T(8,128)S(1)}, f32[112,128]{1,0:T(8,128)S(1)}, u32[]{:S(2)}, u32[]{:S(2)}) collective-permute-start(f32[112,128]{1,0:T(8,128)S(1)} %sum_two.1.refs_0_), channel_id=1, source_target_pairs={{0,128},{4,132},{8,136},{12,140},{16,144},{20,148},{24,152},{28,15... | collective-permute-start | bytes 172040 | tf_op jit(solution)/shard_map/ppermute | solution.py:227
  41.2 0.6 back_terms.1.refs_0_.terms
  41.9 4.5 %collective-permute-done.14.refs_2_ = f32[112,128]{1,0:T(8,128)S(1)} collective-permute-done((f32[112,128]{1,0:T(8,128)S(1)}, f32[112,128]{1,0:T(8,128)S(1)}, u32[]{:S(2)}, u32[]{:S(2)}) %collective-permute-start.14) | collective-permute-done | bytes 57376 | tf_op jit(solution)/shard_map/ppermute | solution.py:227
  46.4 0.2 collective-permute-done.13.refs_1_
  46.7 1.8 %collective-permute-start.18 = (f32[112,128]{1,0:T(8,128)S(1)}, f32[112,128]{1,0:T(8,128)S(1)}, u32[]{:S(2)}, u32[]{:S(2)}) collective-permute-start(f32[112,128]{1,0:T(8,128)S(1)} %sum_four.3.refs_0_), channel_id=1, source_target_pairs={{0,24},{4,28},{8,16},{12,20},{16,8},{20,12},{24,0},{28,4},{32,56},... | collective-permute-start | bytes 172040 | tf_op jit(solution)/shard_map/ppermute | solution.py:227
  48.5 0.2 collective-permute-start.17
  48.7 1.3 %collective-permute-start.16 = (f32[112,128]{1,0:T(8,128)S(1)}, f32[112,128]{1,0:T(8,128)S(1)}, u32[]{:S(2)}, u32[]{:S(2)}) collective-permute-start(f32[112,128]{1,0:T(8,128)S(1)} %sum_four.3.refs_0_), channel_id=1, source_target_pairs={{0,8},{4,12},{8,0},{12,4},{16,24},{20,28},{24,16},{28,20},{32,40},... | collective-permute-start | bytes 172040 | tf_op jit(solution)/shard_map/ppermute | solution.py:227
  50.0 3.2 %back_inner.2.refs_2_ = f32[32,1024]{1,0:T(8,128)S(1)} custom-call(f32[864,1024]{1,0:T(8,128)S(1)} %back_terms.1.refs_0_.terms, s32[27,1024]{1,0:T(8,128)S(1)} %copy-done.4), custom_call_target="tpu_custom_call" | custom-call | flops 3221225472 | bytes 3780608 | tf_op jit(solution)/shard_map/back_inner/pallas_call | solution.py:204
  53.4 5.3 %collective-permute-start.19 = (f32[448,128]{1,0:T(8,128)S(1)}, f32[448,128]{1,0:T(8,128)S(1)}, u32[]{:S(2)}, u32[]{:S(2)}) collective-permute-start(f32[448,128]{1,0:T(8,128)S(1)} %join.1.even_ref), channel_id=1, source_target_pairs={{0,4},{4,0},{8,12},{12,8},{16,20},{20,16},{24,28},{28,24},{32,36},... | collective-permute-start | bytes 688136 | tf_op jit(solution)/shard_map/ppermute | solution.py:227
  58.6 3.2 %back_inner.3.inner = f32[32,1024]{1,0:T(8,128)S(1)} custom-call(f32[864,1024]{1,0:T(8,128)S(1)} %back_terms.1.refs_0_.terms, s32[27,1024]{1,0:T(8,128)S(1)} %copy-done.4, f32[32,1024]{1,0:T(8,128)S(1)} %back_inner.2.refs_2_), custom_call_target="tpu_custom_call", output_to_operand_aliasing={{}: (2, {})} | custom-call | flops 3221225472 | bytes 3911680 | tf_op jit(solution)/shard_map/back_inner/pallas_call | solution.py:204
  61.9 2.4 %edge.1 = (bf16[32,1024]{1,0:T(8,128)(2,1)}, bf16[32,1024]{1,0:T(8,128)(2,1)}) custom-call(f32[864,1024]{1,0:T(8,128)S(1)} %back_terms.1.refs_0_.terms, s32[27,1024]{1,0:T(8,128)S(1)} %copy-done.4, bf16[864,128]{1,0:T(8,128)(2,1)S(1)} %bitcast.4, bf16[64,128]{1,0:T(8,128)(2,1)S(1)} %collective-permute-done.lower_ref, ...), custom_call_target="tpu_custom_call" | custom-call | flops 2147483648 | bytes 4788224 | tf_op jit(solution)/shard_map/edge/pallas_call | solution.py:204
  64.2 0.8 %place.1 = f32[864,128]{1,0:T(8,128)} custom-call(f32[448,128]{1,0:T(8,128)S(1)} %join.1.even_ref, f32[448,128]{1,0:T(8,128)S(1)} %collective-permute-done.19.odd_ref), custom_call_target="tpu_custom_call" | custom-call | bytes 901120 | tf_op jit(solution)/shard_map/place/pallas_call | solution.py:204
  (35 shorter events, 0.4 us)
Async XLA Ops:
  0.6 15.2 %collective-permute-start.2 = (bf16[32,1024]{1,0:T(8,128)(2,1)}, bf16[32,1024]{1,0:T(8,128)(2,1)S(1)}, u32[]{:S(2)}, u32[]{:S(2)}) collective-permute-start(bf16[32,1024]{1,0:T(8,128)(2,1)} %g0.1), channel_id=1, source_target_pairs={{0,1},{1,0},{2,3},{3,2},{4,5},{5,4},{6,7},{7,6},{8,9},{9,8},{10,11... | collective-permute-start | bytes 196616 | tf_op jit(solution)/shard_map/ppermute | solution.py:239
  2.8 13.0 %collective-permute-start.3 = (bf16[32,1024]{1,0:T(8,128)(2,1)}, bf16[32,1024]{1,0:T(8,128)(2,1)S(1)}, u32[]{:S(2)}, u32[]{:S(2)}) collective-permute-start(bf16[32,1024]{1,0:T(8,128)(2,1)} %g0.1), channel_id=1, source_target_pairs={{0,2},{1,3},{2,0},{3,1},{4,6},{5,7},{6,4},{7,5},{8,10},{9,11},{10,... | collective-permute-start | bytes 196616 | tf_op jit(solution)/shard_map/ppermute | solution.py:239
  5.5 10.4 %collective-permute-start.4 = (bf16[32,1024]{1,0:T(8,128)(2,1)}, bf16[32,1024]{1,0:T(8,128)(2,1)S(1)}, u32[]{:S(2)}, u32[]{:S(2)}) collective-permute-start(bf16[32,1024]{1,0:T(8,128)(2,1)} %g0.1), channel_id=1, source_target_pairs={{0,3},{1,2},{2,1},{3,0},{4,7},{5,6},{6,5},{7,4},{8,11},{9,10},{10,... | collective-permute-start | bytes 196616 | tf_op jit(solution)/shard_map/ppermute | solution.py:239
  7.0 8.9 %collective-permute-start = (bf16[64,128]{1,0:T(8,128)(2,1)S(1)}, bf16[64,128]{1,0:T(8,128)(2,1)S(1)}, u32[]{:S(2)}, u32[]{:S(2)}) collective-permute-start(bf16[64,128]{1,0:T(8,128)(2,1)S(1)} %pad_maximum_fusion), channel_id=1, source_target_pairs={{0,4},{4,8},{8,12},{12,16},{16,20},{20,24},{24,28},{28,32},{32,36}... | collective-permute-start | bytes 49160 | tf_op jit(solution)/shard_map/ppermute | solution.py:232
  9.5 6.4 %collective-permute-start.1 = (bf16[64,128]{1,0:T(8,128)(2,1)S(1)}, bf16[64,128]{1,0:T(8,128)(2,1)S(1)}, u32[]{:S(2)}, u32[]{:S(2)}) collective-permute-start(bf16[64,128]{1,0:T(8,128)(2,1)S(1)} %pad_maximum_fusion.1), channel_id=1, source_target_pairs={{0,252},{4,0},{8,4},{12,8},{16,12},{20,16},{24,20},{28,24},{32,28}... | collective-permute-start | bytes 49160 | tf_op jit(solution)/shard_map/ppermute | solution.py:232
  10.2 0.8 %copy-start.1 = (bf16[32,1024]{1,0:T(8,128)(2,1)S(1)}, bf16[32,1024]{1,0:T(8,128)(2,1)}, u32[]{:S(2)}) copy-start(bf16[32,1024]{1,0:T(8,128)(2,1)} %x_ref.1) | copy-start | bytes 196612
  11.0 0.9 %copy-start.3 = (s32[27,1024]{1,0:T(8,128)S(1)}, s32[27,1024]{1,0:T(8,128)}, u32[]{:S(2)}) copy-start(s32[27,1024]{1,0:T(8,128)} %rule_ref.5) | copy-start | bytes 331780
  11.9 3.9 %copy-start.2 = (bf16[32,1024]{1,0:T(8,128)(2,1)S(1)}, bf16[32,1024]{1,0:T(8,128)(2,1)}, u32[]{:S(2)}) copy-start(bf16[32,1024]{1,0:T(8,128)(2,1)} %g0.1) | copy-start | bytes 196612
  11.9 3.9 %copy-start.4 = (s32[27,1024]{1,0:T(8,128)S(1)}, s32[27,1024]{1,0:T(8,128)}, u32[]{:S(2)}) copy-start(s32[27,1024]{1,0:T(8,128)} %rule_ref.5) | copy-start | bytes 331780
  15.8 14.4 %copy-start = (bf16[27,32,128]{2,1,0:T(8,128)(2,1)S(1)}, bf16[27,32,128]{2,1,0:T(8,128)(2,1)}, u32[]{:S(2)}) copy-start(bf16[27,32,128]{2,1,0:T(8,128)(2,1)} %param.5) | copy-start | bytes 663556
  17.3 6.2 %collective-permute-start.8 = (f32[448,128]{1,0:T(8,128)S(1)}, f32[448,128]{1,0:T(8,128)S(1)}, u32[]{:S(2)}, u32[]{:S(2)}) collective-permute-start(f32[448,128]{1,0:T(8,128)S(1)} %get-tuple-element.26), channel_id=1, source_target_pairs={{0,4},{4,0},{8,12},{12,8},{16,20},{20,16},{24,28},{28,24},{32,36},... | collective-permute-start | bytes 688136 | tf_op jit(solution)/shard_map/ppermute | solution.py:227
  23.6 3.9 %collective-permute-start.9 = (f32[112,128]{1,0:T(8,128)S(1)}, f32[112,128]{1,0:T(8,128)S(1)}, u32[]{:S(2)}, u32[]{:S(2)}) collective-permute-start(f32[112,128]{1,0:T(8,128)S(1)} %get-tuple-element.28), channel_id=1, source_target_pairs={{0,8},{4,12},{8,0},{12,4},{16,24},{20,28},{24,16},{28,20},{32,40},... | collective-permute-start | bytes 172040 | tf_op jit(solution)/shard_map/ppermute | solution.py:227
  23.7 4.6 %collective-permute-start.10 = (f32[112,128]{1,0:T(8,128)S(1)}, f32[112,128]{1,0:T(8,128)S(1)}, u32[]{:S(2)}, u32[]{:S(2)}) collective-permute-start(f32[112,128]{1,0:T(8,128)S(1)} %get-tuple-element.29), channel_id=1, source_target_pairs={{0,16},{4,20},{8,24},{12,28},{16,0},{20,4},{24,8},{28,12},{32,48},... | collective-permute-start | bytes 172040 | tf_op jit(solution)/shard_map/ppermute | solution.py:227
  23.8 6.3 %collective-permute-start.11 = (f32[112,128]{1,0:T(8,128)S(1)}, f32[112,128]{1,0:T(8,128)S(1)}, u32[]{:S(2)}, u32[]{:S(2)}) collective-permute-start(f32[112,128]{1,0:T(8,128)S(1)} %get-tuple-element.30), channel_id=1, source_target_pairs={{0,24},{4,28},{8,16},{12,20},{16,8},{20,12},{24,0},{28,4},{32,56},... | collective-permute-start | bytes 172040 | tf_op jit(solution)/shard_map/ppermute | solution.py:227
  30.1 4.5 %collective-permute-start.12 = (f32[112,128]{1,0:T(8,128)S(1)}, f32[112,128]{1,0:T(8,128)S(1)}, u32[]{:S(2)}, u32[]{:S(2)}) collective-permute-start(f32[112,128]{1,0:T(8,128)S(1)} %sum_four.2.refs_0_), channel_id=1, source_target_pairs={{0,32},{4,36},{8,40},{12,44},{16,48},{20,52},{24,56},{28,60},{32,0... | collective-permute-start | bytes 172040 | tf_op jit(solution)/shard_map/ppermute | solution.py:227
  30.7 31.1 %collective-permute-start.5 = (f32[32,1280]{1,0:T(8,128)S(1)}, f32[32,1280]{1,0:T(8,128)S(1)}, u32[]{:S(2)}, u32[]{:S(2)}) collective-permute-start(f32[32,1280]{1,0:T(8,128)S(1)} %get-tuple-element.20), channel_id=1, source_target_pairs={{0,1},{1,0},{2,3},{3,2},{4,5},{5,4},{6,7},{7,6},{8,9},{9,8},{10,11... | collective-permute-start | bytes 491528 | tf_op jit(solution)/shard_map/ppermute | solution.py:239
  30.8 31.0 %collective-permute-start.6 = (f32[32,1280]{1,0:T(8,128)S(1)}, f32[32,1280]{1,0:T(8,128)S(1)}, u32[]{:S(2)}, u32[]{:S(2)}) collective-permute-start(f32[32,1280]{1,0:T(8,128)S(1)} %get-tuple-element.21), channel_id=1, source_target_pairs={{0,2},{1,3},{2,0},{3,1},{4,6},{5,7},{6,4},{7,5},{8,10},{9,11},{10,... | collective-permute-start | bytes 491528 | tf_op jit(solution)/shard_map/ppermute | solution.py:239
  34.6 7.2 %collective-permute-start.15 = (f32[112,128]{1,0:T(8,128)S(1)}, f32[112,128]{1,0:T(8,128)S(1)}, u32[]{:S(2)}, u32[]{:S(2)}) collective-permute-start(f32[112,128]{1,0:T(8,128)S(1)} %sum_two.1.refs_0_), channel_id=1, source_target_pairs={{0,192},{4,196},{8,200},{12,204},{16,208},{20,212},{24,216},{28,22... | collective-permute-start | bytes 172040 | tf_op jit(solution)/shard_map/ppermute | solution.py:227
  38.2 8.2 %collective-permute-start.14 = (f32[112,128]{1,0:T(8,128)S(1)}, f32[112,128]{1,0:T(8,128)S(1)}, u32[]{:S(2)}, u32[]{:S(2)}) collective-permute-start(f32[112,128]{1,0:T(8,128)S(1)} %sum_two.1.refs_0_), channel_id=1, source_target_pairs={{0,128},{4,132},{8,136},{12,140},{16,144},{20,148},{24,152},{28,15... | collective-permute-start | bytes 172040 | tf_op jit(solution)/shard_map/ppermute | solution.py:227
  41.2 5.4 %collective-permute-start.13 = (f32[112,128]{1,0:T(8,128)S(1)}, f32[112,128]{1,0:T(8,128)S(1)}, u32[]{:S(2)}, u32[]{:S(2)}) collective-permute-start(f32[112,128]{1,0:T(8,128)S(1)} %sum_two.1.refs_0_), channel_id=1, source_target_pairs={{0,64},{4,68},{8,72},{12,76},{16,80},{20,84},{24,88},{28,92},{32,9... | collective-permute-start | bytes 172040 | tf_op jit(solution)/shard_map/ppermute | solution.py:227
  46.7 6.5 %collective-permute-start.18 = (f32[112,128]{1,0:T(8,128)S(1)}, f32[112,128]{1,0:T(8,128)S(1)}, u32[]{:S(2)}, u32[]{:S(2)}) collective-permute-start(f32[112,128]{1,0:T(8,128)S(1)} %sum_four.3.refs_0_), channel_id=1, source_target_pairs={{0,24},{4,28},{8,16},{12,20},{16,8},{20,12},{24,0},{28,4},{32,56},... | collective-permute-start | bytes 172040 | tf_op jit(solution)/shard_map/ppermute | solution.py:227
  48.5 4.9 %collective-permute-start.17 = (f32[112,128]{1,0:T(8,128)S(1)}, f32[112,128]{1,0:T(8,128)S(1)}, u32[]{:S(2)}, u32[]{:S(2)}) collective-permute-start(f32[112,128]{1,0:T(8,128)S(1)} %sum_four.3.refs_0_), channel_id=1, source_target_pairs={{0,16},{4,20},{8,24},{12,28},{16,0},{20,4},{24,8},{28,12},{32,48},... | collective-permute-start | bytes 172040 | tf_op jit(solution)/shard_map/ppermute | solution.py:227
  48.7 4.7 %collective-permute-start.16 = (f32[112,128]{1,0:T(8,128)S(1)}, f32[112,128]{1,0:T(8,128)S(1)}, u32[]{:S(2)}, u32[]{:S(2)}) collective-permute-start(f32[112,128]{1,0:T(8,128)S(1)} %sum_four.3.refs_0_), channel_id=1, source_target_pairs={{0,8},{4,12},{8,0},{12,4},{16,24},{20,28},{24,16},{28,20},{32,40},... | collective-permute-start | bytes 172040 | tf_op jit(solution)/shard_map/ppermute | solution.py:227
  53.2 8.6 %collective-permute-start.7 = (f32[32,1280]{1,0:T(8,128)S(1)}, f32[32,1280]{1,0:T(8,128)S(1)}, u32[]{:S(2)}, u32[]{:S(2)}) collective-permute-start(f32[32,1280]{1,0:T(8,128)S(1)} %get-tuple-element.22), channel_id=1, source_target_pairs={{0,3},{1,2},{2,1},{3,0},{4,7},{5,6},{6,5},{7,4},{8,11},{9,10},{10,... | collective-permute-start | bytes 491528 | tf_op jit(solution)/shard_map/ppermute | solution.py:239
  53.4 10.8 %collective-permute-start.19 = (f32[448,128]{1,0:T(8,128)S(1)}, f32[448,128]{1,0:T(8,128)S(1)}, u32[]{:S(2)}, u32[]{:S(2)}) collective-permute-start(f32[448,128]{1,0:T(8,128)S(1)} %join.1.even_ref), channel_id=1, source_target_pairs={{0,4},{4,0},{8,12},{12,8},{16,20},{20,16},{24,28},{28,24},{32,36},... | collective-permute-start | bytes 688136 | tf_op jit(solution)/shard_map/ppermute | solution.py:227

commit v3 on v2

--- a/solution.py
+++ b/solution.py
@@ -12,6 +12,7 @@
 LANES = 128
 PART = 112
 INNER = tuple(range(2, 8))
+EDGE = (0, 1, 7)
 VMEM = pl.BlockSpec(memory_space=pltpu.VMEM)
 
 
@@ -37,6 +38,22 @@
 
 def tile_span(t):
     return slice(LANES * t, LANES * (t + 1))
+
+
+def faces_kernel(x_ref, g_ref, near_ref, far_ref):
+    odd = (lax.axis_index("blk") & 1) == 1
+    for rows, ref in ((slice(0, 32), x_ref), (slice(32, 64), g_ref)):
+        lowest = ref[:, :FACE].astype(jnp.float32)
+        highest = ref[:, FACE : 2 * FACE].astype(jnp.float32)
+        near_ref[rows, :] = jnp.where(odd, lowest, highest).astype(jnp.bfloat16)
+        far_ref[rows, :] = jnp.where(odd, highest, lowest).astype(jnp.bfloat16)
+
+
+def by_side(near, far):
+    odd = (lax.axis_index("blk") & 1) == 1
+    near = near.astype(jnp.float32)
+    far = far.astype(jnp.float32)
+    return jnp.where(odd, near, far), jnp.where(odd, far, near)
 
 
 def gather_kernel(x_ref, rule_ref, dense_ref, table):
@@ -59,15 +76,14 @@
 
 
 def weight_kernel(
-    dense_in, rule_ref, lower_ref, upper_ref, g0, g1, g2, g3,
+    dense_in, rule_ref, near_ref, far_ref, g0, g1, g2, g3,
     dense_ref, grad_ref, keep_ref, send_ref, faces, terms,
 ):
     chan = lax.axis_index("ch")
-    near = lax.axis_index("blk") & 7
+    spot = lax.axis_index("blk") & 7
     for m, part in enumerate((g0, g1, g2, g3)):
         grad_ref[pl.ds(pl.multiple_of(32 * (chan ^ m), 32), 32), :] = part[...]
-    faces[:, :FACE] = lower_ref[:32, :].astype(jnp.float32)
-    faces[:, FACE:] = upper_ref[:32, :].astype(jnp.float32)
+    faces[:, :FACE], faces[:, FACE:] = by_side(near_ref[:32, :], far_ref[:32, :])
 
     def step(j, carry):
         for group, d in ((0, 0), (1, 2)):
@@ -86,22 +102,23 @@
     terms[864:, :] = jnp.zeros((32, LANES), jnp.float32)
     for q in range(4):
         for odd, target in ((0, keep_ref), (1, send_ref)):
-            start = pl.multiple_of(PART * (near ^ (2 * q + odd)), 8)
+            start = pl.multiple_of(PART * (spot ^ (2 * q + odd)), 8)
             target[PART * q : PART * (q + 1), :] = terms[pl.ds(start, PART), :]
 
 
-def forward_kernel(dense_ref, weight_ref, lower_ref, upper_ref, own, s1, s2, s3, sums):
+def forward_kernel(dense_ref, weight_ref, near_ref, far_ref, own, s1, s2, s3, sums):
     chan = lax.axis_index("ch")
     sums[...] = lax.dot_general(
         weight_ref[...], dense_ref[...], (((0,), (0,)), ((), ())),
         preferred_element_type=jnp.float32,
     )
+    lower, upper = by_side(near_ref[32:, :], far_ref[32:, :])
     for m, target in enumerate((own, s1, s2, s3)):
         rows = pl.ds(pl.multiple_of(32 * (chan ^ m), 32), 32)
         target[:, :VOX] = sums[rows, :]
         if m:
-            target[:, VOX : VOX + FACE] = lower_ref[32:, :].astype(jnp.float32)
-            target[:, VOX + FACE :] = upper_ref[32:, :].astype(jnp.float32)
+            target[:, VOX : VOX + FACE] = lower
+            target[:, VOX + FACE :] = upper
 
 
 def back_terms_kernel(weight_ref, grad_ref, terms_ref):
@@ -110,7 +127,7 @@
     )
 
 
-def back_inner_kernel(groups, fresh, *refs):
+def back_inner_kernel(groups, *refs):
     terms, rule_ref = refs[0], refs[1]
     out_ref = refs[-1]
     for group in groups:
@@ -133,15 +150,16 @@
 
 
 def edge_kernel(
-    terms, rule_ref, weight_ref, lower_ref, upper_ref, inner, own, r1, r2, r3,
+    terms, rule_ref, weight_ref, near_ref, far_ref, inner, own, r1, r2, r3,
     out_ref, grad_ref, faces, products, total,
 ):
     chan = lax.axis_index("ch")
     summed = (own[...] + r1[:, :VOX]) + (r2[:, :VOX] + r3[:, :VOX])
     out_ref[...] = summed.astype(jnp.bfloat16)
     rows = pl.ds(pl.multiple_of(32 * chan, 32), 32)
-    faces[rows, :FACE] = lower_ref[32:, :]
-    faces[rows, FACE:] = upper_ref[32:, :]
+    lower, upper = by_side(near_ref[32:, :], far_ref[32:, :])
+    faces[rows, :FACE] = lower.astype(jnp.bfloat16)
+    faces[rows, FACE:] = upper.astype(jnp.bfloat16)
     for m, part in enumerate((r1, r2, r3)):
         rows = pl.ds(pl.multiple_of(32 * (chan ^ (m + 1)), 32), 32)
         faces[rows, :] = part[:, VOX:].astype(jnp.bfloat16)
@@ -152,7 +170,7 @@
 
     def step(j, carry):
         rules = [rule_ref[pl.ds(3 * j + d, 1), :] for d in range(3)]
-        for group in range(2):
+        for group in EDGE:
             running = total[:, tile_span(group)]
             for d in range(3):
                 rows = pl.ds(pl.multiple_of(32 * (26 - 3 * j - d), 32), 32)
@@ -165,8 +183,9 @@
         return carry
 
     lax.fori_loop(0, 9, step, 0)
-    grad_ref[:, : 2 * LANES] = total[...].astype(jnp.bfloat16)
-    grad_ref[:, 2 * LANES :] = inner[:, 2 * LANES :].astype(jnp.bfloat16)
+    for group in range(8):
+        source = total if group in EDGE else inner
+        grad_ref[:, tile_span(group)] = source[:, tile_span(group)].astype(jnp.bfloat16)
 
 
 def split_sum_kernel(keep_ref, came_ref, *outs):
@@ -188,14 +207,14 @@
 
 
 def place_kernel(even_ref, odd_ref, out_ref, held):
-    near = lax.axis_index("blk") & 7
+    spot = lax.axis_index("blk") & 7
     for q in range(4):
         rows = slice(PART * q, PART * (q + 1))
         held[2 * PART * q : 2 * PART * q + PART, :] = even_ref[rows, :]
         held[2 * PART * q + PART : 2 * PART * (q + 1), :] = odd_ref[rows, :]
     for p in range(8):
         count = min(PART, 864 - PART * p)
-        start = pl.multiple_of(PART * (near ^ p), 8)
+        start = pl.multiple_of(PART * (spot ^ p), 8)
         out_ref[PART * p : PART * p + count, :] = held[pl.ds(start, count), :]
 
 
@@ -227,9 +246,14 @@
     return lax.ppermute(value, "blk", [(i, i ^ mask) for i in range(count)])
 
 
-def shifted(value, steps):
+def swap_far(value):
     count = lax.axis_size("blk")
-    return lax.ppermute(value, "blk", [(i, (i + steps) % count) for i in range(count)])
+    pairs = [(i, (i + 1 if i % 2 else i - 1) % count) for i in range(count)]
+    return lax.ppermute(value, "blk", pairs)
+
+
+def after(values, *others):
+    return lax.optimization_barrier((*values, *others))[: len(values)]
 
 
 def per_device(features, weight, grad_out, rulebook):
@@ -238,59 +262,61 @@
     def over_ch(value, mask):
         return lax.ppermute(value, "ch", [(i, i ^ mask) for i in range(4)])
 
-    lowest = jnp.concatenate([features[:, :FACE], grad_out[:, :FACE]])
-    highest = jnp.concatenate([features[:, FACE : 2 * FACE], grad_out[:, FACE : 2 * FACE]])
-    parts = [over_ch(grad_out, m) for m in (1, 2, 3)]
-    from_lower = shifted(highest, 1)
-    from_upper = shifted(lowest, -1)
+    x, g, rules = features, grad_out, rulebook
+    near, far = call(faces_kernel, (bf16(64, FACE),) * 2, (x, g), name="faces")
+    near = swap(near, 1)
+    far = swap_far(far)
+    parts = [over_ch(g, m) for m in (1, 2, 3)]
     dense = call(
-        gather_kernel, bf16(864, VOX), (features, rulebook),
+        gather_kernel, bf16(864, VOX), (x, rules),
         [pltpu.VMEM((32, VOX), jnp.float32)], flops=3 << 30, name="gather",
     )
     dense, grads, keep, send = call(
         weight_kernel,
         (bf16(864, VOX), bf16(128, VOX), f32(4 * PART, 128), f32(4 * PART, 128)),
-        (dense, rulebook, from_lower, from_upper, grad_out, *parts),
+        (dense, rules, near, far, g, *parts),
         [pltpu.VMEM((32, 2 * FACE), jnp.float32), pltpu.VMEM((8 * PART, 128), jnp.float32)],
         aliases={0: 0}, flops=1 << 30, name="weight_terms",
     )
     came = swap(send, 1)
     own, *sends = call(
         forward_kernel, (f32(32, VOX),) + (f32(32, VOX + 2 * FACE),) * 3,
-        (dense, weights, from_lower, from_upper),
+        (dense, weights, near, far),
         [pltpu.VMEM((128, VOX), jnp.float32)], flops=1 << 30, name="forward",
     )
+    back = call(
+        back_terms_kernel, f32(864, VOX), (weights, grads), flops=1 << 30, name="back_terms"
+    )
+    came, = after((came,), own, back)
     pieces = call(split_sum_kernel, (f32(PART, 128),) * 4, (keep, came), name="sum_pair")
     others = [swap(pieces[q], 2 * q) for q in (1, 2, 3)]
-    back = call(
-        back_terms_kernel, f32(864, VOX), (weights, grads), flops=1 << 30, name="back_terms"
-    )
+    shares = [over_ch(send, m) for m, send in zip((1, 2, 3), after(sends, *pieces))]
+    others = after(others, *shares)
     total = call(sum_kernel, f32(PART, 128), (pieces[0], *others), name="sum_four")
-    shares = [over_ch(sends[m - 1], m) for m in (1, 2, 3)]
-    total = call(sum_kernel, f32(PART, 128), (total, swap(total, 8)), name="sum_two")
+    pair = swap(total, 8)
     inner = call(
-        functools.partial(back_inner_kernel, (2, 3, 4), True), f32(32, VOX),
-        (back, rulebook), flops=3 << 30, name="back_inner",
-    )
-    total = call(
-        sum_kernel, f32(PART, 128), (total, *[swap(total, m) for m in (16, 32, 48)]),
-        name="sum_four",
-    )
+        functools.partial(back_inner_kernel, (2, 3)), f32(32, VOX),
+        (back, rules), flops=2 << 30, name="back_inner",
+    )
+    pair, = after((pair,), inner)
+    total = call(sum_kernel, f32(PART, 128), (total, pair), name="sum_two")
+    others = [swap(total, m) for m in (16, 32, 48)]
     inner = call(
-        functools.partial(back_inner_kernel, (5, 6, 7), False), f32(32, VOX),
-        (back, rulebook, inner), aliases={2: 0}, flops=3 << 30, name="back_inner",
-    )
-    even = call(
-        join_kernel, f32(4 * PART, 128),
-        (total, *[swap(total, 2 * q) for q in (1, 2, 3)]), name="join",
-    )
+        functools.partial(back_inner_kernel, (4, 5, 6)), f32(32, VOX),
+        (back, rules, inner), aliases={2: 0}, flops=3 << 30, name="back_inner",
+    )
+    others = after(others, inner)
+    total = call(sum_kernel, f32(PART, 128), (total, *others), name="sum_four")
+    others = [swap(total, 2 * q) for q in (1, 2, 3)]
     output, grad_features = call(
         edge_kernel, (bf16(32, VOX), bf16(32, VOX)),
-        (back, rulebook, weights, from_lower, from_upper, inner, own, *shares),
+        (back, rules, weights, near, far, inner, own, *shares),
         [pltpu.VMEM((128, 2 * FACE), jnp.bfloat16), pltpu.VMEM((864, 2 * FACE), jnp.float32),
-         pltpu.VMEM((32, 2 * LANES), jnp.float32)],
+         pltpu.VMEM((32, VOX), jnp.float32)],
         flops=2 << 30, name="edge",
     )
+    others = after(others, output)
+    even = call(join_kernel, f32(4 * PART, 128), (total, *others), name="join")
     odd = swap(even, 1)
     weight_grad = call(
         place_kernel, f32(864, 128), (even, odd),

time: 65.9 us -> 63.3 us (0.961); the launches traced: 65 us -> 63.1 us
  starting transfers between devices: 36.4 us -> 32 us
  waiting for transfers between devices: 8.51 us -> 11.7 us
    ppermute x2 -> x1, starting transfers between devices: 3.24 us -> 0.01 us  [swap_far(): return lax.ppermute(value, 'blk', pairs)]
    ppermute x6, waiting for transfers between devices: 0.02 us -> 2.41 us  [over_ch(): return lax.ppermute(value, 'ch', [(i, i ^ mask) for i in range(4)])]
    slice x2 -> x0, local copies, waits for them, and re-layouts: 1.48 us -> none  [per_device(): lowest = jnp.concatenate([features[:, :FACE], grad_out[:, :FACE]])]
    ppermute x12 -> x13, starting transfers between devices: 24.3 us -> 23.4 us  [swap(): return lax.ppermute(value, 'blk', [(i, i ^ mask) for i in range(count)])]
    unnamed x10 -> x12, local copies, waits for them, and re-layouts: 1.76 us -> 2.63 us
    ppermute x12 -> x13, waiting for transfers between devices: 8.49 us -> 9.26 us  [swap(): return lax.ppermute(value, 'blk', [(i, i ^ mask) for i in range(count)])]
    pallas_call x13 -> x14, Pallas kernels: 16 us -> 16 us  [call(): pl.pallas_call(kernel, out_shape=outs, in_specs=[VMEM] * len(args), out_s...]
  transfers between devices with their start and end apart: 20 -> 20, of which waited for: 5 -> 7; matrix products, arithmetic and copies ran while one was open for 2% -> 0% of each run, Pallas kernels for 21% -> 22%
where the time goes in v3:
time: 63.3 us; the launch traced here: 63.1 us
  starting transfers between devices  32 us (51%)
  Pallas kernels  16 us (25%)
  waiting for transfers between devices  11.7 us (18%)
  local copies, waits for them, and re-layouts  2.63 us (4%)
  between operations  0.8 us (1%)
    ppermute x13, starting transfers between devices, swap(): return lax.ppermute(value, 'blk', [(i, i ^ mask) for i in range(count)])  23.4 us
    pallas_call x14, Pallas kernels, call(): pl.pallas_call(kernel, out_shape=outs, in_specs=[VMEM] * len(args), out_s...  16 us
    ppermute x13, waiting for transfers between devices, swap(): return lax.ppermute(value, 'blk', [(i, i ^ mask) for i in range(count)])  9.26 us
    ppermute x6, starting transfers between devices, over_ch(): return lax.ppermute(value, 'ch', [(i, i ^ mask) for i in range(4)])  8.55 us
    unnamed x12, local copies, waits for them, and re-layouts  2.63 us
    ppermute x6, waiting for transfers between devices, over_ch(): return lax.ppermute(value, 'ch', [(i, i ^ mask) for i in range(4)])  2.41 us
  transfers between devices with their start and end apart: 20, of which 7 were waited for; matrix products, arithmetic and copies ran while one was open for 0% of the time, Pallas kernels for 22%

profile of v3, /device:TPU:1, one launch (start us, length us, event | category | flops | bytes accessed | tf_op | source)
XLA Modules:
  0.0 63.1 jit_solution(12285094595000227024)
XLA Ops:
  0.6 3.8 %collective-permute-start.3 = (bf16[32,1024]{1,0:T(8,128)(2,1)}, bf16[32,1024]{1,0:T(8,128)(2,1)S(1)}, u32[]{:S(2)}, u32[]{:S(2)}) collective-permute-start(bf16[32,1024]{1,0:T(8,128)(2,1)} %g0.1), channel_id=1, source_target_pairs={{0,2},{1,3},{2,0},{3,1},{4,6},{5,7},{6,4},{7,5},{8,10},{9,11},{10,... | collective-permute-start | bytes 196616 | tf_op jit(solution)/shard_map/ppermute | solution.py:263
  4.5 0.4 collective-permute-start.2
  4.9 0.4 collective-permute-start.4
  5.2 0.8 %copy-done.1 = bf16[32,1024]{1,0:T(8,128)(2,1)S(1)} copy-done((bf16[32,1024]{1,0:T(8,128)(2,1)S(1)}, bf16[32,1024]{1,0:T(8,128)(2,1)}, u32[]{:S(2)}) %copy-start.1) | copy-done | bytes 65560
  6.1 0.8 %copy-done.2 = bf16[32,1024]{1,0:T(8,128)(2,1)S(1)} copy-done((bf16[32,1024]{1,0:T(8,128)(2,1)S(1)}, bf16[32,1024]{1,0:T(8,128)(2,1)}, u32[]{:S(2)}) %copy-start.2) | copy-done | bytes 65560
  6.9 2.9 %collective-permute-start = (bf16[64,128]{1,0:T(8,128)(2,1)S(1)}, bf16[64,128]{1,0:T(8,128)(2,1)S(1)}, u32[]{:S(2)}, u32[]{:S(2)}) collective-permute-start(bf16[64,128]{1,0:T(8,128)(2,1)S(1)} %get-tuple-element.33), channel_id=1, source_target_pairs={{0,4},{4,0},{8,12},{12,8},{16,20},{20,16},{24,28},{28,24},{32,36},... | collective-permute-start | bytes 49160 | tf_op jit(solution)/shard_map/ppermute | solution.py:246
  9.8 0.9 %copy-done.4 = s32[27,1024]{1,0:T(8,128)S(1)} copy-done((s32[27,1024]{1,0:T(8,128)S(1)}, s32[27,1024]{1,0:T(8,128)}, u32[]{:S(2)}) %copy-start.4) | copy-done | bytes 110616
  10.8 3.9 %gather.1.dense_in = bf16[864,1024]{1,0:T(8,128)(2,1)S(1)} custom-call(bf16[32,1024]{1,0:T(8,128)(2,1)S(1)} %copy-done.1, s32[27,1024]{1,0:T(8,128)S(1)} %copy-done.4), custom_call_target="tpu_custom_call" | custom-call | flops 3221225472 | bytes 1945600 | tf_op jit(solution)/shard_map/gather/pallas_call | solution.py:223
  14.7 1.4 %weight_terms.1 = (bf16[864,1024]{1,0:T(8,128)(2,1)S(1)}, bf16[128,1024]{1,0:T(8,128)(2,1)S(1)}, f32[448,128]{1,0:T(8,128)S(1)}, f32[448,128]{1,0:T(8,128)S(1)}) custom-call(bf16[864,1024]{1,0:T(8,128)(2,1)S(1)} %gather.1.dense_in, s32[27,1024]{1,0:T(8,128)S(1)} %copy-done.5, ...), custom_call_target="tpu_custom_call", output_to_operand_aliasing={{0}: (0, {})} | custom-call | flops 1073741824 | bytes 4665344 | tf_op jit(solution)/shard_map/weight_terms/pallas_call | solution.py:223
  16.1 6.6 %collective-permute-start.5 = (f32[448,128]{1,0:T(8,128)S(1)}, f32[448,128]{1,0:T(8,128)S(1)}, u32[]{:S(2)}, u32[]{:S(2)}) collective-permute-start(f32[448,128]{1,0:T(8,128)S(1)} %get-tuple-element.42), channel_id=1, source_target_pairs={{0,4},{4,0},{8,12},{12,8},{16,20},{20,16},{24,28},{28,24},{32,36},... | collective-permute-start | bytes 688136 | tf_op jit(solution)/shard_map/ppermute | solution.py:246
  22.8 0.6 back_terms.1.refs_0_.terms
  23.4 0.5 forward.1
  24.0 1.2 %collective-permute-start.6 = (f32[32,1280]{1,0:T(8,128)S(1)}, f32[32,1280]{1,0:T(8,128)S(1)}, u32[]{:S(2)}, u32[]{:S(2)}) collective-permute-start(f32[32,1280]{1,0:T(8,128)S(1)} %get-tuple-element.48), channel_id=1, source_target_pairs={{0,1},{1,0},{2,3},{3,2},{4,5},{5,4},{6,7},{7,6},{8,9},{9,8},{10,11... | collective-permute-start | bytes 491528 | tf_op jit(solution)/shard_map/ppermute | solution.py:263
  25.2 2.6 %collective-permute-start.7 = (f32[32,1280]{1,0:T(8,128)S(1)}, f32[32,1280]{1,0:T(8,128)S(1)}, u32[]{:S(2)}, u32[]{:S(2)}) collective-permute-start(f32[32,1280]{1,0:T(8,128)S(1)} %get-tuple-element.49), channel_id=1, source_target_pairs={{0,2},{1,3},{2,0},{3,1},{4,6},{5,7},{6,4},{7,5},{8,10},{9,11},{10,... | collective-permute-start | bytes 491528 | tf_op jit(solution)/shard_map/ppermute | solution.py:263
  27.9 3.1 %collective-permute-done.9.refs_1_ = f32[112,128]{1,0:T(8,128)S(1)} collective-permute-done((f32[112,128]{1,0:T(8,128)S(1)}, f32[112,128]{1,0:T(8,128)S(1)}, u32[]{:S(2)}, u32[]{:S(2)}) %collective-permute-start.9) | collective-permute-done | bytes 57376 | tf_op jit(solution)/shard_map/ppermute | solution.py:246
  31.0 0.7 %collective-permute-start.11 = (f32[112,128]{1,0:T(8,128)S(1)}, f32[112,128]{1,0:T(8,128)S(1)}, u32[]{:S(2)}, u32[]{:S(2)}) collective-permute-start(f32[112,128]{1,0:T(8,128)S(1)} %get-tuple-element.47), channel_id=1, source_target_pairs={{0,24},{4,28},{8,16},{12,20},{16,8},{20,12},{24,0},{28,4},{32,56},... | collective-permute-start | bytes 172040 | tf_op jit(solution)/shard_map/ppermute | solution.py:246
  31.8 0.7 %collective-permute-done.10.refs_2_ = f32[112,128]{1,0:T(8,128)S(1)} collective-permute-done((f32[112,128]{1,0:T(8,128)S(1)}, f32[112,128]{1,0:T(8,128)S(1)}, u32[]{:S(2)}, u32[]{:S(2)}) %collective-permute-start.10) | collective-permute-done | bytes 57376 | tf_op jit(solution)/shard_map/ppermute | solution.py:246
  32.4 3.1 %collective-permute-done.11.refs_3_ = f32[112,128]{1,0:T(8,128)S(1)} collective-permute-done((f32[112,128]{1,0:T(8,128)S(1)}, f32[112,128]{1,0:T(8,128)S(1)}, u32[]{:S(2)}, u32[]{:S(2)}) %collective-permute-start.11) | collective-permute-done | bytes 57376 | tf_op jit(solution)/shard_map/ppermute | solution.py:246
  35.6 2.4 %collective-permute-done.8.r3 = f32[32,1280]{1,0:T(8,128)S(1)} collective-permute-done((f32[32,1280]{1,0:T(8,128)S(1)}, f32[32,1280]{1,0:T(8,128)S(1)}, u32[]{:S(2)}, u32[]{:S(2)}) %collective-permute-start.8) | collective-permute-done | bytes 163872 | tf_op jit(solution)/shard_map/ppermute | solution.py:263
  38.1 2.3 %back_inner.2.refs_2_ = f32[32,1024]{1,0:T(8,128)S(1)} custom-call(f32[864,1024]{1,0:T(8,128)S(1)} %back_terms.1.refs_0_.terms, s32[27,1024]{1,0:T(8,128)S(1)} %copy-done.5), custom_call_target="tpu_custom_call" | custom-call | flops 2147483648 | bytes 3780608 | tf_op jit(solution)/shard_map/back_inner/pallas_call | solution.py:223
  40.4 0.7 %collective-permute-done.12.refs_1_ = f32[112,128]{1,0:T(8,128)S(1)} collective-permute-done((f32[112,128]{1,0:T(8,128)S(1)}, f32[112,128]{1,0:T(8,128)S(1)}, u32[]{:S(2)}, u32[]{:S(2)}) %collective-permute-start.12) | collective-permute-done | bytes 57376 | tf_op jit(solution)/shard_map/ppermute | solution.py:246
  41.1 1.3 %collective-permute-start.15 = (f32[112,128]{1,0:T(8,128)S(1)}, f32[112,128]{1,0:T(8,128)S(1)}, u32[]{:S(2)}, u32[]{:S(2)}) collective-permute-start(f32[112,128]{1,0:T(8,128)S(1)} %sum_two.1.refs_0_), channel_id=1, source_target_pairs={{0,192},{4,196},{8,200},{12,204},{16,208},{20,212},{24,216},{28,22... | collective-permute-start | bytes 172040 | tf_op jit(solution)/shard_map/ppermute | solution.py:246
  42.4 1.0 %collective-permute-start.14 = (f32[112,128]{1,0:T(8,128)S(1)}, f32[112,128]{1,0:T(8,128)S(1)}, u32[]{:S(2)}, u32[]{:S(2)}) collective-permute-start(f32[112,128]{1,0:T(8,128)S(1)} %sum_two.1.refs_0_), channel_id=1, source_target_pairs={{0,128},{4,132},{8,136},{12,140},{16,144},{20,148},{24,152},{28,15... | collective-permute-start | bytes 172040 | tf_op jit(solution)/shard_map/ppermute | solution.py:246
  43.4 3.4 %collective-permute-start.13 = (f32[112,128]{1,0:T(8,128)S(1)}, f32[112,128]{1,0:T(8,128)S(1)}, u32[]{:S(2)}, u32[]{:S(2)}) collective-permute-start(f32[112,128]{1,0:T(8,128)S(1)} %sum_two.1.refs_0_), channel_id=1, source_target_pairs={{0,64},{4,68},{8,72},{12,76},{16,80},{20,84},{24,88},{28,92},{32,9... | collective-permute-start | bytes 172040 | tf_op jit(solution)/shard_map/ppermute | solution.py:246
  46.9 3.2 %back_inner.3.inner = f32[32,1024]{1,0:T(8,128)S(1)} custom-call(f32[864,1024]{1,0:T(8,128)S(1)} %back_terms.1.refs_0_.terms, s32[27,1024]{1,0:T(8,128)S(1)} %copy-done.5, f32[32,1024]{1,0:T(8,128)S(1)} %back_inner.2.refs_2_), custom_call_target="tpu_custom_call", output_to_operand_aliasing={{}: (2, {})} | custom-call | flops 3221225472 | bytes 3911680 | tf_op jit(solution)/shard_map/back_inner/pallas_call | solution.py:223
  50.1 0.5 collective-permute-done.13.refs_1_
  50.6 0.7 %collective-permute-start.18 = (f32[112,128]{1,0:T(8,128)S(1)}, f32[112,128]{1,0:T(8,128)S(1)}, u32[]{:S(2)}, u32[]{:S(2)}) collective-permute-start(f32[112,128]{1,0:T(8,128)S(1)} %sum_four.3.refs_0_), channel_id=1, source_target_pairs={{0,24},{4,28},{8,16},{12,20},{16,8},{20,12},{24,0},{28,4},{32,56},... | collective-permute-start | bytes 172040 | tf_op jit(solution)/shard_map/ppermute | solution.py:246
  51.3 2.6 %collective-permute-start.16 = (f32[112,128]{1,0:T(8,128)S(1)}, f32[112,128]{1,0:T(8,128)S(1)}, u32[]{:S(2)}, u32[]{:S(2)}) collective-permute-start(f32[112,128]{1,0:T(8,128)S(1)} %sum_four.3.refs_0_), channel_id=1, source_target_pairs={{0,8},{4,12},{8,0},{12,4},{16,24},{20,28},{24,16},{28,20},{32,40},... | collective-permute-start | bytes 172040 | tf_op jit(solution)/shard_map/ppermute | solution.py:246
  53.9 3.2 %edge.1 = (bf16[32,1024]{1,0:T(8,128)(2,1)}, bf16[32,1024]{1,0:T(8,128)(2,1)}) custom-call(f32[864,1024]{1,0:T(8,128)S(1)} %back_terms.1.refs_0_.terms, s32[27,1024]{1,0:T(8,128)S(1)} %copy-done.5, bf16[864,128]{1,0:T(8,128)(2,1)S(1)} %bitcast.4, bf16[64,128]{1,0:T(8,128)(2,1)S(1)} %collective-permute-done.near_ref, ...), custom_call_target="tpu_custom_call" | custom-call | flops 2147483648 | bytes 4788224 | tf_op jit(solution)/shard_map/edge/pallas_call | solution.py:223
  57.2 4.0 %collective-permute-start.19 = (f32[448,128]{1,0:T(8,128)S(1)}, f32[448,128]{1,0:T(8,128)S(1)}, u32[]{:S(2)}, u32[]{:S(2)}) collective-permute-start(f32[448,128]{1,0:T(8,128)S(1)} %join.1.even_ref), channel_id=1, source_target_pairs={{0,4},{4,0},{8,12},{12,8},{16,20},{20,16},{24,28},{28,24},{32,36},... | collective-permute-start | bytes 688136 | tf_op jit(solution)/shard_map/ppermute | solution.py:246
  61.2 1.1 %collective-permute-done.19.odd_ref = f32[448,128]{1,0:T(8,128)S(1)} collective-permute-done((f32[448,128]{1,0:T(8,128)S(1)}, f32[448,128]{1,0:T(8,128)S(1)}, u32[]{:S(2)}, u32[]{:S(2)}) %collective-permute-start.19) | collective-permute-done | bytes 229408 | tf_op jit(solution)/shard_map/ppermute | solution.py:246
  62.3 0.8 %place.1 = f32[864,128]{1,0:T(8,128)} custom-call(f32[448,128]{1,0:T(8,128)S(1)} %join.1.even_ref, f32[448,128]{1,0:T(8,128)S(1)} %collective-permute-done.19.odd_ref), custom_call_target="tpu_custom_call" | custom-call | bytes 901120 | tf_op jit(solution)/shard_map/place/pallas_call | solution.py:223
  (34 shorter events, 0.4 us)
Async XLA Ops:
  0.6 14.0 %collective-permute-start.3 = (bf16[32,1024]{1,0:T(8,128)(2,1)}, bf16[32,1024]{1,0:T(8,128)(2,1)S(1)}, u32[]{:S(2)}, u32[]{:S(2)}) collective-permute-start(bf16[32,1024]{1,0:T(8,128)(2,1)} %g0.1), channel_id=1, source_target_pairs={{0,2},{1,3},{2,0},{3,1},{4,6},{5,7},{6,4},{7,5},{8,10},{9,11},{10,... | collective-permute-start | bytes 196616 | tf_op jit(solution)/shard_map/ppermute | solution.py:263
  4.5 10.2 %collective-permute-start.2 = (bf16[32,1024]{1,0:T(8,128)(2,1)}, bf16[32,1024]{1,0:T(8,128)(2,1)S(1)}, u32[]{:S(2)}, u32[]{:S(2)}) collective-permute-start(bf16[32,1024]{1,0:T(8,128)(2,1)} %g0.1), channel_id=1, source_target_pairs={{0,1},{1,0},{2,3},{3,2},{4,5},{5,4},{6,7},{7,6},{8,9},{9,8},{10,11... | collective-permute-start | bytes 196616 | tf_op jit(solution)/shard_map/ppermute | solution.py:263
  4.9 9.8 %collective-permute-start.4 = (bf16[32,1024]{1,0:T(8,128)(2,1)}, bf16[32,1024]{1,0:T(8,128)(2,1)S(1)}, u32[]{:S(2)}, u32[]{:S(2)}) collective-permute-start(bf16[32,1024]{1,0:T(8,128)(2,1)} %g0.1), channel_id=1, source_target_pairs={{0,3},{1,2},{2,1},{3,0},{4,7},{5,6},{6,5},{7,4},{8,11},{9,10},{10,... | collective-permute-start | bytes 196616 | tf_op jit(solution)/shard_map/ppermute | solution.py:263
  5.2 0.8 %copy-start.1 = (bf16[32,1024]{1,0:T(8,128)(2,1)S(1)}, bf16[32,1024]{1,0:T(8,128)(2,1)}, u32[]{:S(2)}) copy-start(bf16[32,1024]{1,0:T(8,128)(2,1)} %x_ref.3) | copy-start | bytes 196612
  6.1 0.8 %copy-start.2 = (bf16[32,1024]{1,0:T(8,128)(2,1)S(1)}, bf16[32,1024]{1,0:T(8,128)(2,1)}, u32[]{:S(2)}) copy-start(bf16[32,1024]{1,0:T(8,128)(2,1)} %g0.1) | copy-start | bytes 196612
  6.9 7.7 %collective-permute-start = (bf16[64,128]{1,0:T(8,128)(2,1)S(1)}, bf16[64,128]{1,0:T(8,128)(2,1)S(1)}, u32[]{:S(2)}, u32[]{:S(2)}) collective-permute-start(bf16[64,128]{1,0:T(8,128)(2,1)S(1)} %get-tuple-element.33), channel_id=1, source_target_pairs={{0,4},{4,0},{8,12},{12,8},{16,20},{20,16},{24,28},{28,24},{32,36},... | collective-permute-start | bytes 49160 | tf_op jit(solution)/shard_map/ppermute | solution.py:246
  9.8 4.9 %copy-start.3 = (bf16[32,1024]{1,0:T(8,128)(2,1)S(1)}, bf16[32,1024]{1,0:T(8,128)(2,1)}, u32[]{:S(2)}) copy-start(bf16[32,1024]{1,0:T(8,128)(2,1)} %g0.1) | copy-start | bytes 196612
  9.8 4.8 %collective-permute-start.1 = (bf16[64,128]{1,0:T(8,128)(2,1)S(1)}, bf16[64,128]{1,0:T(8,128)(2,1)S(1)}, u32[]{:S(2)}, u32[]{:S(2)}) collective-permute-start(bf16[64,128]{1,0:T(8,128)(2,1)S(1)} %get-tuple-element.34), channel_id=1, source_target_pairs={{0,252},{4,8},{8,4},{12,16},{16,12},{20,24},{24,20},{28,32},{32,28... | collective-permute-start | bytes 49160 | tf_op jit(solution)/shard_map/ppermute | solution.py:252
  9.8 0.9 %copy-start.4 = (s32[27,1024]{1,0:T(8,128)S(1)}, s32[27,1024]{1,0:T(8,128)}, u32[]{:S(2)}) copy-start(s32[27,1024]{1,0:T(8,128)} %rule_ref.5) | copy-start | bytes 331780
  10.8 3.9 %copy-start.5 = (s32[27,1024]{1,0:T(8,128)S(1)}, s32[27,1024]{1,0:T(8,128)}, u32[]{:S(2)}) copy-start(s32[27,1024]{1,0:T(8,128)} %rule_ref.5) | copy-start | bytes 331780
  14.6 8.2 %copy-start = (bf16[27,32,128]{2,1,0:T(8,128)(2,1)S(1)}, bf16[27,32,128]{2,1,0:T(8,128)(2,1)}, u32[]{:S(2)}) copy-start(bf16[27,32,128]{2,1,0:T(8,128)(2,1)} %param.5) | copy-start | bytes 663556
  16.1 7.8 %collective-permute-start.5 = (f32[448,128]{1,0:T(8,128)S(1)}, f32[448,128]{1,0:T(8,128)S(1)}, u32[]{:S(2)}, u32[]{:S(2)}) collective-permute-start(f32[448,128]{1,0:T(8,128)S(1)} %get-tuple-element.42), channel_id=1, source_target_pairs={{0,4},{4,0},{8,12},{12,8},{16,20},{20,16},{24,28},{28,24},{32,36},... | collective-permute-start | bytes 688136 | tf_op jit(solution)/shard_map/ppermute | solution.py:246
  24.0 11.6 %collective-permute-start.6 = (f32[32,1280]{1,0:T(8,128)S(1)}, f32[32,1280]{1,0:T(8,128)S(1)}, u32[]{:S(2)}, u32[]{:S(2)}) collective-permute-start(f32[32,1280]{1,0:T(8,128)S(1)} %get-tuple-element.48), channel_id=1, source_target_pairs={{0,1},{1,0},{2,3},{3,2},{4,5},{5,4},{6,7},{7,6},{8,9},{9,8},{10,11... | collective-permute-start | bytes 491528 | tf_op jit(solution)/shard_map/ppermute | solution.py:263
  25.2 10.4 %collective-permute-start.7 = (f32[32,1280]{1,0:T(8,128)S(1)}, f32[32,1280]{1,0:T(8,128)S(1)}, u32[]{:S(2)}, u32[]{:S(2)}) collective-permute-start(f32[32,1280]{1,0:T(8,128)S(1)} %get-tuple-element.49), channel_id=1, source_target_pairs={{0,2},{1,3},{2,0},{3,1},{4,6},{5,7},{6,4},{7,5},{8,10},{9,11},{10,... | collective-permute-start | bytes 491528 | tf_op jit(solution)/shard_map/ppermute | solution.py:263
  27.8 10.2 %collective-permute-start.8 = (f32[32,1280]{1,0:T(8,128)S(1)}, f32[32,1280]{1,0:T(8,128)S(1)}, u32[]{:S(2)}, u32[]{:S(2)}) collective-permute-start(f32[32,1280]{1,0:T(8,128)S(1)} %get-tuple-element.50), channel_id=1, source_target_pairs={{0,3},{1,2},{2,1},{3,0},{4,7},{5,6},{6,5},{7,4},{8,11},{9,10},{10,... | collective-permute-start | bytes 491528 | tf_op jit(solution)/shard_map/ppermute | solution.py:263
  27.9 3.1 %collective-permute-start.9 = (f32[112,128]{1,0:T(8,128)S(1)}, f32[112,128]{1,0:T(8,128)S(1)}, u32[]{:S(2)}, u32[]{:S(2)}) collective-permute-start(f32[112,128]{1,0:T(8,128)S(1)} %get-tuple-element.45), channel_id=1, source_target_pairs={{0,8},{4,12},{8,0},{12,4},{16,24},{20,28},{24,16},{28,20},{32,40},... | collective-permute-start | bytes 172040 | tf_op jit(solution)/shard_map/ppermute | solution.py:246
  27.9 4.5 %collective-permute-start.10 = (f32[112,128]{1,0:T(8,128)S(1)}, f32[112,128]{1,0:T(8,128)S(1)}, u32[]{:S(2)}, u32[]{:S(2)}) collective-permute-start(f32[112,128]{1,0:T(8,128)S(1)} %get-tuple-element.46), channel_id=1, source_target_pairs={{0,16},{4,20},{8,24},{12,28},{16,0},{20,4},{24,8},{28,12},{32,48},... | collective-permute-start | bytes 172040 | tf_op jit(solution)/shard_map/ppermute | solution.py:246
  31.0 4.5 %collective-permute-start.11 = (f32[112,128]{1,0:T(8,128)S(1)}, f32[112,128]{1,0:T(8,128)S(1)}, u32[]{:S(2)}, u32[]{:S(2)}) collective-permute-start(f32[112,128]{1,0:T(8,128)S(1)} %get-tuple-element.47), channel_id=1, source_target_pairs={{0,24},{4,28},{8,16},{12,20},{16,8},{20,12},{24,0},{28,4},{32,56},... | collective-permute-start | bytes 172040 | tf_op jit(solution)/shard_map/ppermute | solution.py:246
  38.0 3.1 %collective-permute-start.12 = (f32[112,128]{1,0:T(8,128)S(1)}, f32[112,128]{1,0:T(8,128)S(1)}, u32[]{:S(2)}, u32[]{:S(2)}) collective-permute-start(f32[112,128]{1,0:T(8,128)S(1)} %sum_four.2.refs_0_), channel_id=1, source_target_pairs={{0,32},{4,36},{8,40},{12,44},{16,48},{20,52},{24,56},{28,60},{32,0... | collective-permute-start | bytes 172040 | tf_op jit(solution)/shard_map/ppermute | solution.py:246
  41.1 8.9 %collective-permute-start.15 = (f32[112,128]{1,0:T(8,128)S(1)}, f32[112,128]{1,0:T(8,128)S(1)}, u32[]{:S(2)}, u32[]{:S(2)}) collective-permute-start(f32[112,128]{1,0:T(8,128)S(1)} %sum_two.1.refs_0_), channel_id=1, source_target_pairs={{0,192},{4,196},{8,200},{12,204},{16,208},{20,212},{24,216},{28,22... | collective-permute-start | bytes 172040 | tf_op jit(solution)/shard_map/ppermute | solution.py:246
  42.4 7.6 %collective-permute-start.14 = (f32[112,128]{1,0:T(8,128)S(1)}, f32[112,128]{1,0:T(8,128)S(1)}, u32[]{:S(2)}, u32[]{:S(2)}) collective-permute-start(f32[112,128]{1,0:T(8,128)S(1)} %sum_two.1.refs_0_), channel_id=1, source_target_pairs={{0,128},{4,132},{8,136},{12,140},{16,144},{20,148},{24,152},{28,15... | collective-permute-start | bytes 172040 | tf_op jit(solution)/shard_map/ppermute | solution.py:246
  43.4 7.1 %collective-permute-start.13 = (f32[112,128]{1,0:T(8,128)S(1)}, f32[112,128]{1,0:T(8,128)S(1)}, u32[]{:S(2)}, u32[]{:S(2)}) collective-permute-start(f32[112,128]{1,0:T(8,128)S(1)} %sum_two.1.refs_0_), channel_id=1, source_target_pairs={{0,64},{4,68},{8,72},{12,76},{16,80},{20,84},{24,88},{28,92},{32,9... | collective-permute-start | bytes 172040 | tf_op jit(solution)/shard_map/ppermute | solution.py:246
  50.6 6.6 %collective-permute-start.18 = (f32[112,128]{1,0:T(8,128)S(1)}, f32[112,128]{1,0:T(8,128)S(1)}, u32[]{:S(2)}, u32[]{:S(2)}) collective-permute-start(f32[112,128]{1,0:T(8,128)S(1)} %sum_four.3.refs_0_), channel_id=1, source_target_pairs={{0,24},{4,28},{8,16},{12,20},{16,8},{20,12},{24,0},{28,4},{32,56},... | collective-permute-start | bytes 172040 | tf_op jit(solution)/shard_map/ppermute | solution.py:246
  51.3 5.8 %collective-permute-start.17 = (f32[112,128]{1,0:T(8,128)S(1)}, f32[112,128]{1,0:T(8,128)S(1)}, u32[]{:S(2)}, u32[]{:S(2)}) collective-permute-start(f32[112,128]{1,0:T(8,128)S(1)} %sum_four.3.refs_0_), channel_id=1, source_target_pairs={{0,16},{4,20},{8,24},{12,28},{16,0},{20,4},{24,8},{28,12},{32,48},... | collective-permute-start | bytes 172040 | tf_op jit(solution)/shard_map/ppermute | solution.py:246
  51.3 5.8 %collective-permute-start.16 = (f32[112,128]{1,0:T(8,128)S(1)}, f32[112,128]{1,0:T(8,128)S(1)}, u32[]{:S(2)}, u32[]{:S(2)}) collective-permute-start(f32[112,128]{1,0:T(8,128)S(1)} %sum_four.3.refs_0_), channel_id=1, source_target_pairs={{0,8},{4,12},{8,0},{12,4},{16,24},{20,28},{24,16},{28,20},{32,40},... | collective-permute-start | bytes 172040 | tf_op jit(solution)/shard_map/ppermute | solution.py:246
  57.2 5.1 %collective-permute-start.19 = (f32[448,128]{1,0:T(8,128)S(1)}, f32[448,128]{1,0:T(8,128)S(1)}, u32[]{:S(2)}, u32[]{:S(2)}) collective-permute-start(f32[448,128]{1,0:T(8,128)S(1)} %join.1.even_ref), channel_id=1, source_target_pairs={{0,4},{4,0},{8,12},{12,8},{16,20},{20,16},{24,28},{28,24},{32,36},... | collective-permute-start | bytes 688136 | tf_op jit(solution)/shard_map/ppermute | solution.py:246

commit v4 on v3

--- a/solution.py
+++ b/solution.py
@@ -12,7 +12,7 @@
 LANES = 128
 PART = 112
 INNER = tuple(range(2, 8))
-EDGE = (0, 1, 7)
+EDGE = (0, 1)
 VMEM = pl.BlockSpec(memory_space=pltpu.VMEM)
 
 
@@ -76,13 +76,14 @@
 
 
 def weight_kernel(
-    dense_in, rule_ref, near_ref, far_ref, g0, g1, g2, g3,
+    dense_in, rule_ref, near_ref, far_ref, pair_ref, other_ref,
     dense_ref, grad_ref, keep_ref, send_ref, faces, terms,
 ):
     chan = lax.axis_index("ch")
     spot = lax.axis_index("blk") & 7
-    for m, part in enumerate((g0, g1, g2, g3)):
-        grad_ref[pl.ds(pl.multiple_of(32 * (chan ^ m), 32), 32), :] = part[...]
+    for m in range(4):
+        part = (pair_ref if m < 2 else other_ref)[32 * (m % 2) : 32 * (m % 2) + 32, :]
+        grad_ref[pl.ds(pl.multiple_of(32 * (chan ^ m), 32), 32), :] = part
     faces[:, :FACE], faces[:, FACE:] = by_side(near_ref[:32, :], far_ref[:32, :])
 
     def step(j, carry):
@@ -100,25 +101,35 @@
         preferred_element_type=jnp.float32,
     ) * (1.0 / 256.0)
     terms[864:, :] = jnp.zeros((32, LANES), jnp.float32)
-    for q in range(4):
+    for i, q in enumerate((0, 2, 1, 3)):
         for odd, target in ((0, keep_ref), (1, send_ref)):
             start = pl.multiple_of(PART * (spot ^ (2 * q + odd)), 8)
-            target[PART * q : PART * (q + 1), :] = terms[pl.ds(start, PART), :]
-
-
-def forward_kernel(dense_ref, weight_ref, near_ref, far_ref, own, s1, s2, s3, sums):
+            target[PART * i : PART * (i + 1), :] = terms[pl.ds(start, PART), :]
+
+
+def forward_kernel(dense_ref, weight_ref, near_ref, far_ref, keep_ref, send_ref, sums):
     chan = lax.axis_index("ch")
     sums[...] = lax.dot_general(
         weight_ref[...], dense_ref[...], (((0,), (0,)), ((), ())),
         preferred_element_type=jnp.float32,
     )
+    for m in range(4):
+        target = send_ref if m % 2 else keep_ref
+        rows = pl.ds(pl.multiple_of(32 * (chan ^ m), 32), 32)
+        target[32 * (m // 2) : 32 * (m // 2) + 32, :VOX] = sums[rows, :]
     lower, upper = by_side(near_ref[32:, :], far_ref[32:, :])
-    for m, target in enumerate((own, s1, s2, s3)):
-        rows = pl.ds(pl.multiple_of(32 * (chan ^ m), 32), 32)
-        target[:, :VOX] = sums[rows, :]
-        if m:
-            target[:, VOX : VOX + FACE] = lower
-            target[:, VOX + FACE :] = upper
+    send_ref[:32, VOX:] = lower
+    send_ref[32:, VOX:] = upper
+
+
+def middle_kernel(keep_ref, came_ref, near_ref, far_ref, own_ref, send_ref):
+    own_ref[...] = keep_ref[:32, :] + came_ref[:32, :VOX]
+    send_ref[:, :VOX] = keep_ref[32:, :] + came_ref[32:, :VOX]
+    lower, upper = by_side(near_ref[32:, :], far_ref[32:, :])
+    send_ref[:, VOX : VOX + FACE] = lower
+    send_ref[:, VOX + FACE : VOX + 2 * FACE] = upper
+    send_ref[:, VOX + 2 * FACE : VOX + 3 * FACE] = came_ref[:32, VOX:]
+    send_ref[:, VOX + 3 * FACE :] = came_ref[32:, VOX:]
 
 
 def back_terms_kernel(weight_ref, grad_ref, terms_ref):
@@ -127,8 +138,7 @@
     )
 
 
-def back_inner_kernel(groups, *refs):
-    terms, rule_ref = refs[0], refs[1]
+def back_inner_kernel(groups, terms, rule_ref, *refs):
     out_ref = refs[-1]
     for group in groups:
         out_ref[:, tile_span(group)] = jnp.zeros((32, LANES), jnp.float32)
@@ -150,19 +160,22 @@
 
 
 def edge_kernel(
-    terms, rule_ref, weight_ref, near_ref, far_ref, inner, own, r1, r2, r3,
+    terms, rule_ref, weight_ref, near_ref, far_ref, inner, own_ref, first_ref, second_ref,
     out_ref, grad_ref, faces, products, total,
 ):
     chan = lax.axis_index("ch")
-    summed = (own[...] + r1[:, :VOX]) + (r2[:, :VOX] + r3[:, :VOX])
-    out_ref[...] = summed.astype(jnp.bfloat16)
-    rows = pl.ds(pl.multiple_of(32 * chan, 32), 32)
+    out_ref[...] = (own_ref[...] + second_ref[:, :VOX]).astype(jnp.bfloat16)
     lower, upper = by_side(near_ref[32:, :], far_ref[32:, :])
-    faces[rows, :FACE] = lower.astype(jnp.bfloat16)
-    faces[rows, FACE:] = upper.astype(jnp.bfloat16)
-    for m, part in enumerate((r1, r2, r3)):
-        rows = pl.ds(pl.multiple_of(32 * (chan ^ (m + 1)), 32), 32)
-        faces[rows, :] = part[:, VOX:].astype(jnp.bfloat16)
+    pairs = (
+        (lower, upper),
+        (first_ref[:32, VOX:], first_ref[32:, VOX:]),
+        (second_ref[:, VOX : VOX + FACE], second_ref[:, VOX + FACE : VOX + 2 * FACE]),
+        (second_ref[:, VOX + 2 * FACE : VOX + 3 * FACE], second_ref[:, VOX + 3 * FACE :]),
+    )
+    for m, (lower, upper) in enumerate(pairs):
+        rows = pl.ds(pl.multiple_of(32 * (chan ^ m), 32), 32)
+        faces[rows, :FACE] = lower.astype(jnp.bfloat16)
+        faces[rows, FACE:] = upper.astype(jnp.bfloat16)
     products[...] = jnp.dot(
         weight_ref[...], faces[...], preferred_element_type=jnp.float32
     )
@@ -188,28 +201,26 @@
         grad_ref[:, tile_span(group)] = source[:, tile_span(group)].astype(jnp.bfloat16)
 
 
-def split_sum_kernel(keep_ref, came_ref, *outs):
-    for q, out in enumerate(outs):
-        rows = slice(PART * q, PART * (q + 1))
-        out[...] = keep_ref[rows, :] + came_ref[rows, :]
-
-
-def sum_kernel(*refs):
-    values = [ref[...] for ref in refs[:-1]]
-    while len(values) > 1:
-        values = [values[i] + values[i + 1] for i in range(0, len(values), 2)]
-    refs[-1][...] = values[0]
-
-
-def join_kernel(*refs):
-    for q, ref in enumerate(refs[:-1]):
-        refs[-1][PART * q : PART * (q + 1), :] = ref[...]
+def split_sum_kernel(keep_ref, came_ref, low_ref, high_ref):
+    half = low_ref.shape[0]
+    low_ref[...] = keep_ref[:half, :] + came_ref[:half, :]
+    high_ref[...] = keep_ref[half:, :] + came_ref[half:, :]
+
+
+def sum_kernel(a_ref, b_ref, out_ref):
+    out_ref[...] = a_ref[...] + b_ref[...]
+
+
+def join_kernel(a_ref, b_ref, out_ref):
+    half = a_ref.shape[0]
+    out_ref[:half, :] = a_ref[...]
+    out_ref[half:, :] = b_ref[...]
 
 
 def place_kernel(even_ref, odd_ref, out_ref, held):
     spot = lax.axis_index("blk") & 7
-    for q in range(4):
-        rows = slice(PART * q, PART * (q + 1))
+    for i, q in enumerate((0, 2, 1, 3)):
+        rows = slice(PART * i, PART * (i + 1))
         held[2 * PART * q : 2 * PART * q + PART, :] = even_ref[rows, :]
         held[2 * PART * q + PART : 2 * PART * (q + 1), :] = odd_ref[rows, :]
     for p in range(8):
@@ -263,10 +274,13 @@
         return lax.ppermute(value, "ch", [(i, i ^ mask) for i in range(4)])
 
     x, g, rules = features, grad_out, rulebook
-    near, far = call(faces_kernel, (bf16(64, FACE),) * 2, (x, g), name="faces")
+    near, far = call(
+        faces_kernel, (bf16(64, FACE),) * 2, (x, g), flops=1 << 30, name="faces"
+    )
+    pair = call(join_kernel, bf16(64, VOX), (g, over_ch(g, 1)), name="join")
     near = swap(near, 1)
     far = swap_far(far)
-    parts = [over_ch(g, m) for m in (1, 2, 3)]
+    other = over_ch(pair, 2)
     dense = call(
         gather_kernel, bf16(864, VOX), (x, rules),
         [pltpu.VMEM((32, VOX), jnp.float32)], flops=3 << 30, name="gather",
@@ -274,49 +288,63 @@
     dense, grads, keep, send = call(
         weight_kernel,
         (bf16(864, VOX), bf16(128, VOX), f32(4 * PART, 128), f32(4 * PART, 128)),
-        (dense, rules, near, far, g, *parts),
+        (dense, rules, near, far, pair, other),
         [pltpu.VMEM((32, 2 * FACE), jnp.float32), pltpu.VMEM((8 * PART, 128), jnp.float32)],
         aliases={0: 0}, flops=1 << 30, name="weight_terms",
     )
+
+    def inner_part(groups, inner=None):
+        args = (back, rules) if inner is None else (back, rules, inner)
+        return call(
+            functools.partial(back_inner_kernel, groups), f32(32, VOX), args,
+            aliases=None if inner is None else {2: 0}, flops=len(groups) << 30,
+            name="back_inner",
+        )
+
     came = swap(send, 1)
-    own, *sends = call(
-        forward_kernel, (f32(32, VOX),) + (f32(32, VOX + 2 * FACE),) * 3,
-        (dense, weights, near, far),
+    ours, first = call(
+        forward_kernel, (f32(64, VOX), f32(64, VOX + FACE)), (dense, weights, near, far),
         [pltpu.VMEM((128, VOX), jnp.float32)], flops=1 << 30, name="forward",
     )
     back = call(
         back_terms_kernel, f32(864, VOX), (weights, grads), flops=1 << 30, name="back_terms"
     )
-    came, = after((came,), own, back)
-    pieces = call(split_sum_kernel, (f32(PART, 128),) * 4, (keep, came), name="sum_pair")
-    others = [swap(pieces[q], 2 * q) for q in (1, 2, 3)]
-    shares = [over_ch(send, m) for m, send in zip((1, 2, 3), after(sends, *pieces))]
-    others = after(others, *shares)
-    total = call(sum_kernel, f32(PART, 128), (pieces[0], *others), name="sum_four")
-    pair = swap(total, 8)
-    inner = call(
-        functools.partial(back_inner_kernel, (2, 3)), f32(32, VOX),
-        (back, rules), flops=2 << 30, name="back_inner",
-    )
-    pair, = after((pair,), inner)
-    total = call(sum_kernel, f32(PART, 128), (total, pair), name="sum_two")
-    others = [swap(total, m) for m in (16, 32, 48)]
-    inner = call(
-        functools.partial(back_inner_kernel, (4, 5, 6)), f32(32, VOX),
-        (back, rules, inner), aliases={2: 0}, flops=3 << 30, name="back_inner",
-    )
-    others = after(others, inner)
-    total = call(sum_kernel, f32(PART, 128), (total, *others), name="sum_four")
-    others = [swap(total, 2 * q) for q in (1, 2, 3)]
+    came, = after((came,), ours, back)
+    kept, sent = call(split_sum_kernel, (f32(2 * PART, 128),) * 2, (keep, came), name="halve")
+    came = swap(sent, 2)
+    first, = after((first,), kept)
+    first = over_ch(first, 1)
+    inner = inner_part((2,))
+    came, = after((came,), inner)
+    kept, sent = call(split_sum_kernel, (f32(PART, 128),) * 2, (kept, came), name="halve")
+    came = swap(sent, 4)
+    own, second = call(
+        middle_kernel, (f32(32, VOX), f32(32, VOX + 4 * FACE)), (ours, first, near, far),
+        name="middle",
+    )
+    came, = after((came,), own)
+    total = call(sum_kernel, f32(PART, 128), (kept, came), name="add")
+    second, = after((second,), total)
+    second = over_ch(second, 2)
+    for mask, groups in ((8, (3,)), (16, (4, 5)), (32, (6,))):
+        came = swap(total, mask)
+        inner = inner_part(groups, inner)
+        came, = after((came,), inner)
+        total = call(sum_kernel, f32(PART, 128), (total, came), name="add")
+    came = swap(total, 4)
+    inner = inner_part((7,), inner)
+    came, = after((came,), inner)
+    total = call(join_kernel, f32(2 * PART, 128), (total, came), name="join")
+    came = swap(total, 2)
     output, grad_features = call(
         edge_kernel, (bf16(32, VOX), bf16(32, VOX)),
-        (back, rules, weights, near, far, inner, own, *shares),
+        (back, rules, weights, near, far, inner, own, first, second),
         [pltpu.VMEM((128, 2 * FACE), jnp.bfloat16), pltpu.VMEM((864, 2 * FACE), jnp.float32),
          pltpu.VMEM((32, VOX), jnp.float32)],
         flops=2 << 30, name="edge",
     )
-    others = after(others, output)
-    even = call(join_kernel, f32(4 * PART, 128), (total, *others), name="join")
+    came, = after((came,), output)
+    even = call(join_kernel, f32(4 * PART, 128), (total, came), name="join")
     odd = swap(even, 1)
     weight_grad = call(
         place_kernel, f32(864, 128), (even, odd),

time: 63.3 us -> 65.8 us (1.039)
  waiting for transfers between devices: 11.7 us -> 16.8 us
  starting transfers between devices: 32 us -> 28.3 us
  Pallas kernels: 16 us -> 18 us
  local copies, waits for them, and re-layouts: 2.63 us -> 1.73 us
    ppermute x13 -> x10, waiting for transfers between devices: 9.26 us -> 13.1 us  [swap(): return lax.ppermute(value, 'blk', [(i, i ^ mask) for i in range(count)])]
    ppermute x13 -> x10, starting transfers between devices: 23.4 us -> 19.8 us  [swap(): return lax.ppermute(value, 'blk', [(i, i ^ mask) for i in range(count)])]
    pallas_call x14 -> x22, Pallas kernels: 16 us -> 18 us  [call(): pl.pallas_call(kernel, out_shape=outs, in_specs=[VMEM] * len(args), out_s...]
    ppermute x6 -> x4, waiting for transfers between devices: 2.41 us -> 3.69 us  [over_ch(): return lax.ppermute(value, 'ch', [(i, i ^ mask) for i in range(4)])]
    ppermute x6 -> x4, starting transfers between devices: 8.55 us -> 7.48 us  [over_ch(): return lax.ppermute(value, 'ch', [(i, i ^ mask) for i in range(4)])]
    ppermute x1, starting transfers between devices: 0.01 us -> 1.03 us  [swap_far(): return lax.ppermute(value, 'blk', pairs)]
    unnamed x12 -> x10, local copies, waits for them, and re-layouts: 2.63 us -> 1.73 us
  transfers between devices with their start and end apart: 20 -> 15, of which waited for: 7 -> 8; matrix products, arithmetic and copies ran while one was open for 0% -> 0% of each run, Pallas kernels for 22% -> 24%
where the time goes in v4:
time: 65.8 us; the launch traced here: 65.6 us
  starting transfers between devices  28.3 us (43%)
  Pallas kernels  18 us (27%)
  waiting for transfers between devices  16.8 us (26%)
  local copies, waits for them, and re-layouts  1.73 us (3%)
  between operations  0.83 us (1%)
    ppermute x10, starting transfers between devices, swap(): return lax.ppermute(value, 'blk', [(i, i ^ mask) for i in range(count)])  19.8 us
    pallas_call x22, Pallas kernels, call(): pl.pallas_call(kernel, out_shape=outs, in_specs=[VMEM] * len(args), out_s...  18 us
    ppermute x10, waiting for transfers between devices, swap(): return lax.ppermute(value, 'blk', [(i, i ^ mask) for i in range(count)])  13.1 us
    ppermute x4, starting transfers between devices, over_ch(): return lax.ppermute(value, 'ch', [(i, i ^ mask) for i in range(4)])  7.48 us
    ppermute x4, waiting for transfers between devices, over_ch(): return lax.ppermute(value, 'ch', [(i, i ^ mask) for i in range(4)])  3.69 us
    unnamed x10, local copies, waits for them, and re-layouts  1.73 us
  transfers between devices with their start and end apart: 15, of which 8 were waited for; matrix products, arithmetic and copies ran while one was open for 0% of the time, Pallas kernels for 24%

profile of v4, /device:TPU:1, one launch (start us, length us, event | category | flops | bytes accessed | tf_op | source)
XLA Modules:
  0.0 65.6 jit_solution(9191297897117319674)
XLA Ops:
  0.6 2.2 %collective-permute-start.2 = (bf16[32,1024]{1,0:T(8,128)(2,1)}, bf16[32,1024]{1,0:T(8,128)(2,1)S(1)}, u32[]{:S(2)}, u32[]{:S(2)}) collective-permute-start(bf16[32,1024]{1,0:T(8,128)(2,1)} %a_ref.1), channel_id=1, source_target_pairs={{0,1},{1,0},{2,3},{3,2},{4,5},{5,4},{6,7},{7,6},{8,9},{9,8},{10,11... | collective-permute-start | bytes 196616 | tf_op jit(solution)/shard_map/ppermute | solution.py:274
  2.8 0.9 %copy-done.1 = bf16[32,1024]{1,0:T(8,128)(2,1)S(1)} copy-done((bf16[32,1024]{1,0:T(8,128)(2,1)S(1)}, bf16[32,1024]{1,0:T(8,128)(2,1)}, u32[]{:S(2)}) %copy-start.1) | copy-done | bytes 65560
  3.7 0.8 %copy-done.4 = bf16[32,1024]{1,0:T(8,128)(2,1)S(1)} copy-done((bf16[32,1024]{1,0:T(8,128)(2,1)S(1)}, bf16[32,1024]{1,0:T(8,128)(2,1)}, u32[]{:S(2)}) %copy-start.4) | copy-done | bytes 65560
  4.6 1.2 %collective-permute-start = (bf16[64,128]{1,0:T(8,128)(2,1)S(1)}, bf16[64,128]{1,0:T(8,128)(2,1)S(1)}, u32[]{:S(2)}, u32[]{:S(2)}) collective-permute-start(bf16[64,128]{1,0:T(8,128)(2,1)S(1)} %get-tuple-element.29), channel_id=1, source_target_pairs={{0,4},{4,0},{8,12},{12,8},{16,20},{20,16},{24,28},{28,24},{32,36},... | collective-permute-start | bytes 49160 | tf_op jit(solution)/shard_map/ppermute | solution.py:257
  5.8 1.0 %collective-permute-start.1 = (bf16[64,128]{1,0:T(8,128)(2,1)S(1)}, bf16[64,128]{1,0:T(8,128)(2,1)S(1)}, u32[]{:S(2)}, u32[]{:S(2)}) collective-permute-start(bf16[64,128]{1,0:T(8,128)(2,1)S(1)} %get-tuple-element.30), channel_id=1, source_target_pairs={{0,252},{4,8},{8,4},{12,16},{16,12},{20,24},{24,20},{28,32},{32,28... | collective-permute-start | bytes 49160 | tf_op jit(solution)/shard_map/ppermute | solution.py:263
  6.8 2.7 %collective-permute-start.3 = (bf16[64,1024]{1,0:T(8,128)(2,1)S(1)}, bf16[64,1024]{1,0:T(8,128)(2,1)S(1)}, u32[]{:S(2)}, u32[]{:S(2)}) collective-permute-start(bf16[64,1024]{1,0:T(8,128)(2,1)S(1)} %join.3.pair_ref), channel_id=1, source_target_pairs={{0,2},{1,3},{2,0},{3,1},{4,6},{5,7},{6,4},{7,5},{8,10},{9,11},{10,... | collective-permute-start | bytes 393224 | tf_op jit(solution)/shard_map/ppermute | solution.py:274
  9.6 3.9 %gather.1.dense_in = bf16[864,1024]{1,0:T(8,128)(2,1)S(1)} custom-call(bf16[32,1024]{1,0:T(8,128)(2,1)S(1)} %copy-done.4, s32[27,1024]{1,0:T(8,128)S(1)} %copy-done.3), custom_call_target="tpu_custom_call" | custom-call | flops 3221225472 | bytes 1945600 | tf_op jit(solution)/shard_map/gather/pallas_call | solution.py:234
  13.5 1.4 %weight_terms.1 = (bf16[864,1024]{1,0:T(8,128)(2,1)S(1)}, bf16[128,1024]{1,0:T(8,128)(2,1)S(1)}, f32[448,128]{1,0:T(8,128)S(1)}, f32[448,128]{1,0:T(8,128)S(1)}) custom-call(bf16[864,1024]{1,0:T(8,128)(2,1)S(1)} %gather.1.dense_in, s32[27,1024]{1,0:T(8,128)S(1)} %copy-done.3, ...), custom_call_target="tpu_custom_call", output_to_operand_aliasing={{0}: (0, {})} | custom-call | flops 1073741824 | bytes 4665344 | tf_op jit(solution)/shard_map/weight_terms/pallas_call | solution.py:234
  14.9 7.3 %collective-permute-start.4 = (f32[448,128]{1,0:T(8,128)S(1)}, f32[448,128]{1,0:T(8,128)S(1)}, u32[]{:S(2)}, u32[]{:S(2)}) collective-permute-start(f32[448,128]{1,0:T(8,128)S(1)} %get-tuple-element.36), channel_id=1, source_target_pairs={{0,4},{4,0},{8,12},{12,8},{16,20},{20,16},{24,28},{28,24},{32,36},... | collective-permute-start | bytes 688136 | tf_op jit(solution)/shard_map/ppermute | solution.py:257
  22.2 0.6 back_terms.1.terms
  22.8 0.5 forward.1
  23.6 1.5 %back_inner.5.refs_0_ = f32[32,1024]{1,0:T(8,128)S(1)} custom-call(f32[864,1024]{1,0:T(8,128)S(1)} %back_terms.1.terms, s32[27,1024]{1,0:T(8,128)S(1)} %copy-done.3), custom_call_target="tpu_custom_call" | custom-call | flops 1073741824 | bytes 3780608 | tf_op jit(solution)/shard_map/back_inner/pallas_call | solution.py:234
  25.1 2.8 %collective-permute-done.6.came_ref = f32[224,128]{1,0:T(8,128)S(1)} collective-permute-done((f32[224,128]{1,0:T(8,128)S(1)}, f32[224,128]{1,0:T(8,128)S(1)}, u32[]{:S(2)}, u32[]{:S(2)}) %collective-permute-start.6) | collective-permute-done | bytes 114720 | tf_op jit(solution)/shard_map/ppermute | solution.py:257
  28.0 3.7 %collective-permute-done.5.came_ref.first_ref = f32[64,1152]{1,0:T(8,128)S(1)} collective-permute-done((f32[64,1152]{1,0:T(8,128)S(1)}, f32[64,1152]{1,0:T(8,128)S(1)}, u32[]{:S(2)}, u32[]{:S(2)}) %collective-permute-start.5) | collective-permute-done | bytes 294944 | tf_op jit(solution)/shard_map/ppermute | solution.py:274
  31.7 0.8 %collective-permute-done.7.b_ref = f32[112,128]{1,0:T(8,128)S(1)} collective-permute-done((f32[112,128]{1,0:T(8,128)S(1)}, f32[112,128]{1,0:T(8,128)S(1)}, u32[]{:S(2)}, u32[]{:S(2)}) %collective-permute-start.7) | collective-permute-done | bytes 57376 | tf_op jit(solution)/shard_map/ppermute | solution.py:257
  32.5 0.1 collective-permute-start.9
  32.6 1.5 %back_inner.6.refs_0_ = f32[32,1024]{1,0:T(8,128)S(1)} custom-call(f32[864,1024]{1,0:T(8,128)S(1)} %back_terms.1.terms, s32[27,1024]{1,0:T(8,128)S(1)} %copy-done.3, f32[32,1024]{1,0:T(8,128)S(1)} %back_inner.5.refs_0_), custom_call_target="tpu_custom_call", output_to_operand_aliasing={{}: (2, {})} | custom-call | flops 1073741824 | bytes 3911680 | tf_op jit(solution)/shard_map/back_inner/pallas_call | solution.py:234
  34.1 2.5 %collective-permute-start.8 = (f32[32,1536]{1,0:T(8,128)S(1)}, f32[32,1536]{1,0:T(8,128)S(1)}, u32[]{:S(2)}, u32[]{:S(2)}) collective-permute-start(f32[32,1536]{1,0:T(8,128)S(1)} %get-tuple-element.47), channel_id=1, source_target_pairs={{0,2},{1,3},{2,0},{3,1},{4,6},{5,7},{6,4},{7,5},{8,10},{9,11},{10,... | collective-permute-start | bytes 589832 | tf_op jit(solution)/shard_map/ppermute | solution.py:274
  36.7 2.3 %back_inner.7.refs_0_ = f32[32,1024]{1,0:T(8,128)S(1)} custom-call(f32[864,1024]{1,0:T(8,128)S(1)} %back_terms.1.terms, s32[27,1024]{1,0:T(8,128)S(1)} %copy-done.3, f32[32,1024]{1,0:T(8,128)S(1)} %back_inner.6.refs_0_), custom_call_target="tpu_custom_call", output_to_operand_aliasing={{}: (2, {})} | custom-call | flops 2147483648 | bytes 3911680 | tf_op jit(solution)/shard_map/back_inner/pallas_call | solution.py:234
  39.1 1.6 %collective-permute-done.10.b_ref = f32[112,128]{1,0:T(8,128)S(1)} collective-permute-done((f32[112,128]{1,0:T(8,128)S(1)}, f32[112,128]{1,0:T(8,128)S(1)}, u32[]{:S(2)}, u32[]{:S(2)}) %collective-permute-start.10) | collective-permute-done | bytes 57376 | tf_op jit(solution)/shard_map/ppermute | solution.py:257
  40.7 3.2 %collective-permute-start.11 = (f32[112,128]{1,0:T(8,128)S(1)}, f32[112,128]{1,0:T(8,128)S(1)}, u32[]{:S(2)}, u32[]{:S(2)}) collective-permute-start(f32[112,128]{1,0:T(8,128)S(1)} %add.6.a_ref), channel_id=1, source_target_pairs={{0,128},{4,132},{8,136},{12,140},{16,144},{20,148},{24,152},{28,15... | collective-permute-start | bytes 172040 | tf_op jit(solution)/shard_map/ppermute | solution.py:257
  43.9 1.5 %back_inner.8.refs_0_ = f32[32,1024]{1,0:T(8,128)S(1)} custom-call(f32[864,1024]{1,0:T(8,128)S(1)} %back_terms.1.terms, s32[27,1024]{1,0:T(8,128)S(1)} %copy-done.3, f32[32,1024]{1,0:T(8,128)S(1)} %back_inner.7.refs_0_), custom_call_target="tpu_custom_call", output_to_operand_aliasing={{}: (2, {})} | custom-call | flops 1073741824 | bytes 3911680 | tf_op jit(solution)/shard_map/back_inner/pallas_call | solution.py:234
  45.4 2.3 %collective-permute-done.11.b_ref = f32[112,128]{1,0:T(8,128)S(1)} collective-permute-done((f32[112,128]{1,0:T(8,128)S(1)}, f32[112,128]{1,0:T(8,128)S(1)}, u32[]{:S(2)}, u32[]{:S(2)}) %collective-permute-start.11) | collective-permute-done | bytes 57376 | tf_op jit(solution)/shard_map/ppermute | solution.py:257
  47.7 0.5 collective-permute-start.12
  48.2 1.5 %back_inner.9.inner = f32[32,1024]{1,0:T(8,128)S(1)} custom-call(f32[864,1024]{1,0:T(8,128)S(1)} %back_terms.1.terms, s32[27,1024]{1,0:T(8,128)S(1)} %copy-done.3, f32[32,1024]{1,0:T(8,128)S(1)} %back_inner.8.refs_0_), custom_call_target="tpu_custom_call", output_to_operand_aliasing={{}: (2, {})} | custom-call | flops 1073741824 | bytes 3911680 | tf_op jit(solution)/shard_map/back_inner/pallas_call | solution.py:234
  49.7 2.8 %collective-permute-done.12.b_ref = f32[112,128]{1,0:T(8,128)S(1)} collective-permute-done((f32[112,128]{1,0:T(8,128)S(1)}, f32[112,128]{1,0:T(8,128)S(1)}, u32[]{:S(2)}, u32[]{:S(2)}) %collective-permute-start.12) | collective-permute-done | bytes 57376 | tf_op jit(solution)/shard_map/ppermute | solution.py:257
  52.5 0.2 collective-permute-start.13
  52.7 2.4 %edge.1 = (bf16[32,1024]{1,0:T(8,128)(2,1)}, bf16[32,1024]{1,0:T(8,128)(2,1)}) custom-call(f32[864,1024]{1,0:T(8,128)S(1)} %back_terms.1.terms, s32[27,1024]{1,0:T(8,128)S(1)} %copy-done.3, bf16[864,128]{1,0:T(8,128)(2,1)S(1)} %bitcast.4, bf16[64,128]{1,0:T(8,128)(2,1)S(1)} %collective-permute-done.near_ref, ...), custom_call_target="tpu_custom_call" | custom-call | flops 2147483648 | bytes 4788224 | tf_op jit(solution)/shard_map/edge/pallas_call | solution.py:234
  55.1 1.7 %collective-permute-done.13.b_ref = f32[224,128]{1,0:T(8,128)S(1)} collective-permute-done((f32[224,128]{1,0:T(8,128)S(1)}, f32[224,128]{1,0:T(8,128)S(1)}, u32[]{:S(2)}, u32[]{:S(2)}) %collective-permute-start.13) | collective-permute-done | bytes 114720 | tf_op jit(solution)/shard_map/ppermute | solution.py:257
  56.8 6.9 %collective-permute-start.14 = (f32[448,128]{1,0:T(8,128)S(1)}, f32[448,128]{1,0:T(8,128)S(1)}, u32[]{:S(2)}, u32[]{:S(2)}) collective-permute-start(f32[448,128]{1,0:T(8,128)S(1)} %join.5.even_ref), channel_id=1, source_target_pairs={{0,4},{4,0},{8,12},{12,8},{16,20},{20,16},{24,28},{28,24},{32,36},... | collective-permute-start | bytes 688136 | tf_op jit(solution)/shard_map/ppermute | solution.py:257
  63.7 1.1 %collective-permute-done.14.odd_ref = f32[448,128]{1,0:T(8,128)S(1)} collective-permute-done((f32[448,128]{1,0:T(8,128)S(1)}, f32[448,128]{1,0:T(8,128)S(1)}, u32[]{:S(2)}, u32[]{:S(2)}) %collective-permute-start.14) | collective-permute-done | bytes 229408 | tf_op jit(solution)/shard_map/ppermute | solution.py:257
  64.8 0.8 %place.1 = f32[864,128]{1,0:T(8,128)} custom-call(f32[448,128]{1,0:T(8,128)S(1)} %join.5.even_ref, f32[448,128]{1,0:T(8,128)S(1)} %collective-permute-done.14.odd_ref), custom_call_target="tpu_custom_call" | custom-call | bytes 901120 | tf_op jit(solution)/shard_map/place/pallas_call | solution.py:234
  (30 shorter events, 0.6 us)
Async XLA Ops:
  0.6 6.2 %collective-permute-start.2 = (bf16[32,1024]{1,0:T(8,128)(2,1)}, bf16[32,1024]{1,0:T(8,128)(2,1)S(1)}, u32[]{:S(2)}, u32[]{:S(2)}) collective-permute-start(bf16[32,1024]{1,0:T(8,128)(2,1)} %a_ref.1), channel_id=1, source_target_pairs={{0,1},{1,0},{2,3},{3,2},{4,5},{5,4},{6,7},{7,6},{8,9},{9,8},{10,11... | collective-permute-start | bytes 196616 | tf_op jit(solution)/shard_map/ppermute | solution.py:274
  2.8 0.9 %copy-start.1 = (bf16[32,1024]{1,0:T(8,128)(2,1)S(1)}, bf16[32,1024]{1,0:T(8,128)(2,1)}, u32[]{:S(2)}) copy-start(bf16[32,1024]{1,0:T(8,128)(2,1)} %a_ref.1) | copy-start | bytes 196612
  3.7 0.8 %copy-start.4 = (bf16[32,1024]{1,0:T(8,128)(2,1)S(1)}, bf16[32,1024]{1,0:T(8,128)(2,1)}, u32[]{:S(2)}) copy-start(bf16[32,1024]{1,0:T(8,128)(2,1)} %x_ref.3) | copy-start | bytes 196612
  4.6 2.3 %copy-start.2 = (bf16[32,1024]{1,0:T(8,128)(2,1)S(1)}, bf16[32,1024]{1,0:T(8,128)(2,1)}, u32[]{:S(2)}) copy-start(bf16[32,1024]{1,0:T(8,128)(2,1)} %a_ref.1) | copy-start | bytes 196612
  4.6 5.0 %copy-start.3 = (s32[27,1024]{1,0:T(8,128)S(1)}, s32[27,1024]{1,0:T(8,128)}, u32[]{:S(2)}) copy-start(s32[27,1024]{1,0:T(8,128)} %rule_ref.15) | copy-start | bytes 331780
  4.6 8.8 %collective-permute-start = (bf16[64,128]{1,0:T(8,128)(2,1)S(1)}, bf16[64,128]{1,0:T(8,128)(2,1)S(1)}, u32[]{:S(2)}, u32[]{:S(2)}) collective-permute-start(bf16[64,128]{1,0:T(8,128)(2,1)S(1)} %get-tuple-element.29), channel_id=1, source_target_pairs={{0,4},{4,0},{8,12},{12,8},{16,20},{20,16},{24,28},{28,24},{32,36},... | collective-permute-start | bytes 49160 | tf_op jit(solution)/shard_map/ppermute | solution.py:257
  5.8 7.6 %collective-permute-start.1 = (bf16[64,128]{1,0:T(8,128)(2,1)S(1)}, bf16[64,128]{1,0:T(8,128)(2,1)S(1)}, u32[]{:S(2)}, u32[]{:S(2)}) collective-permute-start(bf16[64,128]{1,0:T(8,128)(2,1)S(1)} %get-tuple-element.30), channel_id=1, source_target_pairs={{0,252},{4,8},{8,4},{12,16},{16,12},{20,24},{24,20},{28,32},{32,28... | collective-permute-start | bytes 49160 | tf_op jit(solution)/shard_map/ppermute | solution.py:263
  6.8 6.6 %collective-permute-start.3 = (bf16[64,1024]{1,0:T(8,128)(2,1)S(1)}, bf16[64,1024]{1,0:T(8,128)(2,1)S(1)}, u32[]{:S(2)}, u32[]{:S(2)}) collective-permute-start(bf16[64,1024]{1,0:T(8,128)(2,1)S(1)} %join.3.pair_ref), channel_id=1, source_target_pairs={{0,2},{1,3},{2,0},{3,1},{4,6},{5,7},{6,4},{7,5},{8,10},{9,11},{10,... | collective-permute-start | bytes 393224 | tf_op jit(solution)/shard_map/ppermute | solution.py:274
  13.4 8.8 %copy-start = (bf16[27,32,128]{2,1,0:T(8,128)(2,1)S(1)}, bf16[27,32,128]{2,1,0:T(8,128)(2,1)}, u32[]{:S(2)}) copy-start(bf16[27,32,128]{2,1,0:T(8,128)(2,1)} %param.5) | copy-start | bytes 663556
  14.9 8.4 %collective-permute-start.4 = (f32[448,128]{1,0:T(8,128)S(1)}, f32[448,128]{1,0:T(8,128)S(1)}, u32[]{:S(2)}, u32[]{:S(2)}) collective-permute-start(f32[448,128]{1,0:T(8,128)S(1)} %get-tuple-element.36), channel_id=1, source_target_pairs={{0,4},{4,0},{8,12},{12,8},{16,20},{20,16},{24,28},{28,24},{32,36},... | collective-permute-start | bytes 688136 | tf_op jit(solution)/shard_map/ppermute | solution.py:257
  23.4 8.3 %collective-permute-start.5 = (f32[64,1152]{1,0:T(8,128)S(1)}, f32[64,1152]{1,0:T(8,128)S(1)}, u32[]{:S(2)}, u32[]{:S(2)}) collective-permute-start(f32[64,1152]{1,0:T(8,128)S(1)} %get-tuple-element.39), channel_id=1, source_target_pairs={{0,1},{1,0},{2,3},{3,2},{4,5},{5,4},{6,7},{7,6},{8,9},{9,8},{10,11... | collective-permute-start | bytes 884744 | tf_op jit(solution)/shard_map/ppermute | solution.py:274
  23.5 4.4 %collective-permute-start.6 = (f32[224,128]{1,0:T(8,128)S(1)}, f32[224,128]{1,0:T(8,128)S(1)}, u32[]{:S(2)}, u32[]{:S(2)}) collective-permute-start(f32[224,128]{1,0:T(8,128)S(1)} %get-tuple-element.42), channel_id=1, source_target_pairs={{0,8},{4,12},{8,0},{12,4},{16,24},{20,28},{24,16},{28,20},{32,40},... | collective-permute-start | bytes 344072 | tf_op jit(solution)/shard_map/ppermute | solution.py:257
  27.9 4.6 %collective-permute-start.7 = (f32[112,128]{1,0:T(8,128)S(1)}, f32[112,128]{1,0:T(8,128)S(1)}, u32[]{:S(2)}, u32[]{:S(2)}) collective-permute-start(f32[112,128]{1,0:T(8,128)S(1)} %get-tuple-element.45), channel_id=1, source_target_pairs={{0,16},{4,20},{8,24},{12,28},{16,0},{20,4},{24,8},{28,12},{32,48},... | collective-permute-start | bytes 172040 | tf_op jit(solution)/shard_map/ppermute | solution.py:257
  32.5 4.1 %collective-permute-start.9 = (f32[112,128]{1,0:T(8,128)S(1)}, f32[112,128]{1,0:T(8,128)S(1)}, u32[]{:S(2)}, u32[]{:S(2)}) collective-permute-start(f32[112,128]{1,0:T(8,128)S(1)} %add.4.a_ref), channel_id=1, source_target_pairs={{0,32},{4,36},{8,40},{12,44},{16,48},{20,52},{24,56},{28,60},{32,0... | collective-permute-start | bytes 172040 | tf_op jit(solution)/shard_map/ppermute | solution.py:257
  34.1 18.6 %collective-permute-start.8 = (f32[32,1536]{1,0:T(8,128)S(1)}, f32[32,1536]{1,0:T(8,128)S(1)}, u32[]{:S(2)}, u32[]{:S(2)}) collective-permute-start(f32[32,1536]{1,0:T(8,128)S(1)} %get-tuple-element.47), channel_id=1, source_target_pairs={{0,2},{1,3},{2,0},{3,1},{4,6},{5,7},{6,4},{7,5},{8,10},{9,11},{10,... | collective-permute-start | bytes 589832 | tf_op jit(solution)/shard_map/ppermute | solution.py:274
  36.6 4.0 %collective-permute-start.10 = (f32[112,128]{1,0:T(8,128)S(1)}, f32[112,128]{1,0:T(8,128)S(1)}, u32[]{:S(2)}, u32[]{:S(2)}) collective-permute-start(f32[112,128]{1,0:T(8,128)S(1)} %add.5.a_ref), channel_id=1, source_target_pairs={{0,64},{4,68},{8,72},{12,76},{16,80},{20,84},{24,88},{28,92},{32,9... | collective-permute-start | bytes 172040 | tf_op jit(solution)/shard_map/ppermute | solution.py:257
  40.7 7.0 %collective-permute-start.11 = (f32[112,128]{1,0:T(8,128)S(1)}, f32[112,128]{1,0:T(8,128)S(1)}, u32[]{:S(2)}, u32[]{:S(2)}) collective-permute-start(f32[112,128]{1,0:T(8,128)S(1)} %add.6.a_ref), channel_id=1, source_target_pairs={{0,128},{4,132},{8,136},{12,140},{16,144},{20,148},{24,152},{28,15... | collective-permute-start | bytes 172040 | tf_op jit(solution)/shard_map/ppermute | solution.py:257
  47.7 4.8 %collective-permute-start.12 = (f32[112,128]{1,0:T(8,128)S(1)}, f32[112,128]{1,0:T(8,128)S(1)}, u32[]{:S(2)}, u32[]{:S(2)}) collective-permute-start(f32[112,128]{1,0:T(8,128)S(1)} %add.7.a_ref), channel_id=1, source_target_pairs={{0,16},{4,20},{8,24},{12,28},{16,0},{20,4},{24,8},{28,12},{32,48},... | collective-permute-start | bytes 172040 | tf_op jit(solution)/shard_map/ppermute | solution.py:257
  52.5 4.2 %collective-permute-start.13 = (f32[224,128]{1,0:T(8,128)S(1)}, f32[224,128]{1,0:T(8,128)S(1)}, u32[]{:S(2)}, u32[]{:S(2)}) collective-permute-start(f32[224,128]{1,0:T(8,128)S(1)} %join.4.a_ref), channel_id=1, source_target_pairs={{0,8},{4,12},{8,0},{12,4},{16,24},{20,28},{24,16},{28,20},{32,40},... | collective-permute-start | bytes 344072 | tf_op jit(solution)/shard_map/ppermute | solution.py:257
  56.8 8.0 %collective-permute-start.14 = (f32[448,128]{1,0:T(8,128)S(1)}, f32[448,128]{1,0:T(8,128)S(1)}, u32[]{:S(2)}, u32[]{:S(2)}) collective-permute-start(f32[448,128]{1,0:T(8,128)S(1)} %join.5.even_ref), channel_id=1, source_target_pairs={{0,4},{4,0},{8,12},{12,8},{16,20},{20,16},{24,28},{28,24},{32,36},... | collective-permute-start | bytes 688136 | tf_op jit(solution)/shard_map/ppermute | solution.py:257

commit v5 on v4

--- a/solution.py
+++ b/solution.py
@@ -101,10 +101,10 @@
         preferred_element_type=jnp.float32,
     ) * (1.0 / 256.0)
     terms[864:, :] = jnp.zeros((32, LANES), jnp.float32)
-    for i, q in enumerate((0, 2, 1, 3)):
+    for q in range(4):
         for odd, target in ((0, keep_ref), (1, send_ref)):
             start = pl.multiple_of(PART * (spot ^ (2 * q + odd)), 8)
-            target[PART * i : PART * (i + 1), :] = terms[pl.ds(start, PART), :]
+            target[PART * q : PART * (q + 1), :] = terms[pl.ds(start, PART), :]
 
 
 def forward_kernel(dense_ref, weight_ref, near_ref, far_ref, keep_ref, send_ref, sums):
@@ -201,26 +201,29 @@
         grad_ref[:, tile_span(group)] = source[:, tile_span(group)].astype(jnp.bfloat16)
 
 
-def split_sum_kernel(keep_ref, came_ref, low_ref, high_ref):
-    half = low_ref.shape[0]
-    low_ref[...] = keep_ref[:half, :] + came_ref[:half, :]
-    high_ref[...] = keep_ref[half:, :] + came_ref[half:, :]
-
-
-def sum_kernel(a_ref, b_ref, out_ref):
-    out_ref[...] = a_ref[...] + b_ref[...]
-
-
-def join_kernel(a_ref, b_ref, out_ref):
-    half = a_ref.shape[0]
-    out_ref[:half, :] = a_ref[...]
-    out_ref[half:, :] = b_ref[...]
+def split_sum_kernel(keep_ref, came_ref, *outs):
+    for q, out in enumerate(outs):
+        rows = slice(PART * q, PART * (q + 1))
+        out[...] = keep_ref[rows, :] + came_ref[rows, :]
+
+
+def sum_kernel(*refs):
+    values = [ref[...] for ref in refs[:-1]]
+    while len(values) > 1:
+        values = [values[i] + values[i + 1] for i in range(0, len(values), 2)]
+    refs[-1][...] = values[0]
+
+
+def join_kernel(*refs):
+    size = refs[0].shape[0]
+    for q, ref in enumerate(refs[:-1]):
+        refs[-1][size * q : size * (q + 1), :] = ref[...]
 
 
 def place_kernel(even_ref, odd_ref, out_ref, held):
     spot = lax.axis_index("blk") & 7
-    for i, q in enumerate((0, 2, 1, 3)):
-        rows = slice(PART * i, PART * (i + 1))
+    for q in range(4):
+        rows = slice(PART * q, PART * (q + 1))
         held[2 * PART * q : 2 * PART * q + PART, :] = even_ref[rows, :]
         held[2 * PART * q + PART : 2 * PART * (q + 1), :] = odd_ref[rows, :]
     for p in range(8):
@@ -310,32 +313,28 @@
         back_terms_kernel, f32(864, VOX), (weights, grads), flops=1 << 30, name="back_terms"
     )
     came, = after((came,), ours, back)
-    kept, sent = call(split_sum_kernel, (f32(2 * PART, 128),) * 2, (keep, came), name="halve")
-    came = swap(sent, 2)
-    first, = after((first,), kept)
+    pieces = call(split_sum_kernel, (f32(PART, 128),) * 4, (keep, came), name="sum_pair")
+    others = [swap(pieces[q], 2 * q) for q in (1, 2, 3)]
+    first, = after((first,), *pieces)
     first = over_ch(first, 1)
-    inner = inner_part((2,))
-    came, = after((came,), inner)
-    kept, sent = call(split_sum_kernel, (f32(PART, 128),) * 2, (kept, came), name="halve")
-    came = swap(sent, 4)
+    inner = inner_part((2, 3))
+    others = after(others, inner)
+    total = call(sum_kernel, f32(PART, 128), (pieces[0], *others), name="sum_four")
+    came = swap(total, 8)
+    ours, first = after((ours, first), total)
     own, second = call(
         middle_kernel, (f32(32, VOX), f32(32, VOX + 4 * FACE)), (ours, first, near, far),
         name="middle",
     )
-    came, = after((came,), own)
-    total = call(sum_kernel, f32(PART, 128), (kept, came), name="add")
-    second, = after((second,), total)
+    inner = inner_part((4,), inner)
+    came, = after((came,), inner, own)
+    total = call(sum_kernel, f32(PART, 128), (total, came), name="sum_two")
     second = over_ch(second, 2)
-    for mask, groups in ((8, (3,)), (16, (4, 5)), (32, (6,))):
-        came = swap(total, mask)
-        inner = inner_part(groups, inner)
-        came, = after((came,), inner)
-        total = call(sum_kernel, f32(PART, 128), (total, came), name="add")
-    came = swap(total, 4)
-    inner = inner_part((7,), inner)
-    came, = after((came,), inner)
-    total = call(join_kernel, f32(2 * PART, 128), (total, came), name="join")
-    came = swap(total, 2)
+    others = [swap(total, m) for m in (16, 32, 48)]
+    inner = inner_part((5, 6, 7), inner)
+    others = after(others, inner)
+    total = call(sum_kernel, f32(PART, 128), (total, *others), name="sum_four")
+    others = [swap(total, 2 * q) for q in (1, 2, 3)]
     output, grad_features = call(
         edge_kernel, (bf16(32, VOX), bf16(32, VOX)),
         (back, rules, weights, near, far, inner, own, first, second),
@@ -343,8 +342,8 @@
          pltpu.VMEM((32, VOX), jnp.float32)],
         flops=2 << 30, name="edge",
     )
-    came, = after((came,), output)
-    even = call(join_kernel, f32(4 * PART, 128), (total, came), name="join")
+    others = after(others, output)
+    even = call(join_kernel, f32(4 * PART, 128), (total, *others), name="join")
     odd = swap(even, 1)
     weight_grad = call(
         place_kernel, f32(864, 128), (even, odd),

time: 65.8 us -> 58.6 us (0.89)
  waiting for transfers between devices: 16.8 us -> 4.48 us
  starting transfers between devices: 28.3 us -> 34.7 us
  Pallas kernels: 18 us -> 16.7 us
    ppermute x10 -> x13, waiting for transfers between devices: 13.1 us -> 1.38 us  [swap(): return lax.ppermute(value, 'blk', [(i, i ^ mask) for i in range(count)])]
    ppermute x10 -> x13, starting transfers between devices: 19.8 us -> 26.4 us  [swap(): return lax.ppermute(value, 'blk', [(i, i ^ mask) for i in range(count)])]
    pallas_call x22 -> x17, Pallas kernels: 18 us -> 16.7 us  [call(): pl.pallas_call(kernel, out_shape=outs, in_specs=[VMEM] * len(args), out_s...]
  transfers between devices with their start and end apart: 15 -> 18, of which waited for: 8 -> 3; matrix products, arithmetic and copies ran while one was open for 0% -> 0% of each run, Pallas kernels for 24% -> 25%
where the time goes in v5:
time: 58.6 us; the launch traced here: 58.4 us
  starting transfers between devices  34.7 us (59%)
  Pallas kernels  16.7 us (28%)
  waiting for transfers between devices  4.48 us (8%)
  local copies, waits for them, and re-layouts  1.73 us (3%)
  between operations  0.84 us (1%)
    ppermute x13, starting transfers between devices, swap(): return lax.ppermute(value, 'blk', [(i, i ^ mask) for i in range(count)])  26.4 us
    pallas_call x17, Pallas kernels, call(): pl.pallas_call(kernel, out_shape=outs, in_specs=[VMEM] * len(args), out_s...  16.7 us
    ppermute x4, starting transfers between devices, over_ch(): return lax.ppermute(value, 'ch', [(i, i ^ mask) for i in range(4)])  7.21 us
    ppermute x4, waiting for transfers between devices, over_ch(): return lax.ppermute(value, 'ch', [(i, i ^ mask) for i in range(4)])  3.1 us
    unnamed x10, local copies, waits for them, and re-layouts  1.73 us
    ppermute x13, waiting for transfers between devices, swap(): return lax.ppermute(value, 'blk', [(i, i ^ mask) for i in range(count)])  1.38 us
  transfers between devices with their start and end apart: 18, of which 3 were waited for; matrix products, arithmetic and copies ran while one was open for 0% of the time, Pallas kernels for 25%

profile of v5, /device:TPU:1, one launch (start us, length us, event | category | flops | bytes accessed | tf_op | source)
XLA Modules:
  0.0 58.4 jit_solution(9880680935573766204)
XLA Ops:
  0.6 2.2 %collective-permute-start.2 = (bf16[32,1024]{1,0:T(8,128)(2,1)}, bf16[32,1024]{1,0:T(8,128)(2,1)S(1)}, u32[]{:S(2)}, u32[]{:S(2)}) collective-permute-start(bf16[32,1024]{1,0:T(8,128)(2,1)} %refs_0_.1), channel_id=1, source_target_pairs={{0,1},{1,0},{2,3},{3,2},{4,5},{5,4},{6,7},{7,6},{8,9},{9,8},{10,11... | collective-permute-start | bytes 196616 | tf_op jit(solution)/shard_map/ppermute | solution.py:277
  2.8 0.9 %copy-done.1 = bf16[32,1024]{1,0:T(8,128)(2,1)S(1)} copy-done((bf16[32,1024]{1,0:T(8,128)(2,1)S(1)}, bf16[32,1024]{1,0:T(8,128)(2,1)}, u32[]{:S(2)}) %copy-start.1) | copy-done | bytes 65560
  3.7 0.8 %copy-done.4 = bf16[32,1024]{1,0:T(8,128)(2,1)S(1)} copy-done((bf16[32,1024]{1,0:T(8,128)(2,1)S(1)}, bf16[32,1024]{1,0:T(8,128)(2,1)}, u32[]{:S(2)}) %copy-start.4) | copy-done | bytes 65560
  4.6 1.2 %collective-permute-start = (bf16[64,128]{1,0:T(8,128)(2,1)S(1)}, bf16[64,128]{1,0:T(8,128)(2,1)S(1)}, u32[]{:S(2)}, u32[]{:S(2)}) collective-permute-start(bf16[64,128]{1,0:T(8,128)(2,1)S(1)} %get-tuple-element.33), channel_id=1, source_target_pairs={{0,4},{4,0},{8,12},{12,8},{16,20},{20,16},{24,28},{28,24},{32,36},... | collective-permute-start | bytes 49160 | tf_op jit(solution)/shard_map/ppermute | solution.py:260
  5.8 1.0 %collective-permute-start.1 = (bf16[64,128]{1,0:T(8,128)(2,1)S(1)}, bf16[64,128]{1,0:T(8,128)(2,1)S(1)}, u32[]{:S(2)}, u32[]{:S(2)}) collective-permute-start(bf16[64,128]{1,0:T(8,128)(2,1)S(1)} %get-tuple-element.34), channel_id=1, source_target_pairs={{0,252},{4,8},{8,4},{12,16},{16,12},{20,24},{24,20},{28,32},{32,28... | collective-permute-start | bytes 49160 | tf_op jit(solution)/shard_map/ppermute | solution.py:266
  6.8 2.7 %collective-permute-start.3 = (bf16[64,1024]{1,0:T(8,128)(2,1)S(1)}, bf16[64,1024]{1,0:T(8,128)(2,1)S(1)}, u32[]{:S(2)}, u32[]{:S(2)}) collective-permute-start(bf16[64,1024]{1,0:T(8,128)(2,1)S(1)} %join.2.pair_ref), channel_id=1, source_target_pairs={{0,2},{1,3},{2,0},{3,1},{4,6},{5,7},{6,4},{7,5},{8,10},{9,11},{10,... | collective-permute-start | bytes 393224 | tf_op jit(solution)/shard_map/ppermute | solution.py:277
  9.6 3.9 %gather.1.dense_in = bf16[864,1024]{1,0:T(8,128)(2,1)S(1)} custom-call(bf16[32,1024]{1,0:T(8,128)(2,1)S(1)} %copy-done.4, s32[27,1024]{1,0:T(8,128)S(1)} %copy-done.3), custom_call_target="tpu_custom_call" | custom-call | flops 3221225472 | bytes 1945600 | tf_op jit(solution)/shard_map/gather/pallas_call | solution.py:237
  13.4 0.0 copy-start
  13.5 1.4 %weight_terms.1 = (bf16[864,1024]{1,0:T(8,128)(2,1)S(1)}, bf16[128,1024]{1,0:T(8,128)(2,1)S(1)}, f32[448,128]{1,0:T(8,128)S(1)}, f32[448,128]{1,0:T(8,128)S(1)}) custom-call(bf16[864,1024]{1,0:T(8,128)(2,1)S(1)} %gather.1.dense_in, s32[27,1024]{1,0:T(8,128)S(1)} %copy-done.3, ...), custom_call_target="tpu_custom_call", output_to_operand_aliasing={{0}: (0, {})} | custom-call | flops 1073741824 | bytes 4665344 | tf_op jit(solution)/shard_map/weight_terms/pallas_call | solution.py:237
  14.9 7.3 %collective-permute-start.4 = (f32[448,128]{1,0:T(8,128)S(1)}, f32[448,128]{1,0:T(8,128)S(1)}, u32[]{:S(2)}, u32[]{:S(2)}) collective-permute-start(f32[448,128]{1,0:T(8,128)S(1)} %get-tuple-element.40), channel_id=1, source_target_pairs={{0,4},{4,0},{8,12},{12,8},{16,20},{20,16},{24,28},{28,24},{32,36},... | collective-permute-start | bytes 688136 | tf_op jit(solution)/shard_map/ppermute | solution.py:260
  22.2 0.6 %back_terms.1.terms = f32[864,1024]{1,0:T(8,128)S(1)} custom-call(bf16[864,128]{1,0:T(8,128)(2,1)S(1)} %bitcast.2, bf16[128,1024]{1,0:T(8,128)(2,1)S(1)} %get-tuple-element.35.grad_ref), custom_call_target="tpu_custom_call" | custom-call | flops 1073741824 | bytes 4022272 | tf_op jit(solution)/shard_map/back_terms/pallas_call | solution.py:237
  22.8 0.5 forward.1
  23.4 0.1 collective-permute-start.6
  23.5 0.1 collective-permute-start.7
  23.6 3.7 %collective-permute-start.8 = (f32[112,128]{1,0:T(8,128)S(1)}, f32[112,128]{1,0:T(8,128)S(1)}, u32[]{:S(2)}, u32[]{:S(2)}) collective-permute-start(f32[112,128]{1,0:T(8,128)S(1)} %get-tuple-element.45), channel_id=1, source_target_pairs={{0,24},{4,28},{8,16},{12,20},{16,8},{20,12},{24,0},{28,4},{32,56},... | collective-permute-start | bytes 172040 | tf_op jit(solution)/shard_map/ppermute | solution.py:260
  27.3 2.3 %back_inner.3.refs_0_ = f32[32,1024]{1,0:T(8,128)S(1)} custom-call(f32[864,1024]{1,0:T(8,128)S(1)} %back_terms.1.terms, s32[27,1024]{1,0:T(8,128)S(1)} %copy-done.3), custom_call_target="tpu_custom_call" | custom-call | flops 2147483648 | bytes 3780608 | tf_op jit(solution)/shard_map/back_inner/pallas_call | solution.py:237
  29.7 0.2 collective-permute-done.8.refs_3_
  29.9 0.1 collective-permute-start.10
  30.0 1.5 %back_inner.4.refs_0_ = f32[32,1024]{1,0:T(8,128)S(1)} custom-call(f32[864,1024]{1,0:T(8,128)S(1)} %back_terms.1.terms, s32[27,1024]{1,0:T(8,128)S(1)} %copy-done.3, f32[32,1024]{1,0:T(8,128)S(1)} %back_inner.3.refs_0_), custom_call_target="tpu_custom_call", output_to_operand_aliasing={{}: (2, {})} | custom-call | flops 1073741824 | bytes 3911680 | tf_op jit(solution)/shard_map/back_inner/pallas_call | solution.py:237
  31.5 3.1 %collective-permute-done.5.came_ref.first_ref = f32[64,1152]{1,0:T(8,128)S(1)} collective-permute-done((f32[64,1152]{1,0:T(8,128)S(1)}, f32[64,1152]{1,0:T(8,128)S(1)}, u32[]{:S(2)}, u32[]{:S(2)}) %collective-permute-start.5) | collective-permute-done | bytes 294944 | tf_op jit(solution)/shard_map/ppermute | solution.py:277
  34.7 1.3 %collective-permute-start.13 = (f32[112,128]{1,0:T(8,128)S(1)}, f32[112,128]{1,0:T(8,128)S(1)}, u32[]{:S(2)}, u32[]{:S(2)}) collective-permute-start(f32[112,128]{1,0:T(8,128)S(1)} %sum_two.1.refs_0_), channel_id=1, source_target_pairs={{0,192},{4,196},{8,200},{12,204},{16,208},{20,212},{24,216},{28,22... | collective-permute-start | bytes 172040 | tf_op jit(solution)/shard_map/ppermute | solution.py:260
  36.0 0.1 collective-permute-start.12
  36.1 4.4 %collective-permute-start.11 = (f32[112,128]{1,0:T(8,128)S(1)}, f32[112,128]{1,0:T(8,128)S(1)}, u32[]{:S(2)}, u32[]{:S(2)}) collective-permute-start(f32[112,128]{1,0:T(8,128)S(1)} %sum_two.1.refs_0_), channel_id=1, source_target_pairs={{0,64},{4,68},{8,72},{12,76},{16,80},{20,84},{24,88},{28,92},{32,9... | collective-permute-start | bytes 172040 | tf_op jit(solution)/shard_map/ppermute | solution.py:260
  40.4 2.3 %collective-permute-start.9 = (f32[32,1536]{1,0:T(8,128)S(1)}, f32[32,1536]{1,0:T(8,128)S(1)}, u32[]{:S(2)}, u32[]{:S(2)}) collective-permute-start(f32[32,1536]{1,0:T(8,128)S(1)} %get-tuple-element.53), channel_id=1, source_target_pairs={{0,2},{1,3},{2,0},{3,1},{4,6},{5,7},{6,4},{7,5},{8,10},{9,11},{10,... | collective-permute-start | bytes 589832 | tf_op jit(solution)/shard_map/ppermute | solution.py:277
  42.7 3.2 %back_inner.5.inner = f32[32,1024]{1,0:T(8,128)S(1)} custom-call(f32[864,1024]{1,0:T(8,128)S(1)} %back_terms.1.terms, s32[27,1024]{1,0:T(8,128)S(1)} %copy-done.3, f32[32,1024]{1,0:T(8,128)S(1)} %back_inner.4.refs_0_), custom_call_target="tpu_custom_call", output_to_operand_aliasing={{}: (2, {})} | custom-call | flops 3221225472 | bytes 3911680 | tf_op jit(solution)/shard_map/back_inner/pallas_call | solution.py:237
  46.0 0.4 collective-permute-start.16
  46.4 0.7 %collective-permute-start.15 = (f32[112,128]{1,0:T(8,128)S(1)}, f32[112,128]{1,0:T(8,128)S(1)}, u32[]{:S(2)}, u32[]{:S(2)}) collective-permute-start(f32[112,128]{1,0:T(8,128)S(1)} %sum_four.3.refs_0_), channel_id=1, source_target_pairs={{0,16},{4,20},{8,24},{12,28},{16,0},{20,4},{24,8},{28,12},{32,48},... | collective-permute-start | bytes 172040 | tf_op jit(solution)/shard_map/ppermute | solution.py:260
  47.0 2.3 %collective-permute-start.14 = (f32[112,128]{1,0:T(8,128)S(1)}, f32[112,128]{1,0:T(8,128)S(1)}, u32[]{:S(2)}, u32[]{:S(2)}) collective-permute-start(f32[112,128]{1,0:T(8,128)S(1)} %sum_four.3.refs_0_), channel_id=1, source_target_pairs={{0,8},{4,12},{8,0},{12,4},{16,24},{20,28},{24,16},{28,20},{32,40},... | collective-permute-start | bytes 172040 | tf_op jit(solution)/shard_map/ppermute | solution.py:260
  49.3 2.3 %edge.1 = (bf16[32,1024]{1,0:T(8,128)(2,1)}, bf16[32,1024]{1,0:T(8,128)(2,1)}) custom-call(f32[864,1024]{1,0:T(8,128)S(1)} %back_terms.1.terms, s32[27,1024]{1,0:T(8,128)S(1)} %copy-done.3, bf16[864,128]{1,0:T(8,128)(2,1)S(1)} %bitcast.4, bf16[64,128]{1,0:T(8,128)(2,1)S(1)} %collective-permute-done.near_ref, ...), custom_call_target="tpu_custom_call" | custom-call | flops 2147483648 | bytes 4788224 | tf_op jit(solution)/shard_map/edge/pallas_call | solution.py:237
  51.7 4.8 %collective-permute-start.17 = (f32[448,128]{1,0:T(8,128)S(1)}, f32[448,128]{1,0:T(8,128)S(1)}, u32[]{:S(2)}, u32[]{:S(2)}) collective-permute-start(f32[448,128]{1,0:T(8,128)S(1)} %join.3.even_ref), channel_id=1, source_target_pairs={{0,4},{4,0},{8,12},{12,8},{16,20},{20,16},{24,28},{28,24},{32,36},... | collective-permute-start | bytes 688136 | tf_op jit(solution)/shard_map/ppermute | solution.py:260
  56.5 1.1 %collective-permute-done.17.odd_ref = f32[448,128]{1,0:T(8,128)S(1)} collective-permute-done((f32[448,128]{1,0:T(8,128)S(1)}, f32[448,128]{1,0:T(8,128)S(1)}, u32[]{:S(2)}, u32[]{:S(2)}) %collective-permute-start.17) | collective-permute-done | bytes 229408 | tf_op jit(solution)/shard_map/ppermute | solution.py:260
  57.6 0.8 %place.1 = f32[864,128]{1,0:T(8,128)} custom-call(f32[448,128]{1,0:T(8,128)S(1)} %join.3.even_ref, f32[448,128]{1,0:T(8,128)S(1)} %collective-permute-done.17.odd_ref), custom_call_target="tpu_custom_call" | custom-call | bytes 901120 | tf_op jit(solution)/shard_map/place/pallas_call | solution.py:237
  (31 shorter events, 0.2 us)
Async XLA Ops:
  0.6 6.2 %collective-permute-start.2 = (bf16[32,1024]{1,0:T(8,128)(2,1)}, bf16[32,1024]{1,0:T(8,128)(2,1)S(1)}, u32[]{:S(2)}, u32[]{:S(2)}) collective-permute-start(bf16[32,1024]{1,0:T(8,128)(2,1)} %refs_0_.1), channel_id=1, source_target_pairs={{0,1},{1,0},{2,3},{3,2},{4,5},{5,4},{6,7},{7,6},{8,9},{9,8},{10,11... | collective-permute-start | bytes 196616 | tf_op jit(solution)/shard_map/ppermute | solution.py:277
  2.8 0.9 %copy-start.1 = (bf16[32,1024]{1,0:T(8,128)(2,1)S(1)}, bf16[32,1024]{1,0:T(8,128)(2,1)}, u32[]{:S(2)}) copy-start(bf16[32,1024]{1,0:T(8,128)(2,1)} %refs_0_.1) | copy-start | bytes 196612
  3.7 0.8 %copy-start.4 = (bf16[32,1024]{1,0:T(8,128)(2,1)S(1)}, bf16[32,1024]{1,0:T(8,128)(2,1)}, u32[]{:S(2)}) copy-start(bf16[32,1024]{1,0:T(8,128)(2,1)} %x_ref.3) | copy-start | bytes 196612
  4.6 2.3 %copy-start.2 = (bf16[32,1024]{1,0:T(8,128)(2,1)S(1)}, bf16[32,1024]{1,0:T(8,128)(2,1)}, u32[]{:S(2)}) copy-start(bf16[32,1024]{1,0:T(8,128)(2,1)} %refs_0_.1) | copy-start | bytes 196612
  4.6 5.0 %copy-start.3 = (s32[27,1024]{1,0:T(8,128)S(1)}, s32[27,1024]{1,0:T(8,128)}, u32[]{:S(2)}) copy-start(s32[27,1024]{1,0:T(8,128)} %rule_ref.11) | copy-start | bytes 331780
  4.6 8.8 %collective-permute-start = (bf16[64,128]{1,0:T(8,128)(2,1)S(1)}, bf16[64,128]{1,0:T(8,128)(2,1)S(1)}, u32[]{:S(2)}, u32[]{:S(2)}) collective-permute-start(bf16[64,128]{1,0:T(8,128)(2,1)S(1)} %get-tuple-element.33), channel_id=1, source_target_pairs={{0,4},{4,0},{8,12},{12,8},{16,20},{20,16},{24,28},{28,24},{32,36},... | collective-permute-start | bytes 49160 | tf_op jit(solution)/shard_map/ppermute | solution.py:260
  5.8 7.6 %collective-permute-start.1 = (bf16[64,128]{1,0:T(8,128)(2,1)S(1)}, bf16[64,128]{1,0:T(8,128)(2,1)S(1)}, u32[]{:S(2)}, u32[]{:S(2)}) collective-permute-start(bf16[64,128]{1,0:T(8,128)(2,1)S(1)} %get-tuple-element.34), channel_id=1, source_target_pairs={{0,252},{4,8},{8,4},{12,16},{16,12},{20,24},{24,20},{28,32},{32,28... | collective-permute-start | bytes 49160 | tf_op jit(solution)/shard_map/ppermute | solution.py:266
  6.8 6.6 %collective-permute-start.3 = (bf16[64,1024]{1,0:T(8,128)(2,1)S(1)}, bf16[64,1024]{1,0:T(8,128)(2,1)S(1)}, u32[]{:S(2)}, u32[]{:S(2)}) collective-permute-start(bf16[64,1024]{1,0:T(8,128)(2,1)S(1)} %join.2.pair_ref), channel_id=1, source_target_pairs={{0,2},{1,3},{2,0},{3,1},{4,6},{5,7},{6,4},{7,5},{8,10},{9,11},{10,... | collective-permute-start | bytes 393224 | tf_op jit(solution)/shard_map/ppermute | solution.py:277
  13.4 8.8 %copy-start = (bf16[27,32,128]{2,1,0:T(8,128)(2,1)S(1)}, bf16[27,32,128]{2,1,0:T(8,128)(2,1)}, u32[]{:S(2)}) copy-start(bf16[27,32,128]{2,1,0:T(8,128)(2,1)} %param.5) | copy-start | bytes 663556
  14.9 8.4 %collective-permute-start.4 = (f32[448,128]{1,0:T(8,128)S(1)}, f32[448,128]{1,0:T(8,128)S(1)}, u32[]{:S(2)}, u32[]{:S(2)}) collective-permute-start(f32[448,128]{1,0:T(8,128)S(1)} %get-tuple-element.40), channel_id=1, source_target_pairs={{0,4},{4,0},{8,12},{12,8},{16,20},{20,16},{24,28},{28,24},{32,36},... | collective-permute-start | bytes 688136 | tf_op jit(solution)/shard_map/ppermute | solution.py:260
  23.4 6.3 %collective-permute-start.6 = (f32[112,128]{1,0:T(8,128)S(1)}, f32[112,128]{1,0:T(8,128)S(1)}, u32[]{:S(2)}, u32[]{:S(2)}) collective-permute-start(f32[112,128]{1,0:T(8,128)S(1)} %get-tuple-element.43), channel_id=1, source_target_pairs={{0,8},{4,12},{8,0},{12,4},{16,24},{20,28},{24,16},{28,20},{32,40},... | collective-permute-start | bytes 172040 | tf_op jit(solution)/shard_map/ppermute | solution.py:260
  23.5 6.2 %collective-permute-start.7 = (f32[112,128]{1,0:T(8,128)S(1)}, f32[112,128]{1,0:T(8,128)S(1)}, u32[]{:S(2)}, u32[]{:S(2)}) collective-permute-start(f32[112,128]{1,0:T(8,128)S(1)} %get-tuple-element.44), channel_id=1, source_target_pairs={{0,16},{4,20},{8,24},{12,28},{16,0},{20,4},{24,8},{28,12},{32,48},... | collective-permute-start | bytes 172040 | tf_op jit(solution)/shard_map/ppermute | solution.py:260
  23.6 6.3 %collective-permute-start.8 = (f32[112,128]{1,0:T(8,128)S(1)}, f32[112,128]{1,0:T(8,128)S(1)}, u32[]{:S(2)}, u32[]{:S(2)}) collective-permute-start(f32[112,128]{1,0:T(8,128)S(1)} %get-tuple-element.45), channel_id=1, source_target_pairs={{0,24},{4,28},{8,16},{12,20},{16,8},{20,12},{24,0},{28,4},{32,56},... | collective-permute-start | bytes 172040 | tf_op jit(solution)/shard_map/ppermute | solution.py:260
  27.3 7.3 %collective-permute-start.5 = (f32[64,1152]{1,0:T(8,128)S(1)}, f32[64,1152]{1,0:T(8,128)S(1)}, u32[]{:S(2)}, u32[]{:S(2)}) collective-permute-start(f32[64,1152]{1,0:T(8,128)S(1)} %get-tuple-element.46), channel_id=1, source_target_pairs={{0,1},{1,0},{2,3},{3,2},{4,5},{5,4},{6,7},{7,6},{8,9},{9,8},{10,11... | collective-permute-start | bytes 884744 | tf_op jit(solution)/shard_map/ppermute | solution.py:277
  29.9 4.7 %collective-permute-start.10 = (f32[112,128]{1,0:T(8,128)S(1)}, f32[112,128]{1,0:T(8,128)S(1)}, u32[]{:S(2)}, u32[]{:S(2)}) collective-permute-start(f32[112,128]{1,0:T(8,128)S(1)} %sum_four.2.refs_0_), channel_id=1, source_target_pairs={{0,32},{4,36},{8,40},{12,44},{16,48},{20,52},{24,56},{28,60},{32,0... | collective-permute-start | bytes 172040 | tf_op jit(solution)/shard_map/ppermute | solution.py:260
  34.7 11.2 %collective-permute-start.13 = (f32[112,128]{1,0:T(8,128)S(1)}, f32[112,128]{1,0:T(8,128)S(1)}, u32[]{:S(2)}, u32[]{:S(2)}) collective-permute-start(f32[112,128]{1,0:T(8,128)S(1)} %sum_two.1.refs_0_), channel_id=1, source_target_pairs={{0,192},{4,196},{8,200},{12,204},{16,208},{20,212},{24,216},{28,22... | collective-permute-start | bytes 172040 | tf_op jit(solution)/shard_map/ppermute | solution.py:260
  36.0 10.0 %collective-permute-start.12 = (f32[112,128]{1,0:T(8,128)S(1)}, f32[112,128]{1,0:T(8,128)S(1)}, u32[]{:S(2)}, u32[]{:S(2)}) collective-permute-start(f32[112,128]{1,0:T(8,128)S(1)} %sum_two.1.refs_0_), channel_id=1, source_target_pairs={{0,128},{4,132},{8,136},{12,140},{16,144},{20,148},{24,152},{28,15... | collective-permute-start | bytes 172040 | tf_op jit(solution)/shard_map/ppermute | solution.py:260
  36.1 9.9 %collective-permute-start.11 = (f32[112,128]{1,0:T(8,128)S(1)}, f32[112,128]{1,0:T(8,128)S(1)}, u32[]{:S(2)}, u32[]{:S(2)}) collective-permute-start(f32[112,128]{1,0:T(8,128)S(1)} %sum_two.1.refs_0_), channel_id=1, source_target_pairs={{0,64},{4,68},{8,72},{12,76},{16,80},{20,84},{24,88},{28,92},{32,9... | collective-permute-start | bytes 172040 | tf_op jit(solution)/shard_map/ppermute | solution.py:260
  40.4 8.9 %collective-permute-start.9 = (f32[32,1536]{1,0:T(8,128)S(1)}, f32[32,1536]{1,0:T(8,128)S(1)}, u32[]{:S(2)}, u32[]{:S(2)}) collective-permute-start(f32[32,1536]{1,0:T(8,128)S(1)} %get-tuple-element.53), channel_id=1, source_target_pairs={{0,2},{1,3},{2,0},{3,1},{4,6},{5,7},{6,4},{7,5},{8,10},{9,11},{10,... | collective-permute-start | bytes 589832 | tf_op jit(solution)/shard_map/ppermute | solution.py:277
  46.0 5.7 %collective-permute-start.16 = (f32[112,128]{1,0:T(8,128)S(1)}, f32[112,128]{1,0:T(8,128)S(1)}, u32[]{:S(2)}, u32[]{:S(2)}) collective-permute-start(f32[112,128]{1,0:T(8,128)S(1)} %sum_four.3.refs_0_), channel_id=1, source_target_pairs={{0,24},{4,28},{8,16},{12,20},{16,8},{20,12},{24,0},{28,4},{32,56},... | collective-permute-start | bytes 172040 | tf_op jit(solution)/shard_map/ppermute | solution.py:260
  46.4 5.3 %collective-permute-start.15 = (f32[112,128]{1,0:T(8,128)S(1)}, f32[112,128]{1,0:T(8,128)S(1)}, u32[]{:S(2)}, u32[]{:S(2)}) collective-permute-start(f32[112,128]{1,0:T(8,128)S(1)} %sum_four.3.refs_0_), channel_id=1, source_target_pairs={{0,16},{4,20},{8,24},{12,28},{16,0},{20,4},{24,8},{28,12},{32,48},... | collective-permute-start | bytes 172040 | tf_op jit(solution)/shard_map/ppermute | solution.py:260
  47.0 4.6 %collective-permute-start.14 = (f32[112,128]{1,0:T(8,128)S(1)}, f32[112,128]{1,0:T(8,128)S(1)}, u32[]{:S(2)}, u32[]{:S(2)}) collective-permute-start(f32[112,128]{1,0:T(8,128)S(1)} %sum_four.3.refs_0_), channel_id=1, source_target_pairs={{0,8},{4,12},{8,0},{12,4},{16,24},{20,28},{24,16},{28,20},{32,40},... | collective-permute-start | bytes 172040 | tf_op jit(solution)/shard_map/ppermute | solution.py:260
  51.7 5.9 %collective-permute-start.17 = (f32[448,128]{1,0:T(8,128)S(1)}, f32[448,128]{1,0:T(8,128)S(1)}, u32[]{:S(2)}, u32[]{:S(2)}) collective-permute-start(f32[448,128]{1,0:T(8,128)S(1)} %join.3.even_ref), channel_id=1, source_target_pairs={{0,4},{4,0},{8,12},{12,8},{16,20},{20,16},{24,28},{28,24},{32,36},... | collective-permute-start | bytes 688136 | tf_op jit(solution)/shard_map/ppermute | solution.py:260

commit v6 on v5

--- a/solution.py
+++ b/solution.py
@@ -38,6 +38,34 @@
 
 def tile_span(t):
     return slice(LANES * t, LANES * (t + 1))
+
+
+def faces_kernel(x_ref, g_ref, near_ref, far_ref):
+    odd = (lax.axis_index("blk") & 1) == 1
+    for rows, ref in ((slice(0, 32), x_ref), (slice(32, 64), g_ref)):
+        lowest = ref[:, :FACE].astype(jnp.float32)
+        highest = ref[:, FACE : 2 * FACE].astype(jnp.float32)
+        near_ref[rows, :] = jnp.where(odd, lowest, highest).astype(jnp.bfloat16)
+        far_ref[rows, :] = jnp.where(odd, highest, lowest).astype(jnp.bfloat16)
+
+
+def by_side(near, far):
+    odd = (lax.axis_index("blk") & 1) == 1
+    near = near.astype(jnp.float32)
+    far = far.astype(jnp.float32)
+    return jnp.where(odd, near, far), jnp.where(odd, far, near)
+
+
+def gather_kernel(x_ref, rule_ref, dense_ref, table):
+    table[...] = x_ref[...].astype(jnp.float32)
+    for k in range(27):
+        row = rule_ref[k : k + 1, :]
+        for group in range(8):
+            tiles = source_tiles(group, k % 3 - 1)
+            if tiles[0] >= 8:
+                continue
+            got = picked(row, group, tiles, lambda t: table[:, tile_span(t)])
+            dense_ref[32 * k : 32 * k + 32, tile_span(group)] = got.astype(jnp.bfloat16)
 
 
 def faces_kernel(x_ref, g_ref, near_ref, far_ref):
@@ -86,16 +114,12 @@
         grad_ref[pl.ds(pl.multiple_of(32 * (chan ^ m), 32), 32), :] = part
     faces[:, :FACE], faces[:, FACE:] = by_side(near_ref[:32, :], far_ref[:32, :])
 
-    def step(j, carry):
+    for j in range(9):
         for group, d in ((0, 0), (1, 2)):
             k = 3 * j + d
-            row = rule_ref[pl.ds(k, 1), :]
+            row = rule_ref[k : k + 1, :]
             got = picked(row, group, (8 + group,), lambda t: faces[:, tile_span(t - 8)])
-            rows = pl.ds(pl.multiple_of(32 * k, 32), 32)
-            dense_ref[rows, tile_span(group)] = got.astype(jnp.bfloat16)
-        return carry
-
-    lax.fori_loop(0, 9, step, 0)
+            dense_ref[32 * k : 32 * k + 32, tile_span(group)] = got.astype(jnp.bfloat16)
     terms[:864, :] = lax.dot_general(
         dense_ref[...], grad_ref[...], (((1,), (1,)), ((), ())),
         preferred_element_type=jnp.float32,
@@ -138,30 +162,26 @@
     )
 
 
+def back_sum(groups, rule_ref, load):
+    totals = {}
+    for k in range(27):
+        row = rule_ref[k : k + 1, :]
+        rows = slice(32 * (26 - k), 32 * (26 - k) + 32)
+        for group in groups:
+            got = picked(row, group, source_tiles(group, k % 3 - 1), lambda t: load(rows, t))
+            totals[group] = got if k == 0 else totals[group] + got
+    return totals
+
+
 def back_inner_kernel(groups, terms, rule_ref, *refs):
-    out_ref = refs[-1]
+    totals = back_sum(groups, rule_ref, lambda rows, t: terms[rows, tile_span(t)])
     for group in groups:
-        out_ref[:, tile_span(group)] = jnp.zeros((32, LANES), jnp.float32)
-
-    def step(j, carry):
-        rules = [rule_ref[pl.ds(3 * j + d, 1), :] for d in range(3)]
-        for group in groups:
-            running = out_ref[:, tile_span(group)]
-            for d in range(3):
-                rows = pl.ds(pl.multiple_of(32 * (26 - 3 * j - d), 32), 32)
-                running = running + picked(
-                    rules[d], group, source_tiles(group, d - 1),
-                    lambda t: terms[rows, tile_span(t)],
-                )
-            out_ref[:, tile_span(group)] = running
-        return carry
-
-    lax.fori_loop(0, 9, step, 0)
+        refs[-1][:, tile_span(group)] = totals[group]
 
 
 def edge_kernel(
     terms, rule_ref, weight_ref, near_ref, far_ref, inner, own_ref, first_ref, second_ref,
-    out_ref, grad_ref, faces, products, total,
+    out_ref, grad_ref, faces, products,
 ):
     chan = lax.axis_index("ch")
     out_ref[...] = (own_ref[...] + second_ref[:, :VOX]).astype(jnp.bfloat16)
@@ -179,26 +199,13 @@
     products[...] = jnp.dot(
         weight_ref[...], faces[...], preferred_element_type=jnp.float32
     )
-    total[...] = jnp.zeros_like(total)
-
-    def step(j, carry):
-        rules = [rule_ref[pl.ds(3 * j + d, 1), :] for d in range(3)]
-        for group in EDGE:
-            running = total[:, tile_span(group)]
-            for d in range(3):
-                rows = pl.ds(pl.multiple_of(32 * (26 - 3 * j - d), 32), 32)
-                running = running + picked(
-                    rules[d], group, source_tiles(group, d - 1),
-                    lambda t: products[rows, tile_span(t - 8)] if t >= 8
-                    else terms[rows, tile_span(t)],
-                )
-            total[:, tile_span(group)] = running
-        return carry
-
-    lax.fori_loop(0, 9, step, 0)
+    totals = back_sum(
+        EDGE, rule_ref,
+        lambda rows, t: products[rows, tile_span(t - 8)] if t >= 8 else terms[rows, tile_span(t)],
+    )
     for group in range(8):
-        source = total if group in EDGE else inner
-        grad_ref[:, tile_span(group)] = source[:, tile_span(group)].astype(jnp.bfloat16)
+        values = totals[group] if group in EDGE else inner[:, tile_span(group)]
+        grad_ref[:, tile_span(group)] = values.astype(jnp.bfloat16)
 
 
 def split_sum_kernel(keep_ref, came_ref, *outs):
@@ -220,12 +227,11 @@
         refs[-1][size * q : size * (q + 1), :] = ref[...]
 
 
-def place_kernel(even_ref, odd_ref, out_ref, held):
+def place_kernel(*refs):
+    out_ref, held = refs[-2:]
     spot = lax.axis_index("blk") & 7
     for q in range(4):
-        rows = slice(PART * q, PART * (q + 1))
-        held[2 * PART * q : 2 * PART * q + PART, :] = even_ref[rows, :]
-        held[2 * PART * q + PART : 2 * PART * (q + 1), :] = odd_ref[rows, :]
+        held[2 * PART * q : 2 * PART * (q + 1), :] = refs[q][...]
     for p in range(8):
         count = min(PART, 864 - PART * p)
         start = pl.multiple_of(PART * (spot ^ p), 8)
@@ -321,32 +327,30 @@
     others = after(others, inner)
     total = call(sum_kernel, f32(PART, 128), (pieces[0], *others), name="sum_four")
     came = swap(total, 8)
+    inner = inner_part((4, 5), inner)
+    came, = after((came,), inner)
+    total = call(sum_kernel, f32(PART, 128), (total, came), name="sum_two")
+    others = [swap(total, m) for m in (16, 32, 48)]
     ours, first = after((ours, first), total)
     own, second = call(
         middle_kernel, (f32(32, VOX), f32(32, VOX + 4 * FACE)), (ours, first, near, far),
         name="middle",
     )
-    inner = inner_part((4,), inner)
-    came, = after((came,), inner, own)
-    total = call(sum_kernel, f32(PART, 128), (total, came), name="sum_two")
     second = over_ch(second, 2)
-    others = [swap(total, m) for m in (16, 32, 48)]
-    inner = inner_part((5, 6, 7), inner)
-    others = after(others, inner)
+    inner = inner_part((6, 7), inner)
+    others = after(others, inner, own)
     total = call(sum_kernel, f32(PART, 128), (total, *others), name="sum_four")
-    others = [swap(total, 2 * q) for q in (1, 2, 3)]
+    both = call(join_kernel, f32(2 * PART, 128), (total, swap(total, 1)), name="join")
+    others = [swap(both, 2 * q) for q in (1, 2, 3)]
     output, grad_features = call(
         edge_kernel, (bf16(32, VOX), bf16(32, VOX)),
         (back, rules, weights, near, far, inner, own, first, second),
-        [pltpu.VMEM((128, 2 * FACE), jnp.bfloat16), pltpu.VMEM((864, 2 * FACE), jnp.float32),
-         pltpu.VMEM((32, VOX), jnp.float32)],
+        [pltpu.VMEM((128, 2 * FACE), jnp.bfloat16), pltpu.VMEM((864, 2 * FACE), jnp.float32)],
         flops=2 << 30, name="edge",
     )
     others = after(others, output)
-    even = call(join_kernel, f32(4 * PART, 128), (total, *others), name="join")
-    odd = swap(even, 1)
     weight_grad = call(
-        place_kernel, f32(864, 128), (even, odd),
+        place_kernel, f32(864, 128), (both, *others),
         [pltpu.VMEM((8 * PART, 128), jnp.float32)], name="place",
     )
     return output, grad_features, weight_grad.reshape(27, 32, 128)

time: 58.6 us -> 56.6 us (0.966)
  Pallas kernels: 16.7 us -> 13.7 us
  waiting for transfers between devices: 4.48 us -> 6.73 us
  starting transfers between devices: 34.7 us -> 33.4 us
    ppermute x13, waiting for transfers between devices: 1.38 us -> 6.72 us  [swap(): return lax.ppermute(value, 'blk', [(i, i ^ mask) for i in range(count)])]
    ppermute x4, waiting for transfers between devices: 3.1 us -> 0.01 us  [over_ch(): return lax.ppermute(value, 'ch', [(i, i ^ mask) for i in range(4)])]
    pallas_call x17, Pallas kernels: 16.7 us -> 13.7 us  [call(): pl.pallas_call(kernel, out_shape=outs, in_specs=[VMEM] * len(args), out_s...]
    ppermute x13, starting transfers between devices: 26.4 us -> 24.9 us  [swap(): return lax.ppermute(value, 'blk', [(i, i ^ mask) for i in range(count)])]
  transfers between devices with their start and end apart: 18 -> 18, of which waited for: 3 -> 6; matrix products, arithmetic and copies ran while one was open for 0% -> 0% of each run, Pallas kernels for 25% -> 21%
where the time goes in v6:
time: 56.6 us; the launch traced here: 56.4 us
  starting transfers between devices  33.4 us (59%)
  Pallas kernels  13.7 us (24%)
  waiting for transfers between devices  6.73 us (12%)
  local copies, waits for them, and re-layouts  1.73 us (3%)
  between operations  0.81 us (1%)
    ppermute x13, starting transfers between devices, swap(): return lax.ppermute(value, 'blk', [(i, i ^ mask) for i in range(count)])  24.9 us
    pallas_call x17, Pallas kernels, call(): pl.pallas_call(kernel, out_shape=outs, in_specs=[VMEM] * len(args), out_s...  13.7 us
    ppermute x4, starting transfers between devices, over_ch(): return lax.ppermute(value, 'ch', [(i, i ^ mask) for i in range(4)])  7.47 us
    ppermute x13, waiting for transfers between devices, swap(): return lax.ppermute(value, 'blk', [(i, i ^ mask) for i in range(count)])  6.72 us
    unnamed x10, local copies, waits for them, and re-layouts  1.73 us
  transfers between devices with their start and end apart: 18, of which 6 were waited for; matrix products, arithmetic and copies ran while one was open for 0% of the time, Pallas kernels for 21%

profile of v6, /device:TPU:1, one launch (start us, length us, event | category | flops | bytes accessed | tf_op | source)
XLA Modules:
  0.0 56.4 jit_solution(11831368991655533239)
XLA Ops:
  0.6 2.2 %collective-permute-start.2 = (bf16[32,1024]{1,0:T(8,128)(2,1)}, bf16[32,1024]{1,0:T(8,128)(2,1)S(1)}, u32[]{:S(2)}, u32[]{:S(2)}) collective-permute-start(bf16[32,1024]{1,0:T(8,128)(2,1)} %refs_0_.1), channel_id=1, source_target_pairs={{0,1},{1,0},{2,3},{3,2},{4,5},{5,4},{6,7},{7,6},{8,9},{9,8},{10,11... | collective-permute-start | bytes 196616 | tf_op jit(solution)/shard_map/ppermute | solution.py:283
  2.8 0.9 %copy-done.1 = bf16[32,1024]{1,0:T(8,128)(2,1)S(1)} copy-done((bf16[32,1024]{1,0:T(8,128)(2,1)S(1)}, bf16[32,1024]{1,0:T(8,128)(2,1)}, u32[]{:S(2)}) %copy-start.1) | copy-done | bytes 65560
  3.7 0.8 %copy-done.4 = bf16[32,1024]{1,0:T(8,128)(2,1)S(1)} copy-done((bf16[32,1024]{1,0:T(8,128)(2,1)S(1)}, bf16[32,1024]{1,0:T(8,128)(2,1)}, u32[]{:S(2)}) %copy-start.4) | copy-done | bytes 65560
  4.6 1.2 %collective-permute-start = (bf16[64,128]{1,0:T(8,128)(2,1)S(1)}, bf16[64,128]{1,0:T(8,128)(2,1)S(1)}, u32[]{:S(2)}, u32[]{:S(2)}) collective-permute-start(bf16[64,128]{1,0:T(8,128)(2,1)S(1)} %get-tuple-element.33), channel_id=1, source_target_pairs={{0,4},{4,0},{8,12},{12,8},{16,20},{20,16},{24,28},{28,24},{32,36},... | collective-permute-start | bytes 49160 | tf_op jit(solution)/shard_map/ppermute | solution.py:266
  5.8 1.0 %collective-permute-start.1 = (bf16[64,128]{1,0:T(8,128)(2,1)S(1)}, bf16[64,128]{1,0:T(8,128)(2,1)S(1)}, u32[]{:S(2)}, u32[]{:S(2)}) collective-permute-start(bf16[64,128]{1,0:T(8,128)(2,1)S(1)} %get-tuple-element.34), channel_id=1, source_target_pairs={{0,252},{4,8},{8,4},{12,16},{16,12},{20,24},{24,20},{28,32},{32,28... | collective-permute-start | bytes 49160 | tf_op jit(solution)/shard_map/ppermute | solution.py:272
  6.8 2.7 %collective-permute-start.3 = (bf16[64,1024]{1,0:T(8,128)(2,1)S(1)}, bf16[64,1024]{1,0:T(8,128)(2,1)S(1)}, u32[]{:S(2)}, u32[]{:S(2)}) collective-permute-start(bf16[64,1024]{1,0:T(8,128)(2,1)S(1)} %join.2.pair_ref), channel_id=1, source_target_pairs={{0,2},{1,3},{2,0},{3,1},{4,6},{5,7},{6,4},{7,5},{8,10},{9,11},{10,... | collective-permute-start | bytes 393224 | tf_op jit(solution)/shard_map/ppermute | solution.py:283
  9.6 3.9 %gather.1.dense_in = bf16[864,1024]{1,0:T(8,128)(2,1)S(1)} custom-call(bf16[32,1024]{1,0:T(8,128)(2,1)S(1)} %copy-done.4, s32[27,1024]{1,0:T(8,128)S(1)} %copy-done.3), custom_call_target="tpu_custom_call" | custom-call | flops 3221225472 | bytes 1945600 | tf_op jit(solution)/shard_map/gather/pallas_call | solution.py:243
  13.5 0.7 %weight_terms.1 = (bf16[864,1024]{1,0:T(8,128)(2,1)S(1)}, bf16[128,1024]{1,0:T(8,128)(2,1)S(1)}, f32[448,128]{1,0:T(8,128)S(1)}, f32[448,128]{1,0:T(8,128)S(1)}) custom-call(bf16[864,1024]{1,0:T(8,128)(2,1)S(1)} %gather.1.dense_in, s32[27,1024]{1,0:T(8,128)S(1)} %copy-done.3, ...), custom_call_target="tpu_custom_call", output_to_operand_aliasing={{0}: (0, {})} | custom-call | flops 1073741824 | bytes 4665344 | tf_op jit(solution)/shard_map/weight_terms/pallas_call | solution.py:243
  14.2 7.3 %collective-permute-start.4 = (f32[448,128]{1,0:T(8,128)S(1)}, f32[448,128]{1,0:T(8,128)S(1)}, u32[]{:S(2)}, u32[]{:S(2)}) collective-permute-start(f32[448,128]{1,0:T(8,128)S(1)} %get-tuple-element.40), channel_id=1, source_target_pairs={{0,4},{4,0},{8,12},{12,8},{16,20},{20,16},{24,28},{28,24},{32,36},... | collective-permute-start | bytes 688136 | tf_op jit(solution)/shard_map/ppermute | solution.py:266
  21.5 0.6 %back_terms.1.terms = f32[864,1024]{1,0:T(8,128)S(1)} custom-call(bf16[864,128]{1,0:T(8,128)(2,1)S(1)} %bitcast.2, bf16[128,1024]{1,0:T(8,128)(2,1)S(1)} %get-tuple-element.35.grad_ref), custom_call_target="tpu_custom_call" | custom-call | flops 1073741824 | bytes 4022272 | tf_op jit(solution)/shard_map/back_terms/pallas_call | solution.py:243
  22.1 0.5 forward.1
  22.7 0.1 collective-permute-start.6
  22.8 0.1 collective-permute-start.7
  22.9 3.7 %collective-permute-start.8 = (f32[112,128]{1,0:T(8,128)S(1)}, f32[112,128]{1,0:T(8,128)S(1)}, u32[]{:S(2)}, u32[]{:S(2)}) collective-permute-start(f32[112,128]{1,0:T(8,128)S(1)} %get-tuple-element.45), channel_id=1, source_target_pairs={{0,24},{4,28},{8,16},{12,20},{16,8},{20,12},{24,0},{28,4},{32,56},... | collective-permute-start | bytes 172040 | tf_op jit(solution)/shard_map/ppermute | solution.py:266
  26.6 1.8 %back_inner.3.refs_0_ = f32[32,1024]{1,0:T(8,128)S(1)} custom-call(f32[864,1024]{1,0:T(8,128)S(1)} %back_terms.1.terms, s32[27,1024]{1,0:T(8,128)S(1)} %copy-done.3), custom_call_target="tpu_custom_call" | custom-call | flops 2147483648 | bytes 3780608 | tf_op jit(solution)/shard_map/back_inner/pallas_call | solution.py:243
  28.5 0.7 %collective-permute-done.8.refs_3_ = f32[112,128]{1,0:T(8,128)S(1)} collective-permute-done((f32[112,128]{1,0:T(8,128)S(1)}, f32[112,128]{1,0:T(8,128)S(1)}, u32[]{:S(2)}, u32[]{:S(2)}) %collective-permute-start.8) | collective-permute-done | bytes 57376 | tf_op jit(solution)/shard_map/ppermute | solution.py:266
  29.3 1.8 %back_inner.4.refs_0_ = f32[32,1024]{1,0:T(8,128)S(1)} custom-call(f32[864,1024]{1,0:T(8,128)S(1)} %back_terms.1.terms, s32[27,1024]{1,0:T(8,128)S(1)} %copy-done.3, f32[32,1024]{1,0:T(8,128)S(1)} %back_inner.3.refs_0_), custom_call_target="tpu_custom_call", output_to_operand_aliasing={{}: (2, {})} | custom-call | flops 2147483648 | bytes 3911680 | tf_op jit(solution)/shard_map/back_inner/pallas_call | solution.py:243
  31.2 1.5 %collective-permute-done.9.refs_1_ = f32[112,128]{1,0:T(8,128)S(1)} collective-permute-done((f32[112,128]{1,0:T(8,128)S(1)}, f32[112,128]{1,0:T(8,128)S(1)}, u32[]{:S(2)}, u32[]{:S(2)}) %collective-permute-start.9) | collective-permute-done | bytes 57376 | tf_op jit(solution)/shard_map/ppermute | solution.py:266
  32.7 0.9 %collective-permute-start.13 = (f32[112,128]{1,0:T(8,128)S(1)}, f32[112,128]{1,0:T(8,128)S(1)}, u32[]{:S(2)}, u32[]{:S(2)}) collective-permute-start(f32[112,128]{1,0:T(8,128)S(1)} %sum_two.1.refs_0_), channel_id=1, source_target_pairs={{0,192},{4,196},{8,200},{12,204},{16,208},{20,212},{24,216},{28,22... | collective-permute-start | bytes 172040 | tf_op jit(solution)/shard_map/ppermute | solution.py:266
  33.5 1.8 %collective-permute-start.12 = (f32[112,128]{1,0:T(8,128)S(1)}, f32[112,128]{1,0:T(8,128)S(1)}, u32[]{:S(2)}, u32[]{:S(2)}) collective-permute-start(f32[112,128]{1,0:T(8,128)S(1)} %sum_two.1.refs_0_), channel_id=1, source_target_pairs={{0,128},{4,132},{8,136},{12,140},{16,144},{20,148},{24,152},{28,15... | collective-permute-start | bytes 172040 | tf_op jit(solution)/shard_map/ppermute | solution.py:266
  35.3 3.1 %collective-permute-start.11 = (f32[112,128]{1,0:T(8,128)S(1)}, f32[112,128]{1,0:T(8,128)S(1)}, u32[]{:S(2)}, u32[]{:S(2)}) collective-permute-start(f32[112,128]{1,0:T(8,128)S(1)} %sum_two.1.refs_0_), channel_id=1, source_target_pairs={{0,64},{4,68},{8,72},{12,76},{16,80},{20,84},{24,88},{28,92},{32,9... | collective-permute-start | bytes 172040 | tf_op jit(solution)/shard_map/ppermute | solution.py:266
  38.5 2.5 %collective-permute-start.10 = (f32[32,1536]{1,0:T(8,128)S(1)}, f32[32,1536]{1,0:T(8,128)S(1)}, u32[]{:S(2)}, u32[]{:S(2)}) collective-permute-start(f32[32,1536]{1,0:T(8,128)S(1)} %get-tuple-element.54), channel_id=1, source_target_pairs={{0,2},{1,3},{2,0},{3,1},{4,6},{5,7},{6,4},{7,5},{8,10},{9,11},{10,... | collective-permute-start | bytes 589832 | tf_op jit(solution)/shard_map/ppermute | solution.py:283
  41.0 1.8 %back_inner.5.inner = f32[32,1024]{1,0:T(8,128)S(1)} custom-call(f32[864,1024]{1,0:T(8,128)S(1)} %back_terms.1.terms, s32[27,1024]{1,0:T(8,128)S(1)} %copy-done.3, f32[32,1024]{1,0:T(8,128)S(1)} %back_inner.4.refs_0_), custom_call_target="tpu_custom_call", output_to_operand_aliasing={{}: (2, {})} | custom-call | flops 2147483648 | bytes 3911680 | tf_op jit(solution)/shard_map/back_inner/pallas_call | solution.py:243
  42.9 3.3 %collective-permute-start.14 = (f32[112,128]{1,0:T(8,128)S(1)}, f32[112,128]{1,0:T(8,128)S(1)}, u32[]{:S(2)}, u32[]{:S(2)}) collective-permute-start(f32[112,128]{1,0:T(8,128)S(1)} %sum_four.3.refs_0_), channel_id=1, source_target_pairs={{0,4},{4,0},{8,12},{12,8},{16,20},{20,16},{24,28},{28,24},{32,36},... | collective-permute-start | bytes 172040 | tf_op jit(solution)/shard_map/ppermute | solution.py:266
  46.2 0.9 %collective-permute-done.14.refs_1_ = f32[112,128]{1,0:T(8,128)S(1)} collective-permute-done((f32[112,128]{1,0:T(8,128)S(1)}, f32[112,128]{1,0:T(8,128)S(1)}, u32[]{:S(2)}, u32[]{:S(2)}) %collective-permute-start.14) | collective-permute-done | bytes 57376 | tf_op jit(solution)/shard_map/ppermute | solution.py:266
  47.1 2.6 %collective-permute-start.17 = (f32[224,128]{1,0:T(8,128)S(1)}, f32[224,128]{1,0:T(8,128)S(1)}, u32[]{:S(2)}, u32[]{:S(2)}) collective-permute-start(f32[224,128]{1,0:T(8,128)S(1)} %join.3.refs_0_), channel_id=1, source_target_pairs={{0,24},{4,28},{8,16},{12,20},{16,8},{20,12},{24,0},{28,4},{32,56},... | collective-permute-start | bytes 344072 | tf_op jit(solution)/shard_map/ppermute | solution.py:266
  49.7 0.8 %collective-permute-start.15 = (f32[224,128]{1,0:T(8,128)S(1)}, f32[224,128]{1,0:T(8,128)S(1)}, u32[]{:S(2)}, u32[]{:S(2)}) collective-permute-start(f32[224,128]{1,0:T(8,128)S(1)} %join.3.refs_0_), channel_id=1, source_target_pairs={{0,8},{4,12},{8,0},{12,4},{16,24},{20,28},{24,16},{28,20},{32,40},... | collective-permute-start | bytes 344072 | tf_op jit(solution)/shard_map/ppermute | solution.py:266
  50.4 1.5 %edge.1 = (bf16[32,1024]{1,0:T(8,128)(2,1)}, bf16[32,1024]{1,0:T(8,128)(2,1)}) custom-call(f32[864,1024]{1,0:T(8,128)S(1)} %back_terms.1.terms, s32[27,1024]{1,0:T(8,128)S(1)} %copy-done.3, bf16[864,128]{1,0:T(8,128)(2,1)S(1)} %bitcast.4, bf16[64,128]{1,0:T(8,128)(2,1)S(1)} %collective-permute-done.near_ref, ...), custom_call_target="tpu_custom_call" | custom-call | flops 2147483648 | bytes 4788224 | tf_op jit(solution)/shard_map/edge/pallas_call | solution.py:243
  52.0 2.4 %collective-permute-done.17.refs_3_ = f32[224,128]{1,0:T(8,128)S(1)} collective-permute-done((f32[224,128]{1,0:T(8,128)S(1)}, f32[224,128]{1,0:T(8,128)S(1)}, u32[]{:S(2)}, u32[]{:S(2)}) %collective-permute-start.17) | collective-permute-done | bytes 114720 | tf_op jit(solution)/shard_map/ppermute | solution.py:266
  54.4 0.9 %collective-permute-done.16.refs_2_ = f32[224,128]{1,0:T(8,128)S(1)} collective-permute-done((f32[224,128]{1,0:T(8,128)S(1)}, f32[224,128]{1,0:T(8,128)S(1)}, u32[]{:S(2)}, u32[]{:S(2)}) %collective-permute-start.16) | collective-permute-done | bytes 114720 | tf_op jit(solution)/shard_map/ppermute | solution.py:266
  55.2 0.3 collective-permute-done.15.refs_1_
  55.6 0.8 %place.1 = f32[864,128]{1,0:T(8,128)} custom-call(f32[224,128]{1,0:T(8,128)S(1)} %join.3.refs_0_, f32[224,128]{1,0:T(8,128)S(1)} %collective-permute-done.15.refs_1_, f32[224,128]{1,0:T(8,128)S(1)} %collective-permute-done.16.refs_2_, f32[224,128]{1,0:T(8,128)S(1)} %collective-permute-done.17.refs_3_), custom_call_target="tpu_custom_call" | custom-call | bytes 901120 | tf_op jit(solution)/shard_map/place/pallas_call | solution.py:243
  (31 shorter events, 0.3 us)
Async XLA Ops:
  0.6 6.2 %collective-permute-start.2 = (bf16[32,1024]{1,0:T(8,128)(2,1)}, bf16[32,1024]{1,0:T(8,128)(2,1)S(1)}, u32[]{:S(2)}, u32[]{:S(2)}) collective-permute-start(bf16[32,1024]{1,0:T(8,128)(2,1)} %refs_0_.1), channel_id=1, source_target_pairs={{0,1},{1,0},{2,3},{3,2},{4,5},{5,4},{6,7},{7,6},{8,9},{9,8},{10,11... | collective-permute-start | bytes 196616 | tf_op jit(solution)/shard_map/ppermute | solution.py:283
  2.8 0.9 %copy-start.1 = (bf16[32,1024]{1,0:T(8,128)(2,1)S(1)}, bf16[32,1024]{1,0:T(8,128)(2,1)}, u32[]{:S(2)}) copy-start(bf16[32,1024]{1,0:T(8,128)(2,1)} %refs_0_.1) | copy-start | bytes 196612
  3.7 0.8 %copy-start.4 = (bf16[32,1024]{1,0:T(8,128)(2,1)S(1)}, bf16[32,1024]{1,0:T(8,128)(2,1)}, u32[]{:S(2)}) copy-start(bf16[32,1024]{1,0:T(8,128)(2,1)} %x_ref.3) | copy-start | bytes 196612
  4.6 2.3 %copy-start.2 = (bf16[32,1024]{1,0:T(8,128)(2,1)S(1)}, bf16[32,1024]{1,0:T(8,128)(2,1)}, u32[]{:S(2)}) copy-start(bf16[32,1024]{1,0:T(8,128)(2,1)} %refs_0_.1) | copy-start | bytes 196612
  4.6 5.0 %copy-start.3 = (s32[27,1024]{1,0:T(8,128)S(1)}, s32[27,1024]{1,0:T(8,128)}, u32[]{:S(2)}) copy-start(s32[27,1024]{1,0:T(8,128)} %rule_ref.11) | copy-start | bytes 331780
  4.6 8.8 %collective-permute-start = (bf16[64,128]{1,0:T(8,128)(2,1)S(1)}, bf16[64,128]{1,0:T(8,128)(2,1)S(1)}, u32[]{:S(2)}, u32[]{:S(2)}) collective-permute-start(bf16[64,128]{1,0:T(8,128)(2,1)S(1)} %get-tuple-element.33), channel_id=1, source_target_pairs={{0,4},{4,0},{8,12},{12,8},{16,20},{20,16},{24,28},{28,24},{32,36},... | collective-permute-start | bytes 49160 | tf_op jit(solution)/shard_map/ppermute | solution.py:266
  5.8 7.6 %collective-permute-start.1 = (bf16[64,128]{1,0:T(8,128)(2,1)S(1)}, bf16[64,128]{1,0:T(8,128)(2,1)S(1)}, u32[]{:S(2)}, u32[]{:S(2)}) collective-permute-start(bf16[64,128]{1,0:T(8,128)(2,1)S(1)} %get-tuple-element.34), channel_id=1, source_target_pairs={{0,252},{4,8},{8,4},{12,16},{16,12},{20,24},{24,20},{28,32},{32,28... | collective-permute-start | bytes 49160 | tf_op jit(solution)/shard_map/ppermute | solution.py:272
  6.8 6.6 %collective-permute-start.3 = (bf16[64,1024]{1,0:T(8,128)(2,1)S(1)}, bf16[64,1024]{1,0:T(8,128)(2,1)S(1)}, u32[]{:S(2)}, u32[]{:S(2)}) collective-permute-start(bf16[64,1024]{1,0:T(8,128)(2,1)S(1)} %join.2.pair_ref), channel_id=1, source_target_pairs={{0,2},{1,3},{2,0},{3,1},{4,6},{5,7},{6,4},{7,5},{8,10},{9,11},{10,... | collective-permute-start | bytes 393224 | tf_op jit(solution)/shard_map/ppermute | solution.py:283
  13.4 8.1 %copy-start = (bf16[27,32,128]{2,1,0:T(8,128)(2,1)S(1)}, bf16[27,32,128]{2,1,0:T(8,128)(2,1)}, u32[]{:S(2)}) copy-start(bf16[27,32,128]{2,1,0:T(8,128)(2,1)} %param.5) | copy-start | bytes 663556
  14.2 8.5 %collective-permute-start.4 = (f32[448,128]{1,0:T(8,128)S(1)}, f32[448,128]{1,0:T(8,128)S(1)}, u32[]{:S(2)}, u32[]{:S(2)}) collective-permute-start(f32[448,128]{1,0:T(8,128)S(1)} %get-tuple-element.40), channel_id=1, source_target_pairs={{0,4},{4,0},{8,12},{12,8},{16,20},{20,16},{24,28},{28,24},{32,36},... | collective-permute-start | bytes 688136 | tf_op jit(solution)/shard_map/ppermute | solution.py:266
  22.7 5.8 %collective-permute-start.6 = (f32[112,128]{1,0:T(8,128)S(1)}, f32[112,128]{1,0:T(8,128)S(1)}, u32[]{:S(2)}, u32[]{:S(2)}) collective-permute-start(f32[112,128]{1,0:T(8,128)S(1)} %get-tuple-element.43), channel_id=1, source_target_pairs={{0,8},{4,12},{8,0},{12,4},{16,24},{20,28},{24,16},{28,20},{32,40},... | collective-permute-start | bytes 172040 | tf_op jit(solution)/shard_map/ppermute | solution.py:266
  22.8 5.7 %collective-permute-start.7 = (f32[112,128]{1,0:T(8,128)S(1)}, f32[112,128]{1,0:T(8,128)S(1)}, u32[]{:S(2)}, u32[]{:S(2)}) collective-permute-start(f32[112,128]{1,0:T(8,128)S(1)} %get-tuple-element.44), channel_id=1, source_target_pairs={{0,16},{4,20},{8,24},{12,28},{16,0},{20,4},{24,8},{28,12},{32,48},... | collective-permute-start | bytes 172040 | tf_op jit(solution)/shard_map/ppermute | solution.py:266
  22.9 6.3 %collective-permute-start.8 = (f32[112,128]{1,0:T(8,128)S(1)}, f32[112,128]{1,0:T(8,128)S(1)}, u32[]{:S(2)}, u32[]{:S(2)}) collective-permute-start(f32[112,128]{1,0:T(8,128)S(1)} %get-tuple-element.45), channel_id=1, source_target_pairs={{0,24},{4,28},{8,16},{12,20},{16,8},{20,12},{24,0},{28,4},{32,56},... | collective-permute-start | bytes 172040 | tf_op jit(solution)/shard_map/ppermute | solution.py:266
  26.6 11.8 %collective-permute-start.5 = (f32[64,1152]{1,0:T(8,128)S(1)}, f32[64,1152]{1,0:T(8,128)S(1)}, u32[]{:S(2)}, u32[]{:S(2)}) collective-permute-start(f32[64,1152]{1,0:T(8,128)S(1)} %get-tuple-element.46), channel_id=1, source_target_pairs={{0,1},{1,0},{2,3},{3,2},{4,5},{5,4},{6,7},{7,6},{8,9},{9,8},{10,11... | collective-permute-start | bytes 884744 | tf_op jit(solution)/shard_map/ppermute | solution.py:283
  29.2 3.4 %collective-permute-start.9 = (f32[112,128]{1,0:T(8,128)S(1)}, f32[112,128]{1,0:T(8,128)S(1)}, u32[]{:S(2)}, u32[]{:S(2)}) collective-permute-start(f32[112,128]{1,0:T(8,128)S(1)} %sum_four.2.refs_0_), channel_id=1, source_target_pairs={{0,32},{4,36},{8,40},{12,44},{16,48},{20,52},{24,56},{28,60},{32,0... | collective-permute-start | bytes 172040 | tf_op jit(solution)/shard_map/ppermute | solution.py:266
  32.7 10.2 %collective-permute-start.13 = (f32[112,128]{1,0:T(8,128)S(1)}, f32[112,128]{1,0:T(8,128)S(1)}, u32[]{:S(2)}, u32[]{:S(2)}) collective-permute-start(f32[112,128]{1,0:T(8,128)S(1)} %sum_two.1.refs_0_), channel_id=1, source_target_pairs={{0,192},{4,196},{8,200},{12,204},{16,208},{20,212},{24,216},{28,22... | collective-permute-start | bytes 172040 | tf_op jit(solution)/shard_map/ppermute | solution.py:266
  33.5 9.3 %collective-permute-start.12 = (f32[112,128]{1,0:T(8,128)S(1)}, f32[112,128]{1,0:T(8,128)S(1)}, u32[]{:S(2)}, u32[]{:S(2)}) collective-permute-start(f32[112,128]{1,0:T(8,128)S(1)} %sum_two.1.refs_0_), channel_id=1, source_target_pairs={{0,128},{4,132},{8,136},{12,140},{16,144},{20,148},{24,152},{28,15... | collective-permute-start | bytes 172040 | tf_op jit(solution)/shard_map/ppermute | solution.py:266
  35.3 7.5 %collective-permute-start.11 = (f32[112,128]{1,0:T(8,128)S(1)}, f32[112,128]{1,0:T(8,128)S(1)}, u32[]{:S(2)}, u32[]{:S(2)}) collective-permute-start(f32[112,128]{1,0:T(8,128)S(1)} %sum_two.1.refs_0_), channel_id=1, source_target_pairs={{0,64},{4,68},{8,72},{12,76},{16,80},{20,84},{24,88},{28,92},{32,9... | collective-permute-start | bytes 172040 | tf_op jit(solution)/shard_map/ppermute | solution.py:266
  38.5 12.0 %collective-permute-start.10 = (f32[32,1536]{1,0:T(8,128)S(1)}, f32[32,1536]{1,0:T(8,128)S(1)}, u32[]{:S(2)}, u32[]{:S(2)}) collective-permute-start(f32[32,1536]{1,0:T(8,128)S(1)} %get-tuple-element.54), channel_id=1, source_target_pairs={{0,2},{1,3},{2,0},{3,1},{4,6},{5,7},{6,4},{7,5},{8,10},{9,11},{10,... | collective-permute-start | bytes 589832 | tf_op jit(solution)/shard_map/ppermute | solution.py:283
  42.9 4.2 %collective-permute-start.14 = (f32[112,128]{1,0:T(8,128)S(1)}, f32[112,128]{1,0:T(8,128)S(1)}, u32[]{:S(2)}, u32[]{:S(2)}) collective-permute-start(f32[112,128]{1,0:T(8,128)S(1)} %sum_four.3.refs_0_), channel_id=1, source_target_pairs={{0,4},{4,0},{8,12},{12,8},{16,20},{20,16},{24,28},{28,24},{32,36},... | collective-permute-start | bytes 172040 | tf_op jit(solution)/shard_map/ppermute | solution.py:266
  47.1 7.3 %collective-permute-start.17 = (f32[224,128]{1,0:T(8,128)S(1)}, f32[224,128]{1,0:T(8,128)S(1)}, u32[]{:S(2)}, u32[]{:S(2)}) collective-permute-start(f32[224,128]{1,0:T(8,128)S(1)} %join.3.refs_0_), channel_id=1, source_target_pairs={{0,24},{4,28},{8,16},{12,20},{16,8},{20,12},{24,0},{28,4},{32,56},... | collective-permute-start | bytes 344072 | tf_op jit(solution)/shard_map/ppermute | solution.py:266
  49.7 5.6 %collective-permute-start.16 = (f32[224,128]{1,0:T(8,128)S(1)}, f32[224,128]{1,0:T(8,128)S(1)}, u32[]{:S(2)}, u32[]{:S(2)}) collective-permute-start(f32[224,128]{1,0:T(8,128)S(1)} %join.3.refs_0_), channel_id=1, source_target_pairs={{0,16},{4,20},{8,24},{12,28},{16,0},{20,4},{24,8},{28,12},{32,48},... | collective-permute-start | bytes 344072 | tf_op jit(solution)/shard_map/ppermute | solution.py:266
  49.7 5.9 %collective-permute-start.15 = (f32[224,128]{1,0:T(8,128)S(1)}, f32[224,128]{1,0:T(8,128)S(1)}, u32[]{:S(2)}, u32[]{:S(2)}) collective-permute-start(f32[224,128]{1,0:T(8,128)S(1)} %join.3.refs_0_), channel_id=1, source_target_pairs={{0,8},{4,12},{8,0},{12,4},{16,24},{20,28},{24,16},{28,20},{32,40},... | collective-permute-start | bytes 344072 | tf_op jit(solution)/shard_map/ppermute | solution.py:266

commit v7 on v6

--- a/solution.py
+++ b/solution.py
@@ -13,6 +13,7 @@
 PART = 112
 INNER = tuple(range(2, 8))
 EDGE = (0, 1)
+ORDER = (0, 1, 3, 2)
 VMEM = pl.BlockSpec(memory_space=pltpu.VMEM)
 
 
@@ -109,8 +110,8 @@
 ):
     chan = lax.axis_index("ch")
     spot = lax.axis_index("blk") & 7
-    for m in range(4):
-        part = (pair_ref if m < 2 else other_ref)[32 * (m % 2) : 32 * (m % 2) + 32, :]
+    for i, m in enumerate(ORDER):
+        part = (pair_ref if i < 2 else other_ref)[32 * (i % 2) : 32 * (i % 2) + 32, :]
         grad_ref[pl.ds(pl.multiple_of(32 * (chan ^ m), 32), 32), :] = part
     faces[:, :FACE], faces[:, FACE:] = by_side(near_ref[:32, :], far_ref[:32, :])
 
@@ -125,10 +126,10 @@
         preferred_element_type=jnp.float32,
     ) * (1.0 / 256.0)
     terms[864:, :] = jnp.zeros((32, LANES), jnp.float32)
-    for q in range(4):
+    for i, q in enumerate((0, 3, 1, 2)):
         for odd, target in ((0, keep_ref), (1, send_ref)):
             start = pl.multiple_of(PART * (spot ^ (2 * q + odd)), 8)
-            target[PART * q : PART * (q + 1), :] = terms[pl.ds(start, PART), :]
+            target[PART * i : PART * (i + 1), :] = terms[pl.ds(start, PART), :]
 
 
 def forward_kernel(dense_ref, weight_ref, near_ref, far_ref, keep_ref, send_ref, sums):
@@ -137,10 +138,10 @@
         weight_ref[...], dense_ref[...], (((0,), (0,)), ((), ())),
         preferred_element_type=jnp.float32,
     )
-    for m in range(4):
-        target = send_ref if m % 2 else keep_ref
-        rows = pl.ds(pl.multiple_of(32 * (chan ^ m), 32), 32)
-        target[32 * (m // 2) : 32 * (m // 2) + 32, :VOX] = sums[rows, :]
+    for target, parts in ((keep_ref, (0, 3)), (send_ref, (1, 2))):
+        for i, m in enumerate(parts):
+            rows = pl.ds(pl.multiple_of(32 * (chan ^ m), 32), 32)
+            target[32 * i : 32 * i + 32, :VOX] = sums[rows, :]
     lower, upper = by_side(near_ref[32:, :], far_ref[32:, :])
     send_ref[:32, VOX:] = lower
     send_ref[32:, VOX:] = upper
@@ -192,7 +193,7 @@
         (second_ref[:, VOX : VOX + FACE], second_ref[:, VOX + FACE : VOX + 2 * FACE]),
         (second_ref[:, VOX + 2 * FACE : VOX + 3 * FACE], second_ref[:, VOX + 3 * FACE :]),
     )
-    for m, (lower, upper) in enumerate(pairs):
+    for m, (lower, upper) in zip(ORDER, pairs):
         rows = pl.ds(pl.multiple_of(32 * (chan ^ m), 32), 32)
         faces[rows, :FACE] = lower.astype(jnp.bfloat16)
         faces[rows, FACE:] = upper.astype(jnp.bfloat16)
@@ -208,30 +209,28 @@
         grad_ref[:, tile_span(group)] = values.astype(jnp.bfloat16)
 
 
-def split_sum_kernel(keep_ref, came_ref, *outs):
-    for q, out in enumerate(outs):
-        rows = slice(PART * q, PART * (q + 1))
-        out[...] = keep_ref[rows, :] + came_ref[rows, :]
-
-
-def sum_kernel(*refs):
-    values = [ref[...] for ref in refs[:-1]]
-    while len(values) > 1:
-        values = [values[i] + values[i + 1] for i in range(0, len(values), 2)]
-    refs[-1][...] = values[0]
-
-
-def join_kernel(*refs):
-    size = refs[0].shape[0]
-    for q, ref in enumerate(refs[:-1]):
-        refs[-1][size * q : size * (q + 1), :] = ref[...]
-
-
-def place_kernel(*refs):
-    out_ref, held = refs[-2:]
+def halve_kernel(keep_ref, came_ref, low_ref, high_ref):
+    half = low_ref.shape[0]
+    low_ref[...] = keep_ref[:half, :] + came_ref[:half, :]
+    high_ref[...] = keep_ref[half:, :] + came_ref[half:, :]
+
+
+def add_kernel(a_ref, b_ref, out_ref):
+    out_ref[...] = a_ref[...] + b_ref[...]
+
+
+def join_kernel(a_ref, b_ref, out_ref):
+    half = a_ref.shape[0]
+    out_ref[:half, :] = a_ref[...]
+    out_ref[half:, :] = b_ref[...]
+
+
+def place_kernel(even_ref, odd_ref, out_ref, held):
     spot = lax.axis_index("blk") & 7
-    for q in range(4):
-        held[2 * PART * q : 2 * PART * (q + 1), :] = refs[q][...]
+    for i, q in enumerate((0, 3, 1, 2)):
+        for odd, ref in enumerate((even_ref, odd_ref)):
+            start = PART * (2 * q + odd)
+            held[start : start + PART, :] = ref[PART * i : PART * (i + 1), :]
     for p in range(8):
         count = min(PART, 864 - PART * p)
         start = pl.multiple_of(PART * (spot ^ p), 8)
@@ -289,7 +288,7 @@
     pair = call(join_kernel, bf16(64, VOX), (g, over_ch(g, 1)), name="join")
     near = swap(near, 1)
     far = swap_far(far)
-    other = over_ch(pair, 2)
+    other = over_ch(pair, 3)
     dense = call(
         gather_kernel, bf16(864, VOX), (x, rules),
         [pltpu.VMEM((32, VOX), jnp.float32)], flops=3 << 30, name="gather",
@@ -319,38 +318,44 @@
         back_terms_kernel, f32(864, VOX), (weights, grads), flops=1 << 30, name="back_terms"
     )
     came, = after((came,), ours, back)
-    pieces = call(split_sum_kernel, (f32(PART, 128),) * 4, (keep, came), name="sum_pair")
-    others = [swap(pieces[q], 2 * q) for q in (1, 2, 3)]
-    first, = after((first,), *pieces)
+    kept, sent = call(halve_kernel, (f32(2 * PART, 128),) * 2, (keep, came), name="halve")
+    came = swap(sent, 2)
+    first, = after((first,), kept)
     first = over_ch(first, 1)
-    inner = inner_part((2, 3))
-    others = after(others, inner)
-    total = call(sum_kernel, f32(PART, 128), (pieces[0], *others), name="sum_four")
+    inner = inner_part((2,))
+    came, = after((came,), inner)
+    kept, sent = call(halve_kernel, (f32(PART, 128),) * 2, (kept, came), name="halve")
+    came = swap(sent, 6)
+    inner = inner_part((3,), inner)
+    came, = after((came,), inner)
+    total = call(add_kernel, f32(PART, 128), (kept, came), name="add")
     came = swap(total, 8)
-    inner = inner_part((4, 5), inner)
-    came, = after((came,), inner)
-    total = call(sum_kernel, f32(PART, 128), (total, came), name="sum_two")
-    others = [swap(total, m) for m in (16, 32, 48)]
     ours, first = after((ours, first), total)
     own, second = call(
         middle_kernel, (f32(32, VOX), f32(32, VOX + 4 * FACE)), (ours, first, near, far),
         name="middle",
     )
-    second = over_ch(second, 2)
-    inner = inner_part((6, 7), inner)
-    others = after(others, inner, own)
-    total = call(sum_kernel, f32(PART, 128), (total, *others), name="sum_four")
-    both = call(join_kernel, f32(2 * PART, 128), (total, swap(total, 1)), name="join")
-    others = [swap(both, 2 * q) for q in (1, 2, 3)]
+    second = over_ch(second, 3)
+    came, = after((came,), own)
+    total = call(add_kernel, f32(PART, 128), (total, came), name="add")
+    for mask, groups in ((16, (4, 5)), (48, (6, 7))):
+        came = swap(total, mask)
+        inner = inner_part(groups, inner)
+        came, = after((came,), inner)
+        total = call(add_kernel, f32(PART, 128), (total, came), name="add")
+    total = call(join_kernel, f32(2 * PART, 128), (total, swap(total, 6)), name="join")
+    came = swap(total, 2)
     output, grad_features = call(
         edge_kernel, (bf16(32, VOX), bf16(32, VOX)),
         (back, rules, weights, near, far, inner, own, first, second),
         [pltpu.VMEM((128, 2 * FACE), jnp.bfloat16), pltpu.VMEM((864, 2 * FACE), jnp.float32)],
         flops=2 << 30, name="edge",
     )
-    others = after(others, output)
+    came, = after((came,), output)
+    even = call(join_kernel, f32(4 * PART, 128), (total, came), name="join")
+    odd = swap(even, 1)
     weight_grad = call(
-        place_kernel, f32(864, 128), (both, *others),
+        place_kernel, f32(864, 128), (even, odd),
         [pltpu.VMEM((8 * PART, 128), jnp.float32)], name="place",
     )
     return output, grad_features, weight_grad.reshape(27, 32, 128)

time: 56.6 us -> 62.5 us (1.10)
  waiting for transfers between devices: 6.73 us -> 18.7 us
  starting transfers between devices: 33.4 us -> 27.3 us
    ppermute x13 -> x10, waiting for transfers between devices: 6.72 us -> 18.7 us  [swap(): return lax.ppermute(value, 'blk', [(i, i ^ mask) for i in range(count)])]
    ppermute x13 -> x10, starting transfers between devices: 24.9 us -> 19.6 us  [swap(): return lax.ppermute(value, 'blk', [(i, i ^ mask) for i in range(count)])]
    ppermute x4, starting transfers between devices: 7.47 us -> 6.71 us  [over_ch(): return lax.ppermute(value, 'ch', [(i, i ^ mask) for i in range(4)])]
    pallas_call x17 -> x21, Pallas kernels: 13.7 us -> 13.8 us  [call(): pl.pallas_call(kernel, out_shape=outs, in_specs=[VMEM] * len(args), out_s...]
  transfers between devices with their start and end apart: 18 -> 15, of which waited for: 6 -> 8; matrix products, arithmetic and copies ran while one was open for 0% -> 0% of each run, Pallas kernels for 21% -> 20%
where the time goes in v7:
time: 62.5 us; the launch traced here: 62.3 us
  starting transfers between devices  27.3 us (44%)
  waiting for transfers between devices  18.7 us (30%)
  Pallas kernels  13.8 us (22%)
  local copies, waits for them, and re-layouts  1.73 us (3%)
  between operations  0.8 us (1%)
    ppermute x10, starting transfers between devices, swap(): return lax.ppermute(value, 'blk', [(i, i ^ mask) for i in range(count)])  19.6 us
    ppermute x10, waiting for transfers between devices, swap(): return lax.ppermute(value, 'blk', [(i, i ^ mask) for i in range(count)])  18.7 us
    pallas_call x21, Pallas kernels, call(): pl.pallas_call(kernel, out_shape=outs, in_specs=[VMEM] * len(args), out_s...  13.8 us
    ppermute x4, starting transfers between devices, over_ch(): return lax.ppermute(value, 'ch', [(i, i ^ mask) for i in range(4)])  6.71 us
    unnamed x10, local copies, waits for them, and re-layouts  1.73 us
  transfers between devices with their start and end apart: 15, of which 8 were waited for; matrix products, arithmetic and copies ran while one was open for 0% of the time, Pallas kernels for 20%

profile of v7, /device:TPU:1, one launch (start us, length us, event | category | flops | bytes accessed | tf_op | source)
XLA Modules:
  0.0 62.3 jit_solution(8650442888757697151)
XLA Ops:
  0.6 2.2 %collective-permute-start.2 = (bf16[32,1024]{1,0:T(8,128)(2,1)}, bf16[32,1024]{1,0:T(8,128)(2,1)S(1)}, u32[]{:S(2)}, u32[]{:S(2)}) collective-permute-start(bf16[32,1024]{1,0:T(8,128)(2,1)} %a_ref.1), channel_id=1, source_target_pairs={{0,1},{1,0},{2,3},{3,2},{4,5},{5,4},{6,7},{7,6},{8,9},{9,8},{10,11... | collective-permute-start | bytes 196616 | tf_op jit(solution)/shard_map/ppermute | solution.py:282
  2.8 0.9 %copy-done.1 = bf16[32,1024]{1,0:T(8,128)(2,1)S(1)} copy-done((bf16[32,1024]{1,0:T(8,128)(2,1)S(1)}, bf16[32,1024]{1,0:T(8,128)(2,1)}, u32[]{:S(2)}) %copy-start.1) | copy-done | bytes 65560
  3.7 0.8 %copy-done.4 = bf16[32,1024]{1,0:T(8,128)(2,1)S(1)} copy-done((bf16[32,1024]{1,0:T(8,128)(2,1)S(1)}, bf16[32,1024]{1,0:T(8,128)(2,1)}, u32[]{:S(2)}) %copy-start.4) | copy-done | bytes 65560
  4.6 1.2 %collective-permute-start = (bf16[64,128]{1,0:T(8,128)(2,1)S(1)}, bf16[64,128]{1,0:T(8,128)(2,1)S(1)}, u32[]{:S(2)}, u32[]{:S(2)}) collective-permute-start(bf16[64,128]{1,0:T(8,128)(2,1)S(1)} %get-tuple-element.29), channel_id=1, source_target_pairs={{0,4},{4,0},{8,12},{12,8},{16,20},{20,16},{24,28},{28,24},{32,36},... | collective-permute-start | bytes 49160 | tf_op jit(solution)/shard_map/ppermute | solution.py:265
  5.8 1.0 %collective-permute-start.1 = (bf16[64,128]{1,0:T(8,128)(2,1)S(1)}, bf16[64,128]{1,0:T(8,128)(2,1)S(1)}, u32[]{:S(2)}, u32[]{:S(2)}) collective-permute-start(bf16[64,128]{1,0:T(8,128)(2,1)S(1)} %get-tuple-element.30), channel_id=1, source_target_pairs={{0,252},{4,8},{8,4},{12,16},{16,12},{20,24},{24,20},{28,32},{32,28... | collective-permute-start | bytes 49160 | tf_op jit(solution)/shard_map/ppermute | solution.py:271
  6.8 2.0 %collective-permute-start.3 = (bf16[64,1024]{1,0:T(8,128)(2,1)S(1)}, bf16[64,1024]{1,0:T(8,128)(2,1)S(1)}, u32[]{:S(2)}, u32[]{:S(2)}) collective-permute-start(bf16[64,1024]{1,0:T(8,128)(2,1)S(1)} %join.3.pair_ref), channel_id=1, source_target_pairs={{0,3},{1,2},{2,1},{3,0},{4,7},{5,6},{6,5},{7,4},{8,11},{9,10},{10,... | collective-permute-start | bytes 393224 | tf_op jit(solution)/shard_map/ppermute | solution.py:282
  8.8 3.9 %gather.1.dense_in = bf16[864,1024]{1,0:T(8,128)(2,1)S(1)} custom-call(bf16[32,1024]{1,0:T(8,128)(2,1)S(1)} %copy-done.4, s32[27,1024]{1,0:T(8,128)S(1)} %copy-done.3), custom_call_target="tpu_custom_call" | custom-call | flops 3221225472 | bytes 1945600 | tf_op jit(solution)/shard_map/gather/pallas_call | solution.py:242
  12.7 0.7 %weight_terms.1 = (bf16[864,1024]{1,0:T(8,128)(2,1)S(1)}, bf16[128,1024]{1,0:T(8,128)(2,1)S(1)}, f32[448,128]{1,0:T(8,128)S(1)}, f32[448,128]{1,0:T(8,128)S(1)}) custom-call(bf16[864,1024]{1,0:T(8,128)(2,1)S(1)} %gather.1.dense_in, s32[27,1024]{1,0:T(8,128)S(1)} %copy-done.3, ...), custom_call_target="tpu_custom_call", output_to_operand_aliasing={{0}: (0, {})} | custom-call | flops 1073741824 | bytes 4665344 | tf_op jit(solution)/shard_map/weight_terms/pallas_call | solution.py:242
  13.5 7.4 %collective-permute-start.4 = (f32[448,128]{1,0:T(8,128)S(1)}, f32[448,128]{1,0:T(8,128)S(1)}, u32[]{:S(2)}, u32[]{:S(2)}) collective-permute-start(f32[448,128]{1,0:T(8,128)S(1)} %get-tuple-element.36), channel_id=1, source_target_pairs={{0,4},{4,0},{8,12},{12,8},{16,20},{20,16},{24,28},{28,24},{32,36},... | collective-permute-start | bytes 688136 | tf_op jit(solution)/shard_map/ppermute | solution.py:265
  20.9 0.6 back_terms.1.terms
  21.5 0.5 forward.1
  22.0 0.4 collective-permute-start.5
  22.4 1.0 %back_inner.4.refs_0_ = f32[32,1024]{1,0:T(8,128)S(1)} custom-call(f32[864,1024]{1,0:T(8,128)S(1)} %back_terms.1.terms, s32[27,1024]{1,0:T(8,128)S(1)} %copy-done.3), custom_call_target="tpu_custom_call" | custom-call | flops 1073741824 | bytes 3780608 | tf_op jit(solution)/shard_map/back_inner/pallas_call | solution.py:242
  23.4 3.1 %collective-permute-done.6.came_ref = f32[224,128]{1,0:T(8,128)S(1)} collective-permute-done((f32[224,128]{1,0:T(8,128)S(1)}, f32[224,128]{1,0:T(8,128)S(1)}, u32[]{:S(2)}, u32[]{:S(2)}) %collective-permute-start.6) | collective-permute-done | bytes 114720 | tf_op jit(solution)/shard_map/ppermute | solution.py:265
  26.6 1.0 %back_inner.5.refs_0_ = f32[32,1024]{1,0:T(8,128)S(1)} custom-call(f32[864,1024]{1,0:T(8,128)S(1)} %back_terms.1.terms, s32[27,1024]{1,0:T(8,128)S(1)} %copy-done.3, f32[32,1024]{1,0:T(8,128)S(1)} %back_inner.4.refs_0_), custom_call_target="tpu_custom_call", output_to_operand_aliasing={{}: (2, {})} | custom-call | flops 1073741824 | bytes 3911680 | tf_op jit(solution)/shard_map/back_inner/pallas_call | solution.py:242
  27.6 3.3 %collective-permute-done.7.b_ref = f32[112,128]{1,0:T(8,128)S(1)} collective-permute-done((f32[112,128]{1,0:T(8,128)S(1)}, f32[112,128]{1,0:T(8,128)S(1)}, u32[]{:S(2)}, u32[]{:S(2)}) %collective-permute-start.7) | collective-permute-done | bytes 57376 | tf_op jit(solution)/shard_map/ppermute | solution.py:265
  30.8 0.1 collective-permute-start.9
  31.0 3.0 %collective-permute-done.9.b_ref = f32[112,128]{1,0:T(8,128)S(1)} collective-permute-done((f32[112,128]{1,0:T(8,128)S(1)}, f32[112,128]{1,0:T(8,128)S(1)}, u32[]{:S(2)}, u32[]{:S(2)}) %collective-permute-start.9) | collective-permute-done | bytes 57376 | tf_op jit(solution)/shard_map/ppermute | solution.py:265
  34.0 0.1 collective-permute-start.10
  34.1 1.8 %back_inner.6.refs_0_ = f32[32,1024]{1,0:T(8,128)S(1)} custom-call(f32[864,1024]{1,0:T(8,128)S(1)} %back_terms.1.terms, s32[27,1024]{1,0:T(8,128)S(1)} %copy-done.3, f32[32,1024]{1,0:T(8,128)S(1)} %back_inner.5.refs_0_), custom_call_target="tpu_custom_call", output_to_operand_aliasing={{}: (2, {})} | custom-call | flops 2147483648 | bytes 3911680 | tf_op jit(solution)/shard_map/back_inner/pallas_call | solution.py:242
  35.9 2.1 %collective-permute-start.8 = (f32[32,1536]{1,0:T(8,128)S(1)}, f32[32,1536]{1,0:T(8,128)S(1)}, u32[]{:S(2)}, u32[]{:S(2)}) collective-permute-start(f32[32,1536]{1,0:T(8,128)S(1)} %get-tuple-element.48), channel_id=1, source_target_pairs={{0,3},{1,2},{2,1},{3,0},{4,7},{5,6},{6,5},{7,4},{8,11},{9,10},{10,... | collective-permute-start | bytes 589832 | tf_op jit(solution)/shard_map/ppermute | solution.py:282
  38.0 0.3 collective-permute-done.10.b_ref
  38.3 1.6 %collective-permute-start.11 = (f32[112,128]{1,0:T(8,128)S(1)}, f32[112,128]{1,0:T(8,128)S(1)}, u32[]{:S(2)}, u32[]{:S(2)}) collective-permute-start(f32[112,128]{1,0:T(8,128)S(1)} %add.6.a_ref), channel_id=1, source_target_pairs={{0,192},{4,196},{8,200},{12,204},{16,208},{20,212},{24,216},{28,22... | collective-permute-start | bytes 172040 | tf_op jit(solution)/shard_map/ppermute | solution.py:265
  39.9 1.8 %back_inner.7.inner = f32[32,1024]{1,0:T(8,128)S(1)} custom-call(f32[864,1024]{1,0:T(8,128)S(1)} %back_terms.1.terms, s32[27,1024]{1,0:T(8,128)S(1)} %copy-done.3, f32[32,1024]{1,0:T(8,128)S(1)} %back_inner.6.refs_0_), custom_call_target="tpu_custom_call", output_to_operand_aliasing={{}: (2, {})} | custom-call | flops 2147483648 | bytes 3911680 | tf_op jit(solution)/shard_map/back_inner/pallas_call | solution.py:242
  41.8 2.0 %collective-permute-done.11.b_ref = f32[112,128]{1,0:T(8,128)S(1)} collective-permute-done((f32[112,128]{1,0:T(8,128)S(1)}, f32[112,128]{1,0:T(8,128)S(1)}, u32[]{:S(2)}, u32[]{:S(2)}) %collective-permute-start.11) | collective-permute-done | bytes 57376 | tf_op jit(solution)/shard_map/ppermute | solution.py:265
  43.7 0.4 collective-permute-start.12
  44.2 3.9 %collective-permute-done.12.b_ref = f32[112,128]{1,0:T(8,128)S(1)} collective-permute-done((f32[112,128]{1,0:T(8,128)S(1)}, f32[112,128]{1,0:T(8,128)S(1)}, u32[]{:S(2)}, u32[]{:S(2)}) %collective-permute-start.12) | collective-permute-done | bytes 57376 | tf_op jit(solution)/shard_map/ppermute | solution.py:265
  48.2 1.5 %edge.1 = (bf16[32,1024]{1,0:T(8,128)(2,1)}, bf16[32,1024]{1,0:T(8,128)(2,1)}) custom-call(f32[864,1024]{1,0:T(8,128)S(1)} %back_terms.1.terms, s32[27,1024]{1,0:T(8,128)S(1)} %copy-done.3, bf16[864,128]{1,0:T(8,128)(2,1)S(1)} %bitcast.4, bf16[64,128]{1,0:T(8,128)(2,1)S(1)} %collective-permute-done.near_ref, ...), custom_call_target="tpu_custom_call" | custom-call | flops 2147483648 | bytes 4788224 | tf_op jit(solution)/shard_map/edge/pallas_call | solution.py:242
  49.7 2.1 %collective-permute-done.13.b_ref = f32[224,128]{1,0:T(8,128)S(1)} collective-permute-done((f32[224,128]{1,0:T(8,128)S(1)}, f32[224,128]{1,0:T(8,128)S(1)}, u32[]{:S(2)}, u32[]{:S(2)}) %collective-permute-start.13) | collective-permute-done | bytes 114720 | tf_op jit(solution)/shard_map/ppermute | solution.py:265
  51.8 8.6 %collective-permute-start.14 = (f32[448,128]{1,0:T(8,128)S(1)}, f32[448,128]{1,0:T(8,128)S(1)}, u32[]{:S(2)}, u32[]{:S(2)}) collective-permute-start(f32[448,128]{1,0:T(8,128)S(1)} %join.5.even_ref), channel_id=1, source_target_pairs={{0,4},{4,0},{8,12},{12,8},{16,20},{20,16},{24,28},{28,24},{32,36},... | collective-permute-start | bytes 688136 | tf_op jit(solution)/shard_map/ppermute | solution.py:265
  60.4 1.1 %collective-permute-done.14.odd_ref = f32[448,128]{1,0:T(8,128)S(1)} collective-permute-done((f32[448,128]{1,0:T(8,128)S(1)}, f32[448,128]{1,0:T(8,128)S(1)}, u32[]{:S(2)}, u32[]{:S(2)}) %collective-permute-start.14) | collective-permute-done | bytes 229408 | tf_op jit(solution)/shard_map/ppermute | solution.py:265
  61.5 0.8 %place.1 = f32[864,128]{1,0:T(8,128)} custom-call(f32[448,128]{1,0:T(8,128)S(1)} %join.5.even_ref, f32[448,128]{1,0:T(8,128)S(1)} %collective-permute-done.14.odd_ref), custom_call_target="tpu_custom_call" | custom-call | bytes 901120 | tf_op jit(solution)/shard_map/place/pallas_call | solution.py:242
  (29 shorter events, 0.4 us)
Async XLA Ops:
  0.6 6.2 %collective-permute-start.2 = (bf16[32,1024]{1,0:T(8,128)(2,1)}, bf16[32,1024]{1,0:T(8,128)(2,1)S(1)}, u32[]{:S(2)}, u32[]{:S(2)}) collective-permute-start(bf16[32,1024]{1,0:T(8,128)(2,1)} %a_ref.1), channel_id=1, source_target_pairs={{0,1},{1,0},{2,3},{3,2},{4,5},{5,4},{6,7},{7,6},{8,9},{9,8},{10,11... | collective-permute-start | bytes 196616 | tf_op jit(solution)/shard_map/ppermute | solution.py:282
  2.8 0.9 %copy-start.1 = (bf16[32,1024]{1,0:T(8,128)(2,1)S(1)}, bf16[32,1024]{1,0:T(8,128)(2,1)}, u32[]{:S(2)}) copy-start(bf16[32,1024]{1,0:T(8,128)(2,1)} %a_ref.1) | copy-start | bytes 196612
  3.7 0.8 %copy-start.4 = (bf16[32,1024]{1,0:T(8,128)(2,1)S(1)}, bf16[32,1024]{1,0:T(8,128)(2,1)}, u32[]{:S(2)}) copy-start(bf16[32,1024]{1,0:T(8,128)(2,1)} %x_ref.3) | copy-start | bytes 196612
  4.6 2.3 %copy-start.2 = (bf16[32,1024]{1,0:T(8,128)(2,1)S(1)}, bf16[32,1024]{1,0:T(8,128)(2,1)}, u32[]{:S(2)}) copy-start(bf16[32,1024]{1,0:T(8,128)(2,1)} %a_ref.1) | copy-start | bytes 196612
  4.6 4.3 %copy-start.3 = (s32[27,1024]{1,0:T(8,128)S(1)}, s32[27,1024]{1,0:T(8,128)}, u32[]{:S(2)}) copy-start(s32[27,1024]{1,0:T(8,128)} %rule_ref.13) | copy-start | bytes 331780
  4.6 8.1 %collective-permute-start = (bf16[64,128]{1,0:T(8,128)(2,1)S(1)}, bf16[64,128]{1,0:T(8,128)(2,1)S(1)}, u32[]{:S(2)}, u32[]{:S(2)}) collective-permute-start(bf16[64,128]{1,0:T(8,128)(2,1)S(1)} %get-tuple-element.29), channel_id=1, source_target_pairs={{0,4},{4,0},{8,12},{12,8},{16,20},{20,16},{24,28},{28,24},{32,36},... | collective-permute-start | bytes 49160 | tf_op jit(solution)/shard_map/ppermute | solution.py:265
  5.8 6.9 %collective-permute-start.1 = (bf16[64,128]{1,0:T(8,128)(2,1)S(1)}, bf16[64,128]{1,0:T(8,128)(2,1)S(1)}, u32[]{:S(2)}, u32[]{:S(2)}) collective-permute-start(bf16[64,128]{1,0:T(8,128)(2,1)S(1)} %get-tuple-element.30), channel_id=1, source_target_pairs={{0,252},{4,8},{8,4},{12,16},{16,12},{20,24},{24,20},{28,32},{32,28... | collective-permute-start | bytes 49160 | tf_op jit(solution)/shard_map/ppermute | solution.py:271
  6.8 5.9 %collective-permute-start.3 = (bf16[64,1024]{1,0:T(8,128)(2,1)S(1)}, bf16[64,1024]{1,0:T(8,128)(2,1)S(1)}, u32[]{:S(2)}, u32[]{:S(2)}) collective-permute-start(bf16[64,1024]{1,0:T(8,128)(2,1)S(1)} %join.3.pair_ref), channel_id=1, source_target_pairs={{0,3},{1,2},{2,1},{3,0},{4,7},{5,6},{6,5},{7,4},{8,11},{9,10},{10,... | collective-permute-start | bytes 393224 | tf_op jit(solution)/shard_map/ppermute | solution.py:282
  12.7 8.2 %copy-start = (bf16[27,32,128]{2,1,0:T(8,128)(2,1)S(1)}, bf16[27,32,128]{2,1,0:T(8,128)(2,1)}, u32[]{:S(2)}) copy-start(bf16[27,32,128]{2,1,0:T(8,128)(2,1)} %param.5) | copy-start | bytes 663556
  13.5 8.5 %collective-permute-start.4 = (f32[448,128]{1,0:T(8,128)S(1)}, f32[448,128]{1,0:T(8,128)S(1)}, u32[]{:S(2)}, u32[]{:S(2)}) collective-permute-start(f32[448,128]{1,0:T(8,128)S(1)} %get-tuple-element.36), channel_id=1, source_target_pairs={{0,4},{4,0},{8,12},{12,8},{16,20},{20,16},{24,28},{28,24},{32,36},... | collective-permute-start | bytes 688136 | tf_op jit(solution)/shard_map/ppermute | solution.py:265
  22.0 8.9 %collective-permute-start.5 = (f32[64,1152]{1,0:T(8,128)S(1)}, f32[64,1152]{1,0:T(8,128)S(1)}, u32[]{:S(2)}, u32[]{:S(2)}) collective-permute-start(f32[64,1152]{1,0:T(8,128)S(1)} %get-tuple-element.39), channel_id=1, source_target_pairs={{0,1},{1,0},{2,3},{3,2},{4,5},{5,4},{6,7},{7,6},{8,9},{9,8},{10,11... | collective-permute-start | bytes 884744 | tf_op jit(solution)/shard_map/ppermute | solution.py:282
  22.4 4.0 %collective-permute-start.6 = (f32[224,128]{1,0:T(8,128)S(1)}, f32[224,128]{1,0:T(8,128)S(1)}, u32[]{:S(2)}, u32[]{:S(2)}) collective-permute-start(f32[224,128]{1,0:T(8,128)S(1)} %get-tuple-element.40), channel_id=1, source_target_pairs={{0,8},{4,12},{8,0},{12,4},{16,24},{20,28},{24,16},{28,20},{32,40},... | collective-permute-start | bytes 344072 | tf_op jit(solution)/shard_map/ppermute | solution.py:265
  26.5 4.3 %collective-permute-start.7 = (f32[112,128]{1,0:T(8,128)S(1)}, f32[112,128]{1,0:T(8,128)S(1)}, u32[]{:S(2)}, u32[]{:S(2)}) collective-permute-start(f32[112,128]{1,0:T(8,128)S(1)} %get-tuple-element.43), channel_id=1, source_target_pairs={{0,24},{4,28},{8,16},{12,20},{16,8},{20,12},{24,0},{28,4},{32,56},... | collective-permute-start | bytes 172040 | tf_op jit(solution)/shard_map/ppermute | solution.py:265
  30.8 3.1 %collective-permute-start.9 = (f32[112,128]{1,0:T(8,128)S(1)}, f32[112,128]{1,0:T(8,128)S(1)}, u32[]{:S(2)}, u32[]{:S(2)}) collective-permute-start(f32[112,128]{1,0:T(8,128)S(1)} %add.4.a_ref), channel_id=1, source_target_pairs={{0,32},{4,36},{8,40},{12,44},{16,48},{20,52},{24,56},{28,60},{32,0... | collective-permute-start | bytes 172040 | tf_op jit(solution)/shard_map/ppermute | solution.py:265
  34.0 4.4 %collective-permute-start.10 = (f32[112,128]{1,0:T(8,128)S(1)}, f32[112,128]{1,0:T(8,128)S(1)}, u32[]{:S(2)}, u32[]{:S(2)}) collective-permute-start(f32[112,128]{1,0:T(8,128)S(1)} %add.5.a_ref), channel_id=1, source_target_pairs={{0,64},{4,68},{8,72},{12,76},{16,80},{20,84},{24,88},{28,92},{32,9... | collective-permute-start | bytes 172040 | tf_op jit(solution)/shard_map/ppermute | solution.py:265
  35.9 12.3 %collective-permute-start.8 = (f32[32,1536]{1,0:T(8,128)S(1)}, f32[32,1536]{1,0:T(8,128)S(1)}, u32[]{:S(2)}, u32[]{:S(2)}) collective-permute-start(f32[32,1536]{1,0:T(8,128)S(1)} %get-tuple-element.48), channel_id=1, source_target_pairs={{0,3},{1,2},{2,1},{3,0},{4,7},{5,6},{6,5},{7,4},{8,11},{9,10},{10,... | collective-permute-start | bytes 589832 | tf_op jit(solution)/shard_map/ppermute | solution.py:282
  38.3 5.4 %collective-permute-start.11 = (f32[112,128]{1,0:T(8,128)S(1)}, f32[112,128]{1,0:T(8,128)S(1)}, u32[]{:S(2)}, u32[]{:S(2)}) collective-permute-start(f32[112,128]{1,0:T(8,128)S(1)} %add.6.a_ref), channel_id=1, source_target_pairs={{0,192},{4,196},{8,200},{12,204},{16,208},{20,212},{24,216},{28,22... | collective-permute-start | bytes 172040 | tf_op jit(solution)/shard_map/ppermute | solution.py:265
  43.7 4.3 %collective-permute-start.12 = (f32[112,128]{1,0:T(8,128)S(1)}, f32[112,128]{1,0:T(8,128)S(1)}, u32[]{:S(2)}, u32[]{:S(2)}) collective-permute-start(f32[112,128]{1,0:T(8,128)S(1)} %add.7.a_ref), channel_id=1, source_target_pairs={{0,24},{4,28},{8,16},{12,20},{16,8},{20,12},{24,0},{28,4},{32,56},... | collective-permute-start | bytes 172040 | tf_op jit(solution)/shard_map/ppermute | solution.py:265
  48.1 3.7 %collective-permute-start.13 = (f32[224,128]{1,0:T(8,128)S(1)}, f32[224,128]{1,0:T(8,128)S(1)}, u32[]{:S(2)}, u32[]{:S(2)}) collective-permute-start(f32[224,128]{1,0:T(8,128)S(1)} %join.4.a_ref), channel_id=1, source_target_pairs={{0,8},{4,12},{8,0},{12,4},{16,24},{20,28},{24,16},{28,20},{32,40},... | collective-permute-start | bytes 344072 | tf_op jit(solution)/shard_map/ppermute | solution.py:265
  51.8 9.7 %collective-permute-start.14 = (f32[448,128]{1,0:T(8,128)S(1)}, f32[448,128]{1,0:T(8,128)S(1)}, u32[]{:S(2)}, u32[]{:S(2)}) collective-permute-start(f32[448,128]{1,0:T(8,128)S(1)} %join.5.even_ref), channel_id=1, source_target_pairs={{0,4},{4,0},{8,12},{12,8},{16,20},{20,16},{24,28},{28,24},{32,36},... | collective-permute-start | bytes 688136 | tf_op jit(solution)/shard_map/ppermute | solution.py:265

commit v8 on v6

--- a/solution.py
+++ b/solution.py
@@ -12,7 +12,8 @@
 LANES = 128
 PART = 112
 INNER = tuple(range(2, 8))
-EDGE = (0, 1)
+EDGE = (0, 1, 6, 7)
+ORDER = (0, 1, 3, 2)
 VMEM = pl.BlockSpec(memory_space=pltpu.VMEM)
 
 
@@ -109,8 +110,8 @@
 ):
     chan = lax.axis_index("ch")
     spot = lax.axis_index("blk") & 7
-    for m in range(4):
-        part = (pair_ref if m < 2 else other_ref)[32 * (m % 2) : 32 * (m % 2) + 32, :]
+    for i, m in enumerate(ORDER):
+        part = (pair_ref if i < 2 else other_ref)[32 * (i % 2) : 32 * (i % 2) + 32, :]
         grad_ref[pl.ds(pl.multiple_of(32 * (chan ^ m), 32), 32), :] = part
     faces[:, :FACE], faces[:, FACE:] = by_side(near_ref[:32, :], far_ref[:32, :])
 
@@ -137,10 +138,10 @@
         weight_ref[...], dense_ref[...], (((0,), (0,)), ((), ())),
         preferred_element_type=jnp.float32,
     )
-    for m in range(4):
-        target = send_ref if m % 2 else keep_ref
-        rows = pl.ds(pl.multiple_of(32 * (chan ^ m), 32), 32)
-        target[32 * (m // 2) : 32 * (m // 2) + 32, :VOX] = sums[rows, :]
+    for target, parts in ((keep_ref, (0, 3)), (send_ref, (1, 2))):
+        for i, m in enumerate(parts):
+            rows = pl.ds(pl.multiple_of(32 * (chan ^ m), 32), 32)
+            target[32 * i : 32 * i + 32, :VOX] = sums[rows, :]
     lower, upper = by_side(near_ref[32:, :], far_ref[32:, :])
     send_ref[:32, VOX:] = lower
     send_ref[32:, VOX:] = upper
@@ -192,7 +193,7 @@
         (second_ref[:, VOX : VOX + FACE], second_ref[:, VOX + FACE : VOX + 2 * FACE]),
         (second_ref[:, VOX + 2 * FACE : VOX + 3 * FACE], second_ref[:, VOX + 3 * FACE :]),
     )
-    for m, (lower, upper) in enumerate(pairs):
+    for m, (lower, upper) in zip(ORDER, pairs):
         rows = pl.ds(pl.multiple_of(32 * (chan ^ m), 32), 32)
         faces[rows, :FACE] = lower.astype(jnp.bfloat16)
         faces[rows, FACE:] = upper.astype(jnp.bfloat16)
@@ -289,7 +290,7 @@
     pair = call(join_kernel, bf16(64, VOX), (g, over_ch(g, 1)), name="join")
     near = swap(near, 1)
     far = swap_far(far)
-    other = over_ch(pair, 2)
+    other = over_ch(pair, 3)
     dense = call(
         gather_kernel, bf16(864, VOX), (x, rules),
         [pltpu.VMEM((32, VOX), jnp.float32)], flops=3 << 30, name="gather",
@@ -336,9 +337,8 @@
         middle_kernel, (f32(32, VOX), f32(32, VOX + 4 * FACE)), (ours, first, near, far),
         name="middle",
     )
-    second = over_ch(second, 2)
-    inner = inner_part((6, 7), inner)
-    others = after(others, inner, own)
+    second = over_ch(second, 3)
+    others = after(others, own)
     total = call(sum_kernel, f32(PART, 128), (total, *others), name="sum_four")
     both = call(join_kernel, f32(2 * PART, 128), (total, swap(total, 1)), name="join")
     others = [swap(both, 2 * q) for q in (1, 2, 3)]

time: 56.6 us -> 57.8 us (1.021)
  waiting for transfers between devices: 6.73 us -> 9.22 us
  starting transfers between devices: 33.4 us -> 32.3 us
    ppermute x4, waiting for transfers between devices: 0.01 us -> 1.28 us  [over_ch(): return lax.ppermute(value, 'ch', [(i, i ^ mask) for i in range(4)])]
    ppermute x13, waiting for transfers between devices: 6.72 us -> 7.94 us  [swap(): return lax.ppermute(value, 'blk', [(i, i ^ mask) for i in range(count)])]
    ppermute x4, starting transfers between devices: 7.47 us -> 6.5 us  [over_ch(): return lax.ppermute(value, 'ch', [(i, i ^ mask) for i in range(4)])]
    pallas_call x17 -> x16, Pallas kernels: 13.7 us -> 13.6 us  [call(): pl.pallas_call(kernel, out_shape=outs, in_specs=[VMEM] * len(args), out_s...]
  transfers between devices with their start and end apart: 18 -> 18, of which waited for: 6 -> 8; matrix products, arithmetic and copies ran while one was open for 0% -> 0% of each run, Pallas kernels for 21% -> 21%
where the time goes in v8:
time: 57.8 us; the launch traced here: 57.6 us
  starting transfers between devices  32.3 us (56%)
  Pallas kernels  13.6 us (24%)
  waiting for transfers between devices  9.22 us (16%)
  local copies, waits for them, and re-layouts  1.73 us (3%)
  between operations  0.78 us (1%)
    ppermute x13, starting transfers between devices, swap(): return lax.ppermute(value, 'blk', [(i, i ^ mask) for i in range(count)])  24.7 us
    pallas_call x16, Pallas kernels, call(): pl.pallas_call(kernel, out_shape=outs, in_specs=[VMEM] * len(args), out_s...  13.6 us
    ppermute x13, waiting for transfers between devices, swap(): return lax.ppermute(value, 'blk', [(i, i ^ mask) for i in range(count)])  7.94 us
    ppermute x4, starting transfers between devices, over_ch(): return lax.ppermute(value, 'ch', [(i, i ^ mask) for i in range(4)])  6.5 us
    unnamed x10, local copies, waits for them, and re-layouts  1.73 us
    ppermute x4, waiting for transfers between devices, over_ch(): return lax.ppermute(value, 'ch', [(i, i ^ mask) for i in range(4)])  1.28 us
  transfers between devices with their start and end apart: 18, of which 8 were waited for; matrix products, arithmetic and copies ran while one was open for 0% of the time, Pallas kernels for 21%

profile of v8, /device:TPU:1, one launch (start us, length us, event | category | flops | bytes accessed | tf_op | source)
XLA Modules:
  0.0 57.6 jit_solution(10666654160642462237)
XLA Ops:
  0.6 2.2 %collective-permute-start.2 = (bf16[32,1024]{1,0:T(8,128)(2,1)}, bf16[32,1024]{1,0:T(8,128)(2,1)S(1)}, u32[]{:S(2)}, u32[]{:S(2)}) collective-permute-start(bf16[32,1024]{1,0:T(8,128)(2,1)} %refs_0_.1), channel_id=1, source_target_pairs={{0,1},{1,0},{2,3},{3,2},{4,5},{5,4},{6,7},{7,6},{8,9},{9,8},{10,11... | collective-permute-start | bytes 196616 | tf_op jit(solution)/shard_map/ppermute | solution.py:284
  2.8 0.9 %copy-done.1 = bf16[32,1024]{1,0:T(8,128)(2,1)S(1)} copy-done((bf16[32,1024]{1,0:T(8,128)(2,1)S(1)}, bf16[32,1024]{1,0:T(8,128)(2,1)}, u32[]{:S(2)}) %copy-start.1) | copy-done | bytes 65560
  3.7 0.8 %copy-done.4 = bf16[32,1024]{1,0:T(8,128)(2,1)S(1)} copy-done((bf16[32,1024]{1,0:T(8,128)(2,1)S(1)}, bf16[32,1024]{1,0:T(8,128)(2,1)}, u32[]{:S(2)}) %copy-start.4) | copy-done | bytes 65560
  4.6 1.2 %collective-permute-start = (bf16[64,128]{1,0:T(8,128)(2,1)S(1)}, bf16[64,128]{1,0:T(8,128)(2,1)S(1)}, u32[]{:S(2)}, u32[]{:S(2)}) collective-permute-start(bf16[64,128]{1,0:T(8,128)(2,1)S(1)} %get-tuple-element.33), channel_id=1, source_target_pairs={{0,4},{4,0},{8,12},{12,8},{16,20},{20,16},{24,28},{28,24},{32,36},... | collective-permute-start | bytes 49160 | tf_op jit(solution)/shard_map/ppermute | solution.py:267
  5.8 1.0 %collective-permute-start.1 = (bf16[64,128]{1,0:T(8,128)(2,1)S(1)}, bf16[64,128]{1,0:T(8,128)(2,1)S(1)}, u32[]{:S(2)}, u32[]{:S(2)}) collective-permute-start(bf16[64,128]{1,0:T(8,128)(2,1)S(1)} %get-tuple-element.34), channel_id=1, source_target_pairs={{0,252},{4,8},{8,4},{12,16},{16,12},{20,24},{24,20},{28,32},{32,28... | collective-permute-start | bytes 49160 | tf_op jit(solution)/shard_map/ppermute | solution.py:273
  6.8 2.0 %collective-permute-start.3 = (bf16[64,1024]{1,0:T(8,128)(2,1)S(1)}, bf16[64,1024]{1,0:T(8,128)(2,1)S(1)}, u32[]{:S(2)}, u32[]{:S(2)}) collective-permute-start(bf16[64,1024]{1,0:T(8,128)(2,1)S(1)} %join.2.pair_ref), channel_id=1, source_target_pairs={{0,3},{1,2},{2,1},{3,0},{4,7},{5,6},{6,5},{7,4},{8,11},{9,10},{10,... | collective-permute-start | bytes 393224 | tf_op jit(solution)/shard_map/ppermute | solution.py:284
  8.8 3.9 %gather.1.dense_in = bf16[864,1024]{1,0:T(8,128)(2,1)S(1)} custom-call(bf16[32,1024]{1,0:T(8,128)(2,1)S(1)} %copy-done.4, s32[27,1024]{1,0:T(8,128)S(1)} %copy-done.3), custom_call_target="tpu_custom_call" | custom-call | flops 3221225472 | bytes 1945600 | tf_op jit(solution)/shard_map/gather/pallas_call | solution.py:244
  12.7 0.7 %weight_terms.1 = (bf16[864,1024]{1,0:T(8,128)(2,1)S(1)}, bf16[128,1024]{1,0:T(8,128)(2,1)S(1)}, f32[448,128]{1,0:T(8,128)S(1)}, f32[448,128]{1,0:T(8,128)S(1)}) custom-call(bf16[864,1024]{1,0:T(8,128)(2,1)S(1)} %gather.1.dense_in, s32[27,1024]{1,0:T(8,128)S(1)} %copy-done.3, ...), custom_call_target="tpu_custom_call", output_to_operand_aliasing={{0}: (0, {})} | custom-call | flops 1073741824 | bytes 4665344 | tf_op jit(solution)/shard_map/weight_terms/pallas_call | solution.py:244
  13.5 7.4 %collective-permute-start.4 = (f32[448,128]{1,0:T(8,128)S(1)}, f32[448,128]{1,0:T(8,128)S(1)}, u32[]{:S(2)}, u32[]{:S(2)}) collective-permute-start(f32[448,128]{1,0:T(8,128)S(1)} %get-tuple-element.40), channel_id=1, source_target_pairs={{0,4},{4,0},{8,12},{12,8},{16,20},{20,16},{24,28},{28,24},{32,36},... | collective-permute-start | bytes 688136 | tf_op jit(solution)/shard_map/ppermute | solution.py:267
  20.9 0.6 %back_terms.1.terms = f32[864,1024]{1,0:T(8,128)S(1)} custom-call(bf16[864,128]{1,0:T(8,128)(2,1)S(1)} %bitcast.2, bf16[128,1024]{1,0:T(8,128)(2,1)S(1)} %get-tuple-element.35.grad_ref), custom_call_target="tpu_custom_call" | custom-call | flops 1073741824 | bytes 4022272 | tf_op jit(solution)/shard_map/back_terms/pallas_call | solution.py:244
  21.5 0.5 forward.1
  22.2 3.7 %collective-permute-start.8 = (f32[112,128]{1,0:T(8,128)S(1)}, f32[112,128]{1,0:T(8,128)S(1)}, u32[]{:S(2)}, u32[]{:S(2)}) collective-permute-start(f32[112,128]{1,0:T(8,128)S(1)} %get-tuple-element.45), channel_id=1, source_target_pairs={{0,24},{4,28},{8,16},{12,20},{16,8},{20,12},{24,0},{28,4},{32,56},... | collective-permute-start | bytes 172040 | tf_op jit(solution)/shard_map/ppermute | solution.py:267
  26.0 0.3 collective-permute-start.5
  26.3 1.8 %back_inner.2.refs_0_ = f32[32,1024]{1,0:T(8,128)S(1)} custom-call(f32[864,1024]{1,0:T(8,128)S(1)} %back_terms.1.terms, s32[27,1024]{1,0:T(8,128)S(1)} %copy-done.3), custom_call_target="tpu_custom_call" | custom-call | flops 2147483648 | bytes 3780608 | tf_op jit(solution)/shard_map/back_inner/pallas_call | solution.py:244
  28.2 0.4 collective-permute-done.8.refs_3_
  28.7 1.8 %back_inner.3.inner = f32[32,1024]{1,0:T(8,128)S(1)} custom-call(f32[864,1024]{1,0:T(8,128)S(1)} %back_terms.1.terms, s32[27,1024]{1,0:T(8,128)S(1)} %copy-done.3, f32[32,1024]{1,0:T(8,128)S(1)} %back_inner.2.refs_0_), custom_call_target="tpu_custom_call", output_to_operand_aliasing={{}: (2, {})} | custom-call | flops 2147483648 | bytes 3911680 | tf_op jit(solution)/shard_map/back_inner/pallas_call | solution.py:244
  30.5 1.5 %collective-permute-done.9.refs_1_ = f32[112,128]{1,0:T(8,128)S(1)} collective-permute-done((f32[112,128]{1,0:T(8,128)S(1)}, f32[112,128]{1,0:T(8,128)S(1)}, u32[]{:S(2)}, u32[]{:S(2)}) %collective-permute-start.9) | collective-permute-done | bytes 57376 | tf_op jit(solution)/shard_map/ppermute | solution.py:267
  32.0 1.3 %collective-permute-done.5.came_ref.first_ref = f32[64,1152]{1,0:T(8,128)S(1)} collective-permute-done((f32[64,1152]{1,0:T(8,128)S(1)}, f32[64,1152]{1,0:T(8,128)S(1)}, u32[]{:S(2)}, u32[]{:S(2)}) %collective-permute-start.5) | collective-permute-done | bytes 294944 | tf_op jit(solution)/shard_map/ppermute | solution.py:284
  33.3 2.0 %collective-permute-start.10 = (f32[32,1536]{1,0:T(8,128)S(1)}, f32[32,1536]{1,0:T(8,128)S(1)}, u32[]{:S(2)}, u32[]{:S(2)}) collective-permute-start(f32[32,1536]{1,0:T(8,128)S(1)} %get-tuple-element.54), channel_id=1, source_target_pairs={{0,3},{1,2},{2,1},{3,0},{4,7},{5,6},{6,5},{7,4},{8,11},{9,10},{10,... | collective-permute-start | bytes 589832 | tf_op jit(solution)/shard_map/ppermute | solution.py:284
  35.3 1.2 %collective-permute-start.13 = (f32[112,128]{1,0:T(8,128)S(1)}, f32[112,128]{1,0:T(8,128)S(1)}, u32[]{:S(2)}, u32[]{:S(2)}) collective-permute-start(f32[112,128]{1,0:T(8,128)S(1)} %sum_two.1.refs_0_), channel_id=1, source_target_pairs={{0,192},{4,196},{8,200},{12,204},{16,208},{20,212},{24,216},{28,22... | collective-permute-start | bytes 172040 | tf_op jit(solution)/shard_map/ppermute | solution.py:267
  36.5 0.3 collective-permute-start.12
  36.8 4.2 %collective-permute-start.11 = (f32[112,128]{1,0:T(8,128)S(1)}, f32[112,128]{1,0:T(8,128)S(1)}, u32[]{:S(2)}, u32[]{:S(2)}) collective-permute-start(f32[112,128]{1,0:T(8,128)S(1)} %sum_two.1.refs_0_), channel_id=1, source_target_pairs={{0,64},{4,68},{8,72},{12,76},{16,80},{20,84},{24,88},{28,92},{32,9... | collective-permute-start | bytes 172040 | tf_op jit(solution)/shard_map/ppermute | solution.py:267
  41.0 2.5 %collective-permute-done.12.refs_2_ = f32[112,128]{1,0:T(8,128)S(1)} collective-permute-done((f32[112,128]{1,0:T(8,128)S(1)}, f32[112,128]{1,0:T(8,128)S(1)}, u32[]{:S(2)}, u32[]{:S(2)}) %collective-permute-start.12) | collective-permute-done | bytes 57376 | tf_op jit(solution)/shard_map/ppermute | solution.py:267
  43.5 0.7 %collective-permute-done.11.refs_1_ = f32[112,128]{1,0:T(8,128)S(1)} collective-permute-done((f32[112,128]{1,0:T(8,128)S(1)}, f32[112,128]{1,0:T(8,128)S(1)}, u32[]{:S(2)}, u32[]{:S(2)}) %collective-permute-start.11) | collective-permute-done | bytes 57376 | tf_op jit(solution)/shard_map/ppermute | solution.py:267
  44.3 3.1 %collective-permute-start.14 = (f32[112,128]{1,0:T(8,128)S(1)}, f32[112,128]{1,0:T(8,128)S(1)}, u32[]{:S(2)}, u32[]{:S(2)}) collective-permute-start(f32[112,128]{1,0:T(8,128)S(1)} %sum_four.3.refs_0_), channel_id=1, source_target_pairs={{0,4},{4,0},{8,12},{12,8},{16,20},{20,16},{24,28},{28,24},{32,36},... | collective-permute-start | bytes 172040 | tf_op jit(solution)/shard_map/ppermute | solution.py:267
  47.4 0.9 %collective-permute-done.14.refs_1_ = f32[112,128]{1,0:T(8,128)S(1)} collective-permute-done((f32[112,128]{1,0:T(8,128)S(1)}, f32[112,128]{1,0:T(8,128)S(1)}, u32[]{:S(2)}, u32[]{:S(2)}) %collective-permute-start.14) | collective-permute-done | bytes 57376 | tf_op jit(solution)/shard_map/ppermute | solution.py:267
  48.3 1.3 %collective-permute-start.17 = (f32[224,128]{1,0:T(8,128)S(1)}, f32[224,128]{1,0:T(8,128)S(1)}, u32[]{:S(2)}, u32[]{:S(2)}) collective-permute-start(f32[224,128]{1,0:T(8,128)S(1)} %join.3.refs_0_), channel_id=1, source_target_pairs={{0,24},{4,28},{8,16},{12,20},{16,8},{20,12},{24,0},{28,4},{32,56},... | collective-permute-start | bytes 344072 | tf_op jit(solution)/shard_map/ppermute | solution.py:267
  49.6 2.1 %collective-permute-start.15 = (f32[224,128]{1,0:T(8,128)S(1)}, f32[224,128]{1,0:T(8,128)S(1)}, u32[]{:S(2)}, u32[]{:S(2)}) collective-permute-start(f32[224,128]{1,0:T(8,128)S(1)} %join.3.refs_0_), channel_id=1, source_target_pairs={{0,8},{4,12},{8,0},{12,4},{16,24},{20,28},{24,16},{28,20},{32,40},... | collective-permute-start | bytes 344072 | tf_op jit(solution)/shard_map/ppermute | solution.py:267
  51.6 3.3 %edge.1 = (bf16[32,1024]{1,0:T(8,128)(2,1)}, bf16[32,1024]{1,0:T(8,128)(2,1)}) custom-call(f32[864,1024]{1,0:T(8,128)S(1)} %back_terms.1.terms, s32[27,1024]{1,0:T(8,128)S(1)} %copy-done.3, bf16[864,128]{1,0:T(8,128)(2,1)S(1)} %bitcast.4, bf16[64,128]{1,0:T(8,128)(2,1)S(1)} %collective-permute-done.near_ref, ...), custom_call_target="tpu_custom_call" | custom-call | flops 2147483648 | bytes 4788224 | tf_op jit(solution)/shard_map/edge/pallas_call | solution.py:244
  54.9 0.6 %collective-permute-done.17.refs_3_ = f32[224,128]{1,0:T(8,128)S(1)} collective-permute-done((f32[224,128]{1,0:T(8,128)S(1)}, f32[224,128]{1,0:T(8,128)S(1)}, u32[]{:S(2)}, u32[]{:S(2)}) %collective-permute-start.17) | collective-permute-done | bytes 114720 | tf_op jit(solution)/shard_map/ppermute | solution.py:267
  55.5 1.3 %collective-permute-done.15.refs_1_ = f32[224,128]{1,0:T(8,128)S(1)} collective-permute-done((f32[224,128]{1,0:T(8,128)S(1)}, f32[224,128]{1,0:T(8,128)S(1)}, u32[]{:S(2)}, u32[]{:S(2)}) %collective-permute-start.15) | collective-permute-done | bytes 114720 | tf_op jit(solution)/shard_map/ppermute | solution.py:267
  56.8 0.8 %place.1 = f32[864,128]{1,0:T(8,128)} custom-call(f32[224,128]{1,0:T(8,128)S(1)} %join.3.refs_0_, f32[224,128]{1,0:T(8,128)S(1)} %collective-permute-done.15.refs_1_, f32[224,128]{1,0:T(8,128)S(1)} %collective-permute-done.16.refs_2_, f32[224,128]{1,0:T(8,128)S(1)} %collective-permute-done.17.refs_3_), custom_call_target="tpu_custom_call" | custom-call | bytes 901120 | tf_op jit(solution)/shard_map/place/pallas_call | solution.py:244
  (30 shorter events, 0.5 us)
Async XLA Ops:
  0.6 6.2 %collective-permute-start.2 = (bf16[32,1024]{1,0:T(8,128)(2,1)}, bf16[32,1024]{1,0:T(8,128)(2,1)S(1)}, u32[]{:S(2)}, u32[]{:S(2)}) collective-permute-start(bf16[32,1024]{1,0:T(8,128)(2,1)} %refs_0_.1), channel_id=1, source_target_pairs={{0,1},{1,0},{2,3},{3,2},{4,5},{5,4},{6,7},{7,6},{8,9},{9,8},{10,11... | collective-permute-start | bytes 196616 | tf_op jit(solution)/shard_map/ppermute | solution.py:284
  2.8 0.9 %copy-start.1 = (bf16[32,1024]{1,0:T(8,128)(2,1)S(1)}, bf16[32,1024]{1,0:T(8,128)(2,1)}, u32[]{:S(2)}) copy-start(bf16[32,1024]{1,0:T(8,128)(2,1)} %refs_0_.1) | copy-start | bytes 196612
  3.7 0.8 %copy-start.4 = (bf16[32,1024]{1,0:T(8,128)(2,1)S(1)}, bf16[32,1024]{1,0:T(8,128)(2,1)}, u32[]{:S(2)}) copy-start(bf16[32,1024]{1,0:T(8,128)(2,1)} %x_ref.3) | copy-start | bytes 196612
  4.6 2.3 %copy-start.2 = (bf16[32,1024]{1,0:T(8,128)(2,1)S(1)}, bf16[32,1024]{1,0:T(8,128)(2,1)}, u32[]{:S(2)}) copy-start(bf16[32,1024]{1,0:T(8,128)(2,1)} %refs_0_.1) | copy-start | bytes 196612
  4.6 4.3 %copy-start.3 = (s32[27,1024]{1,0:T(8,128)S(1)}, s32[27,1024]{1,0:T(8,128)}, u32[]{:S(2)}) copy-start(s32[27,1024]{1,0:T(8,128)} %rule_ref.9) | copy-start | bytes 331780
  4.6 8.1 %collective-permute-start = (bf16[64,128]{1,0:T(8,128)(2,1)S(1)}, bf16[64,128]{1,0:T(8,128)(2,1)S(1)}, u32[]{:S(2)}, u32[]{:S(2)}) collective-permute-start(bf16[64,128]{1,0:T(8,128)(2,1)S(1)} %get-tuple-element.33), channel_id=1, source_target_pairs={{0,4},{4,0},{8,12},{12,8},{16,20},{20,16},{24,28},{28,24},{32,36},... | collective-permute-start | bytes 49160 | tf_op jit(solution)/shard_map/ppermute | solution.py:267
  5.8 6.9 %collective-permute-start.1 = (bf16[64,128]{1,0:T(8,128)(2,1)S(1)}, bf16[64,128]{1,0:T(8,128)(2,1)S(1)}, u32[]{:S(2)}, u32[]{:S(2)}) collective-permute-start(bf16[64,128]{1,0:T(8,128)(2,1)S(1)} %get-tuple-element.34), channel_id=1, source_target_pairs={{0,252},{4,8},{8,4},{12,16},{16,12},{20,24},{24,20},{28,32},{32,28... | collective-permute-start | bytes 49160 | tf_op jit(solution)/shard_map/ppermute | solution.py:273
  6.8 5.9 %collective-permute-start.3 = (bf16[64,1024]{1,0:T(8,128)(2,1)S(1)}, bf16[64,1024]{1,0:T(8,128)(2,1)S(1)}, u32[]{:S(2)}, u32[]{:S(2)}) collective-permute-start(bf16[64,1024]{1,0:T(8,128)(2,1)S(1)} %join.2.pair_ref), channel_id=1, source_target_pairs={{0,3},{1,2},{2,1},{3,0},{4,7},{5,6},{6,5},{7,4},{8,11},{9,10},{10,... | collective-permute-start | bytes 393224 | tf_op jit(solution)/shard_map/ppermute | solution.py:284
  12.7 8.2 %copy-start = (bf16[27,32,128]{2,1,0:T(8,128)(2,1)S(1)}, bf16[27,32,128]{2,1,0:T(8,128)(2,1)}, u32[]{:S(2)}) copy-start(bf16[27,32,128]{2,1,0:T(8,128)(2,1)} %param.5) | copy-start | bytes 663556
  13.5 8.5 %collective-permute-start.4 = (f32[448,128]{1,0:T(8,128)S(1)}, f32[448,128]{1,0:T(8,128)S(1)}, u32[]{:S(2)}, u32[]{:S(2)}) collective-permute-start(f32[448,128]{1,0:T(8,128)S(1)} %get-tuple-element.40), channel_id=1, source_target_pairs={{0,4},{4,0},{8,12},{12,8},{16,20},{20,16},{24,28},{28,24},{32,36},... | collective-permute-start | bytes 688136 | tf_op jit(solution)/shard_map/ppermute | solution.py:267
  22.0 6.1 %collective-permute-start.6 = (f32[112,128]{1,0:T(8,128)S(1)}, f32[112,128]{1,0:T(8,128)S(1)}, u32[]{:S(2)}, u32[]{:S(2)}) collective-permute-start(f32[112,128]{1,0:T(8,128)S(1)} %get-tuple-element.43), channel_id=1, source_target_pairs={{0,8},{4,12},{8,0},{12,4},{16,24},{20,28},{24,16},{28,20},{32,40},... | collective-permute-start | bytes 172040 | tf_op jit(solution)/shard_map/ppermute | solution.py:267
  22.1 6.0 %collective-permute-start.7 = (f32[112,128]{1,0:T(8,128)S(1)}, f32[112,128]{1,0:T(8,128)S(1)}, u32[]{:S(2)}, u32[]{:S(2)}) collective-permute-start(f32[112,128]{1,0:T(8,128)S(1)} %get-tuple-element.44), channel_id=1, source_target_pairs={{0,16},{4,20},{8,24},{12,28},{16,0},{20,4},{24,8},{28,12},{32,48},... | collective-permute-start | bytes 172040 | tf_op jit(solution)/shard_map/ppermute | solution.py:267
  22.2 6.3 %collective-permute-start.8 = (f32[112,128]{1,0:T(8,128)S(1)}, f32[112,128]{1,0:T(8,128)S(1)}, u32[]{:S(2)}, u32[]{:S(2)}) collective-permute-start(f32[112,128]{1,0:T(8,128)S(1)} %get-tuple-element.45), channel_id=1, source_target_pairs={{0,24},{4,28},{8,16},{12,20},{16,8},{20,12},{24,0},{28,4},{32,56},... | collective-permute-start | bytes 172040 | tf_op jit(solution)/shard_map/ppermute | solution.py:267
  26.0 7.3 %collective-permute-start.5 = (f32[64,1152]{1,0:T(8,128)S(1)}, f32[64,1152]{1,0:T(8,128)S(1)}, u32[]{:S(2)}, u32[]{:S(2)}) collective-permute-start(f32[64,1152]{1,0:T(8,128)S(1)} %get-tuple-element.46), channel_id=1, source_target_pairs={{0,1},{1,0},{2,3},{3,2},{4,5},{5,4},{6,7},{7,6},{8,9},{9,8},{10,11... | collective-permute-start | bytes 884744 | tf_op jit(solution)/shard_map/ppermute | solution.py:284
  28.6 3.4 %collective-permute-start.9 = (f32[112,128]{1,0:T(8,128)S(1)}, f32[112,128]{1,0:T(8,128)S(1)}, u32[]{:S(2)}, u32[]{:S(2)}) collective-permute-start(f32[112,128]{1,0:T(8,128)S(1)} %sum_four.2.refs_0_), channel_id=1, source_target_pairs={{0,32},{4,36},{8,40},{12,44},{16,48},{20,52},{24,56},{28,60},{32,0... | collective-permute-start | bytes 172040 | tf_op jit(solution)/shard_map/ppermute | solution.py:267
  33.3 18.3 %collective-permute-start.10 = (f32[32,1536]{1,0:T(8,128)S(1)}, f32[32,1536]{1,0:T(8,128)S(1)}, u32[]{:S(2)}, u32[]{:S(2)}) collective-permute-start(f32[32,1536]{1,0:T(8,128)S(1)} %get-tuple-element.54), channel_id=1, source_target_pairs={{0,3},{1,2},{2,1},{3,0},{4,7},{5,6},{6,5},{7,4},{8,11},{9,10},{10,... | collective-permute-start | bytes 589832 | tf_op jit(solution)/shard_map/ppermute | solution.py:284
  35.3 5.7 %collective-permute-start.13 = (f32[112,128]{1,0:T(8,128)S(1)}, f32[112,128]{1,0:T(8,128)S(1)}, u32[]{:S(2)}, u32[]{:S(2)}) collective-permute-start(f32[112,128]{1,0:T(8,128)S(1)} %sum_two.1.refs_0_), channel_id=1, source_target_pairs={{0,192},{4,196},{8,200},{12,204},{16,208},{20,212},{24,216},{28,22... | collective-permute-start | bytes 172040 | tf_op jit(solution)/shard_map/ppermute | solution.py:267
  36.5 7.0 %collective-permute-start.12 = (f32[112,128]{1,0:T(8,128)S(1)}, f32[112,128]{1,0:T(8,128)S(1)}, u32[]{:S(2)}, u32[]{:S(2)}) collective-permute-start(f32[112,128]{1,0:T(8,128)S(1)} %sum_two.1.refs_0_), channel_id=1, source_target_pairs={{0,128},{4,132},{8,136},{12,140},{16,144},{20,148},{24,152},{28,15... | collective-permute-start | bytes 172040 | tf_op jit(solution)/shard_map/ppermute | solution.py:267
  36.8 7.4 %collective-permute-start.11 = (f32[112,128]{1,0:T(8,128)S(1)}, f32[112,128]{1,0:T(8,128)S(1)}, u32[]{:S(2)}, u32[]{:S(2)}) collective-permute-start(f32[112,128]{1,0:T(8,128)S(1)} %sum_two.1.refs_0_), channel_id=1, source_target_pairs={{0,64},{4,68},{8,72},{12,76},{16,80},{20,84},{24,88},{28,92},{32,9... | collective-permute-start | bytes 172040 | tf_op jit(solution)/shard_map/ppermute | solution.py:267
  44.3 4.0 %collective-permute-start.14 = (f32[112,128]{1,0:T(8,128)S(1)}, f32[112,128]{1,0:T(8,128)S(1)}, u32[]{:S(2)}, u32[]{:S(2)}) collective-permute-start(f32[112,128]{1,0:T(8,128)S(1)} %sum_four.3.refs_0_), channel_id=1, source_target_pairs={{0,4},{4,0},{8,12},{12,8},{16,20},{20,16},{24,28},{28,24},{32,36},... | collective-permute-start | bytes 172040 | tf_op jit(solution)/shard_map/ppermute | solution.py:267
  48.3 7.2 %collective-permute-start.17 = (f32[224,128]{1,0:T(8,128)S(1)}, f32[224,128]{1,0:T(8,128)S(1)}, u32[]{:S(2)}, u32[]{:S(2)}) collective-permute-start(f32[224,128]{1,0:T(8,128)S(1)} %join.3.refs_0_), channel_id=1, source_target_pairs={{0,24},{4,28},{8,16},{12,20},{16,8},{20,12},{24,0},{28,4},{32,56},... | collective-permute-start | bytes 344072 | tf_op jit(solution)/shard_map/ppermute | solution.py:267
  49.6 6.0 %collective-permute-start.16 = (f32[224,128]{1,0:T(8,128)S(1)}, f32[224,128]{1,0:T(8,128)S(1)}, u32[]{:S(2)}, u32[]{:S(2)}) collective-permute-start(f32[224,128]{1,0:T(8,128)S(1)} %join.3.refs_0_), channel_id=1, source_target_pairs={{0,16},{4,20},{8,24},{12,28},{16,0},{20,4},{24,8},{28,12},{32,48},... | collective-permute-start | bytes 344072 | tf_op jit(solution)/shard_map/ppermute | solution.py:267
  49.6 7.2 %collective-permute-start.15 = (f32[224,128]{1,0:T(8,128)S(1)}, f32[224,128]{1,0:T(8,128)S(1)}, u32[]{:S(2)}, u32[]{:S(2)}) collective-permute-start(f32[224,128]{1,0:T(8,128)S(1)} %join.3.refs_0_), channel_id=1, source_target_pairs={{0,8},{4,12},{8,0},{12,4},{16,24},{20,28},{24,16},{28,20},{32,40},... | collective-permute-start | bytes 344072 | tf_op jit(solution)/shard_map/ppermute | solution.py:267

commit v9 on v8

--- a/solution.py
+++ b/solution.py
@@ -12,7 +12,7 @@
 LANES = 128
 PART = 112
 INNER = tuple(range(2, 8))
-EDGE = (0, 1, 6, 7)
+EDGE = (0, 1)
 ORDER = (0, 1, 3, 2)
 VMEM = pl.BlockSpec(memory_space=pltpu.VMEM)
 
@@ -228,11 +228,12 @@
         refs[-1][size * q : size * (q + 1), :] = ref[...]
 
 
-def place_kernel(*refs):
-    out_ref, held = refs[-2:]
+def place_kernel(even_ref, odd_ref, out_ref, held):
     spot = lax.axis_index("blk") & 7
     for q in range(4):
-        held[2 * PART * q : 2 * PART * (q + 1), :] = refs[q][...]
+        for odd, ref in enumerate((even_ref, odd_ref)):
+            start = PART * (2 * q + odd)
+            held[start : start + PART, :] = ref[PART * q : PART * (q + 1), :]
     for p in range(8):
         count = min(PART, 864 - PART * p)
         start = pl.multiple_of(PART * (spot ^ p), 8)
@@ -338,10 +339,10 @@
         name="middle",
     )
     second = over_ch(second, 3)
-    others = after(others, own)
+    inner = inner_part((6, 7), inner)
+    others = after(others, inner, own)
     total = call(sum_kernel, f32(PART, 128), (total, *others), name="sum_four")
-    both = call(join_kernel, f32(2 * PART, 128), (total, swap(total, 1)), name="join")
-    others = [swap(both, 2 * q) for q in (1, 2, 3)]
+    others = [swap(total, 2 * q) for q in (1, 2, 3)]
     output, grad_features = call(
         edge_kernel, (bf16(32, VOX), bf16(32, VOX)),
         (back, rules, weights, near, far, inner, own, first, second),
@@ -349,8 +350,10 @@
         flops=2 << 30, name="edge",
     )
     others = after(others, output)
+    even = call(join_kernel, f32(4 * PART, 128), (total, *others), name="join")
+    odd = swap(even, 1)
     weight_grad = call(
-        place_kernel, f32(864, 128), (both, *others),
+        place_kernel, f32(864, 128), (even, odd),
         [pltpu.VMEM((8 * PART, 128), jnp.float32)], name="place",
     )
     return output, grad_features, weight_grad.reshape(27, 32, 128)

time: 57.8 us -> 55.9 us (0.967)
  waiting for transfers between devices: 9.22 us -> 4.42 us
  starting transfers between devices: 32.3 us -> 35 us
    ppermute x13, waiting for transfers between devices: 7.94 us -> 4.41 us  [swap(): return lax.ppermute(value, 'blk', [(i, i ^ mask) for i in range(count)])]
    ppermute x13, starting transfers between devices: 24.7 us -> 27.3 us  [swap(): return lax.ppermute(value, 'blk', [(i, i ^ mask) for i in range(count)])]
    ppermute x4, waiting for transfers between devices: 1.28 us -> 0.01 us  [over_ch(): return lax.ppermute(value, 'ch', [(i, i ^ mask) for i in range(4)])]
    pallas_call x16 -> x17, Pallas kernels: 13.6 us -> 13.7 us  [call(): pl.pallas_call(kernel, out_shape=outs, in_specs=[VMEM] * len(args), out_s...]
  transfers between devices with their start and end apart: 18 -> 18, of which waited for: 8 -> 4; matrix products, arithmetic and copies ran while one was open for 0% -> 0% of each run, Pallas kernels for 21% -> 22%
where the time goes in v9:
time: 55.9 us; the launch traced here: 55.7 us
  starting transfers between devices  35 us (63%)
  Pallas kernels  13.7 us (25%)
  waiting for transfers between devices  4.42 us (8%)
  local copies, waits for them, and re-layouts  1.73 us (3%)
  between operations  0.81 us (1%)
    ppermute x13, starting transfers between devices, swap(): return lax.ppermute(value, 'blk', [(i, i ^ mask) for i in range(count)])  27.3 us
    pallas_call x17, Pallas kernels, call(): pl.pallas_call(kernel, out_shape=outs, in_specs=[VMEM] * len(args), out_s...  13.7 us
    ppermute x4, starting transfers between devices, over_ch(): return lax.ppermute(value, 'ch', [(i, i ^ mask) for i in range(4)])  6.69 us
    ppermute x13, waiting for transfers between devices, swap(): return lax.ppermute(value, 'blk', [(i, i ^ mask) for i in range(count)])  4.41 us
    unnamed x10, local copies, waits for them, and re-layouts  1.73 us
  transfers between devices with their start and end apart: 18, of which 4 were waited for; matrix products, arithmetic and copies ran while one was open for 0% of the time, Pallas kernels for 22%

profile of v9, /device:TPU:1, one launch (start us, length us, event | category | flops | bytes accessed | tf_op | source)
XLA Modules:
  0.0 55.7 jit_solution(17173875111806493503)
XLA Ops:
  0.6 2.2 %collective-permute-start.2 = (bf16[32,1024]{1,0:T(8,128)(2,1)}, bf16[32,1024]{1,0:T(8,128)(2,1)S(1)}, u32[]{:S(2)}, u32[]{:S(2)}) collective-permute-start(bf16[32,1024]{1,0:T(8,128)(2,1)} %refs_0_.1), channel_id=1, source_target_pairs={{0,1},{1,0},{2,3},{3,2},{4,5},{5,4},{6,7},{7,6},{8,9},{9,8},{10,11... | collective-permute-start | bytes 196616 | tf_op jit(solution)/shard_map/ppermute | solution.py:285
  2.8 0.9 %copy-done.1 = bf16[32,1024]{1,0:T(8,128)(2,1)S(1)} copy-done((bf16[32,1024]{1,0:T(8,128)(2,1)S(1)}, bf16[32,1024]{1,0:T(8,128)(2,1)}, u32[]{:S(2)}) %copy-start.1) | copy-done | bytes 65560
  3.7 0.8 %copy-done.4 = bf16[32,1024]{1,0:T(8,128)(2,1)S(1)} copy-done((bf16[32,1024]{1,0:T(8,128)(2,1)S(1)}, bf16[32,1024]{1,0:T(8,128)(2,1)}, u32[]{:S(2)}) %copy-start.4) | copy-done | bytes 65560
  4.6 1.2 %collective-permute-start = (bf16[64,128]{1,0:T(8,128)(2,1)S(1)}, bf16[64,128]{1,0:T(8,128)(2,1)S(1)}, u32[]{:S(2)}, u32[]{:S(2)}) collective-permute-start(bf16[64,128]{1,0:T(8,128)(2,1)S(1)} %get-tuple-element.33), channel_id=1, source_target_pairs={{0,4},{4,0},{8,12},{12,8},{16,20},{20,16},{24,28},{28,24},{32,36},... | collective-permute-start | bytes 49160 | tf_op jit(solution)/shard_map/ppermute | solution.py:268
  5.8 1.0 %collective-permute-start.1 = (bf16[64,128]{1,0:T(8,128)(2,1)S(1)}, bf16[64,128]{1,0:T(8,128)(2,1)S(1)}, u32[]{:S(2)}, u32[]{:S(2)}) collective-permute-start(bf16[64,128]{1,0:T(8,128)(2,1)S(1)} %get-tuple-element.34), channel_id=1, source_target_pairs={{0,252},{4,8},{8,4},{12,16},{16,12},{20,24},{24,20},{28,32},{32,28... | collective-permute-start | bytes 49160 | tf_op jit(solution)/shard_map/ppermute | solution.py:274
  6.8 2.0 %collective-permute-start.3 = (bf16[64,1024]{1,0:T(8,128)(2,1)S(1)}, bf16[64,1024]{1,0:T(8,128)(2,1)S(1)}, u32[]{:S(2)}, u32[]{:S(2)}) collective-permute-start(bf16[64,1024]{1,0:T(8,128)(2,1)S(1)} %join.2.pair_ref), channel_id=1, source_target_pairs={{0,3},{1,2},{2,1},{3,0},{4,7},{5,6},{6,5},{7,4},{8,11},{9,10},{10,... | collective-permute-start | bytes 393224 | tf_op jit(solution)/shard_map/ppermute | solution.py:285
  8.8 3.9 %gather.1.dense_in = bf16[864,1024]{1,0:T(8,128)(2,1)S(1)} custom-call(bf16[32,1024]{1,0:T(8,128)(2,1)S(1)} %copy-done.4, s32[27,1024]{1,0:T(8,128)S(1)} %copy-done.3), custom_call_target="tpu_custom_call" | custom-call | flops 3221225472 | bytes 1945600 | tf_op jit(solution)/shard_map/gather/pallas_call | solution.py:245
  12.7 0.7 %weight_terms.1 = (bf16[864,1024]{1,0:T(8,128)(2,1)S(1)}, bf16[128,1024]{1,0:T(8,128)(2,1)S(1)}, f32[448,128]{1,0:T(8,128)S(1)}, f32[448,128]{1,0:T(8,128)S(1)}) custom-call(bf16[864,1024]{1,0:T(8,128)(2,1)S(1)} %gather.1.dense_in, s32[27,1024]{1,0:T(8,128)S(1)} %copy-done.3, ...), custom_call_target="tpu_custom_call", output_to_operand_aliasing={{0}: (0, {})} | custom-call | flops 1073741824 | bytes 4665344 | tf_op jit(solution)/shard_map/weight_terms/pallas_call | solution.py:245
  13.5 7.4 %collective-permute-start.4 = (f32[448,128]{1,0:T(8,128)S(1)}, f32[448,128]{1,0:T(8,128)S(1)}, u32[]{:S(2)}, u32[]{:S(2)}) collective-permute-start(f32[448,128]{1,0:T(8,128)S(1)} %get-tuple-element.40), channel_id=1, source_target_pairs={{0,4},{4,0},{8,12},{12,8},{16,20},{20,16},{24,28},{28,24},{32,36},... | collective-permute-start | bytes 688136 | tf_op jit(solution)/shard_map/ppermute | solution.py:268
  20.9 0.6 %back_terms.1.terms = f32[864,1024]{1,0:T(8,128)S(1)} custom-call(bf16[864,128]{1,0:T(8,128)(2,1)S(1)} %bitcast.2, bf16[128,1024]{1,0:T(8,128)(2,1)S(1)} %get-tuple-element.35.grad_ref), custom_call_target="tpu_custom_call" | custom-call | flops 1073741824 | bytes 4022272 | tf_op jit(solution)/shard_map/back_terms/pallas_call | solution.py:245
  21.5 0.5 forward.1
  22.0 0.1 collective-permute-start.6
  22.1 0.1 collective-permute-start.7
  22.2 3.7 %collective-permute-start.8 = (f32[112,128]{1,0:T(8,128)S(1)}, f32[112,128]{1,0:T(8,128)S(1)}, u32[]{:S(2)}, u32[]{:S(2)}) collective-permute-start(f32[112,128]{1,0:T(8,128)S(1)} %get-tuple-element.45), channel_id=1, source_target_pairs={{0,24},{4,28},{8,16},{12,20},{16,8},{20,12},{24,0},{28,4},{32,56},... | collective-permute-start | bytes 172040 | tf_op jit(solution)/shard_map/ppermute | solution.py:268
  26.0 0.3 collective-permute-start.5
  26.3 1.8 %back_inner.3.refs_0_ = f32[32,1024]{1,0:T(8,128)S(1)} custom-call(f32[864,1024]{1,0:T(8,128)S(1)} %back_terms.1.terms, s32[27,1024]{1,0:T(8,128)S(1)} %copy-done.3), custom_call_target="tpu_custom_call" | custom-call | flops 2147483648 | bytes 3780608 | tf_op jit(solution)/shard_map/back_inner/pallas_call | solution.py:245
  28.2 0.4 collective-permute-done.8.refs_3_
  28.7 1.8 %back_inner.4.refs_0_ = f32[32,1024]{1,0:T(8,128)S(1)} custom-call(f32[864,1024]{1,0:T(8,128)S(1)} %back_terms.1.terms, s32[27,1024]{1,0:T(8,128)S(1)} %copy-done.3, f32[32,1024]{1,0:T(8,128)S(1)} %back_inner.3.refs_0_), custom_call_target="tpu_custom_call", output_to_operand_aliasing={{}: (2, {})} | custom-call | flops 2147483648 | bytes 3911680 | tf_op jit(solution)/shard_map/back_inner/pallas_call | solution.py:245
  30.5 1.5 %collective-permute-done.9.refs_1_ = f32[112,128]{1,0:T(8,128)S(1)} collective-permute-done((f32[112,128]{1,0:T(8,128)S(1)}, f32[112,128]{1,0:T(8,128)S(1)}, u32[]{:S(2)}, u32[]{:S(2)}) %collective-permute-start.9) | collective-permute-done | bytes 57376 | tf_op jit(solution)/shard_map/ppermute | solution.py:268
  32.0 1.2 %collective-permute-start.13 = (f32[112,128]{1,0:T(8,128)S(1)}, f32[112,128]{1,0:T(8,128)S(1)}, u32[]{:S(2)}, u32[]{:S(2)}) collective-permute-start(f32[112,128]{1,0:T(8,128)S(1)} %sum_two.1.refs_0_), channel_id=1, source_target_pairs={{0,192},{4,196},{8,200},{12,204},{16,208},{20,212},{24,216},{28,22... | collective-permute-start | bytes 172040 | tf_op jit(solution)/shard_map/ppermute | solution.py:268
  33.2 1.4 %collective-permute-start.12 = (f32[112,128]{1,0:T(8,128)S(1)}, f32[112,128]{1,0:T(8,128)S(1)}, u32[]{:S(2)}, u32[]{:S(2)}) collective-permute-start(f32[112,128]{1,0:T(8,128)S(1)} %sum_two.1.refs_0_), channel_id=1, source_target_pairs={{0,128},{4,132},{8,136},{12,140},{16,144},{20,148},{24,152},{28,15... | collective-permute-start | bytes 172040 | tf_op jit(solution)/shard_map/ppermute | solution.py:268
  34.6 3.2 %collective-permute-start.11 = (f32[112,128]{1,0:T(8,128)S(1)}, f32[112,128]{1,0:T(8,128)S(1)}, u32[]{:S(2)}, u32[]{:S(2)}) collective-permute-start(f32[112,128]{1,0:T(8,128)S(1)} %sum_two.1.refs_0_), channel_id=1, source_target_pairs={{0,64},{4,68},{8,72},{12,76},{16,80},{20,84},{24,88},{28,92},{32,9... | collective-permute-start | bytes 172040 | tf_op jit(solution)/shard_map/ppermute | solution.py:268
  37.8 2.2 %collective-permute-start.10 = (f32[32,1536]{1,0:T(8,128)S(1)}, f32[32,1536]{1,0:T(8,128)S(1)}, u32[]{:S(2)}, u32[]{:S(2)}) collective-permute-start(f32[32,1536]{1,0:T(8,128)S(1)} %get-tuple-element.54), channel_id=1, source_target_pairs={{0,3},{1,2},{2,1},{3,0},{4,7},{5,6},{6,5},{7,4},{8,11},{9,10},{10,... | collective-permute-start | bytes 589832 | tf_op jit(solution)/shard_map/ppermute | solution.py:285
  40.0 1.8 %back_inner.5.inner = f32[32,1024]{1,0:T(8,128)S(1)} custom-call(f32[864,1024]{1,0:T(8,128)S(1)} %back_terms.1.terms, s32[27,1024]{1,0:T(8,128)S(1)} %copy-done.3, f32[32,1024]{1,0:T(8,128)S(1)} %back_inner.4.refs_0_), custom_call_target="tpu_custom_call", output_to_operand_aliasing={{}: (2, {})} | custom-call | flops 2147483648 | bytes 3911680 | tf_op jit(solution)/shard_map/back_inner/pallas_call | solution.py:245
  41.9 1.7 %collective-permute-start.16 = (f32[112,128]{1,0:T(8,128)S(1)}, f32[112,128]{1,0:T(8,128)S(1)}, u32[]{:S(2)}, u32[]{:S(2)}) collective-permute-start(f32[112,128]{1,0:T(8,128)S(1)} %sum_four.3.refs_0_), channel_id=1, source_target_pairs={{0,24},{4,28},{8,16},{12,20},{16,8},{20,12},{24,0},{28,4},{32,56},... | collective-permute-start | bytes 172040 | tf_op jit(solution)/shard_map/ppermute | solution.py:268
  43.6 0.6 %collective-permute-start.15 = (f32[112,128]{1,0:T(8,128)S(1)}, f32[112,128]{1,0:T(8,128)S(1)}, u32[]{:S(2)}, u32[]{:S(2)}) collective-permute-start(f32[112,128]{1,0:T(8,128)S(1)} %sum_four.3.refs_0_), channel_id=1, source_target_pairs={{0,16},{4,20},{8,24},{12,28},{16,0},{20,4},{24,8},{28,12},{32,48},... | collective-permute-start | bytes 172040 | tf_op jit(solution)/shard_map/ppermute | solution.py:268
  44.2 1.0 %collective-permute-start.14 = (f32[112,128]{1,0:T(8,128)S(1)}, f32[112,128]{1,0:T(8,128)S(1)}, u32[]{:S(2)}, u32[]{:S(2)}) collective-permute-start(f32[112,128]{1,0:T(8,128)S(1)} %sum_four.3.refs_0_), channel_id=1, source_target_pairs={{0,8},{4,12},{8,0},{12,4},{16,24},{20,28},{24,16},{28,20},{32,40},... | collective-permute-start | bytes 172040 | tf_op jit(solution)/shard_map/ppermute | solution.py:268
  45.2 1.5 %edge.1 = (bf16[32,1024]{1,0:T(8,128)(2,1)}, bf16[32,1024]{1,0:T(8,128)(2,1)}) custom-call(f32[864,1024]{1,0:T(8,128)S(1)} %back_terms.1.terms, s32[27,1024]{1,0:T(8,128)S(1)} %copy-done.3, bf16[864,128]{1,0:T(8,128)(2,1)S(1)} %bitcast.4, bf16[64,128]{1,0:T(8,128)(2,1)S(1)} %collective-permute-done.near_ref, ...), custom_call_target="tpu_custom_call" | custom-call | flops 2147483648 | bytes 4788224 | tf_op jit(solution)/shard_map/edge/pallas_call | solution.py:245
  46.8 1.4 %collective-permute-done.15.refs_2_ = f32[112,128]{1,0:T(8,128)S(1)} collective-permute-done((f32[112,128]{1,0:T(8,128)S(1)}, f32[112,128]{1,0:T(8,128)S(1)}, u32[]{:S(2)}, u32[]{:S(2)}) %collective-permute-start.15) | collective-permute-done | bytes 57376 | tf_op jit(solution)/shard_map/ppermute | solution.py:268
  48.2 5.6 %collective-permute-start.17 = (f32[448,128]{1,0:T(8,128)S(1)}, f32[448,128]{1,0:T(8,128)S(1)}, u32[]{:S(2)}, u32[]{:S(2)}) collective-permute-start(f32[448,128]{1,0:T(8,128)S(1)} %join.3.even_ref), channel_id=1, source_target_pairs={{0,4},{4,0},{8,12},{12,8},{16,20},{20,16},{24,28},{28,24},{32,36},... | collective-permute-start | bytes 688136 | tf_op jit(solution)/shard_map/ppermute | solution.py:268
  53.7 1.1 %collective-permute-done.17.odd_ref = f32[448,128]{1,0:T(8,128)S(1)} collective-permute-done((f32[448,128]{1,0:T(8,128)S(1)}, f32[448,128]{1,0:T(8,128)S(1)}, u32[]{:S(2)}, u32[]{:S(2)}) %collective-permute-start.17) | collective-permute-done | bytes 229408 | tf_op jit(solution)/shard_map/ppermute | solution.py:268
  54.9 0.8 %place.1 = f32[864,128]{1,0:T(8,128)} custom-call(f32[448,128]{1,0:T(8,128)S(1)} %join.3.even_ref, f32[448,128]{1,0:T(8,128)S(1)} %collective-permute-done.17.odd_ref), custom_call_target="tpu_custom_call" | custom-call | bytes 901120 | tf_op jit(solution)/shard_map/place/pallas_call | solution.py:245
  (31 shorter events, 0.3 us)
Async XLA Ops:
  0.6 6.2 %collective-permute-start.2 = (bf16[32,1024]{1,0:T(8,128)(2,1)}, bf16[32,1024]{1,0:T(8,128)(2,1)S(1)}, u32[]{:S(2)}, u32[]{:S(2)}) collective-permute-start(bf16[32,1024]{1,0:T(8,128)(2,1)} %refs_0_.1), channel_id=1, source_target_pairs={{0,1},{1,0},{2,3},{3,2},{4,5},{5,4},{6,7},{7,6},{8,9},{9,8},{10,11... | collective-permute-start | bytes 196616 | tf_op jit(solution)/shard_map/ppermute | solution.py:285
  2.8 0.9 %copy-start.1 = (bf16[32,1024]{1,0:T(8,128)(2,1)S(1)}, bf16[32,1024]{1,0:T(8,128)(2,1)}, u32[]{:S(2)}) copy-start(bf16[32,1024]{1,0:T(8,128)(2,1)} %refs_0_.1) | copy-start | bytes 196612
  3.7 0.8 %copy-start.4 = (bf16[32,1024]{1,0:T(8,128)(2,1)S(1)}, bf16[32,1024]{1,0:T(8,128)(2,1)}, u32[]{:S(2)}) copy-start(bf16[32,1024]{1,0:T(8,128)(2,1)} %x_ref.3) | copy-start | bytes 196612
  4.6 2.3 %copy-start.2 = (bf16[32,1024]{1,0:T(8,128)(2,1)S(1)}, bf16[32,1024]{1,0:T(8,128)(2,1)}, u32[]{:S(2)}) copy-start(bf16[32,1024]{1,0:T(8,128)(2,1)} %refs_0_.1) | copy-start | bytes 196612
  4.6 4.3 %copy-start.3 = (s32[27,1024]{1,0:T(8,128)S(1)}, s32[27,1024]{1,0:T(8,128)}, u32[]{:S(2)}) copy-start(s32[27,1024]{1,0:T(8,128)} %rule_ref.11) | copy-start | bytes 331780
  4.6 8.1 %collective-permute-start = (bf16[64,128]{1,0:T(8,128)(2,1)S(1)}, bf16[64,128]{1,0:T(8,128)(2,1)S(1)}, u32[]{:S(2)}, u32[]{:S(2)}) collective-permute-start(bf16[64,128]{1,0:T(8,128)(2,1)S(1)} %get-tuple-element.33), channel_id=1, source_target_pairs={{0,4},{4,0},{8,12},{12,8},{16,20},{20,16},{24,28},{28,24},{32,36},... | collective-permute-start | bytes 49160 | tf_op jit(solution)/shard_map/ppermute | solution.py:268
  5.8 6.9 %collective-permute-start.1 = (bf16[64,128]{1,0:T(8,128)(2,1)S(1)}, bf16[64,128]{1,0:T(8,128)(2,1)S(1)}, u32[]{:S(2)}, u32[]{:S(2)}) collective-permute-start(bf16[64,128]{1,0:T(8,128)(2,1)S(1)} %get-tuple-element.34), channel_id=1, source_target_pairs={{0,252},{4,8},{8,4},{12,16},{16,12},{20,24},{24,20},{28,32},{32,28... | collective-permute-start | bytes 49160 | tf_op jit(solution)/shard_map/ppermute | solution.py:274
  6.8 5.9 %collective-permute-start.3 = (bf16[64,1024]{1,0:T(8,128)(2,1)S(1)}, bf16[64,1024]{1,0:T(8,128)(2,1)S(1)}, u32[]{:S(2)}, u32[]{:S(2)}) collective-permute-start(bf16[64,1024]{1,0:T(8,128)(2,1)S(1)} %join.2.pair_ref), channel_id=1, source_target_pairs={{0,3},{1,2},{2,1},{3,0},{4,7},{5,6},{6,5},{7,4},{8,11},{9,10},{10,... | collective-permute-start | bytes 393224 | tf_op jit(solution)/shard_map/ppermute | solution.py:285
  12.7 8.2 %copy-start = (bf16[27,32,128]{2,1,0:T(8,128)(2,1)S(1)}, bf16[27,32,128]{2,1,0:T(8,128)(2,1)}, u32[]{:S(2)}) copy-start(bf16[27,32,128]{2,1,0:T(8,128)(2,1)} %param.5) | copy-start | bytes 663556
  13.5 8.5 %collective-permute-start.4 = (f32[448,128]{1,0:T(8,128)S(1)}, f32[448,128]{1,0:T(8,128)S(1)}, u32[]{:S(2)}, u32[]{:S(2)}) collective-permute-start(f32[448,128]{1,0:T(8,128)S(1)} %get-tuple-element.40), channel_id=1, source_target_pairs={{0,4},{4,0},{8,12},{12,8},{16,20},{20,16},{24,28},{28,24},{32,36},... | collective-permute-start | bytes 688136 | tf_op jit(solution)/shard_map/ppermute | solution.py:268
  22.0 6.1 %collective-permute-start.6 = (f32[112,128]{1,0:T(8,128)S(1)}, f32[112,128]{1,0:T(8,128)S(1)}, u32[]{:S(2)}, u32[]{:S(2)}) collective-permute-start(f32[112,128]{1,0:T(8,128)S(1)} %get-tuple-element.43), channel_id=1, source_target_pairs={{0,8},{4,12},{8,0},{12,4},{16,24},{20,28},{24,16},{28,20},{32,40},... | collective-permute-start | bytes 172040 | tf_op jit(solution)/shard_map/ppermute | solution.py:268
  22.1 6.0 %collective-permute-start.7 = (f32[112,128]{1,0:T(8,128)S(1)}, f32[112,128]{1,0:T(8,128)S(1)}, u32[]{:S(2)}, u32[]{:S(2)}) collective-permute-start(f32[112,128]{1,0:T(8,128)S(1)} %get-tuple-element.44), channel_id=1, source_target_pairs={{0,16},{4,20},{8,24},{12,28},{16,0},{20,4},{24,8},{28,12},{32,48},... | collective-permute-start | bytes 172040 | tf_op jit(solution)/shard_map/ppermute | solution.py:268
  22.2 6.3 %collective-permute-start.8 = (f32[112,128]{1,0:T(8,128)S(1)}, f32[112,128]{1,0:T(8,128)S(1)}, u32[]{:S(2)}, u32[]{:S(2)}) collective-permute-start(f32[112,128]{1,0:T(8,128)S(1)} %get-tuple-element.45), channel_id=1, source_target_pairs={{0,24},{4,28},{8,16},{12,20},{16,8},{20,12},{24,0},{28,4},{32,56},... | collective-permute-start | bytes 172040 | tf_op jit(solution)/shard_map/ppermute | solution.py:268
  26.0 11.8 %collective-permute-start.5 = (f32[64,1152]{1,0:T(8,128)S(1)}, f32[64,1152]{1,0:T(8,128)S(1)}, u32[]{:S(2)}, u32[]{:S(2)}) collective-permute-start(f32[64,1152]{1,0:T(8,128)S(1)} %get-tuple-element.46), channel_id=1, source_target_pairs={{0,1},{1,0},{2,3},{3,2},{4,5},{5,4},{6,7},{7,6},{8,9},{9,8},{10,11... | collective-permute-start | bytes 884744 | tf_op jit(solution)/shard_map/ppermute | solution.py:285
  28.6 3.4 %collective-permute-start.9 = (f32[112,128]{1,0:T(8,128)S(1)}, f32[112,128]{1,0:T(8,128)S(1)}, u32[]{:S(2)}, u32[]{:S(2)}) collective-permute-start(f32[112,128]{1,0:T(8,128)S(1)} %sum_four.2.refs_0_), channel_id=1, source_target_pairs={{0,32},{4,36},{8,40},{12,44},{16,48},{20,52},{24,56},{28,60},{32,0... | collective-permute-start | bytes 172040 | tf_op jit(solution)/shard_map/ppermute | solution.py:268
  32.0 9.8 %collective-permute-start.13 = (f32[112,128]{1,0:T(8,128)S(1)}, f32[112,128]{1,0:T(8,128)S(1)}, u32[]{:S(2)}, u32[]{:S(2)}) collective-permute-start(f32[112,128]{1,0:T(8,128)S(1)} %sum_two.1.refs_0_), channel_id=1, source_target_pairs={{0,192},{4,196},{8,200},{12,204},{16,208},{20,212},{24,216},{28,22... | collective-permute-start | bytes 172040 | tf_op jit(solution)/shard_map/ppermute | solution.py:268
  33.2 8.6 %collective-permute-start.12 = (f32[112,128]{1,0:T(8,128)S(1)}, f32[112,128]{1,0:T(8,128)S(1)}, u32[]{:S(2)}, u32[]{:S(2)}) collective-permute-start(f32[112,128]{1,0:T(8,128)S(1)} %sum_two.1.refs_0_), channel_id=1, source_target_pairs={{0,128},{4,132},{8,136},{12,140},{16,144},{20,148},{24,152},{28,15... | collective-permute-start | bytes 172040 | tf_op jit(solution)/shard_map/ppermute | solution.py:268
  34.6 7.3 %collective-permute-start.11 = (f32[112,128]{1,0:T(8,128)S(1)}, f32[112,128]{1,0:T(8,128)S(1)}, u32[]{:S(2)}, u32[]{:S(2)}) collective-permute-start(f32[112,128]{1,0:T(8,128)S(1)} %sum_two.1.refs_0_), channel_id=1, source_target_pairs={{0,64},{4,68},{8,72},{12,76},{16,80},{20,84},{24,88},{28,92},{32,9... | collective-permute-start | bytes 172040 | tf_op jit(solution)/shard_map/ppermute | solution.py:268
  37.8 7.4 %collective-permute-start.10 = (f32[32,1536]{1,0:T(8,128)S(1)}, f32[32,1536]{1,0:T(8,128)S(1)}, u32[]{:S(2)}, u32[]{:S(2)}) collective-permute-start(f32[32,1536]{1,0:T(8,128)S(1)} %get-tuple-element.54), channel_id=1, source_target_pairs={{0,3},{1,2},{2,1},{3,0},{4,7},{5,6},{6,5},{7,4},{8,11},{9,10},{10,... | collective-permute-start | bytes 589832 | tf_op jit(solution)/shard_map/ppermute | solution.py:285
  41.9 4.9 %collective-permute-start.16 = (f32[112,128]{1,0:T(8,128)S(1)}, f32[112,128]{1,0:T(8,128)S(1)}, u32[]{:S(2)}, u32[]{:S(2)}) collective-permute-start(f32[112,128]{1,0:T(8,128)S(1)} %sum_four.3.refs_0_), channel_id=1, source_target_pairs={{0,24},{4,28},{8,16},{12,20},{16,8},{20,12},{24,0},{28,4},{32,56},... | collective-permute-start | bytes 172040 | tf_op jit(solution)/shard_map/ppermute | solution.py:268
  43.6 4.5 %collective-permute-start.15 = (f32[112,128]{1,0:T(8,128)S(1)}, f32[112,128]{1,0:T(8,128)S(1)}, u32[]{:S(2)}, u32[]{:S(2)}) collective-permute-start(f32[112,128]{1,0:T(8,128)S(1)} %sum_four.3.refs_0_), channel_id=1, source_target_pairs={{0,16},{4,20},{8,24},{12,28},{16,0},{20,4},{24,8},{28,12},{32,48},... | collective-permute-start | bytes 172040 | tf_op jit(solution)/shard_map/ppermute | solution.py:268
  44.2 4.0 %collective-permute-start.14 = (f32[112,128]{1,0:T(8,128)S(1)}, f32[112,128]{1,0:T(8,128)S(1)}, u32[]{:S(2)}, u32[]{:S(2)}) collective-permute-start(f32[112,128]{1,0:T(8,128)S(1)} %sum_four.3.refs_0_), channel_id=1, source_target_pairs={{0,8},{4,12},{8,0},{12,4},{16,24},{20,28},{24,16},{28,20},{32,40},... | collective-permute-start | bytes 172040 | tf_op jit(solution)/shard_map/ppermute | solution.py:268
  48.2 6.7 %collective-permute-start.17 = (f32[448,128]{1,0:T(8,128)S(1)}, f32[448,128]{1,0:T(8,128)S(1)}, u32[]{:S(2)}, u32[]{:S(2)}) collective-permute-start(f32[448,128]{1,0:T(8,128)S(1)} %join.3.even_ref), channel_id=1, source_target_pairs={{0,4},{4,0},{8,12},{12,8},{16,20},{20,16},{24,28},{28,24},{32,36},... | collective-permute-start | bytes 688136 | tf_op jit(solution)/shard_map/ppermute | solution.py:268

commit v10 on v9

--- a/solution.py
+++ b/solution.py
@@ -12,7 +12,7 @@
 LANES = 128
 PART = 112
 INNER = tuple(range(2, 8))
-EDGE = (0, 1)
+EDGE = (0, 1, 3)
 ORDER = (0, 1, 3, 2)
 VMEM = pl.BlockSpec(memory_space=pltpu.VMEM)
 
@@ -228,16 +228,19 @@
         refs[-1][size * q : size * (q + 1), :] = ref[...]
 
 
-def place_kernel(even_ref, odd_ref, out_ref, held):
+def place_kernel(even_ref, odd_ref, out_ref):
     spot = lax.axis_index("blk") & 7
+    short = 864 - 7 * PART
     for q in range(4):
         for odd, ref in enumerate((even_ref, odd_ref)):
-            start = PART * (2 * q + odd)
-            held[start : start + PART, :] = ref[PART * q : PART * (q + 1), :]
-    for p in range(8):
-        count = min(PART, 864 - PART * p)
-        start = pl.multiple_of(PART * (spot ^ p), 8)
-        out_ref[PART * p : PART * p + count, :] = held[pl.ds(start, count), :]
+            part = spot ^ (2 * q + odd)
+            start = pl.multiple_of(PART * part, 8)
+            out_ref[pl.ds(start, short), :] = ref[PART * q : PART * q + short, :]
+
+            @pl.when(part < 7)
+            def _():
+                rows = pl.ds(pl.multiple_of(start + short, 8), PART - short)
+                out_ref[rows, :] = ref[PART * q + short : PART * (q + 1), :]
 
 
 def call(kernel, outs, args, scratch=(), aliases=None, flops=0, name=None):
@@ -325,14 +328,14 @@
     others = [swap(pieces[q], 2 * q) for q in (1, 2, 3)]
     first, = after((first,), *pieces)
     first = over_ch(first, 1)
-    inner = inner_part((2, 3))
+    inner = inner_part((2,))
     others = after(others, inner)
     total = call(sum_kernel, f32(PART, 128), (pieces[0], *others), name="sum_four")
-    came = swap(total, 8)
+    came = swap(total, 48)
     inner = inner_part((4, 5), inner)
     came, = after((came,), inner)
     total = call(sum_kernel, f32(PART, 128), (total, came), name="sum_two")
-    others = [swap(total, m) for m in (16, 32, 48)]
+    others = [swap(total, m) for m in (8, 16, 24)]
     ours, first = after((ours, first), total)
     own, second = call(
         middle_kernel, (f32(32, VOX), f32(32, VOX + 4 * FACE)), (ours, first, near, far),
@@ -353,8 +356,7 @@
     even = call(join_kernel, f32(4 * PART, 128), (total, *others), name="join")
     odd = swap(even, 1)
     weight_grad = call(
-        place_kernel, f32(864, 128), (even, odd),
-        [pltpu.VMEM((8 * PART, 128), jnp.float32)], name="place",
+        place_kernel, f32(864, 128), (even, odd), name="place",
     )
     return output, grad_features, weight_grad.reshape(27, 32, 128)
 

time: 55.9 us -> 55.9 us (level)
  waiting for transfers between devices: 4.42 us -> 5.13 us
  starting transfers between devices: 35 us -> 34.4 us
    ppermute x13, starting transfers between devices: 27.3 us -> 26.6 us  [swap(): return lax.ppermute(value, 'blk', [(i, i ^ mask) for i in range(count)])]
    ppermute x13, waiting for transfers between devices: 4.41 us -> 5.11 us  [swap(): return lax.ppermute(value, 'blk', [(i, i ^ mask) for i in range(count)])]
where the time goes in v10:
time: 55.9 us; the launch traced here: 55.7 us
  starting transfers between devices  34.4 us (62%)
  Pallas kernels  13.6 us (24%)
  waiting for transfers between devices  5.13 us (9%)
  local copies, waits for them, and re-layouts  1.73 us (3%)
  between operations  0.8 us (1%)
    ppermute x13, starting transfers between devices, swap(): return lax.ppermute(value, 'blk', [(i, i ^ mask) for i in range(count)])  26.6 us
    pallas_call x17, Pallas kernels, call(): pl.pallas_call(kernel, out_shape=outs, in_specs=[VMEM] * len(args), out_s...  13.6 us
    ppermute x4, starting transfers between devices, over_ch(): return lax.ppermute(value, 'ch', [(i, i ^ mask) for i in range(4)])  6.74 us
    ppermute x13, waiting for transfers between devices, swap(): return lax.ppermute(value, 'blk', [(i, i ^ mask) for i in range(count)])  5.11 us
    unnamed x10, local copies, waits for them, and re-layouts  1.73 us
  transfers between devices with their start and end apart: 18, of which 4 were waited for; matrix products, arithmetic and copies ran while one was open for 0% of the time, Pallas kernels for 22%

profile of v10, /device:TPU:1, one launch (start us, length us, event | category | flops | bytes accessed | tf_op | source)
XLA Modules:
  0.0 55.7 jit_solution(6725087676092210955)
XLA Ops:
  0.6 2.2 %collective-permute-start.2 = (bf16[32,1024]{1,0:T(8,128)(2,1)}, bf16[32,1024]{1,0:T(8,128)(2,1)S(1)}, u32[]{:S(2)}, u32[]{:S(2)}) collective-permute-start(bf16[32,1024]{1,0:T(8,128)(2,1)} %refs_0_.1), channel_id=1, source_target_pairs={{0,1},{1,0},{2,3},{3,2},{4,5},{5,4},{6,7},{7,6},{8,9},{9,8},{10,11... | collective-permute-start | bytes 196616 | tf_op jit(solution)/shard_map/ppermute | solution.py:288
  2.8 0.9 %copy-done.1 = bf16[32,1024]{1,0:T(8,128)(2,1)S(1)} copy-done((bf16[32,1024]{1,0:T(8,128)(2,1)S(1)}, bf16[32,1024]{1,0:T(8,128)(2,1)}, u32[]{:S(2)}) %copy-start.1) | copy-done | bytes 65560
  3.7 0.8 %copy-done.4 = bf16[32,1024]{1,0:T(8,128)(2,1)S(1)} copy-done((bf16[32,1024]{1,0:T(8,128)(2,1)S(1)}, bf16[32,1024]{1,0:T(8,128)(2,1)}, u32[]{:S(2)}) %copy-start.4) | copy-done | bytes 65560
  4.6 1.2 %collective-permute-start = (bf16[64,128]{1,0:T(8,128)(2,1)S(1)}, bf16[64,128]{1,0:T(8,128)(2,1)S(1)}, u32[]{:S(2)}, u32[]{:S(2)}) collective-permute-start(bf16[64,128]{1,0:T(8,128)(2,1)S(1)} %get-tuple-element.33), channel_id=1, source_target_pairs={{0,4},{4,0},{8,12},{12,8},{16,20},{20,16},{24,28},{28,24},{32,36},... | collective-permute-start | bytes 49160 | tf_op jit(solution)/shard_map/ppermute | solution.py:271
  5.8 1.0 %collective-permute-start.1 = (bf16[64,128]{1,0:T(8,128)(2,1)S(1)}, bf16[64,128]{1,0:T(8,128)(2,1)S(1)}, u32[]{:S(2)}, u32[]{:S(2)}) collective-permute-start(bf16[64,128]{1,0:T(8,128)(2,1)S(1)} %get-tuple-element.34), channel_id=1, source_target_pairs={{0,252},{4,8},{8,4},{12,16},{16,12},{20,24},{24,20},{28,32},{32,28... | collective-permute-start | bytes 49160 | tf_op jit(solution)/shard_map/ppermute | solution.py:277
  6.8 2.0 %collective-permute-start.3 = (bf16[64,1024]{1,0:T(8,128)(2,1)S(1)}, bf16[64,1024]{1,0:T(8,128)(2,1)S(1)}, u32[]{:S(2)}, u32[]{:S(2)}) collective-permute-start(bf16[64,1024]{1,0:T(8,128)(2,1)S(1)} %join.2.pair_ref), channel_id=1, source_target_pairs={{0,3},{1,2},{2,1},{3,0},{4,7},{5,6},{6,5},{7,4},{8,11},{9,10},{10,... | collective-permute-start | bytes 393224 | tf_op jit(solution)/shard_map/ppermute | solution.py:288
  8.8 3.9 %gather.1.dense_in = bf16[864,1024]{1,0:T(8,128)(2,1)S(1)} custom-call(bf16[32,1024]{1,0:T(8,128)(2,1)S(1)} %copy-done.4, s32[27,1024]{1,0:T(8,128)S(1)} %copy-done.3), custom_call_target="tpu_custom_call" | custom-call | flops 3221225472 | bytes 1945600 | tf_op jit(solution)/shard_map/gather/pallas_call | solution.py:248
  12.7 0.0 copy-start
  12.7 0.7 %weight_terms.1 = (bf16[864,1024]{1,0:T(8,128)(2,1)S(1)}, bf16[128,1024]{1,0:T(8,128)(2,1)S(1)}, f32[448,128]{1,0:T(8,128)S(1)}, f32[448,128]{1,0:T(8,128)S(1)}) custom-call(bf16[864,1024]{1,0:T(8,128)(2,1)S(1)} %gather.1.dense_in, s32[27,1024]{1,0:T(8,128)S(1)} %copy-done.3, ...), custom_call_target="tpu_custom_call", output_to_operand_aliasing={{0}: (0, {})} | custom-call | flops 1073741824 | bytes 4665344 | tf_op jit(solution)/shard_map/weight_terms/pallas_call | solution.py:248
  13.5 7.4 %collective-permute-start.4 = (f32[448,128]{1,0:T(8,128)S(1)}, f32[448,128]{1,0:T(8,128)S(1)}, u32[]{:S(2)}, u32[]{:S(2)}) collective-permute-start(f32[448,128]{1,0:T(8,128)S(1)} %get-tuple-element.40), channel_id=1, source_target_pairs={{0,4},{4,0},{8,12},{12,8},{16,20},{20,16},{24,28},{28,24},{32,36},... | collective-permute-start | bytes 688136 | tf_op jit(solution)/shard_map/ppermute | solution.py:271
  20.9 0.6 %back_terms.1.terms = f32[864,1024]{1,0:T(8,128)S(1)} custom-call(bf16[864,128]{1,0:T(8,128)(2,1)S(1)} %bitcast.2, bf16[128,1024]{1,0:T(8,128)(2,1)S(1)} %get-tuple-element.35.grad_ref), custom_call_target="tpu_custom_call" | custom-call | flops 1073741824 | bytes 4022272 | tf_op jit(solution)/shard_map/back_terms/pallas_call | solution.py:248
  21.5 0.5 forward.1
  22.0 0.1 collective-permute-start.6
  22.1 0.1 collective-permute-start.7
  22.2 3.7 %collective-permute-start.8 = (f32[112,128]{1,0:T(8,128)S(1)}, f32[112,128]{1,0:T(8,128)S(1)}, u32[]{:S(2)}, u32[]{:S(2)}) collective-permute-start(f32[112,128]{1,0:T(8,128)S(1)} %get-tuple-element.45), channel_id=1, source_target_pairs={{0,24},{4,28},{8,16},{12,20},{16,8},{20,12},{24,0},{28,4},{32,56},... | collective-permute-start | bytes 172040 | tf_op jit(solution)/shard_map/ppermute | solution.py:271
  26.0 0.3 collective-permute-start.5
  26.3 1.0 %back_inner.3.refs_0_ = f32[32,1024]{1,0:T(8,128)S(1)} custom-call(f32[864,1024]{1,0:T(8,128)S(1)} %back_terms.1.terms, s32[27,1024]{1,0:T(8,128)S(1)} %copy-done.3), custom_call_target="tpu_custom_call" | custom-call | flops 1073741824 | bytes 3780608 | tf_op jit(solution)/shard_map/back_inner/pallas_call | solution.py:248
  27.3 1.3 %collective-permute-done.8.refs_3_ = f32[112,128]{1,0:T(8,128)S(1)} collective-permute-done((f32[112,128]{1,0:T(8,128)S(1)}, f32[112,128]{1,0:T(8,128)S(1)}, u32[]{:S(2)}, u32[]{:S(2)}) %collective-permute-start.8) | collective-permute-done | bytes 57376 | tf_op jit(solution)/shard_map/ppermute | solution.py:271
  28.6 1.2 %collective-permute-start.9 = (f32[112,128]{1,0:T(8,128)S(1)}, f32[112,128]{1,0:T(8,128)S(1)}, u32[]{:S(2)}, u32[]{:S(2)}) collective-permute-start(f32[112,128]{1,0:T(8,128)S(1)} %sum_four.2.refs_0_), channel_id=1, source_target_pairs={{0,192},{4,196},{8,200},{12,204},{16,208},{20,212},{24,216},{28,22... | collective-permute-start | bytes 172040 | tf_op jit(solution)/shard_map/ppermute | solution.py:271
  29.8 1.8 %back_inner.4.refs_0_ = f32[32,1024]{1,0:T(8,128)S(1)} custom-call(f32[864,1024]{1,0:T(8,128)S(1)} %back_terms.1.terms, s32[27,1024]{1,0:T(8,128)S(1)} %copy-done.3, f32[32,1024]{1,0:T(8,128)S(1)} %back_inner.3.refs_0_), custom_call_target="tpu_custom_call", output_to_operand_aliasing={{}: (2, {})} | custom-call | flops 2147483648 | bytes 3911680 | tf_op jit(solution)/shard_map/back_inner/pallas_call | solution.py:248
  31.7 2.2 %collective-permute-done.9.refs_1_ = f32[112,128]{1,0:T(8,128)S(1)} collective-permute-done((f32[112,128]{1,0:T(8,128)S(1)}, f32[112,128]{1,0:T(8,128)S(1)}, u32[]{:S(2)}, u32[]{:S(2)}) %collective-permute-start.9) | collective-permute-done | bytes 57376 | tf_op jit(solution)/shard_map/ppermute | solution.py:271
  33.8 0.5 collective-permute-start.13
  34.3 3.2 %collective-permute-start.11 = (f32[112,128]{1,0:T(8,128)S(1)}, f32[112,128]{1,0:T(8,128)S(1)}, u32[]{:S(2)}, u32[]{:S(2)}) collective-permute-start(f32[112,128]{1,0:T(8,128)S(1)} %sum_two.1.refs_0_), channel_id=1, source_target_pairs={{0,32},{4,36},{8,40},{12,44},{16,48},{20,52},{24,56},{28,60},{32,0... | collective-permute-start | bytes 172040 | tf_op jit(solution)/shard_map/ppermute | solution.py:271
  37.5 2.2 %collective-permute-start.10 = (f32[32,1536]{1,0:T(8,128)S(1)}, f32[32,1536]{1,0:T(8,128)S(1)}, u32[]{:S(2)}, u32[]{:S(2)}) collective-permute-start(f32[32,1536]{1,0:T(8,128)S(1)} %get-tuple-element.54), channel_id=1, source_target_pairs={{0,3},{1,2},{2,1},{3,0},{4,7},{5,6},{6,5},{7,4},{8,11},{9,10},{10,... | collective-permute-start | bytes 589832 | tf_op jit(solution)/shard_map/ppermute | solution.py:288
  39.8 1.8 %back_inner.5.inner = f32[32,1024]{1,0:T(8,128)S(1)} custom-call(f32[864,1024]{1,0:T(8,128)S(1)} %back_terms.1.terms, s32[27,1024]{1,0:T(8,128)S(1)} %copy-done.3, f32[32,1024]{1,0:T(8,128)S(1)} %back_inner.4.refs_0_), custom_call_target="tpu_custom_call", output_to_operand_aliasing={{}: (2, {})} | custom-call | flops 2147483648 | bytes 3911680 | tf_op jit(solution)/shard_map/back_inner/pallas_call | solution.py:248
  41.6 1.7 %collective-permute-start.16 = (f32[112,128]{1,0:T(8,128)S(1)}, f32[112,128]{1,0:T(8,128)S(1)}, u32[]{:S(2)}, u32[]{:S(2)}) collective-permute-start(f32[112,128]{1,0:T(8,128)S(1)} %sum_four.3.refs_0_), channel_id=1, source_target_pairs={{0,24},{4,28},{8,16},{12,20},{16,8},{20,12},{24,0},{28,4},{32,56},... | collective-permute-start | bytes 172040 | tf_op jit(solution)/shard_map/ppermute | solution.py:271
  43.3 1.6 %collective-permute-start.14 = (f32[112,128]{1,0:T(8,128)S(1)}, f32[112,128]{1,0:T(8,128)S(1)}, u32[]{:S(2)}, u32[]{:S(2)}) collective-permute-start(f32[112,128]{1,0:T(8,128)S(1)} %sum_four.3.refs_0_), channel_id=1, source_target_pairs={{0,8},{4,12},{8,0},{12,4},{16,24},{20,28},{24,16},{28,20},{32,40},... | collective-permute-start | bytes 172040 | tf_op jit(solution)/shard_map/ppermute | solution.py:271
  45.0 2.4 %edge.1 = (bf16[32,1024]{1,0:T(8,128)(2,1)}, bf16[32,1024]{1,0:T(8,128)(2,1)}) custom-call(f32[864,1024]{1,0:T(8,128)S(1)} %back_terms.1.terms, s32[27,1024]{1,0:T(8,128)S(1)} %copy-done.3, bf16[864,128]{1,0:T(8,128)(2,1)S(1)} %bitcast.4, bf16[64,128]{1,0:T(8,128)(2,1)S(1)} %collective-permute-done.near_ref, ...), custom_call_target="tpu_custom_call" | custom-call | flops 2147483648 | bytes 4788224 | tf_op jit(solution)/shard_map/edge/pallas_call | solution.py:248
  47.4 0.5 collective-permute-done.15.refs_2_
  47.9 5.8 %collective-permute-start.17 = (f32[448,128]{1,0:T(8,128)S(1)}, f32[448,128]{1,0:T(8,128)S(1)}, u32[]{:S(2)}, u32[]{:S(2)}) collective-permute-start(f32[448,128]{1,0:T(8,128)S(1)} %join.3.even_ref), channel_id=1, source_target_pairs={{0,4},{4,0},{8,12},{12,8},{16,20},{20,16},{24,28},{28,24},{32,36},... | collective-permute-start | bytes 688136 | tf_op jit(solution)/shard_map/ppermute | solution.py:271
  53.7 1.1 %collective-permute-done.17.odd_ref = f32[448,128]{1,0:T(8,128)S(1)} collective-permute-done((f32[448,128]{1,0:T(8,128)S(1)}, f32[448,128]{1,0:T(8,128)S(1)}, u32[]{:S(2)}, u32[]{:S(2)}) %collective-permute-start.17) | collective-permute-done | bytes 229408 | tf_op jit(solution)/shard_map/ppermute | solution.py:271
  54.9 0.8 %place.1 = f32[864,128]{1,0:T(8,128)} custom-call(f32[448,128]{1,0:T(8,128)S(1)} %join.3.even_ref, f32[448,128]{1,0:T(8,128)S(1)} %collective-permute-done.17.odd_ref), custom_call_target="tpu_custom_call" | custom-call | bytes 901120 | tf_op jit(solution)/shard_map/place/pallas_call | solution.py:248
  (31 shorter events, 0.2 us)
Async XLA Ops:
  0.6 6.2 %collective-permute-start.2 = (bf16[32,1024]{1,0:T(8,128)(2,1)}, bf16[32,1024]{1,0:T(8,128)(2,1)S(1)}, u32[]{:S(2)}, u32[]{:S(2)}) collective-permute-start(bf16[32,1024]{1,0:T(8,128)(2,1)} %refs_0_.1), channel_id=1, source_target_pairs={{0,1},{1,0},{2,3},{3,2},{4,5},{5,4},{6,7},{7,6},{8,9},{9,8},{10,11... | collective-permute-start | bytes 196616 | tf_op jit(solution)/shard_map/ppermute | solution.py:288
  2.8 0.9 %copy-start.1 = (bf16[32,1024]{1,0:T(8,128)(2,1)S(1)}, bf16[32,1024]{1,0:T(8,128)(2,1)}, u32[]{:S(2)}) copy-start(bf16[32,1024]{1,0:T(8,128)(2,1)} %refs_0_.1) | copy-start | bytes 196612
  3.7 0.8 %copy-start.4 = (bf16[32,1024]{1,0:T(8,128)(2,1)S(1)}, bf16[32,1024]{1,0:T(8,128)(2,1)}, u32[]{:S(2)}) copy-start(bf16[32,1024]{1,0:T(8,128)(2,1)} %x_ref.3) | copy-start | bytes 196612
  4.6 2.3 %copy-start.2 = (bf16[32,1024]{1,0:T(8,128)(2,1)S(1)}, bf16[32,1024]{1,0:T(8,128)(2,1)}, u32[]{:S(2)}) copy-start(bf16[32,1024]{1,0:T(8,128)(2,1)} %refs_0_.1) | copy-start | bytes 196612
  4.6 4.3 %copy-start.3 = (s32[27,1024]{1,0:T(8,128)S(1)}, s32[27,1024]{1,0:T(8,128)}, u32[]{:S(2)}) copy-start(s32[27,1024]{1,0:T(8,128)} %rule_ref.11) | copy-start | bytes 331780
  4.6 8.1 %collective-permute-start = (bf16[64,128]{1,0:T(8,128)(2,1)S(1)}, bf16[64,128]{1,0:T(8,128)(2,1)S(1)}, u32[]{:S(2)}, u32[]{:S(2)}) collective-permute-start(bf16[64,128]{1,0:T(8,128)(2,1)S(1)} %get-tuple-element.33), channel_id=1, source_target_pairs={{0,4},{4,0},{8,12},{12,8},{16,20},{20,16},{24,28},{28,24},{32,36},... | collective-permute-start | bytes 49160 | tf_op jit(solution)/shard_map/ppermute | solution.py:271
  5.8 6.9 %collective-permute-start.1 = (bf16[64,128]{1,0:T(8,128)(2,1)S(1)}, bf16[64,128]{1,0:T(8,128)(2,1)S(1)}, u32[]{:S(2)}, u32[]{:S(2)}) collective-permute-start(bf16[64,128]{1,0:T(8,128)(2,1)S(1)} %get-tuple-element.34), channel_id=1, source_target_pairs={{0,252},{4,8},{8,4},{12,16},{16,12},{20,24},{24,20},{28,32},{32,28... | collective-permute-start | bytes 49160 | tf_op jit(solution)/shard_map/ppermute | solution.py:277
  6.8 5.9 %collective-permute-start.3 = (bf16[64,1024]{1,0:T(8,128)(2,1)S(1)}, bf16[64,1024]{1,0:T(8,128)(2,1)S(1)}, u32[]{:S(2)}, u32[]{:S(2)}) collective-permute-start(bf16[64,1024]{1,0:T(8,128)(2,1)S(1)} %join.2.pair_ref), channel_id=1, source_target_pairs={{0,3},{1,2},{2,1},{3,0},{4,7},{5,6},{6,5},{7,4},{8,11},{9,10},{10,... | collective-permute-start | bytes 393224 | tf_op jit(solution)/shard_map/ppermute | solution.py:288
  12.7 8.2 %copy-start = (bf16[27,32,128]{2,1,0:T(8,128)(2,1)S(1)}, bf16[27,32,128]{2,1,0:T(8,128)(2,1)}, u32[]{:S(2)}) copy-start(bf16[27,32,128]{2,1,0:T(8,128)(2,1)} %param.5) | copy-start | bytes 663556
  13.5 8.5 %collective-permute-start.4 = (f32[448,128]{1,0:T(8,128)S(1)}, f32[448,128]{1,0:T(8,128)S(1)}, u32[]{:S(2)}, u32[]{:S(2)}) collective-permute-start(f32[448,128]{1,0:T(8,128)S(1)} %get-tuple-element.40), channel_id=1, source_target_pairs={{0,4},{4,0},{8,12},{12,8},{16,20},{20,16},{24,28},{28,24},{32,36},... | collective-permute-start | bytes 688136 | tf_op jit(solution)/shard_map/ppermute | solution.py:271
  22.0 5.2 %collective-permute-start.6 = (f32[112,128]{1,0:T(8,128)S(1)}, f32[112,128]{1,0:T(8,128)S(1)}, u32[]{:S(2)}, u32[]{:S(2)}) collective-permute-start(f32[112,128]{1,0:T(8,128)S(1)} %get-tuple-element.43), channel_id=1, source_target_pairs={{0,8},{4,12},{8,0},{12,4},{16,24},{20,28},{24,16},{28,20},{32,40},... | collective-permute-start | bytes 172040 | tf_op jit(solution)/shard_map/ppermute | solution.py:271
  22.1 5.1 %collective-permute-start.7 = (f32[112,128]{1,0:T(8,128)S(1)}, f32[112,128]{1,0:T(8,128)S(1)}, u32[]{:S(2)}, u32[]{:S(2)}) collective-permute-start(f32[112,128]{1,0:T(8,128)S(1)} %get-tuple-element.44), channel_id=1, source_target_pairs={{0,16},{4,20},{8,24},{12,28},{16,0},{20,4},{24,8},{28,12},{32,48},... | collective-permute-start | bytes 172040 | tf_op jit(solution)/shard_map/ppermute | solution.py:271
  22.2 6.3 %collective-permute-start.8 = (f32[112,128]{1,0:T(8,128)S(1)}, f32[112,128]{1,0:T(8,128)S(1)}, u32[]{:S(2)}, u32[]{:S(2)}) collective-permute-start(f32[112,128]{1,0:T(8,128)S(1)} %get-tuple-element.45), channel_id=1, source_target_pairs={{0,24},{4,28},{8,16},{12,20},{16,8},{20,12},{24,0},{28,4},{32,56},... | collective-permute-start | bytes 172040 | tf_op jit(solution)/shard_map/ppermute | solution.py:271
  26.0 11.5 %collective-permute-start.5 = (f32[64,1152]{1,0:T(8,128)S(1)}, f32[64,1152]{1,0:T(8,128)S(1)}, u32[]{:S(2)}, u32[]{:S(2)}) collective-permute-start(f32[64,1152]{1,0:T(8,128)S(1)} %get-tuple-element.46), channel_id=1, source_target_pairs={{0,1},{1,0},{2,3},{3,2},{4,5},{5,4},{6,7},{7,6},{8,9},{9,8},{10,11... | collective-permute-start | bytes 884744 | tf_op jit(solution)/shard_map/ppermute | solution.py:288
  28.6 5.2 %collective-permute-start.9 = (f32[112,128]{1,0:T(8,128)S(1)}, f32[112,128]{1,0:T(8,128)S(1)}, u32[]{:S(2)}, u32[]{:S(2)}) collective-permute-start(f32[112,128]{1,0:T(8,128)S(1)} %sum_four.2.refs_0_), channel_id=1, source_target_pairs={{0,192},{4,196},{8,200},{12,204},{16,208},{20,212},{24,216},{28,22... | collective-permute-start | bytes 172040 | tf_op jit(solution)/shard_map/ppermute | solution.py:271
  33.8 7.8 %collective-permute-start.13 = (f32[112,128]{1,0:T(8,128)S(1)}, f32[112,128]{1,0:T(8,128)S(1)}, u32[]{:S(2)}, u32[]{:S(2)}) collective-permute-start(f32[112,128]{1,0:T(8,128)S(1)} %sum_two.1.refs_0_), channel_id=1, source_target_pairs={{0,96},{4,100},{8,104},{12,108},{16,112},{20,116},{24,120},{28,124... | collective-permute-start | bytes 172040 | tf_op jit(solution)/shard_map/ppermute | solution.py:271
  34.3 7.3 %collective-permute-start.12 = (f32[112,128]{1,0:T(8,128)S(1)}, f32[112,128]{1,0:T(8,128)S(1)}, u32[]{:S(2)}, u32[]{:S(2)}) collective-permute-start(f32[112,128]{1,0:T(8,128)S(1)} %sum_two.1.refs_0_), channel_id=1, source_target_pairs={{0,64},{4,68},{8,72},{12,76},{16,80},{20,84},{24,88},{28,92},{32,9... | collective-permute-start | bytes 172040 | tf_op jit(solution)/shard_map/ppermute | solution.py:271
  34.3 7.3 %collective-permute-start.11 = (f32[112,128]{1,0:T(8,128)S(1)}, f32[112,128]{1,0:T(8,128)S(1)}, u32[]{:S(2)}, u32[]{:S(2)}) collective-permute-start(f32[112,128]{1,0:T(8,128)S(1)} %sum_two.1.refs_0_), channel_id=1, source_target_pairs={{0,32},{4,36},{8,40},{12,44},{16,48},{20,52},{24,56},{28,60},{32,0... | collective-permute-start | bytes 172040 | tf_op jit(solution)/shard_map/ppermute | solution.py:271
  37.5 7.5 %collective-permute-start.10 = (f32[32,1536]{1,0:T(8,128)S(1)}, f32[32,1536]{1,0:T(8,128)S(1)}, u32[]{:S(2)}, u32[]{:S(2)}) collective-permute-start(f32[32,1536]{1,0:T(8,128)S(1)} %get-tuple-element.54), channel_id=1, source_target_pairs={{0,3},{1,2},{2,1},{3,0},{4,7},{5,6},{6,5},{7,4},{8,11},{9,10},{10,... | collective-permute-start | bytes 589832 | tf_op jit(solution)/shard_map/ppermute | solution.py:288
  41.6 5.7 %collective-permute-start.16 = (f32[112,128]{1,0:T(8,128)S(1)}, f32[112,128]{1,0:T(8,128)S(1)}, u32[]{:S(2)}, u32[]{:S(2)}) collective-permute-start(f32[112,128]{1,0:T(8,128)S(1)} %sum_four.3.refs_0_), channel_id=1, source_target_pairs={{0,24},{4,28},{8,16},{12,20},{16,8},{20,12},{24,0},{28,4},{32,56},... | collective-permute-start | bytes 172040 | tf_op jit(solution)/shard_map/ppermute | solution.py:271
  43.3 4.5 %collective-permute-start.15 = (f32[112,128]{1,0:T(8,128)S(1)}, f32[112,128]{1,0:T(8,128)S(1)}, u32[]{:S(2)}, u32[]{:S(2)}) collective-permute-start(f32[112,128]{1,0:T(8,128)S(1)} %sum_four.3.refs_0_), channel_id=1, source_target_pairs={{0,16},{4,20},{8,24},{12,28},{16,0},{20,4},{24,8},{28,12},{32,48},... | collective-permute-start | bytes 172040 | tf_op jit(solution)/shard_map/ppermute | solution.py:271
  43.3 4.5 %collective-permute-start.14 = (f32[112,128]{1,0:T(8,128)S(1)}, f32[112,128]{1,0:T(8,128)S(1)}, u32[]{:S(2)}, u32[]{:S(2)}) collective-permute-start(f32[112,128]{1,0:T(8,128)S(1)} %sum_four.3.refs_0_), channel_id=1, source_target_pairs={{0,8},{4,12},{8,0},{12,4},{16,24},{20,28},{24,16},{28,20},{32,40},... | collective-permute-start | bytes 172040 | tf_op jit(solution)/shard_map/ppermute | solution.py:271
  47.9 7.0 %collective-permute-start.17 = (f32[448,128]{1,0:T(8,128)S(1)}, f32[448,128]{1,0:T(8,128)S(1)}, u32[]{:S(2)}, u32[]{:S(2)}) collective-permute-start(f32[448,128]{1,0:T(8,128)S(1)} %join.3.even_ref), channel_id=1, source_target_pairs={{0,4},{4,0},{8,12},{12,8},{16,20},{20,16},{24,28},{28,24},{32,36},... | collective-permute-start | bytes 688136 | tf_op jit(solution)/shard_map/ppermute | solution.py:271

commit v11 on v10

--- a/solution.py
+++ b/solution.py
@@ -12,7 +12,7 @@
 LANES = 128
 PART = 112
 INNER = tuple(range(2, 8))
-EDGE = (0, 1, 3)
+EDGE = (0, 1)
 ORDER = (0, 1, 3, 2)
 VMEM = pl.BlockSpec(memory_space=pltpu.VMEM)
 
@@ -288,9 +288,15 @@
         return lax.ppermute(value, "ch", [(i, i ^ mask) for i in range(4)])
 
     x, g, rules = features, grad_out, rulebook
-    near, far = call(
-        faces_kernel, (bf16(64, FACE),) * 2, (x, g), flops=1 << 30, name="faces"
-    )
+    cut = pl.BlockSpec((32, 2 * FACE), lambda i: (0, 0))
+    face = pl.BlockSpec((64, FACE), lambda i: (0, 0))
+    near, far = pl.pallas_call(
+        faces_kernel, out_shape=(bf16(64, FACE),) * 2, grid=(1,),
+        in_specs=[cut, cut], out_specs=(face, face),
+        compiler_params=pltpu.CompilerParams(vmem_limit_bytes=56 << 20),
+        cost_estimate=pl.CostEstimate(flops=1 << 30, bytes_accessed=1 << 16, transcendentals=0),
+        name="faces",
+    )(x, g)
     pair = call(join_kernel, bf16(64, VOX), (g, over_ch(g, 1)), name="join")
     near = swap(near, 1)
     far = swap_far(far)
@@ -328,22 +334,22 @@
     others = [swap(pieces[q], 2 * q) for q in (1, 2, 3)]
     first, = after((first,), *pieces)
     first = over_ch(first, 1)
-    inner = inner_part((2,))
+    inner = inner_part((2, 3))
     others = after(others, inner)
     total = call(sum_kernel, f32(PART, 128), (pieces[0], *others), name="sum_four")
     came = swap(total, 48)
     inner = inner_part((4, 5), inner)
-    came, = after((came,), inner)
-    total = call(sum_kernel, f32(PART, 128), (total, came), name="sum_two")
-    others = [swap(total, m) for m in (8, 16, 24)]
-    ours, first = after((ours, first), total)
+    ours, first = after((ours, first), inner)
     own, second = call(
         middle_kernel, (f32(32, VOX), f32(32, VOX + 4 * FACE)), (ours, first, near, far),
         name="middle",
     )
     second = over_ch(second, 3)
+    came, = after((came,), own)
+    total = call(sum_kernel, f32(PART, 128), (total, came), name="sum_two")
+    others = [swap(total, m) for m in (8, 16, 24)]
     inner = inner_part((6, 7), inner)
-    others = after(others, inner, own)
+    others = after(others, inner)
     total = call(sum_kernel, f32(PART, 128), (total, *others), name="sum_four")
     others = [swap(total, 2 * q) for q in (1, 2, 3)]
     output, grad_features = call(

time: 55.9 us -> 55.1 us (0.986)
  local copies, waits for them, and re-layouts: 1.73 us -> 0.02 us
  Pallas kernels: 13.6 us -> 15 us
    unnamed x10 -> x8, local copies, waits for them, and re-layouts: 1.73 us -> 0.02 us
    ppermute x13, waiting for transfers between devices: 5.11 us -> 3.44 us  [swap(): return lax.ppermute(value, 'blk', [(i, i ^ mask) for i in range(count)])]
    pallas_call x0 -> x1, Pallas kernels: none -> 1.37 us  [per_device(): pl.pallas_call(faces_kernel, out_shape=(bf16(64, FACE),) * 2, grid=(1,),...]
    ppermute x4, waiting for transfers between devices: 0.01 us -> 1.2 us  [over_ch(): return lax.ppermute(value, 'ch', [(i, i ^ mask) for i in range(4)])]
    pallas_call x17 -> x16, Pallas kernels: 13.6 us -> 13.7 us  [call(): pl.pallas_call(kernel, out_shape=outs, in_specs=[VMEM] * len(args), out_s...]
  transfers between devices with their start and end apart: 18 -> 18, of which waited for: 4 -> 5; matrix products, arithmetic and copies ran while one was open for 0% -> 0% of each run, Pallas kernels for 22% -> 25%
where the time goes in v11:
time: 55.1 us; the launch traced here: 54.9 us
  starting transfers between devices  34.4 us (62%)
  Pallas kernels  15 us (27%)
  waiting for transfers between devices  4.64 us (8%)
  between operations  0.81 us (1%)
    ppermute x13, starting transfers between devices, swap(): return lax.ppermute(value, 'blk', [(i, i ^ mask) for i in range(count)])  27 us
    pallas_call x16, Pallas kernels, call(): pl.pallas_call(kernel, out_shape=outs, in_specs=[VMEM] * len(args), out_s...  13.7 us
    ppermute x4, starting transfers between devices, over_ch(): return lax.ppermute(value, 'ch', [(i, i ^ mask) for i in range(4)])  6.42 us
    ppermute x13, waiting for transfers between devices, swap(): return lax.ppermute(value, 'blk', [(i, i ^ mask) for i in range(count)])  3.44 us
    pallas_call x1, Pallas kernels, per_device(): pl.pallas_call(faces_kernel, out_shape=(bf16(64, FACE),) * 2, grid=(1,),...  1.37 us
    ppermute x4, waiting for transfers between devices, over_ch(): return lax.ppermute(value, 'ch', [(i, i ^ mask) for i in range(4)])  1.2 us
  transfers between devices with their start and end apart: 18, of which 5 were waited for; matrix products, arithmetic and copies ran while one was open for 0% of the time, Pallas kernels for 25%

profile of v11, /device:TPU:1, one launch (start us, length us, event | category | flops | bytes accessed | tf_op | source)
XLA Modules:
  0.0 54.9 jit_solution(197396515764198416)
XLA Ops:
  0.7 2.2 %collective-permute-start.2 = (bf16[32,1024]{1,0:T(8,128)(2,1)}, bf16[32,1024]{1,0:T(8,128)(2,1)S(1)}, u32[]{:S(2)}, u32[]{:S(2)}) collective-permute-start(bf16[32,1024]{1,0:T(8,128)(2,1)} %refs_0_.1), channel_id=1, source_target_pairs={{0,1},{1,0},{2,3},{3,2},{4,5},{5,4},{6,7},{7,6},{8,9},{9,8},{10,11... | collective-permute-start | bytes 196616 | tf_op jit(solution)/shard_map/ppermute | solution.py:288
  2.9 1.4 %faces.1 = (bf16[64,128]{1,0:T(8,128)(2,1)}, bf16[64,128]{1,0:T(8,128)(2,1)}) custom-call(bf16[32,1024]{1,0:T(8,128)(2,1)} %x_ref.3, bf16[32,1024]{1,0:T(8,128)(2,1)} %refs_0_.1), custom_call_target="tpu_custom_call" | custom-call | flops 1073741824 | bytes 65536 | tf_op jit(solution)/shard_map/faces/pallas_call | solution.py:293
  4.2 1.1 %collective-permute-start = (bf16[64,128]{1,0:T(8,128)(2,1)}, bf16[64,128]{1,0:T(8,128)(2,1)S(1)}, u32[]{:S(2)}, u32[]{:S(2)}) collective-permute-start(bf16[64,128]{1,0:T(8,128)(2,1)} %get-tuple-element.33), channel_id=1, source_target_pairs={{0,4},{4,0},{8,12},{12,8},{16,20},{20,16},{24,28},{28,24},{32,36},... | collective-permute-start | bytes 49160 | tf_op jit(solution)/shard_map/ppermute | solution.py:271
  5.4 0.9 %collective-permute-start.1 = (bf16[64,128]{1,0:T(8,128)(2,1)}, bf16[64,128]{1,0:T(8,128)(2,1)S(1)}, u32[]{:S(2)}, u32[]{:S(2)}) collective-permute-start(bf16[64,128]{1,0:T(8,128)(2,1)} %get-tuple-element.34), channel_id=1, source_target_pairs={{0,252},{4,8},{8,4},{12,16},{16,12},{20,24},{24,20},{28,32},{32,28... | collective-permute-start | bytes 49160 | tf_op jit(solution)/shard_map/ppermute | solution.py:277
  6.3 2.0 %collective-permute-start.3 = (bf16[64,1024]{1,0:T(8,128)(2,1)S(1)}, bf16[64,1024]{1,0:T(8,128)(2,1)S(1)}, u32[]{:S(2)}, u32[]{:S(2)}) collective-permute-start(bf16[64,1024]{1,0:T(8,128)(2,1)S(1)} %join.2.pair_ref), channel_id=1, source_target_pairs={{0,3},{1,2},{2,1},{3,0},{4,7},{5,6},{6,5},{7,4},{8,11},{9,10},{10,... | collective-permute-start | bytes 393224 | tf_op jit(solution)/shard_map/ppermute | solution.py:288
  8.3 3.9 %gather.1.dense_in = bf16[864,1024]{1,0:T(8,128)(2,1)S(1)} custom-call(bf16[32,1024]{1,0:T(8,128)(2,1)S(1)} %copy-done.3, s32[27,1024]{1,0:T(8,128)S(1)} %copy-done.2), custom_call_target="tpu_custom_call" | custom-call | flops 3221225472 | bytes 1945600 | tf_op jit(solution)/shard_map/gather/pallas_call | solution.py:248
  12.2 0.0 copy-start
  12.2 0.7 %weight_terms.1 = (bf16[864,1024]{1,0:T(8,128)(2,1)S(1)}, bf16[128,1024]{1,0:T(8,128)(2,1)S(1)}, f32[448,128]{1,0:T(8,128)S(1)}, f32[448,128]{1,0:T(8,128)S(1)}) custom-call(bf16[864,1024]{1,0:T(8,128)(2,1)S(1)} %gather.1.dense_in, s32[27,1024]{1,0:T(8,128)S(1)} %copy-done.2, ...), custom_call_target="tpu_custom_call", output_to_operand_aliasing={{0}: (0, {})} | custom-call | flops 1073741824 | bytes 4665344 | tf_op jit(solution)/shard_map/weight_terms/pallas_call | solution.py:248
  12.9 7.5 %collective-permute-start.4 = (f32[448,128]{1,0:T(8,128)S(1)}, f32[448,128]{1,0:T(8,128)S(1)}, u32[]{:S(2)}, u32[]{:S(2)}) collective-permute-start(f32[448,128]{1,0:T(8,128)S(1)} %get-tuple-element.40), channel_id=1, source_target_pairs={{0,4},{4,0},{8,12},{12,8},{16,20},{20,16},{24,28},{28,24},{32,36},... | collective-permute-start | bytes 688136 | tf_op jit(solution)/shard_map/ppermute | solution.py:271
  20.5 0.6 %back_terms.1.terms = f32[864,1024]{1,0:T(8,128)S(1)} custom-call(bf16[864,128]{1,0:T(8,128)(2,1)S(1)} %bitcast.2, bf16[128,1024]{1,0:T(8,128)(2,1)S(1)} %get-tuple-element.35.grad_ref), custom_call_target="tpu_custom_call" | custom-call | flops 1073741824 | bytes 4022272 | tf_op jit(solution)/shard_map/back_terms/pallas_call | solution.py:248
  21.1 0.5 forward.1
  21.6 0.1 collective-permute-start.7
  21.7 0.1 collective-permute-start.8
  21.8 3.7 %collective-permute-start.9 = (f32[112,128]{1,0:T(8,128)S(1)}, f32[112,128]{1,0:T(8,128)S(1)}, u32[]{:S(2)}, u32[]{:S(2)}) collective-permute-start(f32[112,128]{1,0:T(8,128)S(1)} %get-tuple-element.45), channel_id=1, source_target_pairs={{0,24},{4,28},{8,16},{12,20},{16,8},{20,12},{24,0},{28,4},{32,56},... | collective-permute-start | bytes 172040 | tf_op jit(solution)/shard_map/ppermute | solution.py:271
  25.6 0.3 collective-permute-start.5
  25.9 1.8 %back_inner.3.refs_0_ = f32[32,1024]{1,0:T(8,128)S(1)} custom-call(f32[864,1024]{1,0:T(8,128)S(1)} %back_terms.1.terms, s32[27,1024]{1,0:T(8,128)S(1)} %copy-done.2), custom_call_target="tpu_custom_call" | custom-call | flops 2147483648 | bytes 3780608 | tf_op jit(solution)/shard_map/back_inner/pallas_call | solution.py:248
  27.7 0.4 collective-permute-done.9.refs_3_
  28.2 1.7 %collective-permute-start.10 = (f32[112,128]{1,0:T(8,128)S(1)}, f32[112,128]{1,0:T(8,128)S(1)}, u32[]{:S(2)}, u32[]{:S(2)}) collective-permute-start(f32[112,128]{1,0:T(8,128)S(1)} %sum_four.2.refs_0_), channel_id=1, source_target_pairs={{0,192},{4,196},{8,200},{12,204},{16,208},{20,212},{24,216},{28,22... | collective-permute-start | bytes 172040 | tf_op jit(solution)/shard_map/ppermute | solution.py:271
  29.8 1.8 %back_inner.4.refs_0_ = f32[32,1024]{1,0:T(8,128)S(1)} custom-call(f32[864,1024]{1,0:T(8,128)S(1)} %back_terms.1.terms, s32[27,1024]{1,0:T(8,128)S(1)} %copy-done.2, f32[32,1024]{1,0:T(8,128)S(1)} %back_inner.3.refs_0_), custom_call_target="tpu_custom_call", output_to_operand_aliasing={{}: (2, {})} | custom-call | flops 2147483648 | bytes 3911680 | tf_op jit(solution)/shard_map/back_inner/pallas_call | solution.py:248
  31.7 1.2 %collective-permute-done.5.came_ref.first_ref = f32[64,1152]{1,0:T(8,128)S(1)} collective-permute-done((f32[64,1152]{1,0:T(8,128)S(1)}, f32[64,1152]{1,0:T(8,128)S(1)}, u32[]{:S(2)}, u32[]{:S(2)}) %collective-permute-start.5) | collective-permute-done | bytes 294944 | tf_op jit(solution)/shard_map/ppermute | solution.py:288
  32.9 0.6 %collective-permute-done.10.refs_1_ = f32[112,128]{1,0:T(8,128)S(1)} collective-permute-done((f32[112,128]{1,0:T(8,128)S(1)}, f32[112,128]{1,0:T(8,128)S(1)}, u32[]{:S(2)}, u32[]{:S(2)}) %collective-permute-start.10) | collective-permute-done | bytes 57376 | tf_op jit(solution)/shard_map/ppermute | solution.py:271
  33.5 0.3 collective-permute-start.13
  33.8 3.4 %collective-permute-start.11 = (f32[112,128]{1,0:T(8,128)S(1)}, f32[112,128]{1,0:T(8,128)S(1)}, u32[]{:S(2)}, u32[]{:S(2)}) collective-permute-start(f32[112,128]{1,0:T(8,128)S(1)} %sum_two.1.refs_0_), channel_id=1, source_target_pairs={{0,32},{4,36},{8,40},{12,44},{16,48},{20,52},{24,56},{28,60},{32,0... | collective-permute-start | bytes 172040 | tf_op jit(solution)/shard_map/ppermute | solution.py:271
  37.2 1.9 %collective-permute-start.6 = (f32[32,1536]{1,0:T(8,128)S(1)}, f32[32,1536]{1,0:T(8,128)S(1)}, u32[]{:S(2)}, u32[]{:S(2)}) collective-permute-start(f32[32,1536]{1,0:T(8,128)S(1)} %get-tuple-element.50), channel_id=1, source_target_pairs={{0,3},{1,2},{2,1},{3,0},{4,7},{5,6},{6,5},{7,4},{8,11},{9,10},{10,... | collective-permute-start | bytes 589832 | tf_op jit(solution)/shard_map/ppermute | solution.py:288
  39.1 1.8 %back_inner.5.inner = f32[32,1024]{1,0:T(8,128)S(1)} custom-call(f32[864,1024]{1,0:T(8,128)S(1)} %back_terms.1.terms, s32[27,1024]{1,0:T(8,128)S(1)} %copy-done.2, f32[32,1024]{1,0:T(8,128)S(1)} %back_inner.4.refs_0_), custom_call_target="tpu_custom_call", output_to_operand_aliasing={{}: (2, {})} | custom-call | flops 2147483648 | bytes 3911680 | tf_op jit(solution)/shard_map/back_inner/pallas_call | solution.py:248
  41.0 1.6 %collective-permute-start.16 = (f32[112,128]{1,0:T(8,128)S(1)}, f32[112,128]{1,0:T(8,128)S(1)}, u32[]{:S(2)}, u32[]{:S(2)}) collective-permute-start(f32[112,128]{1,0:T(8,128)S(1)} %sum_four.3.refs_0_), channel_id=1, source_target_pairs={{0,24},{4,28},{8,16},{12,20},{16,8},{20,12},{24,0},{28,4},{32,56},... | collective-permute-start | bytes 172040 | tf_op jit(solution)/shard_map/ppermute | solution.py:271
  42.6 1.7 %collective-permute-start.14 = (f32[112,128]{1,0:T(8,128)S(1)}, f32[112,128]{1,0:T(8,128)S(1)}, u32[]{:S(2)}, u32[]{:S(2)}) collective-permute-start(f32[112,128]{1,0:T(8,128)S(1)} %sum_four.3.refs_0_), channel_id=1, source_target_pairs={{0,8},{4,12},{8,0},{12,4},{16,24},{20,28},{24,16},{28,20},{32,40},... | collective-permute-start | bytes 172040 | tf_op jit(solution)/shard_map/ppermute | solution.py:271
  44.3 1.5 %edge.1 = (bf16[32,1024]{1,0:T(8,128)(2,1)}, bf16[32,1024]{1,0:T(8,128)(2,1)}) custom-call(f32[864,1024]{1,0:T(8,128)S(1)} %back_terms.1.terms, s32[27,1024]{1,0:T(8,128)S(1)} %copy-done.2, bf16[864,128]{1,0:T(8,128)(2,1)S(1)} %bitcast.4, bf16[64,128]{1,0:T(8,128)(2,1)S(1)} %collective-permute-done.near_ref, ...), custom_call_target="tpu_custom_call" | custom-call | flops 2147483648 | bytes 4788224 | tf_op jit(solution)/shard_map/edge/pallas_call | solution.py:248
  45.8 1.3 %collective-permute-done.15.refs_2_ = f32[112,128]{1,0:T(8,128)S(1)} collective-permute-done((f32[112,128]{1,0:T(8,128)S(1)}, f32[112,128]{1,0:T(8,128)S(1)}, u32[]{:S(2)}, u32[]{:S(2)}) %collective-permute-start.15) | collective-permute-done | bytes 57376 | tf_op jit(solution)/shard_map/ppermute | solution.py:271
  47.2 5.8 %collective-permute-start.17 = (f32[448,128]{1,0:T(8,128)S(1)}, f32[448,128]{1,0:T(8,128)S(1)}, u32[]{:S(2)}, u32[]{:S(2)}) collective-permute-start(f32[448,128]{1,0:T(8,128)S(1)} %join.3.even_ref), channel_id=1, source_target_pairs={{0,4},{4,0},{8,12},{12,8},{16,20},{20,16},{24,28},{28,24},{32,36},... | collective-permute-start | bytes 688136 | tf_op jit(solution)/shard_map/ppermute | solution.py:271
  53.0 1.1 %collective-permute-done.17.odd_ref = f32[448,128]{1,0:T(8,128)S(1)} collective-permute-done((f32[448,128]{1,0:T(8,128)S(1)}, f32[448,128]{1,0:T(8,128)S(1)}, u32[]{:S(2)}, u32[]{:S(2)}) %collective-permute-start.17) | collective-permute-done | bytes 229408 | tf_op jit(solution)/shard_map/ppermute | solution.py:271
  54.1 0.8 %place.1 = f32[864,128]{1,0:T(8,128)} custom-call(f32[448,128]{1,0:T(8,128)S(1)} %join.3.even_ref, f32[448,128]{1,0:T(8,128)S(1)} %collective-permute-done.17.odd_ref), custom_call_target="tpu_custom_call" | custom-call | bytes 901120 | tf_op jit(solution)/shard_map/place/pallas_call | solution.py:248
  (29 shorter events, 0.2 us)
Async XLA Ops:
  0.6 5.7 %copy-start.1 = (bf16[32,1024]{1,0:T(8,128)(2,1)S(1)}, bf16[32,1024]{1,0:T(8,128)(2,1)}, u32[]{:S(2)}) copy-start(bf16[32,1024]{1,0:T(8,128)(2,1)} %refs_0_.1) | copy-start | bytes 196612
  0.6 7.7 %copy-start.3 = (bf16[32,1024]{1,0:T(8,128)(2,1)S(1)}, bf16[32,1024]{1,0:T(8,128)(2,1)}, u32[]{:S(2)}) copy-start(bf16[32,1024]{1,0:T(8,128)(2,1)} %x_ref.3) | copy-start | bytes 196612
  0.7 7.7 %copy-start.2 = (s32[27,1024]{1,0:T(8,128)S(1)}, s32[27,1024]{1,0:T(8,128)}, u32[]{:S(2)}) copy-start(s32[27,1024]{1,0:T(8,128)} %rule_ref.11) | copy-start | bytes 331780
  0.7 5.6 %collective-permute-start.2 = (bf16[32,1024]{1,0:T(8,128)(2,1)}, bf16[32,1024]{1,0:T(8,128)(2,1)S(1)}, u32[]{:S(2)}, u32[]{:S(2)}) collective-permute-start(bf16[32,1024]{1,0:T(8,128)(2,1)} %refs_0_.1), channel_id=1, source_target_pairs={{0,1},{1,0},{2,3},{3,2},{4,5},{5,4},{6,7},{7,6},{8,9},{9,8},{10,11... | collective-permute-start | bytes 196616 | tf_op jit(solution)/shard_map/ppermute | solution.py:288
  4.2 7.9 %collective-permute-start = (bf16[64,128]{1,0:T(8,128)(2,1)}, bf16[64,128]{1,0:T(8,128)(2,1)S(1)}, u32[]{:S(2)}, u32[]{:S(2)}) collective-permute-start(bf16[64,128]{1,0:T(8,128)(2,1)} %get-tuple-element.33), channel_id=1, source_target_pairs={{0,4},{4,0},{8,12},{12,8},{16,20},{20,16},{24,28},{28,24},{32,36},... | collective-permute-start | bytes 49160 | tf_op jit(solution)/shard_map/ppermute | solution.py:271
  5.4 6.8 %collective-permute-start.1 = (bf16[64,128]{1,0:T(8,128)(2,1)}, bf16[64,128]{1,0:T(8,128)(2,1)S(1)}, u32[]{:S(2)}, u32[]{:S(2)}) collective-permute-start(bf16[64,128]{1,0:T(8,128)(2,1)} %get-tuple-element.34), channel_id=1, source_target_pairs={{0,252},{4,8},{8,4},{12,16},{16,12},{20,24},{24,20},{28,32},{32,28... | collective-permute-start | bytes 49160 | tf_op jit(solution)/shard_map/ppermute | solution.py:277
  6.3 5.9 %collective-permute-start.3 = (bf16[64,1024]{1,0:T(8,128)(2,1)S(1)}, bf16[64,1024]{1,0:T(8,128)(2,1)S(1)}, u32[]{:S(2)}, u32[]{:S(2)}) collective-permute-start(bf16[64,1024]{1,0:T(8,128)(2,1)S(1)} %join.2.pair_ref), channel_id=1, source_target_pairs={{0,3},{1,2},{2,1},{3,0},{4,7},{5,6},{6,5},{7,4},{8,11},{9,10},{10,... | collective-permute-start | bytes 393224 | tf_op jit(solution)/shard_map/ppermute | solution.py:288
  12.2 8.3 %copy-start = (bf16[27,32,128]{2,1,0:T(8,128)(2,1)S(1)}, bf16[27,32,128]{2,1,0:T(8,128)(2,1)}, u32[]{:S(2)}) copy-start(bf16[27,32,128]{2,1,0:T(8,128)(2,1)} %param.5) | copy-start | bytes 663556
  12.9 8.6 %collective-permute-start.4 = (f32[448,128]{1,0:T(8,128)S(1)}, f32[448,128]{1,0:T(8,128)S(1)}, u32[]{:S(2)}, u32[]{:S(2)}) collective-permute-start(f32[448,128]{1,0:T(8,128)S(1)} %get-tuple-element.40), channel_id=1, source_target_pairs={{0,4},{4,0},{8,12},{12,8},{16,20},{20,16},{24,28},{28,24},{32,36},... | collective-permute-start | bytes 688136 | tf_op jit(solution)/shard_map/ppermute | solution.py:271
  21.6 6.1 %collective-permute-start.7 = (f32[112,128]{1,0:T(8,128)S(1)}, f32[112,128]{1,0:T(8,128)S(1)}, u32[]{:S(2)}, u32[]{:S(2)}) collective-permute-start(f32[112,128]{1,0:T(8,128)S(1)} %get-tuple-element.43), channel_id=1, source_target_pairs={{0,8},{4,12},{8,0},{12,4},{16,24},{20,28},{24,16},{28,20},{32,40},... | collective-permute-start | bytes 172040 | tf_op jit(solution)/shard_map/ppermute | solution.py:271
  21.7 6.0 %collective-permute-start.8 = (f32[112,128]{1,0:T(8,128)S(1)}, f32[112,128]{1,0:T(8,128)S(1)}, u32[]{:S(2)}, u32[]{:S(2)}) collective-permute-start(f32[112,128]{1,0:T(8,128)S(1)} %get-tuple-element.44), channel_id=1, source_target_pairs={{0,16},{4,20},{8,24},{12,28},{16,0},{20,4},{24,8},{28,12},{32,48},... | collective-permute-start | bytes 172040 | tf_op jit(solution)/shard_map/ppermute | solution.py:271
  21.8 6.3 %collective-permute-start.9 = (f32[112,128]{1,0:T(8,128)S(1)}, f32[112,128]{1,0:T(8,128)S(1)}, u32[]{:S(2)}, u32[]{:S(2)}) collective-permute-start(f32[112,128]{1,0:T(8,128)S(1)} %get-tuple-element.45), channel_id=1, source_target_pairs={{0,24},{4,28},{8,16},{12,20},{16,8},{20,12},{24,0},{28,4},{32,56},... | collective-permute-start | bytes 172040 | tf_op jit(solution)/shard_map/ppermute | solution.py:271
  25.6 7.3 %collective-permute-start.5 = (f32[64,1152]{1,0:T(8,128)S(1)}, f32[64,1152]{1,0:T(8,128)S(1)}, u32[]{:S(2)}, u32[]{:S(2)}) collective-permute-start(f32[64,1152]{1,0:T(8,128)S(1)} %get-tuple-element.46), channel_id=1, source_target_pairs={{0,1},{1,0},{2,3},{3,2},{4,5},{5,4},{6,7},{7,6},{8,9},{9,8},{10,11... | collective-permute-start | bytes 884744 | tf_op jit(solution)/shard_map/ppermute | solution.py:288
  28.2 5.3 %collective-permute-start.10 = (f32[112,128]{1,0:T(8,128)S(1)}, f32[112,128]{1,0:T(8,128)S(1)}, u32[]{:S(2)}, u32[]{:S(2)}) collective-permute-start(f32[112,128]{1,0:T(8,128)S(1)} %sum_four.2.refs_0_), channel_id=1, source_target_pairs={{0,192},{4,196},{8,200},{12,204},{16,208},{20,212},{24,216},{28,22... | collective-permute-start | bytes 172040 | tf_op jit(solution)/shard_map/ppermute | solution.py:271
  33.5 7.4 %collective-permute-start.13 = (f32[112,128]{1,0:T(8,128)S(1)}, f32[112,128]{1,0:T(8,128)S(1)}, u32[]{:S(2)}, u32[]{:S(2)}) collective-permute-start(f32[112,128]{1,0:T(8,128)S(1)} %sum_two.1.refs_0_), channel_id=1, source_target_pairs={{0,96},{4,100},{8,104},{12,108},{16,112},{20,116},{24,120},{28,124... | collective-permute-start | bytes 172040 | tf_op jit(solution)/shard_map/ppermute | solution.py:271
  33.8 7.1 %collective-permute-start.12 = (f32[112,128]{1,0:T(8,128)S(1)}, f32[112,128]{1,0:T(8,128)S(1)}, u32[]{:S(2)}, u32[]{:S(2)}) collective-permute-start(f32[112,128]{1,0:T(8,128)S(1)} %sum_two.1.refs_0_), channel_id=1, source_target_pairs={{0,64},{4,68},{8,72},{12,76},{16,80},{20,84},{24,88},{28,92},{32,9... | collective-permute-start | bytes 172040 | tf_op jit(solution)/shard_map/ppermute | solution.py:271
  33.8 7.1 %collective-permute-start.11 = (f32[112,128]{1,0:T(8,128)S(1)}, f32[112,128]{1,0:T(8,128)S(1)}, u32[]{:S(2)}, u32[]{:S(2)}) collective-permute-start(f32[112,128]{1,0:T(8,128)S(1)} %sum_two.1.refs_0_), channel_id=1, source_target_pairs={{0,32},{4,36},{8,40},{12,44},{16,48},{20,52},{24,56},{28,60},{32,0... | collective-permute-start | bytes 172040 | tf_op jit(solution)/shard_map/ppermute | solution.py:271
  37.2 7.1 %collective-permute-start.6 = (f32[32,1536]{1,0:T(8,128)S(1)}, f32[32,1536]{1,0:T(8,128)S(1)}, u32[]{:S(2)}, u32[]{:S(2)}) collective-permute-start(f32[32,1536]{1,0:T(8,128)S(1)} %get-tuple-element.50), channel_id=1, source_target_pairs={{0,3},{1,2},{2,1},{3,0},{4,7},{5,6},{6,5},{7,4},{8,11},{9,10},{10,... | collective-permute-start | bytes 589832 | tf_op jit(solution)/shard_map/ppermute | solution.py:288
  41.0 4.9 %collective-permute-start.16 = (f32[112,128]{1,0:T(8,128)S(1)}, f32[112,128]{1,0:T(8,128)S(1)}, u32[]{:S(2)}, u32[]{:S(2)}) collective-permute-start(f32[112,128]{1,0:T(8,128)S(1)} %sum_four.3.refs_0_), channel_id=1, source_target_pairs={{0,24},{4,28},{8,16},{12,20},{16,8},{20,12},{24,0},{28,4},{32,56},... | collective-permute-start | bytes 172040 | tf_op jit(solution)/shard_map/ppermute | solution.py:271
  42.6 4.5 %collective-permute-start.15 = (f32[112,128]{1,0:T(8,128)S(1)}, f32[112,128]{1,0:T(8,128)S(1)}, u32[]{:S(2)}, u32[]{:S(2)}) collective-permute-start(f32[112,128]{1,0:T(8,128)S(1)} %sum_four.3.refs_0_), channel_id=1, source_target_pairs={{0,16},{4,20},{8,24},{12,28},{16,0},{20,4},{24,8},{28,12},{32,48},... | collective-permute-start | bytes 172040 | tf_op jit(solution)/shard_map/ppermute | solution.py:271
  42.6 4.5 %collective-permute-start.14 = (f32[112,128]{1,0:T(8,128)S(1)}, f32[112,128]{1,0:T(8,128)S(1)}, u32[]{:S(2)}, u32[]{:S(2)}) collective-permute-start(f32[112,128]{1,0:T(8,128)S(1)} %sum_four.3.refs_0_), channel_id=1, source_target_pairs={{0,8},{4,12},{8,0},{12,4},{16,24},{20,28},{24,16},{28,20},{32,40},... | collective-permute-start | bytes 172040 | tf_op jit(solution)/shard_map/ppermute | solution.py:271
  47.2 7.0 %collective-permute-start.17 = (f32[448,128]{1,0:T(8,128)S(1)}, f32[448,128]{1,0:T(8,128)S(1)}, u32[]{:S(2)}, u32[]{:S(2)}) collective-permute-start(f32[448,128]{1,0:T(8,128)S(1)} %join.3.even_ref), channel_id=1, source_target_pairs={{0,4},{4,0},{8,12},{12,8},{16,20},{20,16},{24,28},{28,24},{32,36},... | collective-permute-start | bytes 688136 | tf_op jit(solution)/shard_map/ppermute | solution.py:271

commit v12 on v11

--- a/solution.py
+++ b/solution.py
@@ -228,19 +228,38 @@
         refs[-1][size * q : size * (q + 1), :] = ref[...]
 
 
-def place_kernel(even_ref, odd_ref, out_ref):
+def place_kernel(*refs):
+    out_ref, sems = refs[-2:]
     spot = lax.axis_index("blk") & 7
     short = 864 - 7 * PART
-    for q in range(4):
-        for odd, ref in enumerate((even_ref, odd_ref)):
-            part = spot ^ (2 * q + odd)
-            start = pl.multiple_of(PART * part, 8)
-            out_ref[pl.ds(start, short), :] = ref[PART * q : PART * q + short, :]
-
-            @pl.when(part < 7)
-            def _():
-                rows = pl.ds(pl.multiple_of(start + short, 8), PART - short)
-                out_ref[rows, :] = ref[PART * q + short : PART * (q + 1), :]
+
+    def copies(r):
+        part = spot ^ r
+        start = pl.multiple_of(PART * part, 8)
+        head = pltpu.make_async_copy(
+            refs[r].at[pl.ds(0, short), :], out_ref.at[pl.ds(start, short), :], sems.at[r, 0]
+        )
+        rest = pl.ds(pl.multiple_of(start + short, 8), PART - short)
+        tail = pltpu.make_async_copy(
+            refs[r].at[pl.ds(short, PART - short), :], out_ref.at[rest, :], sems.at[r, 1]
+        )
+        return part, head, tail
+
+    for r in range(8):
+        part, head, tail = copies(r)
+        head.start()
+
+        @pl.when(part < 7)
+        def _():
+            tail.start()
+
+    for r in range(8):
+        part, head, tail = copies(r)
+        head.wait()
+
+        @pl.when(part < 7)
+        def _():
+            tail.wait()
 
 
 def call(kernel, outs, args, scratch=(), aliases=None, flops=0, name=None):
@@ -359,11 +378,15 @@
         flops=2 << 30, name="edge",
     )
     others = after(others, output)
-    even = call(join_kernel, f32(4 * PART, 128), (total, *others), name="join")
-    odd = swap(even, 1)
-    weight_grad = call(
-        place_kernel, f32(864, 128), (even, odd), name="place",
-    )
+    even = [total, *others]
+    odd = [swap(part, 1) for part in even]
+    parts = [part for pair in zip(even, odd) for part in pair]
+    weight_grad = pl.pallas_call(
+        place_kernel, out_shape=f32(864, 128), in_specs=[VMEM] * 8,
+        out_specs=pl.BlockSpec(memory_space=pltpu.HBM),
+        scratch_shapes=[pltpu.SemaphoreType.DMA((8, 2))],
+        compiler_params=pltpu.CompilerParams(vmem_limit_bytes=40 << 20), name="place",
+    )(*parts)
     return output, grad_features, weight_grad.reshape(27, 32, 128)
 
 

time: 55.1 us -> 55.5 us (level)
  starting transfers between devices: 34.4 us -> 36.1 us
  waiting for transfers between devices: 4.64 us -> 3.12 us
    ppermute x13 -> x16, starting transfers between devices: 27 us -> 28.8 us  [swap(): return lax.ppermute(value, 'blk', [(i, i ^ mask) for i in range(count)])]
    ppermute x13 -> x16, waiting for transfers between devices: 3.44 us -> 1.92 us  [swap(): return lax.ppermute(value, 'blk', [(i, i ^ mask) for i in range(count)])]
    pallas_call x0 -> x1, Pallas kernels: none -> 0.88 us  [per_device(): pl.pallas_call(place_kernel, out_shape=f32(864, 128), in_specs=[VMEM] * 8...]
    pallas_call x16 -> x14, Pallas kernels: 13.7 us -> 12.9 us  [call(): pl.pallas_call(kernel, out_shape=outs, in_specs=[VMEM] * len(args), out_s...]
  transfers between devices with their start and end apart: 18 -> 21, of which waited for: 5 -> 6; matrix products, arithmetic and copies ran while one was open for 0% -> 0% of each run, Pallas kernels for 25% -> 24%
where the time goes in v12:
time: 55.5 us; the launch traced here: 55.3 us
  starting transfers between devices  36.1 us (65%)
  Pallas kernels  15.1 us (27%)
  waiting for transfers between devices  3.12 us (6%)
  between operations  0.97 us (2%)
    ppermute x16, starting transfers between devices, swap(): return lax.ppermute(value, 'blk', [(i, i ^ mask) for i in range(count)])  28.8 us
    pallas_call x14, Pallas kernels, call(): pl.pallas_call(kernel, out_shape=outs, in_specs=[VMEM] * len(args), out_s...  12.9 us
    ppermute x4, starting transfers between devices, over_ch(): return lax.ppermute(value, 'ch', [(i, i ^ mask) for i in range(4)])  6.43 us
    ppermute x16, waiting for transfers between devices, swap(): return lax.ppermute(value, 'blk', [(i, i ^ mask) for i in range(count)])  1.92 us
    pallas_call x1, Pallas kernels, per_device(): pl.pallas_call(faces_kernel, out_shape=(bf16(64, FACE),) * 2, grid=(1,),...  1.37 us
    ppermute x4, waiting for transfers between devices, over_ch(): return lax.ppermute(value, 'ch', [(i, i ^ mask) for i in range(4)])  1.2 us
  transfers between devices with their start and end apart: 21, of which 6 were waited for; matrix products, arithmetic and copies ran while one was open for 0% of the time, Pallas kernels for 24%

profile of v12, /device:TPU:1, one launch (start us, length us, event | category | flops | bytes accessed | tf_op | source)
XLA Modules:
  0.0 55.3 jit_solution(1279430274083550323)
XLA Ops:
  0.7 2.2 %collective-permute-start.2 = (bf16[32,1024]{1,0:T(8,128)(2,1)}, bf16[32,1024]{1,0:T(8,128)(2,1)S(1)}, u32[]{:S(2)}, u32[]{:S(2)}) collective-permute-start(bf16[32,1024]{1,0:T(8,128)(2,1)} %refs_0_.1), channel_id=1, source_target_pairs={{0,1},{1,0},{2,3},{3,2},{4,5},{5,4},{6,7},{7,6},{8,9},{9,8},{10,11... | collective-permute-start | bytes 196616 | tf_op jit(solution)/shard_map/ppermute | solution.py:307
  2.9 1.4 %faces.1 = (bf16[64,128]{1,0:T(8,128)(2,1)}, bf16[64,128]{1,0:T(8,128)(2,1)}) custom-call(bf16[32,1024]{1,0:T(8,128)(2,1)} %x_ref.3, bf16[32,1024]{1,0:T(8,128)(2,1)} %refs_0_.1), custom_call_target="tpu_custom_call" | custom-call | flops 1073741824 | bytes 65536 | tf_op jit(solution)/shard_map/faces/pallas_call | solution.py:312
  4.2 1.1 %collective-permute-start = (bf16[64,128]{1,0:T(8,128)(2,1)}, bf16[64,128]{1,0:T(8,128)(2,1)S(1)}, u32[]{:S(2)}, u32[]{:S(2)}) collective-permute-start(bf16[64,128]{1,0:T(8,128)(2,1)} %get-tuple-element.33), channel_id=1, source_target_pairs={{0,4},{4,0},{8,12},{12,8},{16,20},{20,16},{24,28},{28,24},{32,36},... | collective-permute-start | bytes 49160 | tf_op jit(solution)/shard_map/ppermute | solution.py:290
  5.4 0.9 %collective-permute-start.1 = (bf16[64,128]{1,0:T(8,128)(2,1)}, bf16[64,128]{1,0:T(8,128)(2,1)S(1)}, u32[]{:S(2)}, u32[]{:S(2)}) collective-permute-start(bf16[64,128]{1,0:T(8,128)(2,1)} %get-tuple-element.34), channel_id=1, source_target_pairs={{0,252},{4,8},{8,4},{12,16},{16,12},{20,24},{24,20},{28,32},{32,28... | collective-permute-start | bytes 49160 | tf_op jit(solution)/shard_map/ppermute | solution.py:296
  6.3 2.0 %collective-permute-start.3 = (bf16[64,1024]{1,0:T(8,128)(2,1)S(1)}, bf16[64,1024]{1,0:T(8,128)(2,1)S(1)}, u32[]{:S(2)}, u32[]{:S(2)}) collective-permute-start(bf16[64,1024]{1,0:T(8,128)(2,1)S(1)} %join.1.pair_ref), channel_id=1, source_target_pairs={{0,3},{1,2},{2,1},{3,0},{4,7},{5,6},{6,5},{7,4},{8,11},{9,10},{10,... | collective-permute-start | bytes 393224 | tf_op jit(solution)/shard_map/ppermute | solution.py:307
  8.3 3.9 %gather.1.dense_in = bf16[864,1024]{1,0:T(8,128)(2,1)S(1)} custom-call(bf16[32,1024]{1,0:T(8,128)(2,1)S(1)} %copy-done.3, s32[27,1024]{1,0:T(8,128)S(1)} %copy-done.2), custom_call_target="tpu_custom_call" | custom-call | flops 3221225472 | bytes 1945600 | tf_op jit(solution)/shard_map/gather/pallas_call | solution.py:267
  12.2 0.7 %weight_terms.1 = (bf16[864,1024]{1,0:T(8,128)(2,1)S(1)}, bf16[128,1024]{1,0:T(8,128)(2,1)S(1)}, f32[448,128]{1,0:T(8,128)S(1)}, f32[448,128]{1,0:T(8,128)S(1)}) custom-call(bf16[864,1024]{1,0:T(8,128)(2,1)S(1)} %gather.1.dense_in, s32[27,1024]{1,0:T(8,128)S(1)} %copy-done.2, ...), custom_call_target="tpu_custom_call", output_to_operand_aliasing={{0}: (0, {})} | custom-call | flops 1073741824 | bytes 4665344 | tf_op jit(solution)/shard_map/weight_terms/pallas_call | solution.py:267
  12.9 7.5 %collective-permute-start.4 = (f32[448,128]{1,0:T(8,128)S(1)}, f32[448,128]{1,0:T(8,128)S(1)}, u32[]{:S(2)}, u32[]{:S(2)}) collective-permute-start(f32[448,128]{1,0:T(8,128)S(1)} %get-tuple-element.40), channel_id=1, source_target_pairs={{0,4},{4,0},{8,12},{12,8},{16,20},{20,16},{24,28},{28,24},{32,36},... | collective-permute-start | bytes 688136 | tf_op jit(solution)/shard_map/ppermute | solution.py:290
  20.5 0.6 %back_terms.1.terms = f32[864,1024]{1,0:T(8,128)S(1)} custom-call(bf16[864,128]{1,0:T(8,128)(2,1)S(1)} %bitcast.2, bf16[128,1024]{1,0:T(8,128)(2,1)S(1)} %get-tuple-element.35.grad_ref), custom_call_target="tpu_custom_call" | custom-call | flops 1073741824 | bytes 4022272 | tf_op jit(solution)/shard_map/back_terms/pallas_call | solution.py:267
  21.1 0.5 forward.1
  21.8 3.7 %collective-permute-start.9 = (f32[112,128]{1,0:T(8,128)S(1)}, f32[112,128]{1,0:T(8,128)S(1)}, u32[]{:S(2)}, u32[]{:S(2)}) collective-permute-start(f32[112,128]{1,0:T(8,128)S(1)} %get-tuple-element.45), channel_id=1, source_target_pairs={{0,24},{4,28},{8,16},{12,20},{16,8},{20,12},{24,0},{28,4},{32,56},... | collective-permute-start | bytes 172040 | tf_op jit(solution)/shard_map/ppermute | solution.py:290
  25.6 0.3 collective-permute-start.5
  25.9 1.8 %back_inner.3.refs_0_ = f32[32,1024]{1,0:T(8,128)S(1)} custom-call(f32[864,1024]{1,0:T(8,128)S(1)} %back_terms.1.terms, s32[27,1024]{1,0:T(8,128)S(1)} %copy-done.2), custom_call_target="tpu_custom_call" | custom-call | flops 2147483648 | bytes 3780608 | tf_op jit(solution)/shard_map/back_inner/pallas_call | solution.py:267
  27.7 0.4 collective-permute-done.9.refs_3_
  28.2 1.7 %collective-permute-start.10 = (f32[112,128]{1,0:T(8,128)S(1)}, f32[112,128]{1,0:T(8,128)S(1)}, u32[]{:S(2)}, u32[]{:S(2)}) collective-permute-start(f32[112,128]{1,0:T(8,128)S(1)} %sum_four.2.refs_0_), channel_id=1, source_target_pairs={{0,192},{4,196},{8,200},{12,204},{16,208},{20,212},{24,216},{28,22... | collective-permute-start | bytes 172040 | tf_op jit(solution)/shard_map/ppermute | solution.py:290
  29.8 1.8 %back_inner.4.refs_0_ = f32[32,1024]{1,0:T(8,128)S(1)} custom-call(f32[864,1024]{1,0:T(8,128)S(1)} %back_terms.1.terms, s32[27,1024]{1,0:T(8,128)S(1)} %copy-done.2, f32[32,1024]{1,0:T(8,128)S(1)} %back_inner.3.refs_0_), custom_call_target="tpu_custom_call", output_to_operand_aliasing={{}: (2, {})} | custom-call | flops 2147483648 | bytes 3911680 | tf_op jit(solution)/shard_map/back_inner/pallas_call | solution.py:267
  31.7 1.2 %collective-permute-done.5.came_ref.first_ref = f32[64,1152]{1,0:T(8,128)S(1)} collective-permute-done((f32[64,1152]{1,0:T(8,128)S(1)}, f32[64,1152]{1,0:T(8,128)S(1)}, u32[]{:S(2)}, u32[]{:S(2)}) %collective-permute-start.5) | collective-permute-done | bytes 294944 | tf_op jit(solution)/shard_map/ppermute | solution.py:307
  32.9 0.6 %collective-permute-done.10.refs_1_ = f32[112,128]{1,0:T(8,128)S(1)} collective-permute-done((f32[112,128]{1,0:T(8,128)S(1)}, f32[112,128]{1,0:T(8,128)S(1)}, u32[]{:S(2)}, u32[]{:S(2)}) %collective-permute-start.10) | collective-permute-done | bytes 57376 | tf_op jit(solution)/shard_map/ppermute | solution.py:290
  33.5 0.3 collective-permute-start.13
  33.8 3.4 %collective-permute-start.11 = (f32[112,128]{1,0:T(8,128)S(1)}, f32[112,128]{1,0:T(8,128)S(1)}, u32[]{:S(2)}, u32[]{:S(2)}) collective-permute-start(f32[112,128]{1,0:T(8,128)S(1)} %sum_two.1.refs_0_), channel_id=1, source_target_pairs={{0,32},{4,36},{8,40},{12,44},{16,48},{20,52},{24,56},{28,60},{32,0... | collective-permute-start | bytes 172040 | tf_op jit(solution)/shard_map/ppermute | solution.py:290
  37.2 1.9 %collective-permute-start.6 = (f32[32,1536]{1,0:T(8,128)S(1)}, f32[32,1536]{1,0:T(8,128)S(1)}, u32[]{:S(2)}, u32[]{:S(2)}) collective-permute-start(f32[32,1536]{1,0:T(8,128)S(1)} %get-tuple-element.50), channel_id=1, source_target_pairs={{0,3},{1,2},{2,1},{3,0},{4,7},{5,6},{6,5},{7,4},{8,11},{9,10},{10,... | collective-permute-start | bytes 589832 | tf_op jit(solution)/shard_map/ppermute | solution.py:307
  39.1 1.8 %back_inner.5.inner = f32[32,1024]{1,0:T(8,128)S(1)} custom-call(f32[864,1024]{1,0:T(8,128)S(1)} %back_terms.1.terms, s32[27,1024]{1,0:T(8,128)S(1)} %copy-done.2, f32[32,1024]{1,0:T(8,128)S(1)} %back_inner.4.refs_0_), custom_call_target="tpu_custom_call", output_to_operand_aliasing={{}: (2, {})} | custom-call | flops 2147483648 | bytes 3911680 | tf_op jit(solution)/shard_map/back_inner/pallas_call | solution.py:267
  41.0 1.6 %collective-permute-start.17 = (f32[112,128]{1,0:T(8,128)S(1)}, f32[112,128]{1,0:T(8,128)S(1)}, u32[]{:S(2)}, u32[]{:S(2)}) collective-permute-start(f32[112,128]{1,0:T(8,128)S(1)} %sum_four.3.refs_0_), channel_id=1, source_target_pairs={{0,24},{4,28},{8,16},{12,20},{16,8},{20,12},{24,0},{28,4},{32,56},... | collective-permute-start | bytes 172040 | tf_op jit(solution)/shard_map/ppermute | solution.py:290
  42.6 1.7 %collective-permute-start.15 = (f32[112,128]{1,0:T(8,128)S(1)}, f32[112,128]{1,0:T(8,128)S(1)}, u32[]{:S(2)}, u32[]{:S(2)}) collective-permute-start(f32[112,128]{1,0:T(8,128)S(1)} %sum_four.3.refs_0_), channel_id=1, source_target_pairs={{0,8},{4,12},{8,0},{12,4},{16,24},{20,28},{24,16},{28,20},{32,40},... | collective-permute-start | bytes 172040 | tf_op jit(solution)/shard_map/ppermute | solution.py:290
  44.3 3.9 %collective-permute-start.14 = (f32[112,128]{1,0:T(8,128)S(1)}, f32[112,128]{1,0:T(8,128)S(1)}, u32[]{:S(2)}, u32[]{:S(2)}) collective-permute-start(f32[112,128]{1,0:T(8,128)S(1)} %sum_four.3.refs_0_), channel_id=1, source_target_pairs={{0,4},{4,0},{8,12},{12,8},{16,20},{20,16},{24,28},{28,24},{32,36},... | collective-permute-start | bytes 172040 | tf_op jit(solution)/shard_map/ppermute | solution.py:290
  48.2 1.5 %edge.1 = (bf16[32,1024]{1,0:T(8,128)(2,1)}, bf16[32,1024]{1,0:T(8,128)(2,1)}) custom-call(f32[864,1024]{1,0:T(8,128)S(1)} %back_terms.1.terms, s32[27,1024]{1,0:T(8,128)S(1)} %copy-done.2, bf16[864,128]{1,0:T(8,128)(2,1)S(1)} %bitcast.4, bf16[64,128]{1,0:T(8,128)(2,1)S(1)} %collective-permute-done.near_ref, ...), custom_call_target="tpu_custom_call" | custom-call | flops 2147483648 | bytes 4788224 | tf_op jit(solution)/shard_map/edge/pallas_call | solution.py:267
  49.7 3.1 %collective-permute-start.18 = (f32[112,128]{1,0:T(8,128)S(1)}, f32[112,128]{1,0:T(8,128)S(1)}, u32[]{:S(2)}, u32[]{:S(2)}) collective-permute-start(f32[112,128]{1,0:T(8,128)S(1)} %collective-permute-done.15.refs_2_), channel_id=1, source_target_pairs={{0,4},{4,0},{8,12},{12,8},{16,20},{20,16},{24,28},{28,24},{32,36},... | collective-permute-start | bytes 172040 | tf_op jit(solution)/shard_map/ppermute | solution.py:290
  52.9 0.5 collective-permute-start.20
  53.4 0.4 collective-permute-done.18.refs_3_
  53.8 0.4 collective-permute-done.19.refs_5_
  54.1 0.2 collective-permute-done.20.refs_7_
  54.3 0.9 %place.1 = f32[864,128]{1,0:T(8,128)} custom-call(f32[112,128]{1,0:T(8,128)S(1)} %sum_four.3.refs_0_, f32[112,128]{1,0:T(8,128)S(1)} %collective-permute-done.14.refs_1_, f32[112,128]{1,0:T(8,128)S(1)} %collective-permute-done.15.refs_2_, f32[112,128]{1,0:T(8,128)S(1)} %collective-permute-done.18.refs_3_, f32[112,128]{1,0:T(8,128)S(1)} %collective-permute-done.16.refs_4_, ...), custom_call_target="tpu_custom_call" | custom-call | tf_op jit(solution)/shard_map/place/pallas_call | solution.py:384
  (34 shorter events, 0.4 us)
Async XLA Ops:
  0.6 5.7 %copy-start.1 = (bf16[32,1024]{1,0:T(8,128)(2,1)S(1)}, bf16[32,1024]{1,0:T(8,128)(2,1)}, u32[]{:S(2)}) copy-start(bf16[32,1024]{1,0:T(8,128)(2,1)} %refs_0_.1) | copy-start | bytes 196612
  0.6 7.7 %copy-start.3 = (bf16[32,1024]{1,0:T(8,128)(2,1)S(1)}, bf16[32,1024]{1,0:T(8,128)(2,1)}, u32[]{:S(2)}) copy-start(bf16[32,1024]{1,0:T(8,128)(2,1)} %x_ref.3) | copy-start | bytes 196612
  0.7 7.7 %copy-start.2 = (s32[27,1024]{1,0:T(8,128)S(1)}, s32[27,1024]{1,0:T(8,128)}, u32[]{:S(2)}) copy-start(s32[27,1024]{1,0:T(8,128)} %rule_ref.11) | copy-start | bytes 331780
  0.7 5.6 %collective-permute-start.2 = (bf16[32,1024]{1,0:T(8,128)(2,1)}, bf16[32,1024]{1,0:T(8,128)(2,1)S(1)}, u32[]{:S(2)}, u32[]{:S(2)}) collective-permute-start(bf16[32,1024]{1,0:T(8,128)(2,1)} %refs_0_.1), channel_id=1, source_target_pairs={{0,1},{1,0},{2,3},{3,2},{4,5},{5,4},{6,7},{7,6},{8,9},{9,8},{10,11... | collective-permute-start | bytes 196616 | tf_op jit(solution)/shard_map/ppermute | solution.py:307
  4.2 7.9 %collective-permute-start = (bf16[64,128]{1,0:T(8,128)(2,1)}, bf16[64,128]{1,0:T(8,128)(2,1)S(1)}, u32[]{:S(2)}, u32[]{:S(2)}) collective-permute-start(bf16[64,128]{1,0:T(8,128)(2,1)} %get-tuple-element.33), channel_id=1, source_target_pairs={{0,4},{4,0},{8,12},{12,8},{16,20},{20,16},{24,28},{28,24},{32,36},... | collective-permute-start | bytes 49160 | tf_op jit(solution)/shard_map/ppermute | solution.py:290
  5.4 6.8 %collective-permute-start.1 = (bf16[64,128]{1,0:T(8,128)(2,1)}, bf16[64,128]{1,0:T(8,128)(2,1)S(1)}, u32[]{:S(2)}, u32[]{:S(2)}) collective-permute-start(bf16[64,128]{1,0:T(8,128)(2,1)} %get-tuple-element.34), channel_id=1, source_target_pairs={{0,252},{4,8},{8,4},{12,16},{16,12},{20,24},{24,20},{28,32},{32,28... | collective-permute-start | bytes 49160 | tf_op jit(solution)/shard_map/ppermute | solution.py:296
  6.3 5.9 %collective-permute-start.3 = (bf16[64,1024]{1,0:T(8,128)(2,1)S(1)}, bf16[64,1024]{1,0:T(8,128)(2,1)S(1)}, u32[]{:S(2)}, u32[]{:S(2)}) collective-permute-start(bf16[64,1024]{1,0:T(8,128)(2,1)S(1)} %join.1.pair_ref), channel_id=1, source_target_pairs={{0,3},{1,2},{2,1},{3,0},{4,7},{5,6},{6,5},{7,4},{8,11},{9,10},{10,... | collective-permute-start | bytes 393224 | tf_op jit(solution)/shard_map/ppermute | solution.py:307
  12.2 8.3 %copy-start = (bf16[27,32,128]{2,1,0:T(8,128)(2,1)S(1)}, bf16[27,32,128]{2,1,0:T(8,128)(2,1)}, u32[]{:S(2)}) copy-start(bf16[27,32,128]{2,1,0:T(8,128)(2,1)} %param.5) | copy-start | bytes 663556
  12.9 8.6 %collective-permute-start.4 = (f32[448,128]{1,0:T(8,128)S(1)}, f32[448,128]{1,0:T(8,128)S(1)}, u32[]{:S(2)}, u32[]{:S(2)}) collective-permute-start(f32[448,128]{1,0:T(8,128)S(1)} %get-tuple-element.40), channel_id=1, source_target_pairs={{0,4},{4,0},{8,12},{12,8},{16,20},{20,16},{24,28},{28,24},{32,36},... | collective-permute-start | bytes 688136 | tf_op jit(solution)/shard_map/ppermute | solution.py:290
  21.6 6.1 %collective-permute-start.7 = (f32[112,128]{1,0:T(8,128)S(1)}, f32[112,128]{1,0:T(8,128)S(1)}, u32[]{:S(2)}, u32[]{:S(2)}) collective-permute-start(f32[112,128]{1,0:T(8,128)S(1)} %get-tuple-element.43), channel_id=1, source_target_pairs={{0,8},{4,12},{8,0},{12,4},{16,24},{20,28},{24,16},{28,20},{32,40},... | collective-permute-start | bytes 172040 | tf_op jit(solution)/shard_map/ppermute | solution.py:290
  21.7 6.0 %collective-permute-start.8 = (f32[112,128]{1,0:T(8,128)S(1)}, f32[112,128]{1,0:T(8,128)S(1)}, u32[]{:S(2)}, u32[]{:S(2)}) collective-permute-start(f32[112,128]{1,0:T(8,128)S(1)} %get-tuple-element.44), channel_id=1, source_target_pairs={{0,16},{4,20},{8,24},{12,28},{16,0},{20,4},{24,8},{28,12},{32,48},... | collective-permute-start | bytes 172040 | tf_op jit(solution)/shard_map/ppermute | solution.py:290
  21.8 6.3 %collective-permute-start.9 = (f32[112,128]{1,0:T(8,128)S(1)}, f32[112,128]{1,0:T(8,128)S(1)}, u32[]{:S(2)}, u32[]{:S(2)}) collective-permute-start(f32[112,128]{1,0:T(8,128)S(1)} %get-tuple-element.45), channel_id=1, source_target_pairs={{0,24},{4,28},{8,16},{12,20},{16,8},{20,12},{24,0},{28,4},{32,56},... | collective-permute-start | bytes 172040 | tf_op jit(solution)/shard_map/ppermute | solution.py:290
  25.6 7.3 %collective-permute-start.5 = (f32[64,1152]{1,0:T(8,128)S(1)}, f32[64,1152]{1,0:T(8,128)S(1)}, u32[]{:S(2)}, u32[]{:S(2)}) collective-permute-start(f32[64,1152]{1,0:T(8,128)S(1)} %get-tuple-element.46), channel_id=1, source_target_pairs={{0,1},{1,0},{2,3},{3,2},{4,5},{5,4},{6,7},{7,6},{8,9},{9,8},{10,11... | collective-permute-start | bytes 884744 | tf_op jit(solution)/shard_map/ppermute | solution.py:307
  28.2 5.3 %collective-permute-start.10 = (f32[112,128]{1,0:T(8,128)S(1)}, f32[112,128]{1,0:T(8,128)S(1)}, u32[]{:S(2)}, u32[]{:S(2)}) collective-permute-start(f32[112,128]{1,0:T(8,128)S(1)} %sum_four.2.refs_0_), channel_id=1, source_target_pairs={{0,192},{4,196},{8,200},{12,204},{16,208},{20,212},{24,216},{28,22... | collective-permute-start | bytes 172040 | tf_op jit(solution)/shard_map/ppermute | solution.py:290
  33.5 7.4 %collective-permute-start.13 = (f32[112,128]{1,0:T(8,128)S(1)}, f32[112,128]{1,0:T(8,128)S(1)}, u32[]{:S(2)}, u32[]{:S(2)}) collective-permute-start(f32[112,128]{1,0:T(8,128)S(1)} %sum_two.1.refs_0_), channel_id=1, source_target_pairs={{0,96},{4,100},{8,104},{12,108},{16,112},{20,116},{24,120},{28,124... | collective-permute-start | bytes 172040 | tf_op jit(solution)/shard_map/ppermute | solution.py:290
  33.8 7.1 %collective-permute-start.12 = (f32[112,128]{1,0:T(8,128)S(1)}, f32[112,128]{1,0:T(8,128)S(1)}, u32[]{:S(2)}, u32[]{:S(2)}) collective-permute-start(f32[112,128]{1,0:T(8,128)S(1)} %sum_two.1.refs_0_), channel_id=1, source_target_pairs={{0,64},{4,68},{8,72},{12,76},{16,80},{20,84},{24,88},{28,92},{32,9... | collective-permute-start | bytes 172040 | tf_op jit(solution)/shard_map/ppermute | solution.py:290
  33.8 7.1 %collective-permute-start.11 = (f32[112,128]{1,0:T(8,128)S(1)}, f32[112,128]{1,0:T(8,128)S(1)}, u32[]{:S(2)}, u32[]{:S(2)}) collective-permute-start(f32[112,128]{1,0:T(8,128)S(1)} %sum_two.1.refs_0_), channel_id=1, source_target_pairs={{0,32},{4,36},{8,40},{12,44},{16,48},{20,52},{24,56},{28,60},{32,0... | collective-permute-start | bytes 172040 | tf_op jit(solution)/shard_map/ppermute | solution.py:290
  37.2 11.0 %collective-permute-start.6 = (f32[32,1536]{1,0:T(8,128)S(1)}, f32[32,1536]{1,0:T(8,128)S(1)}, u32[]{:S(2)}, u32[]{:S(2)}) collective-permute-start(f32[32,1536]{1,0:T(8,128)S(1)} %get-tuple-element.50), channel_id=1, source_target_pairs={{0,3},{1,2},{2,1},{3,0},{4,7},{5,6},{6,5},{7,4},{8,11},{9,10},{10,... | collective-permute-start | bytes 589832 | tf_op jit(solution)/shard_map/ppermute | solution.py:307
  41.0 8.8 %collective-permute-start.17 = (f32[112,128]{1,0:T(8,128)S(1)}, f32[112,128]{1,0:T(8,128)S(1)}, u32[]{:S(2)}, u32[]{:S(2)}) collective-permute-start(f32[112,128]{1,0:T(8,128)S(1)} %sum_four.3.refs_0_), channel_id=1, source_target_pairs={{0,24},{4,28},{8,16},{12,20},{16,8},{20,12},{24,0},{28,4},{32,56},... | collective-permute-start | bytes 172040 | tf_op jit(solution)/shard_map/ppermute | solution.py:290
  42.6 7.1 %collective-permute-start.16 = (f32[112,128]{1,0:T(8,128)S(1)}, f32[112,128]{1,0:T(8,128)S(1)}, u32[]{:S(2)}, u32[]{:S(2)}) collective-permute-start(f32[112,128]{1,0:T(8,128)S(1)} %sum_four.3.refs_0_), channel_id=1, source_target_pairs={{0,16},{4,20},{8,24},{12,28},{16,0},{20,4},{24,8},{28,12},{32,48},... | collective-permute-start | bytes 172040 | tf_op jit(solution)/shard_map/ppermute | solution.py:290
  42.6 7.1 %collective-permute-start.15 = (f32[112,128]{1,0:T(8,128)S(1)}, f32[112,128]{1,0:T(8,128)S(1)}, u32[]{:S(2)}, u32[]{:S(2)}) collective-permute-start(f32[112,128]{1,0:T(8,128)S(1)} %sum_four.3.refs_0_), channel_id=1, source_target_pairs={{0,8},{4,12},{8,0},{12,4},{16,24},{20,28},{24,16},{28,20},{32,40},... | collective-permute-start | bytes 172040 | tf_op jit(solution)/shard_map/ppermute | solution.py:290
  44.3 9.1 %collective-permute-start.14 = (f32[112,128]{1,0:T(8,128)S(1)}, f32[112,128]{1,0:T(8,128)S(1)}, u32[]{:S(2)}, u32[]{:S(2)}) collective-permute-start(f32[112,128]{1,0:T(8,128)S(1)} %sum_four.3.refs_0_), channel_id=1, source_target_pairs={{0,4},{4,0},{8,12},{12,8},{16,20},{20,16},{24,28},{28,24},{32,36},... | collective-permute-start | bytes 172040 | tf_op jit(solution)/shard_map/ppermute | solution.py:290
  49.7 4.0 %collective-permute-start.18 = (f32[112,128]{1,0:T(8,128)S(1)}, f32[112,128]{1,0:T(8,128)S(1)}, u32[]{:S(2)}, u32[]{:S(2)}) collective-permute-start(f32[112,128]{1,0:T(8,128)S(1)} %collective-permute-done.15.refs_2_), channel_id=1, source_target_pairs={{0,4},{4,0},{8,12},{12,8},{16,20},{20,16},{24,28},{28,24},{32,36},... | collective-permute-start | bytes 172040 | tf_op jit(solution)/shard_map/ppermute | solution.py:290
  52.9 1.2 %collective-permute-start.19 = (f32[112,128]{1,0:T(8,128)S(1)}, f32[112,128]{1,0:T(8,128)S(1)}, u32[]{:S(2)}, u32[]{:S(2)}) collective-permute-start(f32[112,128]{1,0:T(8,128)S(1)} %collective-permute-done.16.refs_4_), channel_id=1, source_target_pairs={{0,4},{4,0},{8,12},{12,8},{16,20},{20,16},{24,28},{28,24},{32,36},... | collective-permute-start | bytes 172040 | tf_op jit(solution)/shard_map/ppermute | solution.py:290
  52.9 1.4 %collective-permute-start.20 = (f32[112,128]{1,0:T(8,128)S(1)}, f32[112,128]{1,0:T(8,128)S(1)}, u32[]{:S(2)}, u32[]{:S(2)}) collective-permute-start(f32[112,128]{1,0:T(8,128)S(1)} %collective-permute-done.17.refs_6_), channel_id=1, source_target_pairs={{0,4},{4,0},{8,12},{12,8},{16,20},{20,16},{24,28},{28,24},{32,36},... | collective-permute-start | bytes 172040 | tf_op jit(solution)/shard_map/ppermute | solution.py:290

commit v13 on v11

--- a/solution.py
+++ b/solution.py
@@ -13,6 +13,7 @@
 PART = 112
 INNER = tuple(range(2, 8))
 EDGE = (0, 1)
+X1, X3, Z1, Z2, Z6 = 2, 6, 8, 16, 48
 ORDER = (0, 1, 3, 2)
 VMEM = pl.BlockSpec(memory_space=pltpu.VMEM)
 
@@ -35,6 +36,11 @@
         values = jnp.take_along_axis(load(t), lane, axis=1, mode="promise_in_bounds")
         total = jnp.where(tile == t, values, total)
     return total
+
+
+def own_part():
+    place = lax.axis_index("blk")
+    return (place & 1) | ((place ^ (place >> 1)) & 2) | ((place >> 1) & 4)
 
 
 def tile_span(t):
@@ -109,7 +115,7 @@
     dense_ref, grad_ref, keep_ref, send_ref, faces, terms,
 ):
     chan = lax.axis_index("ch")
-    spot = lax.axis_index("blk") & 7
+    spot = own_part()
     for i, m in enumerate(ORDER):
         part = (pair_ref if i < 2 else other_ref)[32 * (i % 2) : 32 * (i % 2) + 32, :]
         grad_ref[pl.ds(pl.multiple_of(32 * (chan ^ m), 32), 32), :] = part
@@ -229,7 +235,7 @@
 
 
 def place_kernel(even_ref, odd_ref, out_ref):
-    spot = lax.axis_index("blk") & 7
+    spot = own_part()
     short = 864 - 7 * PART
     for q in range(4):
         for odd, ref in enumerate((even_ref, odd_ref)):
@@ -331,13 +337,13 @@
     )
     came, = after((came,), ours, back)
     pieces = call(split_sum_kernel, (f32(PART, 128),) * 4, (keep, came), name="sum_pair")
-    others = [swap(pieces[q], 2 * q) for q in (1, 2, 3)]
+    others = [swap(pieces[q], m) for q, m in ((1, X1), (2, Z1), (3, X1 | Z1))]
     first, = after((first,), *pieces)
     first = over_ch(first, 1)
     inner = inner_part((2, 3))
     others = after(others, inner)
     total = call(sum_kernel, f32(PART, 128), (pieces[0], *others), name="sum_four")
-    came = swap(total, 48)
+    came = swap(total, Z6)
     inner = inner_part((4, 5), inner)
     ours, first = after((ours, first), inner)
     own, second = call(
@@ -347,11 +353,11 @@
     second = over_ch(second, 3)
     came, = after((came,), own)
     total = call(sum_kernel, f32(PART, 128), (total, came), name="sum_two")
-    others = [swap(total, m) for m in (8, 16, 24)]
+    others = [swap(total, m) for m in (X3, Z2, X3 | Z2)]
     inner = inner_part((6, 7), inner)
     others = after(others, inner)
     total = call(sum_kernel, f32(PART, 128), (total, *others), name="sum_four")
-    others = [swap(total, 2 * q) for q in (1, 2, 3)]
+    others = [swap(total, m) for m in (X1, Z1, X1 | Z1)]
     output, grad_features = call(
         edge_kernel, (bf16(32, VOX), bf16(32, VOX)),
         (back, rules, weights, near, far, inner, own, first, second),

time: 55.1 us -> 52.6 us (0.955)
  starting transfers between devices: 34.4 us -> 32.6 us
  waiting for transfers between devices: 4.64 us -> 3.99 us
    ppermute x13, starting transfers between devices: 27 us -> 25.2 us  [swap(): return lax.ppermute(value, 'blk', [(i, i ^ mask) for i in range(count)])]
    ppermute x13, waiting for transfers between devices: 3.44 us -> 2.19 us  [swap(): return lax.ppermute(value, 'blk', [(i, i ^ mask) for i in range(count)])]
    ppermute x4, waiting for transfers between devices: 1.2 us -> 1.79 us  [over_ch(): return lax.ppermute(value, 'ch', [(i, i ^ mask) for i in range(4)])]
  transfers between devices with their start and end apart: 18 -> 18, of which waited for: 5 -> 5; matrix products, arithmetic and copies ran while one was open for 0% -> 0% of each run, Pallas kernels for 25% -> 26%
where the time goes in v13:
time: 52.6 us; the launch traced here: 52.4 us
  starting transfers between devices  32.6 us (62%)
  Pallas kernels  15 us (29%)
  waiting for transfers between devices  3.99 us (8%)
  between operations  0.81 us (2%)
    ppermute x13, starting transfers between devices, swap(): return lax.ppermute(value, 'blk', [(i, i ^ mask) for i in range(count)])  25.2 us
    pallas_call x16, Pallas kernels, call(): pl.pallas_call(kernel, out_shape=outs, in_specs=[VMEM] * len(args), out_s...  13.7 us
    ppermute x4, starting transfers between devices, over_ch(): return lax.ppermute(value, 'ch', [(i, i ^ mask) for i in range(4)])  6.43 us
    ppermute x13, waiting for transfers between devices, swap(): return lax.ppermute(value, 'blk', [(i, i ^ mask) for i in range(count)])  2.19 us
    ppermute x4, waiting for transfers between devices, over_ch(): return lax.ppermute(value, 'ch', [(i, i ^ mask) for i in range(4)])  1.79 us
    pallas_call x1, Pallas kernels, per_device(): pl.pallas_call(faces_kernel, out_shape=(bf16(64, FACE),) * 2, grid=(1,),...  1.37 us
  transfers between devices with their start and end apart: 18, of which 5 were waited for; matrix products, arithmetic and copies ran while one was open for 0% of the time, Pallas kernels for 26%

profile of v13, /device:TPU:1, one launch (start us, length us, event | category | flops | bytes accessed | tf_op | source)
XLA Modules:
  0.0 52.4 jit_solution(5676233300053606382)
XLA Ops:
  0.7 2.2 %collective-permute-start.2 = (bf16[32,1024]{1,0:T(8,128)(2,1)}, bf16[32,1024]{1,0:T(8,128)(2,1)S(1)}, u32[]{:S(2)}, u32[]{:S(2)}) collective-permute-start(bf16[32,1024]{1,0:T(8,128)(2,1)} %refs_0_.1), channel_id=1, source_target_pairs={{0,1},{1,0},{2,3},{3,2},{4,5},{5,4},{6,7},{7,6},{8,9},{9,8},{10,11... | collective-permute-start | bytes 196616 | tf_op jit(solution)/shard_map/ppermute | solution.py:294
  2.9 1.4 %faces.1 = (bf16[64,128]{1,0:T(8,128)(2,1)}, bf16[64,128]{1,0:T(8,128)(2,1)}) custom-call(bf16[32,1024]{1,0:T(8,128)(2,1)} %x_ref.3, bf16[32,1024]{1,0:T(8,128)(2,1)} %refs_0_.1), custom_call_target="tpu_custom_call" | custom-call | flops 1073741824 | bytes 65536 | tf_op jit(solution)/shard_map/faces/pallas_call | solution.py:299
  4.2 1.1 %collective-permute-start = (bf16[64,128]{1,0:T(8,128)(2,1)}, bf16[64,128]{1,0:T(8,128)(2,1)S(1)}, u32[]{:S(2)}, u32[]{:S(2)}) collective-permute-start(bf16[64,128]{1,0:T(8,128)(2,1)} %get-tuple-element.33), channel_id=1, source_target_pairs={{0,4},{4,0},{8,12},{12,8},{16,20},{20,16},{24,28},{28,24},{32,36},... | collective-permute-start | bytes 49160 | tf_op jit(solution)/shard_map/ppermute | solution.py:277
  5.4 0.9 %collective-permute-start.1 = (bf16[64,128]{1,0:T(8,128)(2,1)}, bf16[64,128]{1,0:T(8,128)(2,1)S(1)}, u32[]{:S(2)}, u32[]{:S(2)}) collective-permute-start(bf16[64,128]{1,0:T(8,128)(2,1)} %get-tuple-element.34), channel_id=1, source_target_pairs={{0,252},{4,8},{8,4},{12,16},{16,12},{20,24},{24,20},{28,32},{32,28... | collective-permute-start | bytes 49160 | tf_op jit(solution)/shard_map/ppermute | solution.py:283
  6.3 2.0 %collective-permute-start.3 = (bf16[64,1024]{1,0:T(8,128)(2,1)S(1)}, bf16[64,1024]{1,0:T(8,128)(2,1)S(1)}, u32[]{:S(2)}, u32[]{:S(2)}) collective-permute-start(bf16[64,1024]{1,0:T(8,128)(2,1)S(1)} %join.2.pair_ref), channel_id=1, source_target_pairs={{0,3},{1,2},{2,1},{3,0},{4,7},{5,6},{6,5},{7,4},{8,11},{9,10},{10,... | collective-permute-start | bytes 393224 | tf_op jit(solution)/shard_map/ppermute | solution.py:294
  8.3 3.9 %gather.1.dense_in = bf16[864,1024]{1,0:T(8,128)(2,1)S(1)} custom-call(bf16[32,1024]{1,0:T(8,128)(2,1)S(1)} %copy-done.3, s32[27,1024]{1,0:T(8,128)S(1)} %copy-done.2), custom_call_target="tpu_custom_call" | custom-call | flops 3221225472 | bytes 1945600 | tf_op jit(solution)/shard_map/gather/pallas_call | solution.py:254
  12.2 0.7 %weight_terms.1 = (bf16[864,1024]{1,0:T(8,128)(2,1)S(1)}, bf16[128,1024]{1,0:T(8,128)(2,1)S(1)}, f32[448,128]{1,0:T(8,128)S(1)}, f32[448,128]{1,0:T(8,128)S(1)}) custom-call(bf16[864,1024]{1,0:T(8,128)(2,1)S(1)} %gather.1.dense_in, s32[27,1024]{1,0:T(8,128)S(1)} %copy-done.2, ...), custom_call_target="tpu_custom_call", output_to_operand_aliasing={{0}: (0, {})} | custom-call | flops 1073741824 | bytes 4665344 | tf_op jit(solution)/shard_map/weight_terms/pallas_call | solution.py:254
  12.9 7.5 %collective-permute-start.4 = (f32[448,128]{1,0:T(8,128)S(1)}, f32[448,128]{1,0:T(8,128)S(1)}, u32[]{:S(2)}, u32[]{:S(2)}) collective-permute-start(f32[448,128]{1,0:T(8,128)S(1)} %get-tuple-element.40), channel_id=1, source_target_pairs={{0,4},{4,0},{8,12},{12,8},{16,20},{20,16},{24,28},{28,24},{32,36},... | collective-permute-start | bytes 688136 | tf_op jit(solution)/shard_map/ppermute | solution.py:277
  20.5 0.6 %back_terms.1.terms = f32[864,1024]{1,0:T(8,128)S(1)} custom-call(bf16[864,128]{1,0:T(8,128)(2,1)S(1)} %bitcast.2, bf16[128,1024]{1,0:T(8,128)(2,1)S(1)} %get-tuple-element.35.grad_ref), custom_call_target="tpu_custom_call" | custom-call | flops 1073741824 | bytes 4022272 | tf_op jit(solution)/shard_map/back_terms/pallas_call | solution.py:254
  21.1 0.5 forward.1
  21.7 0.1 collective-permute-start.8
  21.8 2.5 %collective-permute-start.9 = (f32[112,128]{1,0:T(8,128)S(1)}, f32[112,128]{1,0:T(8,128)S(1)}, u32[]{:S(2)}, u32[]{:S(2)}) collective-permute-start(f32[112,128]{1,0:T(8,128)S(1)} %get-tuple-element.45), channel_id=1, source_target_pairs={{0,40},{4,44},{8,32},{12,36},{16,56},{20,60},{24,48},{28,52},{32,8... | collective-permute-start | bytes 172040 | tf_op jit(solution)/shard_map/ppermute | solution.py:277
  24.4 0.3 collective-permute-start.5
  24.7 1.8 %back_inner.3.refs_0_ = f32[32,1024]{1,0:T(8,128)S(1)} custom-call(f32[864,1024]{1,0:T(8,128)S(1)} %back_terms.1.terms, s32[27,1024]{1,0:T(8,128)S(1)} %copy-done.2), custom_call_target="tpu_custom_call" | custom-call | flops 2147483648 | bytes 3780608 | tf_op jit(solution)/shard_map/back_inner/pallas_call | solution.py:254
  26.5 0.1 collective-permute-done.9.refs_3_
  26.7 1.4 %collective-permute-start.10 = (f32[112,128]{1,0:T(8,128)S(1)}, f32[112,128]{1,0:T(8,128)S(1)}, u32[]{:S(2)}, u32[]{:S(2)}) collective-permute-start(f32[112,128]{1,0:T(8,128)S(1)} %sum_four.2.refs_0_), channel_id=1, source_target_pairs={{0,192},{4,196},{8,200},{12,204},{16,208},{20,212},{24,216},{28,22... | collective-permute-start | bytes 172040 | tf_op jit(solution)/shard_map/ppermute | solution.py:277
  28.0 1.8 %back_inner.4.refs_0_ = f32[32,1024]{1,0:T(8,128)S(1)} custom-call(f32[864,1024]{1,0:T(8,128)S(1)} %back_terms.1.terms, s32[27,1024]{1,0:T(8,128)S(1)} %copy-done.2, f32[32,1024]{1,0:T(8,128)S(1)} %back_inner.3.refs_0_), custom_call_target="tpu_custom_call", output_to_operand_aliasing={{}: (2, {})} | custom-call | flops 2147483648 | bytes 3911680 | tf_op jit(solution)/shard_map/back_inner/pallas_call | solution.py:254
  29.9 1.8 %collective-permute-done.5.came_ref.first_ref = f32[64,1152]{1,0:T(8,128)S(1)} collective-permute-done((f32[64,1152]{1,0:T(8,128)S(1)}, f32[64,1152]{1,0:T(8,128)S(1)}, u32[]{:S(2)}, u32[]{:S(2)}) %collective-permute-start.5) | collective-permute-done | bytes 294944 | tf_op jit(solution)/shard_map/ppermute | solution.py:294
  31.7 0.3 collective-permute-done.10.refs_1_
  32.0 1.1 %collective-permute-start.13 = (f32[112,128]{1,0:T(8,128)S(1)}, f32[112,128]{1,0:T(8,128)S(1)}, u32[]{:S(2)}, u32[]{:S(2)}) collective-permute-start(f32[112,128]{1,0:T(8,128)S(1)} %sum_two.1.refs_0_), channel_id=1, source_target_pairs={{0,88},{4,92},{8,80},{12,84},{16,72},{20,76},{24,64},{28,68},{32,1... | collective-permute-start | bytes 172040 | tf_op jit(solution)/shard_map/ppermute | solution.py:277
  33.1 1.2 %collective-permute-start.12 = (f32[112,128]{1,0:T(8,128)S(1)}, f32[112,128]{1,0:T(8,128)S(1)}, u32[]{:S(2)}, u32[]{:S(2)}) collective-permute-start(f32[112,128]{1,0:T(8,128)S(1)} %sum_two.1.refs_0_), channel_id=1, source_target_pairs={{0,64},{4,68},{8,72},{12,76},{16,80},{20,84},{24,88},{28,92},{32,9... | collective-permute-start | bytes 172040 | tf_op jit(solution)/shard_map/ppermute | solution.py:277
  34.2 2.6 %collective-permute-start.11 = (f32[112,128]{1,0:T(8,128)S(1)}, f32[112,128]{1,0:T(8,128)S(1)}, u32[]{:S(2)}, u32[]{:S(2)}) collective-permute-start(f32[112,128]{1,0:T(8,128)S(1)} %sum_two.1.refs_0_), channel_id=1, source_target_pairs={{0,24},{4,28},{8,16},{12,20},{16,8},{20,12},{24,0},{28,4},{32,56},... | collective-permute-start | bytes 172040 | tf_op jit(solution)/shard_map/ppermute | solution.py:277
  36.8 1.9 %collective-permute-start.6 = (f32[32,1536]{1,0:T(8,128)S(1)}, f32[32,1536]{1,0:T(8,128)S(1)}, u32[]{:S(2)}, u32[]{:S(2)}) collective-permute-start(f32[32,1536]{1,0:T(8,128)S(1)} %get-tuple-element.50), channel_id=1, source_target_pairs={{0,3},{1,2},{2,1},{3,0},{4,7},{5,6},{6,5},{7,4},{8,11},{9,10},{10,... | collective-permute-start | bytes 589832 | tf_op jit(solution)/shard_map/ppermute | solution.py:294
  38.8 1.8 %back_inner.5.inner = f32[32,1024]{1,0:T(8,128)S(1)} custom-call(f32[864,1024]{1,0:T(8,128)S(1)} %back_terms.1.terms, s32[27,1024]{1,0:T(8,128)S(1)} %copy-done.2, f32[32,1024]{1,0:T(8,128)S(1)} %back_inner.4.refs_0_), custom_call_target="tpu_custom_call", output_to_operand_aliasing={{}: (2, {})} | custom-call | flops 2147483648 | bytes 3911680 | tf_op jit(solution)/shard_map/back_inner/pallas_call | solution.py:254
  40.7 1.0 %collective-permute-start.16 = (f32[112,128]{1,0:T(8,128)S(1)}, f32[112,128]{1,0:T(8,128)S(1)}, u32[]{:S(2)}, u32[]{:S(2)}) collective-permute-start(f32[112,128]{1,0:T(8,128)S(1)} %sum_four.3.refs_0_), channel_id=1, source_target_pairs={{0,40},{4,44},{8,32},{12,36},{16,56},{20,60},{24,48},{28,52},{32,8... | collective-permute-start | bytes 172040 | tf_op jit(solution)/shard_map/ppermute | solution.py:277
  41.7 0.4 collective-permute-start.15
  42.0 1.3 %collective-permute-start.14 = (f32[112,128]{1,0:T(8,128)S(1)}, f32[112,128]{1,0:T(8,128)S(1)}, u32[]{:S(2)}, u32[]{:S(2)}) collective-permute-start(f32[112,128]{1,0:T(8,128)S(1)} %sum_four.3.refs_0_), channel_id=1, source_target_pairs={{0,8},{4,12},{8,0},{12,4},{16,24},{20,28},{24,16},{28,20},{32,40},... | collective-permute-start | bytes 172040 | tf_op jit(solution)/shard_map/ppermute | solution.py:277
  43.4 1.5 %edge.1 = (bf16[32,1024]{1,0:T(8,128)(2,1)}, bf16[32,1024]{1,0:T(8,128)(2,1)}) custom-call(f32[864,1024]{1,0:T(8,128)S(1)} %back_terms.1.terms, s32[27,1024]{1,0:T(8,128)S(1)} %copy-done.2, bf16[864,128]{1,0:T(8,128)(2,1)S(1)} %bitcast.4, bf16[64,128]{1,0:T(8,128)(2,1)S(1)} %collective-permute-done.near_ref, ...), custom_call_target="tpu_custom_call" | custom-call | flops 2147483648 | bytes 4788224 | tf_op jit(solution)/shard_map/edge/pallas_call | solution.py:254
  45.0 0.6 %collective-permute-done.14.refs_1_ = f32[112,128]{1,0:T(8,128)S(1)} collective-permute-done((f32[112,128]{1,0:T(8,128)S(1)}, f32[112,128]{1,0:T(8,128)S(1)}, u32[]{:S(2)}, u32[]{:S(2)}) %collective-permute-start.14) | collective-permute-done | bytes 57376 | tf_op jit(solution)/shard_map/ppermute | solution.py:277
  45.6 4.9 %collective-permute-start.17 = (f32[448,128]{1,0:T(8,128)S(1)}, f32[448,128]{1,0:T(8,128)S(1)}, u32[]{:S(2)}, u32[]{:S(2)}) collective-permute-start(f32[448,128]{1,0:T(8,128)S(1)} %join.3.even_ref), channel_id=1, source_target_pairs={{0,4},{4,0},{8,12},{12,8},{16,20},{20,16},{24,28},{28,24},{32,36},... | collective-permute-start | bytes 688136 | tf_op jit(solution)/shard_map/ppermute | solution.py:277
  50.5 1.1 %collective-permute-done.17.odd_ref = f32[448,128]{1,0:T(8,128)S(1)} collective-permute-done((f32[448,128]{1,0:T(8,128)S(1)}, f32[448,128]{1,0:T(8,128)S(1)}, u32[]{:S(2)}, u32[]{:S(2)}) %collective-permute-start.17) | collective-permute-done | bytes 229408 | tf_op jit(solution)/shard_map/ppermute | solution.py:277
  51.6 0.8 %place.1 = f32[864,128]{1,0:T(8,128)} custom-call(f32[448,128]{1,0:T(8,128)S(1)} %join.3.even_ref, f32[448,128]{1,0:T(8,128)S(1)} %collective-permute-done.17.odd_ref), custom_call_target="tpu_custom_call" | custom-call | bytes 901120 | tf_op jit(solution)/shard_map/place/pallas_call | solution.py:254
  (29 shorter events, 0.4 us)
Async XLA Ops:
  0.6 5.7 %copy-start.1 = (bf16[32,1024]{1,0:T(8,128)(2,1)S(1)}, bf16[32,1024]{1,0:T(8,128)(2,1)}, u32[]{:S(2)}) copy-start(bf16[32,1024]{1,0:T(8,128)(2,1)} %refs_0_.1) | copy-start | bytes 196612
  0.6 7.7 %copy-start.3 = (bf16[32,1024]{1,0:T(8,128)(2,1)S(1)}, bf16[32,1024]{1,0:T(8,128)(2,1)}, u32[]{:S(2)}) copy-start(bf16[32,1024]{1,0:T(8,128)(2,1)} %x_ref.3) | copy-start | bytes 196612
  0.7 7.7 %copy-start.2 = (s32[27,1024]{1,0:T(8,128)S(1)}, s32[27,1024]{1,0:T(8,128)}, u32[]{:S(2)}) copy-start(s32[27,1024]{1,0:T(8,128)} %rule_ref.11) | copy-start | bytes 331780
  0.7 5.6 %collective-permute-start.2 = (bf16[32,1024]{1,0:T(8,128)(2,1)}, bf16[32,1024]{1,0:T(8,128)(2,1)S(1)}, u32[]{:S(2)}, u32[]{:S(2)}) collective-permute-start(bf16[32,1024]{1,0:T(8,128)(2,1)} %refs_0_.1), channel_id=1, source_target_pairs={{0,1},{1,0},{2,3},{3,2},{4,5},{5,4},{6,7},{7,6},{8,9},{9,8},{10,11... | collective-permute-start | bytes 196616 | tf_op jit(solution)/shard_map/ppermute | solution.py:294
  4.2 7.9 %collective-permute-start = (bf16[64,128]{1,0:T(8,128)(2,1)}, bf16[64,128]{1,0:T(8,128)(2,1)S(1)}, u32[]{:S(2)}, u32[]{:S(2)}) collective-permute-start(bf16[64,128]{1,0:T(8,128)(2,1)} %get-tuple-element.33), channel_id=1, source_target_pairs={{0,4},{4,0},{8,12},{12,8},{16,20},{20,16},{24,28},{28,24},{32,36},... | collective-permute-start | bytes 49160 | tf_op jit(solution)/shard_map/ppermute | solution.py:277
  5.4 6.8 %collective-permute-start.1 = (bf16[64,128]{1,0:T(8,128)(2,1)}, bf16[64,128]{1,0:T(8,128)(2,1)S(1)}, u32[]{:S(2)}, u32[]{:S(2)}) collective-permute-start(bf16[64,128]{1,0:T(8,128)(2,1)} %get-tuple-element.34), channel_id=1, source_target_pairs={{0,252},{4,8},{8,4},{12,16},{16,12},{20,24},{24,20},{28,32},{32,28... | collective-permute-start | bytes 49160 | tf_op jit(solution)/shard_map/ppermute | solution.py:283
  6.3 5.9 %collective-permute-start.3 = (bf16[64,1024]{1,0:T(8,128)(2,1)S(1)}, bf16[64,1024]{1,0:T(8,128)(2,1)S(1)}, u32[]{:S(2)}, u32[]{:S(2)}) collective-permute-start(bf16[64,1024]{1,0:T(8,128)(2,1)S(1)} %join.2.pair_ref), channel_id=1, source_target_pairs={{0,3},{1,2},{2,1},{3,0},{4,7},{5,6},{6,5},{7,4},{8,11},{9,10},{10,... | collective-permute-start | bytes 393224 | tf_op jit(solution)/shard_map/ppermute | solution.py:294
  12.2 8.3 %copy-start = (bf16[27,32,128]{2,1,0:T(8,128)(2,1)S(1)}, bf16[27,32,128]{2,1,0:T(8,128)(2,1)}, u32[]{:S(2)}) copy-start(bf16[27,32,128]{2,1,0:T(8,128)(2,1)} %param.5) | copy-start | bytes 663556
  12.9 8.6 %collective-permute-start.4 = (f32[448,128]{1,0:T(8,128)S(1)}, f32[448,128]{1,0:T(8,128)S(1)}, u32[]{:S(2)}, u32[]{:S(2)}) collective-permute-start(f32[448,128]{1,0:T(8,128)S(1)} %get-tuple-element.40), channel_id=1, source_target_pairs={{0,4},{4,0},{8,12},{12,8},{16,20},{20,16},{24,28},{28,24},{32,36},... | collective-permute-start | bytes 688136 | tf_op jit(solution)/shard_map/ppermute | solution.py:277
  21.6 4.9 %collective-permute-start.7 = (f32[112,128]{1,0:T(8,128)S(1)}, f32[112,128]{1,0:T(8,128)S(1)}, u32[]{:S(2)}, u32[]{:S(2)}) collective-permute-start(f32[112,128]{1,0:T(8,128)S(1)} %get-tuple-element.43), channel_id=1, source_target_pairs={{0,8},{4,12},{8,0},{12,4},{16,24},{20,28},{24,16},{28,20},{32,40},... | collective-permute-start | bytes 172040 | tf_op jit(solution)/shard_map/ppermute | solution.py:277
  21.7 4.8 %collective-permute-start.8 = (f32[112,128]{1,0:T(8,128)S(1)}, f32[112,128]{1,0:T(8,128)S(1)}, u32[]{:S(2)}, u32[]{:S(2)}) collective-permute-start(f32[112,128]{1,0:T(8,128)S(1)} %get-tuple-element.44), channel_id=1, source_target_pairs={{0,32},{4,36},{8,40},{12,44},{16,48},{20,52},{24,56},{28,60},{32,0... | collective-permute-start | bytes 172040 | tf_op jit(solution)/shard_map/ppermute | solution.py:277
  21.8 4.8 %collective-permute-start.9 = (f32[112,128]{1,0:T(8,128)S(1)}, f32[112,128]{1,0:T(8,128)S(1)}, u32[]{:S(2)}, u32[]{:S(2)}) collective-permute-start(f32[112,128]{1,0:T(8,128)S(1)} %get-tuple-element.45), channel_id=1, source_target_pairs={{0,40},{4,44},{8,32},{12,36},{16,56},{20,60},{24,48},{28,52},{32,8... | collective-permute-start | bytes 172040 | tf_op jit(solution)/shard_map/ppermute | solution.py:277
  24.4 7.3 %collective-permute-start.5 = (f32[64,1152]{1,0:T(8,128)S(1)}, f32[64,1152]{1,0:T(8,128)S(1)}, u32[]{:S(2)}, u32[]{:S(2)}) collective-permute-start(f32[64,1152]{1,0:T(8,128)S(1)} %get-tuple-element.46), channel_id=1, source_target_pairs={{0,1},{1,0},{2,3},{3,2},{4,5},{5,4},{6,7},{7,6},{8,9},{9,8},{10,11... | collective-permute-start | bytes 884744 | tf_op jit(solution)/shard_map/ppermute | solution.py:294
  26.7 5.3 %collective-permute-start.10 = (f32[112,128]{1,0:T(8,128)S(1)}, f32[112,128]{1,0:T(8,128)S(1)}, u32[]{:S(2)}, u32[]{:S(2)}) collective-permute-start(f32[112,128]{1,0:T(8,128)S(1)} %sum_four.2.refs_0_), channel_id=1, source_target_pairs={{0,192},{4,196},{8,200},{12,204},{16,208},{20,212},{24,216},{28,22... | collective-permute-start | bytes 172040 | tf_op jit(solution)/shard_map/ppermute | solution.py:277
  32.0 8.6 %collective-permute-start.13 = (f32[112,128]{1,0:T(8,128)S(1)}, f32[112,128]{1,0:T(8,128)S(1)}, u32[]{:S(2)}, u32[]{:S(2)}) collective-permute-start(f32[112,128]{1,0:T(8,128)S(1)} %sum_two.1.refs_0_), channel_id=1, source_target_pairs={{0,88},{4,92},{8,80},{12,84},{16,72},{20,76},{24,64},{28,68},{32,1... | collective-permute-start | bytes 172040 | tf_op jit(solution)/shard_map/ppermute | solution.py:277
  33.1 7.6 %collective-permute-start.12 = (f32[112,128]{1,0:T(8,128)S(1)}, f32[112,128]{1,0:T(8,128)S(1)}, u32[]{:S(2)}, u32[]{:S(2)}) collective-permute-start(f32[112,128]{1,0:T(8,128)S(1)} %sum_two.1.refs_0_), channel_id=1, source_target_pairs={{0,64},{4,68},{8,72},{12,76},{16,80},{20,84},{24,88},{28,92},{32,9... | collective-permute-start | bytes 172040 | tf_op jit(solution)/shard_map/ppermute | solution.py:277
  34.2 6.4 %collective-permute-start.11 = (f32[112,128]{1,0:T(8,128)S(1)}, f32[112,128]{1,0:T(8,128)S(1)}, u32[]{:S(2)}, u32[]{:S(2)}) collective-permute-start(f32[112,128]{1,0:T(8,128)S(1)} %sum_two.1.refs_0_), channel_id=1, source_target_pairs={{0,24},{4,28},{8,16},{12,20},{16,8},{20,12},{24,0},{28,4},{32,56},... | collective-permute-start | bytes 172040 | tf_op jit(solution)/shard_map/ppermute | solution.py:277
  36.8 6.6 %collective-permute-start.6 = (f32[32,1536]{1,0:T(8,128)S(1)}, f32[32,1536]{1,0:T(8,128)S(1)}, u32[]{:S(2)}, u32[]{:S(2)}) collective-permute-start(f32[32,1536]{1,0:T(8,128)S(1)} %get-tuple-element.50), channel_id=1, source_target_pairs={{0,3},{1,2},{2,1},{3,0},{4,7},{5,6},{6,5},{7,4},{8,11},{9,10},{10,... | collective-permute-start | bytes 589832 | tf_op jit(solution)/shard_map/ppermute | solution.py:294
  40.7 4.3 %collective-permute-start.16 = (f32[112,128]{1,0:T(8,128)S(1)}, f32[112,128]{1,0:T(8,128)S(1)}, u32[]{:S(2)}, u32[]{:S(2)}) collective-permute-start(f32[112,128]{1,0:T(8,128)S(1)} %sum_four.3.refs_0_), channel_id=1, source_target_pairs={{0,40},{4,44},{8,32},{12,36},{16,56},{20,60},{24,48},{28,52},{32,8... | collective-permute-start | bytes 172040 | tf_op jit(solution)/shard_map/ppermute | solution.py:277
  41.7 3.3 %collective-permute-start.15 = (f32[112,128]{1,0:T(8,128)S(1)}, f32[112,128]{1,0:T(8,128)S(1)}, u32[]{:S(2)}, u32[]{:S(2)}) collective-permute-start(f32[112,128]{1,0:T(8,128)S(1)} %sum_four.3.refs_0_), channel_id=1, source_target_pairs={{0,32},{4,36},{8,40},{12,44},{16,48},{20,52},{24,56},{28,60},{32,0... | collective-permute-start | bytes 172040 | tf_op jit(solution)/shard_map/ppermute | solution.py:277
  42.0 3.5 %collective-permute-start.14 = (f32[112,128]{1,0:T(8,128)S(1)}, f32[112,128]{1,0:T(8,128)S(1)}, u32[]{:S(2)}, u32[]{:S(2)}) collective-permute-start(f32[112,128]{1,0:T(8,128)S(1)} %sum_four.3.refs_0_), channel_id=1, source_target_pairs={{0,8},{4,12},{8,0},{12,4},{16,24},{20,28},{24,16},{28,20},{32,40},... | collective-permute-start | bytes 172040 | tf_op jit(solution)/shard_map/ppermute | solution.py:277
  45.6 6.0 %collective-permute-start.17 = (f32[448,128]{1,0:T(8,128)S(1)}, f32[448,128]{1,0:T(8,128)S(1)}, u32[]{:S(2)}, u32[]{:S(2)}) collective-permute-start(f32[448,128]{1,0:T(8,128)S(1)} %join.3.even_ref), channel_id=1, source_target_pairs={{0,4},{4,0},{8,12},{12,8},{16,20},{20,16},{24,28},{28,24},{32,36},... | collective-permute-start | bytes 688136 | tf_op jit(solution)/shard_map/ppermute | solution.py:277

commit v14 on v13

--- a/solution.py
+++ b/solution.py
@@ -344,7 +344,7 @@
     others = after(others, inner)
     total = call(sum_kernel, f32(PART, 128), (pieces[0], *others), name="sum_four")
     came = swap(total, Z6)
-    inner = inner_part((4, 5), inner)
+    inner = inner_part((4, 5, 6), inner)
     ours, first = after((ours, first), inner)
     own, second = call(
         middle_kernel, (f32(32, VOX), f32(32, VOX + 4 * FACE)), (ours, first, near, far),
@@ -354,7 +354,7 @@
     came, = after((came,), own)
     total = call(sum_kernel, f32(PART, 128), (total, came), name="sum_two")
     others = [swap(total, m) for m in (X3, Z2, X3 | Z2)]
-    inner = inner_part((6, 7), inner)
+    inner = inner_part((7,), inner)
     others = after(others, inner)
     total = call(sum_kernel, f32(PART, 128), (total, *others), name="sum_four")
     others = [swap(total, m) for m in (X1, Z1, X1 | Z1)]

time: 52.6 us -> 61 us (1.16)
  waiting for transfers between devices: 3.99 us -> 11.3 us
  starting transfers between devices: 32.6 us -> 33.5 us
    ppermute x13, waiting for transfers between devices: 2.19 us -> 7.05 us  [swap(): return lax.ppermute(value, 'blk', [(i, i ^ mask) for i in range(count)])]
    ppermute x4, waiting for transfers between devices: 1.79 us -> 4.22 us  [over_ch(): return lax.ppermute(value, 'ch', [(i, i ^ mask) for i in range(4)])]
    ppermute x13, starting transfers between devices: 25.2 us -> 26 us  [swap(): return lax.ppermute(value, 'blk', [(i, i ^ mask) for i in range(count)])]
  transfers between devices with their start and end apart: 18 -> 18, of which waited for: 5 -> 5; matrix products, arithmetic and copies ran while one was open for 0% -> 0% of each run, Pallas kernels for 26% -> 22%
where the time goes in v14:
time: 61 us; the launch traced here: 60.7 us
  starting transfers between devices  33.5 us (55%)
  Pallas kernels  15 us (25%)
  waiting for transfers between devices  11.3 us (19%)
  between operations  0.79 us (1%)
    ppermute x13, starting transfers between devices, swap(): return lax.ppermute(value, 'blk', [(i, i ^ mask) for i in range(count)])  26 us
    pallas_call x16, Pallas kernels, call(): pl.pallas_call(kernel, out_shape=outs, in_specs=[VMEM] * len(args), out_s...  13.7 us
    ppermute x13, waiting for transfers between devices, swap(): return lax.ppermute(value, 'blk', [(i, i ^ mask) for i in range(count)])  7.05 us
    ppermute x4, starting transfers between devices, over_ch(): return lax.ppermute(value, 'ch', [(i, i ^ mask) for i in range(4)])  6.6 us
    ppermute x4, waiting for transfers between devices, over_ch(): return lax.ppermute(value, 'ch', [(i, i ^ mask) for i in range(4)])  4.22 us
    pallas_call x1, Pallas kernels, per_device(): pl.pallas_call(faces_kernel, out_shape=(bf16(64, FACE),) * 2, grid=(1,),...  1.37 us
  transfers between devices with their start and end apart: 18, of which 5 were waited for; matrix products, arithmetic and copies ran while one was open for 0% of the time, Pallas kernels for 22%

profile of v14, /device:TPU:1, one launch (start us, length us, event | category | flops | bytes accessed | tf_op | source)
XLA Modules:
  0.0 60.7 jit_solution(12081352098595050571)
XLA Ops:
  0.7 2.2 %collective-permute-start.2 = (bf16[32,1024]{1,0:T(8,128)(2,1)}, bf16[32,1024]{1,0:T(8,128)(2,1)S(1)}, u32[]{:S(2)}, u32[]{:S(2)}) collective-permute-start(bf16[32,1024]{1,0:T(8,128)(2,1)} %refs_0_.1), channel_id=1, source_target_pairs={{0,1},{1,0},{2,3},{3,2},{4,5},{5,4},{6,7},{7,6},{8,9},{9,8},{10,11... | collective-permute-start | bytes 196616 | tf_op jit(solution)/shard_map/ppermute | solution.py:294
  2.9 1.4 %faces.1 = (bf16[64,128]{1,0:T(8,128)(2,1)}, bf16[64,128]{1,0:T(8,128)(2,1)}) custom-call(bf16[32,1024]{1,0:T(8,128)(2,1)} %x_ref.3, bf16[32,1024]{1,0:T(8,128)(2,1)} %refs_0_.1), custom_call_target="tpu_custom_call" | custom-call | flops 1073741824 | bytes 65536 | tf_op jit(solution)/shard_map/faces/pallas_call | solution.py:299
  4.2 1.1 %collective-permute-start = (bf16[64,128]{1,0:T(8,128)(2,1)}, bf16[64,128]{1,0:T(8,128)(2,1)S(1)}, u32[]{:S(2)}, u32[]{:S(2)}) collective-permute-start(bf16[64,128]{1,0:T(8,128)(2,1)} %get-tuple-element.33), channel_id=1, source_target_pairs={{0,4},{4,0},{8,12},{12,8},{16,20},{20,16},{24,28},{28,24},{32,36},... | collective-permute-start | bytes 49160 | tf_op jit(solution)/shard_map/ppermute | solution.py:277
  5.4 0.9 %collective-permute-start.1 = (bf16[64,128]{1,0:T(8,128)(2,1)}, bf16[64,128]{1,0:T(8,128)(2,1)S(1)}, u32[]{:S(2)}, u32[]{:S(2)}) collective-permute-start(bf16[64,128]{1,0:T(8,128)(2,1)} %get-tuple-element.34), channel_id=1, source_target_pairs={{0,252},{4,8},{8,4},{12,16},{16,12},{20,24},{24,20},{28,32},{32,28... | collective-permute-start | bytes 49160 | tf_op jit(solution)/shard_map/ppermute | solution.py:283
  6.3 2.0 %collective-permute-start.3 = (bf16[64,1024]{1,0:T(8,128)(2,1)S(1)}, bf16[64,1024]{1,0:T(8,128)(2,1)S(1)}, u32[]{:S(2)}, u32[]{:S(2)}) collective-permute-start(bf16[64,1024]{1,0:T(8,128)(2,1)S(1)} %join.2.pair_ref), channel_id=1, source_target_pairs={{0,3},{1,2},{2,1},{3,0},{4,7},{5,6},{6,5},{7,4},{8,11},{9,10},{10,... | collective-permute-start | bytes 393224 | tf_op jit(solution)/shard_map/ppermute | solution.py:294
  8.3 3.9 %gather.1.dense_in = bf16[864,1024]{1,0:T(8,128)(2,1)S(1)} custom-call(bf16[32,1024]{1,0:T(8,128)(2,1)S(1)} %copy-done.3, s32[27,1024]{1,0:T(8,128)S(1)} %copy-done.2), custom_call_target="tpu_custom_call" | custom-call | flops 3221225472 | bytes 1945600 | tf_op jit(solution)/shard_map/gather/pallas_call | solution.py:254
  12.2 0.7 %weight_terms.1 = (bf16[864,1024]{1,0:T(8,128)(2,1)S(1)}, bf16[128,1024]{1,0:T(8,128)(2,1)S(1)}, f32[448,128]{1,0:T(8,128)S(1)}, f32[448,128]{1,0:T(8,128)S(1)}) custom-call(bf16[864,1024]{1,0:T(8,128)(2,1)S(1)} %gather.1.dense_in, s32[27,1024]{1,0:T(8,128)S(1)} %copy-done.2, ...), custom_call_target="tpu_custom_call", output_to_operand_aliasing={{0}: (0, {})} | custom-call | flops 1073741824 | bytes 4665344 | tf_op jit(solution)/shard_map/weight_terms/pallas_call | solution.py:254
  12.9 7.5 %collective-permute-start.4 = (f32[448,128]{1,0:T(8,128)S(1)}, f32[448,128]{1,0:T(8,128)S(1)}, u32[]{:S(2)}, u32[]{:S(2)}) collective-permute-start(f32[448,128]{1,0:T(8,128)S(1)} %get-tuple-element.40), channel_id=1, source_target_pairs={{0,4},{4,0},{8,12},{12,8},{16,20},{20,16},{24,28},{28,24},{32,36},... | collective-permute-start | bytes 688136 | tf_op jit(solution)/shard_map/ppermute | solution.py:277
  20.5 0.6 back_terms.1.terms
  21.1 0.5 forward.1
  21.7 0.1 collective-permute-start.8
  21.8 2.5 %collective-permute-start.9 = (f32[112,128]{1,0:T(8,128)S(1)}, f32[112,128]{1,0:T(8,128)S(1)}, u32[]{:S(2)}, u32[]{:S(2)}) collective-permute-start(f32[112,128]{1,0:T(8,128)S(1)} %get-tuple-element.45), channel_id=1, source_target_pairs={{0,40},{4,44},{8,32},{12,36},{16,56},{20,60},{24,48},{28,52},{32,8... | collective-permute-start | bytes 172040 | tf_op jit(solution)/shard_map/ppermute | solution.py:277
  24.4 1.8 %back_inner.3.refs_0_ = f32[32,1024]{1,0:T(8,128)S(1)} custom-call(f32[864,1024]{1,0:T(8,128)S(1)} %back_terms.1.terms, s32[27,1024]{1,0:T(8,128)S(1)} %copy-done.2), custom_call_target="tpu_custom_call" | custom-call | flops 2147483648 | bytes 3780608 | tf_op jit(solution)/shard_map/back_inner/pallas_call | solution.py:254
  26.2 0.4 collective-permute-start.5
  26.6 2.7 %back_inner.4.refs_0_ = f32[32,1024]{1,0:T(8,128)S(1)} custom-call(f32[864,1024]{1,0:T(8,128)S(1)} %back_terms.1.terms, s32[27,1024]{1,0:T(8,128)S(1)} %copy-done.2, f32[32,1024]{1,0:T(8,128)S(1)} %back_inner.3.refs_0_), custom_call_target="tpu_custom_call", output_to_operand_aliasing={{}: (2, {})} | custom-call | flops 3221225472 | bytes 3911680 | tf_op jit(solution)/shard_map/back_inner/pallas_call | solution.py:254
  29.4 4.2 %collective-permute-done.5.came_ref.first_ref = f32[64,1152]{1,0:T(8,128)S(1)} collective-permute-done((f32[64,1152]{1,0:T(8,128)S(1)}, f32[64,1152]{1,0:T(8,128)S(1)}, u32[]{:S(2)}, u32[]{:S(2)}) %collective-permute-start.5) | collective-permute-done | bytes 294944 | tf_op jit(solution)/shard_map/ppermute | solution.py:294
  33.6 2.0 %collective-permute-start.6 = (f32[32,1536]{1,0:T(8,128)S(1)}, f32[32,1536]{1,0:T(8,128)S(1)}, u32[]{:S(2)}, u32[]{:S(2)}) collective-permute-start(f32[32,1536]{1,0:T(8,128)S(1)} %get-tuple-element.50), channel_id=1, source_target_pairs={{0,3},{1,2},{2,1},{3,0},{4,7},{5,6},{6,5},{7,4},{8,11},{9,10},{10,... | collective-permute-start | bytes 589832 | tf_op jit(solution)/shard_map/ppermute | solution.py:294
  35.6 1.3 %collective-permute-start.10 = (f32[112,128]{1,0:T(8,128)S(1)}, f32[112,128]{1,0:T(8,128)S(1)}, u32[]{:S(2)}, u32[]{:S(2)}) collective-permute-start(f32[112,128]{1,0:T(8,128)S(1)} %sum_four.2.refs_0_), channel_id=1, source_target_pairs={{0,192},{4,196},{8,200},{12,204},{16,208},{20,212},{24,216},{28,22... | collective-permute-start | bytes 172040 | tf_op jit(solution)/shard_map/ppermute | solution.py:277
  36.9 4.0 %collective-permute-done.10.refs_1_ = f32[112,128]{1,0:T(8,128)S(1)} collective-permute-done((f32[112,128]{1,0:T(8,128)S(1)}, f32[112,128]{1,0:T(8,128)S(1)}, u32[]{:S(2)}, u32[]{:S(2)}) %collective-permute-start.10) | collective-permute-done | bytes 57376 | tf_op jit(solution)/shard_map/ppermute | solution.py:277
  40.9 1.2 %collective-permute-start.13 = (f32[112,128]{1,0:T(8,128)S(1)}, f32[112,128]{1,0:T(8,128)S(1)}, u32[]{:S(2)}, u32[]{:S(2)}) collective-permute-start(f32[112,128]{1,0:T(8,128)S(1)} %sum_two.1.refs_0_), channel_id=1, source_target_pairs={{0,88},{4,92},{8,80},{12,84},{16,72},{20,76},{24,64},{28,68},{32,1... | collective-permute-start | bytes 172040 | tf_op jit(solution)/shard_map/ppermute | solution.py:277
  42.0 0.2 collective-permute-start.12
  42.3 3.5 %collective-permute-start.11 = (f32[112,128]{1,0:T(8,128)S(1)}, f32[112,128]{1,0:T(8,128)S(1)}, u32[]{:S(2)}, u32[]{:S(2)}) collective-permute-start(f32[112,128]{1,0:T(8,128)S(1)} %sum_two.1.refs_0_), channel_id=1, source_target_pairs={{0,24},{4,28},{8,16},{12,20},{16,8},{20,12},{24,0},{28,4},{32,56},... | collective-permute-start | bytes 172040 | tf_op jit(solution)/shard_map/ppermute | solution.py:277
  45.7 1.0 %back_inner.5.inner = f32[32,1024]{1,0:T(8,128)S(1)} custom-call(f32[864,1024]{1,0:T(8,128)S(1)} %back_terms.1.terms, s32[27,1024]{1,0:T(8,128)S(1)} %copy-done.2, f32[32,1024]{1,0:T(8,128)S(1)} %back_inner.4.refs_0_), custom_call_target="tpu_custom_call", output_to_operand_aliasing={{}: (2, {})} | custom-call | flops 1073741824 | bytes 3911680 | tf_op jit(solution)/shard_map/back_inner/pallas_call | solution.py:254
  46.7 1.5 %collective-permute-done.13.refs_3_ = f32[112,128]{1,0:T(8,128)S(1)} collective-permute-done((f32[112,128]{1,0:T(8,128)S(1)}, f32[112,128]{1,0:T(8,128)S(1)}, u32[]{:S(2)}, u32[]{:S(2)}) %collective-permute-start.13) | collective-permute-done | bytes 57376 | tf_op jit(solution)/shard_map/ppermute | solution.py:277
  48.3 0.1 collective-permute-start.16
  48.4 0.3 collective-permute-start.15
  48.6 2.4 %collective-permute-start.14 = (f32[112,128]{1,0:T(8,128)S(1)}, f32[112,128]{1,0:T(8,128)S(1)}, u32[]{:S(2)}, u32[]{:S(2)}) collective-permute-start(f32[112,128]{1,0:T(8,128)S(1)} %sum_four.3.refs_0_), channel_id=1, source_target_pairs={{0,8},{4,12},{8,0},{12,4},{16,24},{20,28},{24,16},{28,20},{32,40},... | collective-permute-start | bytes 172040 | tf_op jit(solution)/shard_map/ppermute | solution.py:277
  51.0 1.5 %edge.1 = (bf16[32,1024]{1,0:T(8,128)(2,1)}, bf16[32,1024]{1,0:T(8,128)(2,1)}) custom-call(f32[864,1024]{1,0:T(8,128)S(1)} %back_terms.1.terms, s32[27,1024]{1,0:T(8,128)S(1)} %copy-done.2, bf16[864,128]{1,0:T(8,128)(2,1)S(1)} %bitcast.4, bf16[64,128]{1,0:T(8,128)(2,1)S(1)} %collective-permute-done.near_ref, ...), custom_call_target="tpu_custom_call" | custom-call | flops 2147483648 | bytes 4788224 | tf_op jit(solution)/shard_map/edge/pallas_call | solution.py:254
  52.5 0.4 collective-permute-done.14.refs_1_
  52.9 5.8 %collective-permute-start.17 = (f32[448,128]{1,0:T(8,128)S(1)}, f32[448,128]{1,0:T(8,128)S(1)}, u32[]{:S(2)}, u32[]{:S(2)}) collective-permute-start(f32[448,128]{1,0:T(8,128)S(1)} %join.3.even_ref), channel_id=1, source_target_pairs={{0,4},{4,0},{8,12},{12,8},{16,20},{20,16},{24,28},{28,24},{32,36},... | collective-permute-start | bytes 688136 | tf_op jit(solution)/shard_map/ppermute | solution.py:277
  58.7 1.1 %collective-permute-done.17.odd_ref = f32[448,128]{1,0:T(8,128)S(1)} collective-permute-done((f32[448,128]{1,0:T(8,128)S(1)}, f32[448,128]{1,0:T(8,128)S(1)}, u32[]{:S(2)}, u32[]{:S(2)}) %collective-permute-start.17) | collective-permute-done | bytes 229408 | tf_op jit(solution)/shard_map/ppermute | solution.py:277
  59.8 0.8 %place.1 = f32[864,128]{1,0:T(8,128)} custom-call(f32[448,128]{1,0:T(8,128)S(1)} %join.3.even_ref, f32[448,128]{1,0:T(8,128)S(1)} %collective-permute-done.17.odd_ref), custom_call_target="tpu_custom_call" | custom-call | bytes 901120 | tf_op jit(solution)/shard_map/place/pallas_call | solution.py:254
  (29 shorter events, 0.3 us)
Async XLA Ops:
  0.6 5.7 %copy-start.1 = (bf16[32,1024]{1,0:T(8,128)(2,1)S(1)}, bf16[32,1024]{1,0:T(8,128)(2,1)}, u32[]{:S(2)}) copy-start(bf16[32,1024]{1,0:T(8,128)(2,1)} %refs_0_.1) | copy-start | bytes 196612
  0.6 7.7 %copy-start.3 = (bf16[32,1024]{1,0:T(8,128)(2,1)S(1)}, bf16[32,1024]{1,0:T(8,128)(2,1)}, u32[]{:S(2)}) copy-start(bf16[32,1024]{1,0:T(8,128)(2,1)} %x_ref.3) | copy-start | bytes 196612
  0.7 7.7 %copy-start.2 = (s32[27,1024]{1,0:T(8,128)S(1)}, s32[27,1024]{1,0:T(8,128)}, u32[]{:S(2)}) copy-start(s32[27,1024]{1,0:T(8,128)} %rule_ref.11) | copy-start | bytes 331780
  0.7 5.6 %collective-permute-start.2 = (bf16[32,1024]{1,0:T(8,128)(2,1)}, bf16[32,1024]{1,0:T(8,128)(2,1)S(1)}, u32[]{:S(2)}, u32[]{:S(2)}) collective-permute-start(bf16[32,1024]{1,0:T(8,128)(2,1)} %refs_0_.1), channel_id=1, source_target_pairs={{0,1},{1,0},{2,3},{3,2},{4,5},{5,4},{6,7},{7,6},{8,9},{9,8},{10,11... | collective-permute-start | bytes 196616 | tf_op jit(solution)/shard_map/ppermute | solution.py:294
  4.2 7.9 %collective-permute-start = (bf16[64,128]{1,0:T(8,128)(2,1)}, bf16[64,128]{1,0:T(8,128)(2,1)S(1)}, u32[]{:S(2)}, u32[]{:S(2)}) collective-permute-start(bf16[64,128]{1,0:T(8,128)(2,1)} %get-tuple-element.33), channel_id=1, source_target_pairs={{0,4},{4,0},{8,12},{12,8},{16,20},{20,16},{24,28},{28,24},{32,36},... | collective-permute-start | bytes 49160 | tf_op jit(solution)/shard_map/ppermute | solution.py:277
  5.4 6.8 %collective-permute-start.1 = (bf16[64,128]{1,0:T(8,128)(2,1)}, bf16[64,128]{1,0:T(8,128)(2,1)S(1)}, u32[]{:S(2)}, u32[]{:S(2)}) collective-permute-start(bf16[64,128]{1,0:T(8,128)(2,1)} %get-tuple-element.34), channel_id=1, source_target_pairs={{0,252},{4,8},{8,4},{12,16},{16,12},{20,24},{24,20},{28,32},{32,28... | collective-permute-start | bytes 49160 | tf_op jit(solution)/shard_map/ppermute | solution.py:283
  6.3 5.9 %collective-permute-start.3 = (bf16[64,1024]{1,0:T(8,128)(2,1)S(1)}, bf16[64,1024]{1,0:T(8,128)(2,1)S(1)}, u32[]{:S(2)}, u32[]{:S(2)}) collective-permute-start(bf16[64,1024]{1,0:T(8,128)(2,1)S(1)} %join.2.pair_ref), channel_id=1, source_target_pairs={{0,3},{1,2},{2,1},{3,0},{4,7},{5,6},{6,5},{7,4},{8,11},{9,10},{10,... | collective-permute-start | bytes 393224 | tf_op jit(solution)/shard_map/ppermute | solution.py:294
  12.2 8.3 %copy-start = (bf16[27,32,128]{2,1,0:T(8,128)(2,1)S(1)}, bf16[27,32,128]{2,1,0:T(8,128)(2,1)}, u32[]{:S(2)}) copy-start(bf16[27,32,128]{2,1,0:T(8,128)(2,1)} %param.5) | copy-start | bytes 663556
  12.9 8.6 %collective-permute-start.4 = (f32[448,128]{1,0:T(8,128)S(1)}, f32[448,128]{1,0:T(8,128)S(1)}, u32[]{:S(2)}, u32[]{:S(2)}) collective-permute-start(f32[448,128]{1,0:T(8,128)S(1)} %get-tuple-element.40), channel_id=1, source_target_pairs={{0,4},{4,0},{8,12},{12,8},{16,20},{20,16},{24,28},{28,24},{32,36},... | collective-permute-start | bytes 688136 | tf_op jit(solution)/shard_map/ppermute | solution.py:277
  21.6 5.0 %collective-permute-start.7 = (f32[112,128]{1,0:T(8,128)S(1)}, f32[112,128]{1,0:T(8,128)S(1)}, u32[]{:S(2)}, u32[]{:S(2)}) collective-permute-start(f32[112,128]{1,0:T(8,128)S(1)} %get-tuple-element.43), channel_id=1, source_target_pairs={{0,8},{4,12},{8,0},{12,4},{16,24},{20,28},{24,16},{28,20},{32,40},... | collective-permute-start | bytes 172040 | tf_op jit(solution)/shard_map/ppermute | solution.py:277
  21.7 4.9 %collective-permute-start.8 = (f32[112,128]{1,0:T(8,128)S(1)}, f32[112,128]{1,0:T(8,128)S(1)}, u32[]{:S(2)}, u32[]{:S(2)}) collective-permute-start(f32[112,128]{1,0:T(8,128)S(1)} %get-tuple-element.44), channel_id=1, source_target_pairs={{0,32},{4,36},{8,40},{12,44},{16,48},{20,52},{24,56},{28,60},{32,0... | collective-permute-start | bytes 172040 | tf_op jit(solution)/shard_map/ppermute | solution.py:277
  21.8 4.8 %collective-permute-start.9 = (f32[112,128]{1,0:T(8,128)S(1)}, f32[112,128]{1,0:T(8,128)S(1)}, u32[]{:S(2)}, u32[]{:S(2)}) collective-permute-start(f32[112,128]{1,0:T(8,128)S(1)} %get-tuple-element.45), channel_id=1, source_target_pairs={{0,40},{4,44},{8,32},{12,36},{16,56},{20,60},{24,48},{28,52},{32,8... | collective-permute-start | bytes 172040 | tf_op jit(solution)/shard_map/ppermute | solution.py:277
  26.2 7.4 %collective-permute-start.5 = (f32[64,1152]{1,0:T(8,128)S(1)}, f32[64,1152]{1,0:T(8,128)S(1)}, u32[]{:S(2)}, u32[]{:S(2)}) collective-permute-start(f32[64,1152]{1,0:T(8,128)S(1)} %get-tuple-element.46), channel_id=1, source_target_pairs={{0,1},{1,0},{2,3},{3,2},{4,5},{5,4},{6,7},{7,6},{8,9},{9,8},{10,11... | collective-permute-start | bytes 884744 | tf_op jit(solution)/shard_map/ppermute | solution.py:294
  33.6 17.4 %collective-permute-start.6 = (f32[32,1536]{1,0:T(8,128)S(1)}, f32[32,1536]{1,0:T(8,128)S(1)}, u32[]{:S(2)}, u32[]{:S(2)}) collective-permute-start(f32[32,1536]{1,0:T(8,128)S(1)} %get-tuple-element.50), channel_id=1, source_target_pairs={{0,3},{1,2},{2,1},{3,0},{4,7},{5,6},{6,5},{7,4},{8,11},{9,10},{10,... | collective-permute-start | bytes 589832 | tf_op jit(solution)/shard_map/ppermute | solution.py:294
  35.6 5.2 %collective-permute-start.10 = (f32[112,128]{1,0:T(8,128)S(1)}, f32[112,128]{1,0:T(8,128)S(1)}, u32[]{:S(2)}, u32[]{:S(2)}) collective-permute-start(f32[112,128]{1,0:T(8,128)S(1)} %sum_four.2.refs_0_), channel_id=1, source_target_pairs={{0,192},{4,196},{8,200},{12,204},{16,208},{20,212},{24,216},{28,22... | collective-permute-start | bytes 172040 | tf_op jit(solution)/shard_map/ppermute | solution.py:277
  40.9 7.4 %collective-permute-start.13 = (f32[112,128]{1,0:T(8,128)S(1)}, f32[112,128]{1,0:T(8,128)S(1)}, u32[]{:S(2)}, u32[]{:S(2)}) collective-permute-start(f32[112,128]{1,0:T(8,128)S(1)} %sum_two.1.refs_0_), channel_id=1, source_target_pairs={{0,88},{4,92},{8,80},{12,84},{16,72},{20,76},{24,64},{28,68},{32,1... | collective-permute-start | bytes 172040 | tf_op jit(solution)/shard_map/ppermute | solution.py:277
  42.0 6.2 %collective-permute-start.12 = (f32[112,128]{1,0:T(8,128)S(1)}, f32[112,128]{1,0:T(8,128)S(1)}, u32[]{:S(2)}, u32[]{:S(2)}) collective-permute-start(f32[112,128]{1,0:T(8,128)S(1)} %sum_two.1.refs_0_), channel_id=1, source_target_pairs={{0,64},{4,68},{8,72},{12,76},{16,80},{20,84},{24,88},{28,92},{32,9... | collective-permute-start | bytes 172040 | tf_op jit(solution)/shard_map/ppermute | solution.py:277
  42.3 6.0 %collective-permute-start.11 = (f32[112,128]{1,0:T(8,128)S(1)}, f32[112,128]{1,0:T(8,128)S(1)}, u32[]{:S(2)}, u32[]{:S(2)}) collective-permute-start(f32[112,128]{1,0:T(8,128)S(1)} %sum_two.1.refs_0_), channel_id=1, source_target_pairs={{0,24},{4,28},{8,16},{12,20},{16,8},{20,12},{24,0},{28,4},{32,56},... | collective-permute-start | bytes 172040 | tf_op jit(solution)/shard_map/ppermute | solution.py:277
  48.3 4.3 %collective-permute-start.16 = (f32[112,128]{1,0:T(8,128)S(1)}, f32[112,128]{1,0:T(8,128)S(1)}, u32[]{:S(2)}, u32[]{:S(2)}) collective-permute-start(f32[112,128]{1,0:T(8,128)S(1)} %sum_four.3.refs_0_), channel_id=1, source_target_pairs={{0,40},{4,44},{8,32},{12,36},{16,56},{20,60},{24,48},{28,52},{32,8... | collective-permute-start | bytes 172040 | tf_op jit(solution)/shard_map/ppermute | solution.py:277
  48.4 4.2 %collective-permute-start.15 = (f32[112,128]{1,0:T(8,128)S(1)}, f32[112,128]{1,0:T(8,128)S(1)}, u32[]{:S(2)}, u32[]{:S(2)}) collective-permute-start(f32[112,128]{1,0:T(8,128)S(1)} %sum_four.3.refs_0_), channel_id=1, source_target_pairs={{0,32},{4,36},{8,40},{12,44},{16,48},{20,52},{24,56},{28,60},{32,0... | collective-permute-start | bytes 172040 | tf_op jit(solution)/shard_map/ppermute | solution.py:277
  48.6 4.3 %collective-permute-start.14 = (f32[112,128]{1,0:T(8,128)S(1)}, f32[112,128]{1,0:T(8,128)S(1)}, u32[]{:S(2)}, u32[]{:S(2)}) collective-permute-start(f32[112,128]{1,0:T(8,128)S(1)} %sum_four.3.refs_0_), channel_id=1, source_target_pairs={{0,8},{4,12},{8,0},{12,4},{16,24},{20,28},{24,16},{28,20},{32,40},... | collective-permute-start | bytes 172040 | tf_op jit(solution)/shard_map/ppermute | solution.py:277
  52.9 6.9 %collective-permute-start.17 = (f32[448,128]{1,0:T(8,128)S(1)}, f32[448,128]{1,0:T(8,128)S(1)}, u32[]{:S(2)}, u32[]{:S(2)}) collective-permute-start(f32[448,128]{1,0:T(8,128)S(1)} %join.3.even_ref), channel_id=1, source_target_pairs={{0,4},{4,0},{8,12},{12,8},{16,20},{20,16},{24,28},{28,24},{32,36},... | collective-permute-start | bytes 688136 | tf_op jit(solution)/shard_map/ppermute | solution.py:277

commit v15 on v13

--- a/solution.py
+++ b/solution.py
@@ -13,7 +13,7 @@
 PART = 112
 INNER = tuple(range(2, 8))
 EDGE = (0, 1)
-X1, X3, Z1, Z2, Z6 = 2, 6, 8, 16, 48
+X1, X3, Z1, Z3, Z6 = 2, 6, 8, 24, 48
 ORDER = (0, 1, 3, 2)
 VMEM = pl.BlockSpec(memory_space=pltpu.VMEM)
 
@@ -40,7 +40,9 @@
 
 def own_part():
     place = lax.axis_index("blk")
-    return (place & 1) | ((place ^ (place >> 1)) & 2) | ((place >> 1) & 4)
+    over_x = (place >> 1) ^ (place >> 2)
+    over_z = (place >> 3) ^ (place >> 4) ^ (place >> 5)
+    return (place & 1) | ((over_x & 1) << 1) | ((over_z & 1) << 2)
 
 
 def tile_span(t):
@@ -343,19 +345,19 @@
     inner = inner_part((2, 3))
     others = after(others, inner)
     total = call(sum_kernel, f32(PART, 128), (pieces[0], *others), name="sum_four")
-    came = swap(total, Z6)
+    came = swap(total, X3)
     inner = inner_part((4, 5), inner)
-    ours, first = after((ours, first), inner)
+    came, = after((came,), inner)
+    total = call(sum_kernel, f32(PART, 128), (total, came), name="sum_two")
+    others = [swap(total, m) for m in (Z3, Z6, Z3 ^ Z6)]
+    ours, first = after((ours, first), total)
     own, second = call(
         middle_kernel, (f32(32, VOX), f32(32, VOX + 4 * FACE)), (ours, first, near, far),
         name="middle",
     )
     second = over_ch(second, 3)
-    came, = after((came,), own)
-    total = call(sum_kernel, f32(PART, 128), (total, came), name="sum_two")
-    others = [swap(total, m) for m in (X3, Z2, X3 | Z2)]
     inner = inner_part((6, 7), inner)
-    others = after(others, inner)
+    others = after(others, inner, own)
     total = call(sum_kernel, f32(PART, 128), (total, *others), name="sum_four")
     others = [swap(total, m) for m in (X1, Z1, X1 | Z1)]
     output, grad_features = call(

time: 52.6 us -> 52.9 us (level)
    ppermute x13, waiting for transfers between devices: 2.19 us -> 4.3 us  [swap(): return lax.ppermute(value, 'blk', [(i, i ^ mask) for i in range(count)])]
    ppermute x4, waiting for transfers between devices: 1.79 us -> 0.01 us  [over_ch(): return lax.ppermute(value, 'ch', [(i, i ^ mask) for i in range(4)])]
  transfers between devices with their start and end apart: 18 -> 18, of which waited for: 5 -> 4; matrix products, arithmetic and copies ran while one was open for 0% -> 0% of each run, Pallas kernels for 26% -> 26%
where the time goes in v15:
time: 52.9 us; the launch traced here: 52.7 us
  starting transfers between devices  32.5 us (61%)
  Pallas kernels  15 us (28%)
  waiting for transfers between devices  4.31 us (8%)
  between operations  0.83 us (2%)
    ppermute x13, starting transfers between devices, swap(): return lax.ppermute(value, 'blk', [(i, i ^ mask) for i in range(count)])  24.9 us
    pallas_call x16, Pallas kernels, call(): pl.pallas_call(kernel, out_shape=outs, in_specs=[VMEM] * len(args), out_s...  13.7 us
    ppermute x4, starting transfers between devices, over_ch(): return lax.ppermute(value, 'ch', [(i, i ^ mask) for i in range(4)])  6.67 us
    ppermute x13, waiting for transfers between devices, swap(): return lax.ppermute(value, 'blk', [(i, i ^ mask) for i in range(count)])  4.3 us
    pallas_call x1, Pallas kernels, per_device(): pl.pallas_call(faces_kernel, out_shape=(bf16(64, FACE),) * 2, grid=(1,),...  1.37 us
  transfers between devices with their start and end apart: 18, of which 4 were waited for; matrix products, arithmetic and copies ran while one was open for 0% of the time, Pallas kernels for 26%

profile of v15, /device:TPU:1, one launch (start us, length us, event | category | flops | bytes accessed | tf_op | source)
XLA Modules:
  0.0 52.7 jit_solution(2323893673145159900)
XLA Ops:
  0.7 2.2 %collective-permute-start.2 = (bf16[32,1024]{1,0:T(8,128)(2,1)}, bf16[32,1024]{1,0:T(8,128)(2,1)S(1)}, u32[]{:S(2)}, u32[]{:S(2)}) collective-permute-start(bf16[32,1024]{1,0:T(8,128)(2,1)} %refs_0_.1), channel_id=1, source_target_pairs={{0,1},{1,0},{2,3},{3,2},{4,5},{5,4},{6,7},{7,6},{8,9},{9,8},{10,11... | collective-permute-start | bytes 196616 | tf_op jit(solution)/shard_map/ppermute | solution.py:296
  2.9 1.4 %faces.1 = (bf16[64,128]{1,0:T(8,128)(2,1)}, bf16[64,128]{1,0:T(8,128)(2,1)}) custom-call(bf16[32,1024]{1,0:T(8,128)(2,1)} %x_ref.3, bf16[32,1024]{1,0:T(8,128)(2,1)} %refs_0_.1), custom_call_target="tpu_custom_call" | custom-call | flops 1073741824 | bytes 65536 | tf_op jit(solution)/shard_map/faces/pallas_call | solution.py:301
  4.2 1.1 %collective-permute-start = (bf16[64,128]{1,0:T(8,128)(2,1)}, bf16[64,128]{1,0:T(8,128)(2,1)S(1)}, u32[]{:S(2)}, u32[]{:S(2)}) collective-permute-start(bf16[64,128]{1,0:T(8,128)(2,1)} %get-tuple-element.33), channel_id=1, source_target_pairs={{0,4},{4,0},{8,12},{12,8},{16,20},{20,16},{24,28},{28,24},{32,36},... | collective-permute-start | bytes 49160 | tf_op jit(solution)/shard_map/ppermute | solution.py:279
  5.4 0.9 %collective-permute-start.1 = (bf16[64,128]{1,0:T(8,128)(2,1)}, bf16[64,128]{1,0:T(8,128)(2,1)S(1)}, u32[]{:S(2)}, u32[]{:S(2)}) collective-permute-start(bf16[64,128]{1,0:T(8,128)(2,1)} %get-tuple-element.34), channel_id=1, source_target_pairs={{0,252},{4,8},{8,4},{12,16},{16,12},{20,24},{24,20},{28,32},{32,28... | collective-permute-start | bytes 49160 | tf_op jit(solution)/shard_map/ppermute | solution.py:285
  6.3 2.0 %collective-permute-start.3 = (bf16[64,1024]{1,0:T(8,128)(2,1)S(1)}, bf16[64,1024]{1,0:T(8,128)(2,1)S(1)}, u32[]{:S(2)}, u32[]{:S(2)}) collective-permute-start(bf16[64,1024]{1,0:T(8,128)(2,1)S(1)} %join.2.pair_ref), channel_id=1, source_target_pairs={{0,3},{1,2},{2,1},{3,0},{4,7},{5,6},{6,5},{7,4},{8,11},{9,10},{10,... | collective-permute-start | bytes 393224 | tf_op jit(solution)/shard_map/ppermute | solution.py:296
  8.3 3.9 %gather.1.dense_in = bf16[864,1024]{1,0:T(8,128)(2,1)S(1)} custom-call(bf16[32,1024]{1,0:T(8,128)(2,1)S(1)} %copy-done.3, s32[27,1024]{1,0:T(8,128)S(1)} %copy-done.2), custom_call_target="tpu_custom_call" | custom-call | flops 3221225472 | bytes 1945600 | tf_op jit(solution)/shard_map/gather/pallas_call | solution.py:256
  12.2 0.0 copy-start
  12.2 0.7 %weight_terms.1 = (bf16[864,1024]{1,0:T(8,128)(2,1)S(1)}, bf16[128,1024]{1,0:T(8,128)(2,1)S(1)}, f32[448,128]{1,0:T(8,128)S(1)}, f32[448,128]{1,0:T(8,128)S(1)}) custom-call(bf16[864,1024]{1,0:T(8,128)(2,1)S(1)} %gather.1.dense_in, s32[27,1024]{1,0:T(8,128)S(1)} %copy-done.2, ...), custom_call_target="tpu_custom_call", output_to_operand_aliasing={{0}: (0, {})} | custom-call | flops 1073741824 | bytes 4665344 | tf_op jit(solution)/shard_map/weight_terms/pallas_call | solution.py:256
  12.9 7.5 %collective-permute-start.4 = (f32[448,128]{1,0:T(8,128)S(1)}, f32[448,128]{1,0:T(8,128)S(1)}, u32[]{:S(2)}, u32[]{:S(2)}) collective-permute-start(f32[448,128]{1,0:T(8,128)S(1)} %get-tuple-element.40), channel_id=1, source_target_pairs={{0,4},{4,0},{8,12},{12,8},{16,20},{20,16},{24,28},{28,24},{32,36},... | collective-permute-start | bytes 688136 | tf_op jit(solution)/shard_map/ppermute | solution.py:279
  20.5 0.6 %back_terms.1.terms = f32[864,1024]{1,0:T(8,128)S(1)} custom-call(bf16[864,128]{1,0:T(8,128)(2,1)S(1)} %bitcast.2, bf16[128,1024]{1,0:T(8,128)(2,1)S(1)} %get-tuple-element.35.grad_ref), custom_call_target="tpu_custom_call" | custom-call | flops 1073741824 | bytes 4022272 | tf_op jit(solution)/shard_map/back_terms/pallas_call | solution.py:256
  21.1 0.5 forward.1
  21.6 0.1 collective-permute-start.6
  21.7 0.1 collective-permute-start.7
  21.8 2.5 %collective-permute-start.8 = (f32[112,128]{1,0:T(8,128)S(1)}, f32[112,128]{1,0:T(8,128)S(1)}, u32[]{:S(2)}, u32[]{:S(2)}) collective-permute-start(f32[112,128]{1,0:T(8,128)S(1)} %get-tuple-element.45), channel_id=1, source_target_pairs={{0,40},{4,44},{8,32},{12,36},{16,56},{20,60},{24,48},{28,52},{32,8... | collective-permute-start | bytes 172040 | tf_op jit(solution)/shard_map/ppermute | solution.py:279
  24.4 0.3 collective-permute-start.5
  24.7 1.8 %back_inner.3.refs_0_ = f32[32,1024]{1,0:T(8,128)S(1)} custom-call(f32[864,1024]{1,0:T(8,128)S(1)} %back_terms.1.terms, s32[27,1024]{1,0:T(8,128)S(1)} %copy-done.2), custom_call_target="tpu_custom_call" | custom-call | flops 2147483648 | bytes 3780608 | tf_op jit(solution)/shard_map/back_inner/pallas_call | solution.py:256
  26.5 0.1 collective-permute-done.8.refs_3_
  26.7 0.1 collective-permute-start.9
  26.8 1.8 %back_inner.4.refs_0_ = f32[32,1024]{1,0:T(8,128)S(1)} custom-call(f32[864,1024]{1,0:T(8,128)S(1)} %back_terms.1.terms, s32[27,1024]{1,0:T(8,128)S(1)} %copy-done.2, f32[32,1024]{1,0:T(8,128)S(1)} %back_inner.3.refs_0_), custom_call_target="tpu_custom_call", output_to_operand_aliasing={{}: (2, {})} | custom-call | flops 2147483648 | bytes 3911680 | tf_op jit(solution)/shard_map/back_inner/pallas_call | solution.py:256
  28.6 2.4 %collective-permute-done.9.refs_1_ = f32[112,128]{1,0:T(8,128)S(1)} collective-permute-done((f32[112,128]{1,0:T(8,128)S(1)}, f32[112,128]{1,0:T(8,128)S(1)}, u32[]{:S(2)}, u32[]{:S(2)}) %collective-permute-start.9) | collective-permute-done | bytes 57376 | tf_op jit(solution)/shard_map/ppermute | solution.py:279
  31.0 1.8 %collective-permute-start.13 = (f32[112,128]{1,0:T(8,128)S(1)}, f32[112,128]{1,0:T(8,128)S(1)}, u32[]{:S(2)}, u32[]{:S(2)}) collective-permute-start(f32[112,128]{1,0:T(8,128)S(1)} %sum_two.1.refs_0_), channel_id=1, source_target_pairs={{0,160},{4,164},{8,168},{12,172},{16,176},{20,180},{24,184},{28,18... | collective-permute-start | bytes 172040 | tf_op jit(solution)/shard_map/ppermute | solution.py:279
  32.8 4.0 %collective-permute-start.11 = (f32[112,128]{1,0:T(8,128)S(1)}, f32[112,128]{1,0:T(8,128)S(1)}, u32[]{:S(2)}, u32[]{:S(2)}) collective-permute-start(f32[112,128]{1,0:T(8,128)S(1)} %sum_two.1.refs_0_), channel_id=1, source_target_pairs={{0,96},{4,100},{8,104},{12,108},{16,112},{20,116},{24,120},{28,124... | collective-permute-start | bytes 172040 | tf_op jit(solution)/shard_map/ppermute | solution.py:279
  36.8 2.2 %collective-permute-start.10 = (f32[32,1536]{1,0:T(8,128)S(1)}, f32[32,1536]{1,0:T(8,128)S(1)}, u32[]{:S(2)}, u32[]{:S(2)}) collective-permute-start(f32[32,1536]{1,0:T(8,128)S(1)} %get-tuple-element.54), channel_id=1, source_target_pairs={{0,3},{1,2},{2,1},{3,0},{4,7},{5,6},{6,5},{7,4},{8,11},{9,10},{10,... | collective-permute-start | bytes 589832 | tf_op jit(solution)/shard_map/ppermute | solution.py:296
  39.0 1.8 %back_inner.5.inner = f32[32,1024]{1,0:T(8,128)S(1)} custom-call(f32[864,1024]{1,0:T(8,128)S(1)} %back_terms.1.terms, s32[27,1024]{1,0:T(8,128)S(1)} %copy-done.2, f32[32,1024]{1,0:T(8,128)S(1)} %back_inner.4.refs_0_), custom_call_target="tpu_custom_call", output_to_operand_aliasing={{}: (2, {})} | custom-call | flops 2147483648 | bytes 3911680 | tf_op jit(solution)/shard_map/back_inner/pallas_call | solution.py:256
  40.9 0.1 collective-permute-start.16
  41.0 1.1 %collective-permute-start.15 = (f32[112,128]{1,0:T(8,128)S(1)}, f32[112,128]{1,0:T(8,128)S(1)}, u32[]{:S(2)}, u32[]{:S(2)}) collective-permute-start(f32[112,128]{1,0:T(8,128)S(1)} %sum_four.3.refs_0_), channel_id=1, source_target_pairs={{0,32},{4,36},{8,40},{12,44},{16,48},{20,52},{24,56},{28,60},{32,0... | collective-permute-start | bytes 172040 | tf_op jit(solution)/shard_map/ppermute | solution.py:279
  42.0 1.6 %collective-permute-start.14 = (f32[112,128]{1,0:T(8,128)S(1)}, f32[112,128]{1,0:T(8,128)S(1)}, u32[]{:S(2)}, u32[]{:S(2)}) collective-permute-start(f32[112,128]{1,0:T(8,128)S(1)} %sum_four.3.refs_0_), channel_id=1, source_target_pairs={{0,8},{4,12},{8,0},{12,4},{16,24},{20,28},{24,16},{28,20},{32,40},... | collective-permute-start | bytes 172040 | tf_op jit(solution)/shard_map/ppermute | solution.py:279
  43.6 1.5 %edge.1 = (bf16[32,1024]{1,0:T(8,128)(2,1)}, bf16[32,1024]{1,0:T(8,128)(2,1)}) custom-call(f32[864,1024]{1,0:T(8,128)S(1)} %back_terms.1.terms, s32[27,1024]{1,0:T(8,128)S(1)} %copy-done.2, bf16[864,128]{1,0:T(8,128)(2,1)S(1)} %bitcast.4, bf16[64,128]{1,0:T(8,128)(2,1)S(1)} %collective-permute-done.near_ref, ...), custom_call_target="tpu_custom_call" | custom-call | flops 2147483648 | bytes 4788224 | tf_op jit(solution)/shard_map/edge/pallas_call | solution.py:256
  45.1 0.7 %collective-permute-done.14.refs_1_ = f32[112,128]{1,0:T(8,128)S(1)} collective-permute-done((f32[112,128]{1,0:T(8,128)S(1)}, f32[112,128]{1,0:T(8,128)S(1)}, u32[]{:S(2)}, u32[]{:S(2)}) %collective-permute-start.14) | collective-permute-done | bytes 57376 | tf_op jit(solution)/shard_map/ppermute | solution.py:279
  45.8 5.0 %collective-permute-start.17 = (f32[448,128]{1,0:T(8,128)S(1)}, f32[448,128]{1,0:T(8,128)S(1)}, u32[]{:S(2)}, u32[]{:S(2)}) collective-permute-start(f32[448,128]{1,0:T(8,128)S(1)} %join.3.even_ref), channel_id=1, source_target_pairs={{0,4},{4,0},{8,12},{12,8},{16,20},{20,16},{24,28},{28,24},{32,36},... | collective-permute-start | bytes 688136 | tf_op jit(solution)/shard_map/ppermute | solution.py:279
  50.8 1.1 %collective-permute-done.17.odd_ref = f32[448,128]{1,0:T(8,128)S(1)} collective-permute-done((f32[448,128]{1,0:T(8,128)S(1)}, f32[448,128]{1,0:T(8,128)S(1)}, u32[]{:S(2)}, u32[]{:S(2)}) %collective-permute-start.17) | collective-permute-done | bytes 229408 | tf_op jit(solution)/shard_map/ppermute | solution.py:279
  51.9 0.8 %place.1 = f32[864,128]{1,0:T(8,128)} custom-call(f32[448,128]{1,0:T(8,128)S(1)} %join.3.even_ref, f32[448,128]{1,0:T(8,128)S(1)} %collective-permute-done.17.odd_ref), custom_call_target="tpu_custom_call" | custom-call | bytes 901120 | tf_op jit(solution)/shard_map/place/pallas_call | solution.py:256
  (29 shorter events, 0.2 us)
Async XLA Ops:
  0.6 5.7 %copy-start.1 = (bf16[32,1024]{1,0:T(8,128)(2,1)S(1)}, bf16[32,1024]{1,0:T(8,128)(2,1)}, u32[]{:S(2)}) copy-start(bf16[32,1024]{1,0:T(8,128)(2,1)} %refs_0_.1) | copy-start | bytes 196612
  0.6 7.7 %copy-start.3 = (bf16[32,1024]{1,0:T(8,128)(2,1)S(1)}, bf16[32,1024]{1,0:T(8,128)(2,1)}, u32[]{:S(2)}) copy-start(bf16[32,1024]{1,0:T(8,128)(2,1)} %x_ref.3) | copy-start | bytes 196612
  0.7 7.7 %copy-start.2 = (s32[27,1024]{1,0:T(8,128)S(1)}, s32[27,1024]{1,0:T(8,128)}, u32[]{:S(2)}) copy-start(s32[27,1024]{1,0:T(8,128)} %rule_ref.11) | copy-start | bytes 331780
  0.7 5.6 %collective-permute-start.2 = (bf16[32,1024]{1,0:T(8,128)(2,1)}, bf16[32,1024]{1,0:T(8,128)(2,1)S(1)}, u32[]{:S(2)}, u32[]{:S(2)}) collective-permute-start(bf16[32,1024]{1,0:T(8,128)(2,1)} %refs_0_.1), channel_id=1, source_target_pairs={{0,1},{1,0},{2,3},{3,2},{4,5},{5,4},{6,7},{7,6},{8,9},{9,8},{10,11... | collective-permute-start | bytes 196616 | tf_op jit(solution)/shard_map/ppermute | solution.py:296
  4.2 7.9 %collective-permute-start = (bf16[64,128]{1,0:T(8,128)(2,1)}, bf16[64,128]{1,0:T(8,128)(2,1)S(1)}, u32[]{:S(2)}, u32[]{:S(2)}) collective-permute-start(bf16[64,128]{1,0:T(8,128)(2,1)} %get-tuple-element.33), channel_id=1, source_target_pairs={{0,4},{4,0},{8,12},{12,8},{16,20},{20,16},{24,28},{28,24},{32,36},... | collective-permute-start | bytes 49160 | tf_op jit(solution)/shard_map/ppermute | solution.py:279
  5.4 6.8 %collective-permute-start.1 = (bf16[64,128]{1,0:T(8,128)(2,1)}, bf16[64,128]{1,0:T(8,128)(2,1)S(1)}, u32[]{:S(2)}, u32[]{:S(2)}) collective-permute-start(bf16[64,128]{1,0:T(8,128)(2,1)} %get-tuple-element.34), channel_id=1, source_target_pairs={{0,252},{4,8},{8,4},{12,16},{16,12},{20,24},{24,20},{28,32},{32,28... | collective-permute-start | bytes 49160 | tf_op jit(solution)/shard_map/ppermute | solution.py:285
  6.3 5.9 %collective-permute-start.3 = (bf16[64,1024]{1,0:T(8,128)(2,1)S(1)}, bf16[64,1024]{1,0:T(8,128)(2,1)S(1)}, u32[]{:S(2)}, u32[]{:S(2)}) collective-permute-start(bf16[64,1024]{1,0:T(8,128)(2,1)S(1)} %join.2.pair_ref), channel_id=1, source_target_pairs={{0,3},{1,2},{2,1},{3,0},{4,7},{5,6},{6,5},{7,4},{8,11},{9,10},{10,... | collective-permute-start | bytes 393224 | tf_op jit(solution)/shard_map/ppermute | solution.py:296
  12.2 8.3 %copy-start = (bf16[27,32,128]{2,1,0:T(8,128)(2,1)S(1)}, bf16[27,32,128]{2,1,0:T(8,128)(2,1)}, u32[]{:S(2)}) copy-start(bf16[27,32,128]{2,1,0:T(8,128)(2,1)} %param.5) | copy-start | bytes 663556
  12.9 8.6 %collective-permute-start.4 = (f32[448,128]{1,0:T(8,128)S(1)}, f32[448,128]{1,0:T(8,128)S(1)}, u32[]{:S(2)}, u32[]{:S(2)}) collective-permute-start(f32[448,128]{1,0:T(8,128)S(1)} %get-tuple-element.40), channel_id=1, source_target_pairs={{0,4},{4,0},{8,12},{12,8},{16,20},{20,16},{24,28},{28,24},{32,36},... | collective-permute-start | bytes 688136 | tf_op jit(solution)/shard_map/ppermute | solution.py:279
  21.6 4.9 %collective-permute-start.6 = (f32[112,128]{1,0:T(8,128)S(1)}, f32[112,128]{1,0:T(8,128)S(1)}, u32[]{:S(2)}, u32[]{:S(2)}) collective-permute-start(f32[112,128]{1,0:T(8,128)S(1)} %get-tuple-element.43), channel_id=1, source_target_pairs={{0,8},{4,12},{8,0},{12,4},{16,24},{20,28},{24,16},{28,20},{32,40},... | collective-permute-start | bytes 172040 | tf_op jit(solution)/shard_map/ppermute | solution.py:279
  21.7 4.8 %collective-permute-start.7 = (f32[112,128]{1,0:T(8,128)S(1)}, f32[112,128]{1,0:T(8,128)S(1)}, u32[]{:S(2)}, u32[]{:S(2)}) collective-permute-start(f32[112,128]{1,0:T(8,128)S(1)} %get-tuple-element.44), channel_id=1, source_target_pairs={{0,32},{4,36},{8,40},{12,44},{16,48},{20,52},{24,56},{28,60},{32,0... | collective-permute-start | bytes 172040 | tf_op jit(solution)/shard_map/ppermute | solution.py:279
  21.8 4.8 %collective-permute-start.8 = (f32[112,128]{1,0:T(8,128)S(1)}, f32[112,128]{1,0:T(8,128)S(1)}, u32[]{:S(2)}, u32[]{:S(2)}) collective-permute-start(f32[112,128]{1,0:T(8,128)S(1)} %get-tuple-element.45), channel_id=1, source_target_pairs={{0,40},{4,44},{8,32},{12,36},{16,56},{20,60},{24,48},{28,52},{32,8... | collective-permute-start | bytes 172040 | tf_op jit(solution)/shard_map/ppermute | solution.py:279
  24.4 12.4 %collective-permute-start.5 = (f32[64,1152]{1,0:T(8,128)S(1)}, f32[64,1152]{1,0:T(8,128)S(1)}, u32[]{:S(2)}, u32[]{:S(2)}) collective-permute-start(f32[64,1152]{1,0:T(8,128)S(1)} %get-tuple-element.46), channel_id=1, source_target_pairs={{0,1},{1,0},{2,3},{3,2},{4,5},{5,4},{6,7},{7,6},{8,9},{9,8},{10,11... | collective-permute-start | bytes 884744 | tf_op jit(solution)/shard_map/ppermute | solution.py:296
  26.7 4.3 %collective-permute-start.9 = (f32[112,128]{1,0:T(8,128)S(1)}, f32[112,128]{1,0:T(8,128)S(1)}, u32[]{:S(2)}, u32[]{:S(2)}) collective-permute-start(f32[112,128]{1,0:T(8,128)S(1)} %sum_four.2.refs_0_), channel_id=1, source_target_pairs={{0,24},{4,28},{8,16},{12,20},{16,8},{20,12},{24,0},{28,4},{32,56},... | collective-permute-start | bytes 172040 | tf_op jit(solution)/shard_map/ppermute | solution.py:279
  31.0 9.8 %collective-permute-start.13 = (f32[112,128]{1,0:T(8,128)S(1)}, f32[112,128]{1,0:T(8,128)S(1)}, u32[]{:S(2)}, u32[]{:S(2)}) collective-permute-start(f32[112,128]{1,0:T(8,128)S(1)} %sum_two.1.refs_0_), channel_id=1, source_target_pairs={{0,160},{4,164},{8,168},{12,172},{16,176},{20,180},{24,184},{28,18... | collective-permute-start | bytes 172040 | tf_op jit(solution)/shard_map/ppermute | solution.py:279
  32.8 8.0 %collective-permute-start.12 = (f32[112,128]{1,0:T(8,128)S(1)}, f32[112,128]{1,0:T(8,128)S(1)}, u32[]{:S(2)}, u32[]{:S(2)}) collective-permute-start(f32[112,128]{1,0:T(8,128)S(1)} %sum_two.1.refs_0_), channel_id=1, source_target_pairs={{0,192},{4,196},{8,200},{12,204},{16,208},{20,212},{24,216},{28,22... | collective-permute-start | bytes 172040 | tf_op jit(solution)/shard_map/ppermute | solution.py:279
  32.8 8.0 %collective-permute-start.11 = (f32[112,128]{1,0:T(8,128)S(1)}, f32[112,128]{1,0:T(8,128)S(1)}, u32[]{:S(2)}, u32[]{:S(2)}) collective-permute-start(f32[112,128]{1,0:T(8,128)S(1)} %sum_two.1.refs_0_), channel_id=1, source_target_pairs={{0,96},{4,100},{8,104},{12,108},{16,112},{20,116},{24,120},{28,124... | collective-permute-start | bytes 172040 | tf_op jit(solution)/shard_map/ppermute | solution.py:279
  36.8 6.8 %collective-permute-start.10 = (f32[32,1536]{1,0:T(8,128)S(1)}, f32[32,1536]{1,0:T(8,128)S(1)}, u32[]{:S(2)}, u32[]{:S(2)}) collective-permute-start(f32[32,1536]{1,0:T(8,128)S(1)} %get-tuple-element.54), channel_id=1, source_target_pairs={{0,3},{1,2},{2,1},{3,0},{4,7},{5,6},{6,5},{7,4},{8,11},{9,10},{10,... | collective-permute-start | bytes 589832 | tf_op jit(solution)/shard_map/ppermute | solution.py:296
  40.9 4.3 %collective-permute-start.16 = (f32[112,128]{1,0:T(8,128)S(1)}, f32[112,128]{1,0:T(8,128)S(1)}, u32[]{:S(2)}, u32[]{:S(2)}) collective-permute-start(f32[112,128]{1,0:T(8,128)S(1)} %sum_four.3.refs_0_), channel_id=1, source_target_pairs={{0,40},{4,44},{8,32},{12,36},{16,56},{20,60},{24,48},{28,52},{32,8... | collective-permute-start | bytes 172040 | tf_op jit(solution)/shard_map/ppermute | solution.py:279
  41.0 4.2 %collective-permute-start.15 = (f32[112,128]{1,0:T(8,128)S(1)}, f32[112,128]{1,0:T(8,128)S(1)}, u32[]{:S(2)}, u32[]{:S(2)}) collective-permute-start(f32[112,128]{1,0:T(8,128)S(1)} %sum_four.3.refs_0_), channel_id=1, source_target_pairs={{0,32},{4,36},{8,40},{12,44},{16,48},{20,52},{24,56},{28,60},{32,0... | collective-permute-start | bytes 172040 | tf_op jit(solution)/shard_map/ppermute | solution.py:279
  42.0 3.8 %collective-permute-start.14 = (f32[112,128]{1,0:T(8,128)S(1)}, f32[112,128]{1,0:T(8,128)S(1)}, u32[]{:S(2)}, u32[]{:S(2)}) collective-permute-start(f32[112,128]{1,0:T(8,128)S(1)} %sum_four.3.refs_0_), channel_id=1, source_target_pairs={{0,8},{4,12},{8,0},{12,4},{16,24},{20,28},{24,16},{28,20},{32,40},... | collective-permute-start | bytes 172040 | tf_op jit(solution)/shard_map/ppermute | solution.py:279
  45.8 6.1 %collective-permute-start.17 = (f32[448,128]{1,0:T(8,128)S(1)}, f32[448,128]{1,0:T(8,128)S(1)}, u32[]{:S(2)}, u32[]{:S(2)}) collective-permute-start(f32[448,128]{1,0:T(8,128)S(1)} %join.3.even_ref), channel_id=1, source_target_pairs={{0,4},{4,0},{8,12},{12,8},{16,20},{20,16},{24,28},{28,24},{32,36},... | collective-permute-start | bytes 688136 | tf_op jit(solution)/shard_map/ppermute | solution.py:279

commit v16 on v15

--- a/solution.py
+++ b/solution.py
@@ -325,7 +325,7 @@
         args = (back, rules) if inner is None else (back, rules, inner)
         return call(
             functools.partial(back_inner_kernel, groups), f32(32, VOX), args,
-            aliases=None if inner is None else {2: 0}, flops=len(groups) << 30,
+            aliases=None if inner is None else {2: 0}, flops=max(2, len(groups)) << 30,
             name="back_inner",
         )
 
@@ -346,7 +346,8 @@
     others = after(others, inner)
     total = call(sum_kernel, f32(PART, 128), (pieces[0], *others), name="sum_four")
     came = swap(total, X3)
-    inner = inner_part((4, 5), inner)
+    inner, = after((inner,), total)
+    inner = inner_part((4, 5, 6), inner)
     came, = after((came,), inner)
     total = call(sum_kernel, f32(PART, 128), (total, came), name="sum_two")
     others = [swap(total, m) for m in (Z3, Z6, Z3 ^ Z6)]
@@ -356,7 +357,7 @@
         name="middle",
     )
     second = over_ch(second, 3)
-    inner = inner_part((6, 7), inner)
+    inner = inner_part((7,), inner)
     others = after(others, inner, own)
     total = call(sum_kernel, f32(PART, 128), (total, *others), name="sum_four")
     others = [swap(total, m) for m in (X1, Z1, X1 | Z1)]

time: 52.9 us -> 51.8 us (0.979)
  waiting for transfers between devices: 4.31 us -> 3.06 us
    ppermute x13, waiting for transfers between devices: 4.3 us -> 2.97 us  [swap(): return lax.ppermute(value, 'blk', [(i, i ^ mask) for i in range(count)])]
  transfers between devices with their start and end apart: 18 -> 18, of which waited for: 4 -> 5; matrix products, arithmetic and copies ran while one was open for 0% -> 0% of each run, Pallas kernels for 26% -> 26%
where the time goes in v16:
time: 51.8 us; the launch traced here: 51.7 us
  starting transfers between devices  32.7 us (63%)
  Pallas kernels  15 us (29%)
  waiting for transfers between devices  3.06 us (6%)
  between operations  0.82 us (2%)
    ppermute x13, starting transfers between devices, swap(): return lax.ppermute(value, 'blk', [(i, i ^ mask) for i in range(count)])  25.2 us
    pallas_call x16, Pallas kernels, call(): pl.pallas_call(kernel, out_shape=outs, in_specs=[VMEM] * len(args), out_s...  13.7 us
    ppermute x4, starting transfers between devices, over_ch(): return lax.ppermute(value, 'ch', [(i, i ^ mask) for i in range(4)])  6.58 us
    ppermute x13, waiting for transfers between devices, swap(): return lax.ppermute(value, 'blk', [(i, i ^ mask) for i in range(count)])  2.97 us
    pallas_call x1, Pallas kernels, per_device(): pl.pallas_call(faces_kernel, out_shape=(bf16(64, FACE),) * 2, grid=(1,),...  1.37 us
  transfers between devices with their start and end apart: 18, of which 5 were waited for; matrix products, arithmetic and copies ran while one was open for 0% of the time, Pallas kernels for 26%

profile of v16, /device:TPU:1, one launch (start us, length us, event | category | flops | bytes accessed | tf_op | source)
XLA Modules:
  0.0 51.7 jit_solution(10210548022633563002)
XLA Ops:
  0.7 2.2 %collective-permute-start.2 = (bf16[32,1024]{1,0:T(8,128)(2,1)}, bf16[32,1024]{1,0:T(8,128)(2,1)S(1)}, u32[]{:S(2)}, u32[]{:S(2)}) collective-permute-start(bf16[32,1024]{1,0:T(8,128)(2,1)} %refs_0_.1), channel_id=1, source_target_pairs={{0,1},{1,0},{2,3},{3,2},{4,5},{5,4},{6,7},{7,6},{8,9},{9,8},{10,11... | collective-permute-start | bytes 196616 | tf_op jit(solution)/shard_map/ppermute | solution.py:296
  2.9 1.4 %faces.1 = (bf16[64,128]{1,0:T(8,128)(2,1)}, bf16[64,128]{1,0:T(8,128)(2,1)}) custom-call(bf16[32,1024]{1,0:T(8,128)(2,1)} %x_ref.3, bf16[32,1024]{1,0:T(8,128)(2,1)} %refs_0_.1), custom_call_target="tpu_custom_call" | custom-call | flops 1073741824 | bytes 65536 | tf_op jit(solution)/shard_map/faces/pallas_call | solution.py:301
  4.2 1.1 %collective-permute-start = (bf16[64,128]{1,0:T(8,128)(2,1)}, bf16[64,128]{1,0:T(8,128)(2,1)S(1)}, u32[]{:S(2)}, u32[]{:S(2)}) collective-permute-start(bf16[64,128]{1,0:T(8,128)(2,1)} %get-tuple-element.34), channel_id=1, source_target_pairs={{0,4},{4,0},{8,12},{12,8},{16,20},{20,16},{24,28},{28,24},{32,36},... | collective-permute-start | bytes 49160 | tf_op jit(solution)/shard_map/ppermute | solution.py:279
  5.4 0.9 %collective-permute-start.1 = (bf16[64,128]{1,0:T(8,128)(2,1)}, bf16[64,128]{1,0:T(8,128)(2,1)S(1)}, u32[]{:S(2)}, u32[]{:S(2)}) collective-permute-start(bf16[64,128]{1,0:T(8,128)(2,1)} %get-tuple-element.35), channel_id=1, source_target_pairs={{0,252},{4,8},{8,4},{12,16},{16,12},{20,24},{24,20},{28,32},{32,28... | collective-permute-start | bytes 49160 | tf_op jit(solution)/shard_map/ppermute | solution.py:285
  6.3 2.0 %collective-permute-start.3 = (bf16[64,1024]{1,0:T(8,128)(2,1)S(1)}, bf16[64,1024]{1,0:T(8,128)(2,1)S(1)}, u32[]{:S(2)}, u32[]{:S(2)}) collective-permute-start(bf16[64,1024]{1,0:T(8,128)(2,1)S(1)} %join.2.pair_ref), channel_id=1, source_target_pairs={{0,3},{1,2},{2,1},{3,0},{4,7},{5,6},{6,5},{7,4},{8,11},{9,10},{10,... | collective-permute-start | bytes 393224 | tf_op jit(solution)/shard_map/ppermute | solution.py:296
  8.3 3.9 %gather.1.dense_in = bf16[864,1024]{1,0:T(8,128)(2,1)S(1)} custom-call(bf16[32,1024]{1,0:T(8,128)(2,1)S(1)} %copy-done.3, s32[27,1024]{1,0:T(8,128)S(1)} %copy-done.2), custom_call_target="tpu_custom_call" | custom-call | flops 3221225472 | bytes 1945600 | tf_op jit(solution)/shard_map/gather/pallas_call | solution.py:256
  12.2 0.7 %weight_terms.1 = (bf16[864,1024]{1,0:T(8,128)(2,1)S(1)}, bf16[128,1024]{1,0:T(8,128)(2,1)S(1)}, f32[448,128]{1,0:T(8,128)S(1)}, f32[448,128]{1,0:T(8,128)S(1)}) custom-call(bf16[864,1024]{1,0:T(8,128)(2,1)S(1)} %gather.1.dense_in, s32[27,1024]{1,0:T(8,128)S(1)} %copy-done.2, ...), custom_call_target="tpu_custom_call", output_to_operand_aliasing={{0}: (0, {})} | custom-call | flops 1073741824 | bytes 4665344 | tf_op jit(solution)/shard_map/weight_terms/pallas_call | solution.py:256
  12.9 7.5 %collective-permute-start.4 = (f32[448,128]{1,0:T(8,128)S(1)}, f32[448,128]{1,0:T(8,128)S(1)}, u32[]{:S(2)}, u32[]{:S(2)}) collective-permute-start(f32[448,128]{1,0:T(8,128)S(1)} %get-tuple-element.38), channel_id=1, source_target_pairs={{0,4},{4,0},{8,12},{12,8},{16,20},{20,16},{24,28},{28,24},{32,36},... | collective-permute-start | bytes 688136 | tf_op jit(solution)/shard_map/ppermute | solution.py:279
  20.5 0.6 %back_terms.1.terms = f32[864,1024]{1,0:T(8,128)S(1)} custom-call(bf16[864,128]{1,0:T(8,128)(2,1)S(1)} %bitcast.2, bf16[128,1024]{1,0:T(8,128)(2,1)S(1)} %get-tuple-element.36.grad_ref), custom_call_target="tpu_custom_call" | custom-call | flops 1073741824 | bytes 4022272 | tf_op jit(solution)/shard_map/back_terms/pallas_call | solution.py:256
  21.1 0.5 forward.1
  21.6 0.1 collective-permute-start.5
  21.7 0.1 collective-permute-start.6
  21.8 2.5 %collective-permute-start.7 = (f32[112,128]{1,0:T(8,128)S(1)}, f32[112,128]{1,0:T(8,128)S(1)}, u32[]{:S(2)}, u32[]{:S(2)}) collective-permute-start(f32[112,128]{1,0:T(8,128)S(1)} %get-tuple-element.45), channel_id=1, source_target_pairs={{0,40},{4,44},{8,32},{12,36},{16,56},{20,60},{24,48},{28,52},{32,8... | collective-permute-start | bytes 172040 | tf_op jit(solution)/shard_map/ppermute | solution.py:279
  24.4 1.8 %back_inner.3.refs_0_ = f32[32,1024]{1,0:T(8,128)S(1)} custom-call(f32[864,1024]{1,0:T(8,128)S(1)} %back_terms.1.terms, s32[27,1024]{1,0:T(8,128)S(1)} %copy-done.2), custom_call_target="tpu_custom_call" | custom-call | flops 2147483648 | bytes 3780608 | tf_op jit(solution)/shard_map/back_inner/pallas_call | solution.py:256
  26.2 0.4 collective-permute-start.8
  26.7 0.1 collective-permute-start.9
  26.8 2.7 %back_inner.4.refs_0_ = f32[32,1024]{1,0:T(8,128)S(1)} custom-call(f32[864,1024]{1,0:T(8,128)S(1)} %back_terms.1.terms, s32[27,1024]{1,0:T(8,128)S(1)} %copy-done.2, f32[32,1024]{1,0:T(8,128)S(1)} %back_inner.3.refs_0_), custom_call_target="tpu_custom_call", output_to_operand_aliasing={{}: (2, {})} | custom-call | flops 3221225472 | bytes 3911680 | tf_op jit(solution)/shard_map/back_inner/pallas_call | solution.py:256
  29.5 1.5 %collective-permute-done.9.refs_1_ = f32[112,128]{1,0:T(8,128)S(1)} collective-permute-done((f32[112,128]{1,0:T(8,128)S(1)}, f32[112,128]{1,0:T(8,128)S(1)}, u32[]{:S(2)}, u32[]{:S(2)}) %collective-permute-start.9) | collective-permute-done | bytes 57376 | tf_op jit(solution)/shard_map/ppermute | solution.py:279
  31.0 2.4 %collective-permute-start.13 = (f32[112,128]{1,0:T(8,128)S(1)}, f32[112,128]{1,0:T(8,128)S(1)}, u32[]{:S(2)}, u32[]{:S(2)}) collective-permute-start(f32[112,128]{1,0:T(8,128)S(1)} %sum_two.1.refs_0_), channel_id=1, source_target_pairs={{0,160},{4,164},{8,168},{12,172},{16,176},{20,180},{24,184},{28,18... | collective-permute-start | bytes 172040 | tf_op jit(solution)/shard_map/ppermute | solution.py:279
  33.4 0.1 collective-permute-start.12
  33.5 3.2 %collective-permute-start.11 = (f32[112,128]{1,0:T(8,128)S(1)}, f32[112,128]{1,0:T(8,128)S(1)}, u32[]{:S(2)}, u32[]{:S(2)}) collective-permute-start(f32[112,128]{1,0:T(8,128)S(1)} %sum_two.1.refs_0_), channel_id=1, source_target_pairs={{0,96},{4,100},{8,104},{12,108},{16,112},{20,116},{24,120},{28,124... | collective-permute-start | bytes 172040 | tf_op jit(solution)/shard_map/ppermute | solution.py:279
  36.8 2.0 %collective-permute-start.10 = (f32[32,1536]{1,0:T(8,128)S(1)}, f32[32,1536]{1,0:T(8,128)S(1)}, u32[]{:S(2)}, u32[]{:S(2)}) collective-permute-start(f32[32,1536]{1,0:T(8,128)S(1)} %get-tuple-element.56), channel_id=1, source_target_pairs={{0,3},{1,2},{2,1},{3,0},{4,7},{5,6},{6,5},{7,4},{8,11},{9,10},{10,... | collective-permute-start | bytes 589832 | tf_op jit(solution)/shard_map/ppermute | solution.py:296
  38.8 1.0 %back_inner.5.inner = f32[32,1024]{1,0:T(8,128)S(1)} custom-call(f32[864,1024]{1,0:T(8,128)S(1)} %back_terms.1.terms, s32[27,1024]{1,0:T(8,128)S(1)} %copy-done.2, f32[32,1024]{1,0:T(8,128)S(1)} %back_inner.4.refs_0_), custom_call_target="tpu_custom_call", output_to_operand_aliasing={{}: (2, {})} | custom-call | flops 2147483648 | bytes 3911680 | tf_op jit(solution)/shard_map/back_inner/pallas_call | solution.py:256
  39.8 0.1 collective-permute-start.16
  39.9 1.1 %collective-permute-start.15 = (f32[112,128]{1,0:T(8,128)S(1)}, f32[112,128]{1,0:T(8,128)S(1)}, u32[]{:S(2)}, u32[]{:S(2)}) collective-permute-start(f32[112,128]{1,0:T(8,128)S(1)} %sum_four.3.refs_0_), channel_id=1, source_target_pairs={{0,32},{4,36},{8,40},{12,44},{16,48},{20,52},{24,56},{28,60},{32,0... | collective-permute-start | bytes 172040 | tf_op jit(solution)/shard_map/ppermute | solution.py:279
  41.0 1.6 %collective-permute-start.14 = (f32[112,128]{1,0:T(8,128)S(1)}, f32[112,128]{1,0:T(8,128)S(1)}, u32[]{:S(2)}, u32[]{:S(2)}) collective-permute-start(f32[112,128]{1,0:T(8,128)S(1)} %sum_four.3.refs_0_), channel_id=1, source_target_pairs={{0,8},{4,12},{8,0},{12,4},{16,24},{20,28},{24,16},{28,20},{32,40},... | collective-permute-start | bytes 172040 | tf_op jit(solution)/shard_map/ppermute | solution.py:279
  42.5 0.1 collective-permute-done.10.second_ref
  42.6 1.5 %edge.1 = (bf16[32,1024]{1,0:T(8,128)(2,1)}, bf16[32,1024]{1,0:T(8,128)(2,1)}) custom-call(f32[864,1024]{1,0:T(8,128)S(1)} %back_terms.1.terms, s32[27,1024]{1,0:T(8,128)S(1)} %copy-done.2, bf16[864,128]{1,0:T(8,128)(2,1)S(1)} %bitcast.4, bf16[64,128]{1,0:T(8,128)(2,1)S(1)} %collective-permute-done.near_ref, ...), custom_call_target="tpu_custom_call" | custom-call | flops 2147483648 | bytes 4788224 | tf_op jit(solution)/shard_map/edge/pallas_call | solution.py:256
  44.1 0.3 collective-permute-done.14.refs_1_
  44.4 5.3 %collective-permute-start.17 = (f32[448,128]{1,0:T(8,128)S(1)}, f32[448,128]{1,0:T(8,128)S(1)}, u32[]{:S(2)}, u32[]{:S(2)}) collective-permute-start(f32[448,128]{1,0:T(8,128)S(1)} %join.3.even_ref), channel_id=1, source_target_pairs={{0,4},{4,0},{8,12},{12,8},{16,20},{20,16},{24,28},{28,24},{32,36},... | collective-permute-start | bytes 688136 | tf_op jit(solution)/shard_map/ppermute | solution.py:279
  49.8 1.1 %collective-permute-done.17.odd_ref = f32[448,128]{1,0:T(8,128)S(1)} collective-permute-done((f32[448,128]{1,0:T(8,128)S(1)}, f32[448,128]{1,0:T(8,128)S(1)}, u32[]{:S(2)}, u32[]{:S(2)}) %collective-permute-start.17) | collective-permute-done | bytes 229408 | tf_op jit(solution)/shard_map/ppermute | solution.py:279
  50.9 0.8 %place.1 = f32[864,128]{1,0:T(8,128)} custom-call(f32[448,128]{1,0:T(8,128)S(1)} %join.3.even_ref, f32[448,128]{1,0:T(8,128)S(1)} %collective-permute-done.17.odd_ref), custom_call_target="tpu_custom_call" | custom-call | bytes 901120 | tf_op jit(solution)/shard_map/place/pallas_call | solution.py:256
  (29 shorter events, 0.3 us)
Async XLA Ops:
  0.6 5.7 %copy-start.1 = (bf16[32,1024]{1,0:T(8,128)(2,1)S(1)}, bf16[32,1024]{1,0:T(8,128)(2,1)}, u32[]{:S(2)}) copy-start(bf16[32,1024]{1,0:T(8,128)(2,1)} %refs_0_.1) | copy-start | bytes 196612
  0.6 7.7 %copy-start.3 = (bf16[32,1024]{1,0:T(8,128)(2,1)S(1)}, bf16[32,1024]{1,0:T(8,128)(2,1)}, u32[]{:S(2)}) copy-start(bf16[32,1024]{1,0:T(8,128)(2,1)} %x_ref.3) | copy-start | bytes 196612
  0.7 7.7 %copy-start.2 = (s32[27,1024]{1,0:T(8,128)S(1)}, s32[27,1024]{1,0:T(8,128)}, u32[]{:S(2)}) copy-start(s32[27,1024]{1,0:T(8,128)} %rule_ref.11) | copy-start | bytes 331780
  0.7 5.6 %collective-permute-start.2 = (bf16[32,1024]{1,0:T(8,128)(2,1)}, bf16[32,1024]{1,0:T(8,128)(2,1)S(1)}, u32[]{:S(2)}, u32[]{:S(2)}) collective-permute-start(bf16[32,1024]{1,0:T(8,128)(2,1)} %refs_0_.1), channel_id=1, source_target_pairs={{0,1},{1,0},{2,3},{3,2},{4,5},{5,4},{6,7},{7,6},{8,9},{9,8},{10,11... | collective-permute-start | bytes 196616 | tf_op jit(solution)/shard_map/ppermute | solution.py:296
  4.2 7.9 %collective-permute-start = (bf16[64,128]{1,0:T(8,128)(2,1)}, bf16[64,128]{1,0:T(8,128)(2,1)S(1)}, u32[]{:S(2)}, u32[]{:S(2)}) collective-permute-start(bf16[64,128]{1,0:T(8,128)(2,1)} %get-tuple-element.34), channel_id=1, source_target_pairs={{0,4},{4,0},{8,12},{12,8},{16,20},{20,16},{24,28},{28,24},{32,36},... | collective-permute-start | bytes 49160 | tf_op jit(solution)/shard_map/ppermute | solution.py:279
  5.4 6.8 %collective-permute-start.1 = (bf16[64,128]{1,0:T(8,128)(2,1)}, bf16[64,128]{1,0:T(8,128)(2,1)S(1)}, u32[]{:S(2)}, u32[]{:S(2)}) collective-permute-start(bf16[64,128]{1,0:T(8,128)(2,1)} %get-tuple-element.35), channel_id=1, source_target_pairs={{0,252},{4,8},{8,4},{12,16},{16,12},{20,24},{24,20},{28,32},{32,28... | collective-permute-start | bytes 49160 | tf_op jit(solution)/shard_map/ppermute | solution.py:285
  6.3 5.9 %collective-permute-start.3 = (bf16[64,1024]{1,0:T(8,128)(2,1)S(1)}, bf16[64,1024]{1,0:T(8,128)(2,1)S(1)}, u32[]{:S(2)}, u32[]{:S(2)}) collective-permute-start(bf16[64,1024]{1,0:T(8,128)(2,1)S(1)} %join.2.pair_ref), channel_id=1, source_target_pairs={{0,3},{1,2},{2,1},{3,0},{4,7},{5,6},{6,5},{7,4},{8,11},{9,10},{10,... | collective-permute-start | bytes 393224 | tf_op jit(solution)/shard_map/ppermute | solution.py:296
  12.2 8.3 %copy-start = (bf16[27,32,128]{2,1,0:T(8,128)(2,1)S(1)}, bf16[27,32,128]{2,1,0:T(8,128)(2,1)}, u32[]{:S(2)}) copy-start(bf16[27,32,128]{2,1,0:T(8,128)(2,1)} %param.5) | copy-start | bytes 663556
  12.9 8.6 %collective-permute-start.4 = (f32[448,128]{1,0:T(8,128)S(1)}, f32[448,128]{1,0:T(8,128)S(1)}, u32[]{:S(2)}, u32[]{:S(2)}) collective-permute-start(f32[448,128]{1,0:T(8,128)S(1)} %get-tuple-element.38), channel_id=1, source_target_pairs={{0,4},{4,0},{8,12},{12,8},{16,20},{20,16},{24,28},{28,24},{32,36},... | collective-permute-start | bytes 688136 | tf_op jit(solution)/shard_map/ppermute | solution.py:279
  21.6 5.0 %collective-permute-start.5 = (f32[112,128]{1,0:T(8,128)S(1)}, f32[112,128]{1,0:T(8,128)S(1)}, u32[]{:S(2)}, u32[]{:S(2)}) collective-permute-start(f32[112,128]{1,0:T(8,128)S(1)} %get-tuple-element.43), channel_id=1, source_target_pairs={{0,8},{4,12},{8,0},{12,4},{16,24},{20,28},{24,16},{28,20},{32,40},... | collective-permute-start | bytes 172040 | tf_op jit(solution)/shard_map/ppermute | solution.py:279
  21.7 4.9 %collective-permute-start.6 = (f32[112,128]{1,0:T(8,128)S(1)}, f32[112,128]{1,0:T(8,128)S(1)}, u32[]{:S(2)}, u32[]{:S(2)}) collective-permute-start(f32[112,128]{1,0:T(8,128)S(1)} %get-tuple-element.44), channel_id=1, source_target_pairs={{0,32},{4,36},{8,40},{12,44},{16,48},{20,52},{24,56},{28,60},{32,0... | collective-permute-start | bytes 172040 | tf_op jit(solution)/shard_map/ppermute | solution.py:279
  21.8 4.8 %collective-permute-start.7 = (f32[112,128]{1,0:T(8,128)S(1)}, f32[112,128]{1,0:T(8,128)S(1)}, u32[]{:S(2)}, u32[]{:S(2)}) collective-permute-start(f32[112,128]{1,0:T(8,128)S(1)} %get-tuple-element.45), channel_id=1, source_target_pairs={{0,40},{4,44},{8,32},{12,36},{16,56},{20,60},{24,48},{28,52},{32,8... | collective-permute-start | bytes 172040 | tf_op jit(solution)/shard_map/ppermute | solution.py:279
  26.2 10.6 %collective-permute-start.8 = (f32[64,1152]{1,0:T(8,128)S(1)}, f32[64,1152]{1,0:T(8,128)S(1)}, u32[]{:S(2)}, u32[]{:S(2)}) collective-permute-start(f32[64,1152]{1,0:T(8,128)S(1)} %get-tuple-element.51), channel_id=1, source_target_pairs={{0,1},{1,0},{2,3},{3,2},{4,5},{5,4},{6,7},{7,6},{8,9},{9,8},{10,11... | collective-permute-start | bytes 884744 | tf_op jit(solution)/shard_map/ppermute | solution.py:296
  26.7 4.3 %collective-permute-start.9 = (f32[112,128]{1,0:T(8,128)S(1)}, f32[112,128]{1,0:T(8,128)S(1)}, u32[]{:S(2)}, u32[]{:S(2)}) collective-permute-start(f32[112,128]{1,0:T(8,128)S(1)} %sum_four.2.refs_0_), channel_id=1, source_target_pairs={{0,24},{4,28},{8,16},{12,20},{16,8},{20,12},{24,0},{28,4},{32,56},... | collective-permute-start | bytes 172040 | tf_op jit(solution)/shard_map/ppermute | solution.py:279
  31.0 8.7 %collective-permute-start.13 = (f32[112,128]{1,0:T(8,128)S(1)}, f32[112,128]{1,0:T(8,128)S(1)}, u32[]{:S(2)}, u32[]{:S(2)}) collective-permute-start(f32[112,128]{1,0:T(8,128)S(1)} %sum_two.1.refs_0_), channel_id=1, source_target_pairs={{0,160},{4,164},{8,168},{12,172},{16,176},{20,180},{24,184},{28,18... | collective-permute-start | bytes 172040 | tf_op jit(solution)/shard_map/ppermute | solution.py:279
  33.4 6.3 %collective-permute-start.12 = (f32[112,128]{1,0:T(8,128)S(1)}, f32[112,128]{1,0:T(8,128)S(1)}, u32[]{:S(2)}, u32[]{:S(2)}) collective-permute-start(f32[112,128]{1,0:T(8,128)S(1)} %sum_two.1.refs_0_), channel_id=1, source_target_pairs={{0,192},{4,196},{8,200},{12,204},{16,208},{20,212},{24,216},{28,22... | collective-permute-start | bytes 172040 | tf_op jit(solution)/shard_map/ppermute | solution.py:279
  33.5 6.3 %collective-permute-start.11 = (f32[112,128]{1,0:T(8,128)S(1)}, f32[112,128]{1,0:T(8,128)S(1)}, u32[]{:S(2)}, u32[]{:S(2)}) collective-permute-start(f32[112,128]{1,0:T(8,128)S(1)} %sum_two.1.refs_0_), channel_id=1, source_target_pairs={{0,96},{4,100},{8,104},{12,108},{16,112},{20,116},{24,120},{28,124... | collective-permute-start | bytes 172040 | tf_op jit(solution)/shard_map/ppermute | solution.py:279
  36.8 5.8 %collective-permute-start.10 = (f32[32,1536]{1,0:T(8,128)S(1)}, f32[32,1536]{1,0:T(8,128)S(1)}, u32[]{:S(2)}, u32[]{:S(2)}) collective-permute-start(f32[32,1536]{1,0:T(8,128)S(1)} %get-tuple-element.56), channel_id=1, source_target_pairs={{0,3},{1,2},{2,1},{3,0},{4,7},{5,6},{6,5},{7,4},{8,11},{9,10},{10,... | collective-permute-start | bytes 589832 | tf_op jit(solution)/shard_map/ppermute | solution.py:296
  39.8 4.3 %collective-permute-start.16 = (f32[112,128]{1,0:T(8,128)S(1)}, f32[112,128]{1,0:T(8,128)S(1)}, u32[]{:S(2)}, u32[]{:S(2)}) collective-permute-start(f32[112,128]{1,0:T(8,128)S(1)} %sum_four.3.refs_0_), channel_id=1, source_target_pairs={{0,40},{4,44},{8,32},{12,36},{16,56},{20,60},{24,48},{28,52},{32,8... | collective-permute-start | bytes 172040 | tf_op jit(solution)/shard_map/ppermute | solution.py:279
  39.9 4.3 %collective-permute-start.15 = (f32[112,128]{1,0:T(8,128)S(1)}, f32[112,128]{1,0:T(8,128)S(1)}, u32[]{:S(2)}, u32[]{:S(2)}) collective-permute-start(f32[112,128]{1,0:T(8,128)S(1)} %sum_four.3.refs_0_), channel_id=1, source_target_pairs={{0,32},{4,36},{8,40},{12,44},{16,48},{20,52},{24,56},{28,60},{32,0... | collective-permute-start | bytes 172040 | tf_op jit(solution)/shard_map/ppermute | solution.py:279
  41.0 3.5 %collective-permute-start.14 = (f32[112,128]{1,0:T(8,128)S(1)}, f32[112,128]{1,0:T(8,128)S(1)}, u32[]{:S(2)}, u32[]{:S(2)}) collective-permute-start(f32[112,128]{1,0:T(8,128)S(1)} %sum_four.3.refs_0_), channel_id=1, source_target_pairs={{0,8},{4,12},{8,0},{12,4},{16,24},{20,28},{24,16},{28,20},{32,40},... | collective-permute-start | bytes 172040 | tf_op jit(solution)/shard_map/ppermute | solution.py:279
  44.4 6.4 %collective-permute-start.17 = (f32[448,128]{1,0:T(8,128)S(1)}, f32[448,128]{1,0:T(8,128)S(1)}, u32[]{:S(2)}, u32[]{:S(2)}) collective-permute-start(f32[448,128]{1,0:T(8,128)S(1)} %join.3.even_ref), channel_id=1, source_target_pairs={{0,4},{4,0},{8,12},{12,8},{16,20},{20,16},{24,28},{28,24},{32,36},... | collective-permute-start | bytes 688136 | tf_op jit(solution)/shard_map/ppermute | solution.py:279

commit v17 on v16

--- a/solution.py
+++ b/solution.py
@@ -339,7 +339,7 @@
     )
     came, = after((came,), ours, back)
     pieces = call(split_sum_kernel, (f32(PART, 128),) * 4, (keep, came), name="sum_pair")
-    others = [swap(pieces[q], m) for q, m in ((1, X1), (2, Z1), (3, X1 | Z1))]
+    others = [swap(pieces[q], m) for q, m in ((3, X1 | Z1), (2, Z1), (1, X1))]
     first, = after((first,), *pieces)
     first = over_ch(first, 1)
     inner = inner_part((2, 3))

time: 51.8 us -> 51.9 us (level)
  waiting for transfers between devices: 3.06 us -> 3.99 us
  starting transfers between devices: 32.7 us -> 31.8 us
    ppermute x13, waiting for transfers between devices: 2.97 us -> 3.9 us  [swap(): return lax.ppermute(value, 'blk', [(i, i ^ mask) for i in range(count)])]
    ppermute x13, starting transfers between devices: 25.2 us -> 24.3 us  [swap(): return lax.ppermute(value, 'blk', [(i, i ^ mask) for i in range(count)])]
where the time goes in v17:
time: 51.9 us; the launch traced here: 51.7 us
  starting transfers between devices  31.8 us (61%)
  Pallas kernels  15 us (29%)
  waiting for transfers between devices  3.99 us (8%)
  between operations  0.82 us (2%)
    ppermute x13, starting transfers between devices, swap(): return lax.ppermute(value, 'blk', [(i, i ^ mask) for i in range(count)])  24.3 us
    pallas_call x16, Pallas kernels, call(): pl.pallas_call(kernel, out_shape=outs, in_specs=[VMEM] * len(args), out_s...  13.7 us
    ppermute x4, starting transfers between devices, over_ch(): return lax.ppermute(value, 'ch', [(i, i ^ mask) for i in range(4)])  6.58 us
    ppermute x13, waiting for transfers between devices, swap(): return lax.ppermute(value, 'blk', [(i, i ^ mask) for i in range(count)])  3.9 us
    pallas_call x1, Pallas kernels, per_device(): pl.pallas_call(faces_kernel, out_shape=(bf16(64, FACE),) * 2, grid=(1,),...  1.37 us
  transfers between devices with their start and end apart: 18, of which 5 were waited for; matrix products, arithmetic and copies ran while one was open for 0% of the time, Pallas kernels for 26%

profile of v17, /device:TPU:1, one launch (start us, length us, event | category | flops | bytes accessed | tf_op | source)
XLA Modules:
  0.0 51.7 jit_solution(16324977888809403369)
XLA Ops:
  0.7 2.2 %collective-permute-start.2 = (bf16[32,1024]{1,0:T(8,128)(2,1)}, bf16[32,1024]{1,0:T(8,128)(2,1)S(1)}, u32[]{:S(2)}, u32[]{:S(2)}) collective-permute-start(bf16[32,1024]{1,0:T(8,128)(2,1)} %refs_0_.1), channel_id=1, source_target_pairs={{0,1},{1,0},{2,3},{3,2},{4,5},{5,4},{6,7},{7,6},{8,9},{9,8},{10,11... | collective-permute-start | bytes 196616 | tf_op jit(solution)/shard_map/ppermute | solution.py:296
  2.9 1.4 %faces.1 = (bf16[64,128]{1,0:T(8,128)(2,1)}, bf16[64,128]{1,0:T(8,128)(2,1)}) custom-call(bf16[32,1024]{1,0:T(8,128)(2,1)} %x_ref.3, bf16[32,1024]{1,0:T(8,128)(2,1)} %refs_0_.1), custom_call_target="tpu_custom_call" | custom-call | flops 1073741824 | bytes 65536 | tf_op jit(solution)/shard_map/faces/pallas_call | solution.py:301
  4.2 1.1 %collective-permute-start = (bf16[64,128]{1,0:T(8,128)(2,1)}, bf16[64,128]{1,0:T(8,128)(2,1)S(1)}, u32[]{:S(2)}, u32[]{:S(2)}) collective-permute-start(bf16[64,128]{1,0:T(8,128)(2,1)} %get-tuple-element.34), channel_id=1, source_target_pairs={{0,4},{4,0},{8,12},{12,8},{16,20},{20,16},{24,28},{28,24},{32,36},... | collective-permute-start | bytes 49160 | tf_op jit(solution)/shard_map/ppermute | solution.py:279
  5.4 0.9 %collective-permute-start.1 = (bf16[64,128]{1,0:T(8,128)(2,1)}, bf16[64,128]{1,0:T(8,128)(2,1)S(1)}, u32[]{:S(2)}, u32[]{:S(2)}) collective-permute-start(bf16[64,128]{1,0:T(8,128)(2,1)} %get-tuple-element.35), channel_id=1, source_target_pairs={{0,252},{4,8},{8,4},{12,16},{16,12},{20,24},{24,20},{28,32},{32,28... | collective-permute-start | bytes 49160 | tf_op jit(solution)/shard_map/ppermute | solution.py:285
  6.3 2.0 %collective-permute-start.3 = (bf16[64,1024]{1,0:T(8,128)(2,1)S(1)}, bf16[64,1024]{1,0:T(8,128)(2,1)S(1)}, u32[]{:S(2)}, u32[]{:S(2)}) collective-permute-start(bf16[64,1024]{1,0:T(8,128)(2,1)S(1)} %join.2.pair_ref), channel_id=1, source_target_pairs={{0,3},{1,2},{2,1},{3,0},{4,7},{5,6},{6,5},{7,4},{8,11},{9,10},{10,... | collective-permute-start | bytes 393224 | tf_op jit(solution)/shard_map/ppermute | solution.py:296
  8.3 3.9 %gather.1.dense_in = bf16[864,1024]{1,0:T(8,128)(2,1)S(1)} custom-call(bf16[32,1024]{1,0:T(8,128)(2,1)S(1)} %copy-done.3, s32[27,1024]{1,0:T(8,128)S(1)} %copy-done.2), custom_call_target="tpu_custom_call" | custom-call | flops 3221225472 | bytes 1945600 | tf_op jit(solution)/shard_map/gather/pallas_call | solution.py:256
  12.2 0.7 %weight_terms.1 = (bf16[864,1024]{1,0:T(8,128)(2,1)S(1)}, bf16[128,1024]{1,0:T(8,128)(2,1)S(1)}, f32[448,128]{1,0:T(8,128)S(1)}, f32[448,128]{1,0:T(8,128)S(1)}) custom-call(bf16[864,1024]{1,0:T(8,128)(2,1)S(1)} %gather.1.dense_in, s32[27,1024]{1,0:T(8,128)S(1)} %copy-done.2, ...), custom_call_target="tpu_custom_call", output_to_operand_aliasing={{0}: (0, {})} | custom-call | flops 1073741824 | bytes 4665344 | tf_op jit(solution)/shard_map/weight_terms/pallas_call | solution.py:256
  12.9 7.5 %collective-permute-start.4 = (f32[448,128]{1,0:T(8,128)S(1)}, f32[448,128]{1,0:T(8,128)S(1)}, u32[]{:S(2)}, u32[]{:S(2)}) collective-permute-start(f32[448,128]{1,0:T(8,128)S(1)} %get-tuple-element.38), channel_id=1, source_target_pairs={{0,4},{4,0},{8,12},{12,8},{16,20},{20,16},{24,28},{28,24},{32,36},... | collective-permute-start | bytes 688136 | tf_op jit(solution)/shard_map/ppermute | solution.py:279
  20.5 0.6 %back_terms.1.terms = f32[864,1024]{1,0:T(8,128)S(1)} custom-call(bf16[864,128]{1,0:T(8,128)(2,1)S(1)} %bitcast.2, bf16[128,1024]{1,0:T(8,128)(2,1)S(1)} %get-tuple-element.36.grad_ref), custom_call_target="tpu_custom_call" | custom-call | flops 1073741824 | bytes 4022272 | tf_op jit(solution)/shard_map/back_terms/pallas_call | solution.py:256
  21.1 0.5 forward.1
  21.6 0.1 collective-permute-start.5
  21.7 0.1 collective-permute-start.6
  21.8 2.5 %collective-permute-start.7 = (f32[112,128]{1,0:T(8,128)S(1)}, f32[112,128]{1,0:T(8,128)S(1)}, u32[]{:S(2)}, u32[]{:S(2)}) collective-permute-start(f32[112,128]{1,0:T(8,128)S(1)} %get-tuple-element.45), channel_id=1, source_target_pairs={{0,8},{4,12},{8,0},{12,4},{16,24},{20,28},{24,16},{28,20},{32,40},... | collective-permute-start | bytes 172040 | tf_op jit(solution)/shard_map/ppermute | solution.py:279
  24.4 1.8 %back_inner.3.refs_0_ = f32[32,1024]{1,0:T(8,128)S(1)} custom-call(f32[864,1024]{1,0:T(8,128)S(1)} %back_terms.1.terms, s32[27,1024]{1,0:T(8,128)S(1)} %copy-done.2), custom_call_target="tpu_custom_call" | custom-call | flops 2147483648 | bytes 3780608 | tf_op jit(solution)/shard_map/back_inner/pallas_call | solution.py:256
  26.2 0.4 collective-permute-start.8
  26.6 0.7 %collective-permute-done.7.refs_3_ = f32[112,128]{1,0:T(8,128)S(1)} collective-permute-done((f32[112,128]{1,0:T(8,128)S(1)}, f32[112,128]{1,0:T(8,128)S(1)}, u32[]{:S(2)}, u32[]{:S(2)}) %collective-permute-start.7) | collective-permute-done | bytes 57376 | tf_op jit(solution)/shard_map/ppermute | solution.py:279
  27.3 0.1 collective-permute-start.9
  27.4 2.7 %back_inner.4.refs_0_ = f32[32,1024]{1,0:T(8,128)S(1)} custom-call(f32[864,1024]{1,0:T(8,128)S(1)} %back_terms.1.terms, s32[27,1024]{1,0:T(8,128)S(1)} %copy-done.2, f32[32,1024]{1,0:T(8,128)S(1)} %back_inner.3.refs_0_), custom_call_target="tpu_custom_call", output_to_operand_aliasing={{}: (2, {})} | custom-call | flops 3221225472 | bytes 3911680 | tf_op jit(solution)/shard_map/back_inner/pallas_call | solution.py:256
  30.1 1.5 %collective-permute-done.9.refs_1_ = f32[112,128]{1,0:T(8,128)S(1)} collective-permute-done((f32[112,128]{1,0:T(8,128)S(1)}, f32[112,128]{1,0:T(8,128)S(1)}, u32[]{:S(2)}, u32[]{:S(2)}) %collective-permute-start.9) | collective-permute-done | bytes 57376 | tf_op jit(solution)/shard_map/ppermute | solution.py:279
  31.6 1.6 %collective-permute-start.13 = (f32[112,128]{1,0:T(8,128)S(1)}, f32[112,128]{1,0:T(8,128)S(1)}, u32[]{:S(2)}, u32[]{:S(2)}) collective-permute-start(f32[112,128]{1,0:T(8,128)S(1)} %sum_two.1.refs_0_), channel_id=1, source_target_pairs={{0,160},{4,164},{8,168},{12,172},{16,176},{20,180},{24,184},{28,18... | collective-permute-start | bytes 172040 | tf_op jit(solution)/shard_map/ppermute | solution.py:279
  33.3 0.5 collective-permute-start.12
  33.7 3.6 %collective-permute-start.11 = (f32[112,128]{1,0:T(8,128)S(1)}, f32[112,128]{1,0:T(8,128)S(1)}, u32[]{:S(2)}, u32[]{:S(2)}) collective-permute-start(f32[112,128]{1,0:T(8,128)S(1)} %sum_two.1.refs_0_), channel_id=1, source_target_pairs={{0,96},{4,100},{8,104},{12,108},{16,112},{20,116},{24,120},{28,124... | collective-permute-start | bytes 172040 | tf_op jit(solution)/shard_map/ppermute | solution.py:279
  37.4 2.0 %collective-permute-start.10 = (f32[32,1536]{1,0:T(8,128)S(1)}, f32[32,1536]{1,0:T(8,128)S(1)}, u32[]{:S(2)}, u32[]{:S(2)}) collective-permute-start(f32[32,1536]{1,0:T(8,128)S(1)} %get-tuple-element.56), channel_id=1, source_target_pairs={{0,3},{1,2},{2,1},{3,0},{4,7},{5,6},{6,5},{7,4},{8,11},{9,10},{10,... | collective-permute-start | bytes 589832 | tf_op jit(solution)/shard_map/ppermute | solution.py:296
  39.4 1.0 %back_inner.5.inner = f32[32,1024]{1,0:T(8,128)S(1)} custom-call(f32[864,1024]{1,0:T(8,128)S(1)} %back_terms.1.terms, s32[27,1024]{1,0:T(8,128)S(1)} %copy-done.2, f32[32,1024]{1,0:T(8,128)S(1)} %back_inner.4.refs_0_), custom_call_target="tpu_custom_call", output_to_operand_aliasing={{}: (2, {})} | custom-call | flops 2147483648 | bytes 3911680 | tf_op jit(solution)/shard_map/back_inner/pallas_call | solution.py:256
  40.4 0.1 collective-permute-start.16
  40.5 0.6 %collective-permute-start.15 = (f32[112,128]{1,0:T(8,128)S(1)}, f32[112,128]{1,0:T(8,128)S(1)}, u32[]{:S(2)}, u32[]{:S(2)}) collective-permute-start(f32[112,128]{1,0:T(8,128)S(1)} %sum_four.3.refs_0_), channel_id=1, source_target_pairs={{0,32},{4,36},{8,40},{12,44},{16,48},{20,52},{24,56},{28,60},{32,0... | collective-permute-start | bytes 172040 | tf_op jit(solution)/shard_map/ppermute | solution.py:279
  41.2 2.0 %collective-permute-start.14 = (f32[112,128]{1,0:T(8,128)S(1)}, f32[112,128]{1,0:T(8,128)S(1)}, u32[]{:S(2)}, u32[]{:S(2)}) collective-permute-start(f32[112,128]{1,0:T(8,128)S(1)} %sum_four.3.refs_0_), channel_id=1, source_target_pairs={{0,8},{4,12},{8,0},{12,4},{16,24},{20,28},{24,16},{28,20},{32,40},... | collective-permute-start | bytes 172040 | tf_op jit(solution)/shard_map/ppermute | solution.py:279
  43.3 1.5 %edge.1 = (bf16[32,1024]{1,0:T(8,128)(2,1)}, bf16[32,1024]{1,0:T(8,128)(2,1)}) custom-call(f32[864,1024]{1,0:T(8,128)S(1)} %back_terms.1.terms, s32[27,1024]{1,0:T(8,128)S(1)} %copy-done.2, bf16[864,128]{1,0:T(8,128)(2,1)S(1)} %bitcast.4, bf16[64,128]{1,0:T(8,128)(2,1)S(1)} %collective-permute-done.near_ref, ...), custom_call_target="tpu_custom_call" | custom-call | flops 2147483648 | bytes 4788224 | tf_op jit(solution)/shard_map/edge/pallas_call | solution.py:256
  44.8 0.6 %collective-permute-done.14.refs_1_ = f32[112,128]{1,0:T(8,128)S(1)} collective-permute-done((f32[112,128]{1,0:T(8,128)S(1)}, f32[112,128]{1,0:T(8,128)S(1)}, u32[]{:S(2)}, u32[]{:S(2)}) %collective-permute-start.14) | collective-permute-done | bytes 57376 | tf_op jit(solution)/shard_map/ppermute | solution.py:279
  45.4 4.4 %collective-permute-start.17 = (f32[448,128]{1,0:T(8,128)S(1)}, f32[448,128]{1,0:T(8,128)S(1)}, u32[]{:S(2)}, u32[]{:S(2)}) collective-permute-start(f32[448,128]{1,0:T(8,128)S(1)} %join.3.even_ref), channel_id=1, source_target_pairs={{0,4},{4,0},{8,12},{12,8},{16,20},{20,16},{24,28},{28,24},{32,36},... | collective-permute-start | bytes 688136 | tf_op jit(solution)/shard_map/ppermute | solution.py:279
  49.8 1.1 %collective-permute-done.17.odd_ref = f32[448,128]{1,0:T(8,128)S(1)} collective-permute-done((f32[448,128]{1,0:T(8,128)S(1)}, f32[448,128]{1,0:T(8,128)S(1)}, u32[]{:S(2)}, u32[]{:S(2)}) %collective-permute-start.17) | collective-permute-done | bytes 229408 | tf_op jit(solution)/shard_map/ppermute | solution.py:279
  50.9 0.8 %place.1 = f32[864,128]{1,0:T(8,128)} custom-call(f32[448,128]{1,0:T(8,128)S(1)} %join.3.even_ref, f32[448,128]{1,0:T(8,128)S(1)} %collective-permute-done.17.odd_ref), custom_call_target="tpu_custom_call" | custom-call | bytes 901120 | tf_op jit(solution)/shard_map/place/pallas_call | solution.py:256
  (29 shorter events, 0.3 us)
Async XLA Ops:
  0.6 5.7 %copy-start.1 = (bf16[32,1024]{1,0:T(8,128)(2,1)S(1)}, bf16[32,1024]{1,0:T(8,128)(2,1)}, u32[]{:S(2)}) copy-start(bf16[32,1024]{1,0:T(8,128)(2,1)} %refs_0_.1) | copy-start | bytes 196612
  0.6 7.7 %copy-start.3 = (bf16[32,1024]{1,0:T(8,128)(2,1)S(1)}, bf16[32,1024]{1,0:T(8,128)(2,1)}, u32[]{:S(2)}) copy-start(bf16[32,1024]{1,0:T(8,128)(2,1)} %x_ref.3) | copy-start | bytes 196612
  0.7 7.7 %copy-start.2 = (s32[27,1024]{1,0:T(8,128)S(1)}, s32[27,1024]{1,0:T(8,128)}, u32[]{:S(2)}) copy-start(s32[27,1024]{1,0:T(8,128)} %rule_ref.11) | copy-start | bytes 331780
  0.7 5.6 %collective-permute-start.2 = (bf16[32,1024]{1,0:T(8,128)(2,1)}, bf16[32,1024]{1,0:T(8,128)(2,1)S(1)}, u32[]{:S(2)}, u32[]{:S(2)}) collective-permute-start(bf16[32,1024]{1,0:T(8,128)(2,1)} %refs_0_.1), channel_id=1, source_target_pairs={{0,1},{1,0},{2,3},{3,2},{4,5},{5,4},{6,7},{7,6},{8,9},{9,8},{10,11... | collective-permute-start | bytes 196616 | tf_op jit(solution)/shard_map/ppermute | solution.py:296
  4.2 7.9 %collective-permute-start = (bf16[64,128]{1,0:T(8,128)(2,1)}, bf16[64,128]{1,0:T(8,128)(2,1)S(1)}, u32[]{:S(2)}, u32[]{:S(2)}) collective-permute-start(bf16[64,128]{1,0:T(8,128)(2,1)} %get-tuple-element.34), channel_id=1, source_target_pairs={{0,4},{4,0},{8,12},{12,8},{16,20},{20,16},{24,28},{28,24},{32,36},... | collective-permute-start | bytes 49160 | tf_op jit(solution)/shard_map/ppermute | solution.py:279
  5.4 6.8 %collective-permute-start.1 = (bf16[64,128]{1,0:T(8,128)(2,1)}, bf16[64,128]{1,0:T(8,128)(2,1)S(1)}, u32[]{:S(2)}, u32[]{:S(2)}) collective-permute-start(bf16[64,128]{1,0:T(8,128)(2,1)} %get-tuple-element.35), channel_id=1, source_target_pairs={{0,252},{4,8},{8,4},{12,16},{16,12},{20,24},{24,20},{28,32},{32,28... | collective-permute-start | bytes 49160 | tf_op jit(solution)/shard_map/ppermute | solution.py:285
  6.3 5.9 %collective-permute-start.3 = (bf16[64,1024]{1,0:T(8,128)(2,1)S(1)}, bf16[64,1024]{1,0:T(8,128)(2,1)S(1)}, u32[]{:S(2)}, u32[]{:S(2)}) collective-permute-start(bf16[64,1024]{1,0:T(8,128)(2,1)S(1)} %join.2.pair_ref), channel_id=1, source_target_pairs={{0,3},{1,2},{2,1},{3,0},{4,7},{5,6},{6,5},{7,4},{8,11},{9,10},{10,... | collective-permute-start | bytes 393224 | tf_op jit(solution)/shard_map/ppermute | solution.py:296
  12.2 8.3 %copy-start = (bf16[27,32,128]{2,1,0:T(8,128)(2,1)S(1)}, bf16[27,32,128]{2,1,0:T(8,128)(2,1)}, u32[]{:S(2)}) copy-start(bf16[27,32,128]{2,1,0:T(8,128)(2,1)} %param.5) | copy-start | bytes 663556
  12.9 8.6 %collective-permute-start.4 = (f32[448,128]{1,0:T(8,128)S(1)}, f32[448,128]{1,0:T(8,128)S(1)}, u32[]{:S(2)}, u32[]{:S(2)}) collective-permute-start(f32[448,128]{1,0:T(8,128)S(1)} %get-tuple-element.38), channel_id=1, source_target_pairs={{0,4},{4,0},{8,12},{12,8},{16,20},{20,16},{24,28},{28,24},{32,36},... | collective-permute-start | bytes 688136 | tf_op jit(solution)/shard_map/ppermute | solution.py:279
  21.6 5.0 %collective-permute-start.5 = (f32[112,128]{1,0:T(8,128)S(1)}, f32[112,128]{1,0:T(8,128)S(1)}, u32[]{:S(2)}, u32[]{:S(2)}) collective-permute-start(f32[112,128]{1,0:T(8,128)S(1)} %get-tuple-element.43), channel_id=1, source_target_pairs={{0,40},{4,44},{8,32},{12,36},{16,56},{20,60},{24,48},{28,52},{32,8... | collective-permute-start | bytes 172040 | tf_op jit(solution)/shard_map/ppermute | solution.py:279
  21.7 4.9 %collective-permute-start.6 = (f32[112,128]{1,0:T(8,128)S(1)}, f32[112,128]{1,0:T(8,128)S(1)}, u32[]{:S(2)}, u32[]{:S(2)}) collective-permute-start(f32[112,128]{1,0:T(8,128)S(1)} %get-tuple-element.44), channel_id=1, source_target_pairs={{0,32},{4,36},{8,40},{12,44},{16,48},{20,52},{24,56},{28,60},{32,0... | collective-permute-start | bytes 172040 | tf_op jit(solution)/shard_map/ppermute | solution.py:279
  21.8 5.5 %collective-permute-start.7 = (f32[112,128]{1,0:T(8,128)S(1)}, f32[112,128]{1,0:T(8,128)S(1)}, u32[]{:S(2)}, u32[]{:S(2)}) collective-permute-start(f32[112,128]{1,0:T(8,128)S(1)} %get-tuple-element.45), channel_id=1, source_target_pairs={{0,8},{4,12},{8,0},{12,4},{16,24},{20,28},{24,16},{28,20},{32,40},... | collective-permute-start | bytes 172040 | tf_op jit(solution)/shard_map/ppermute | solution.py:279
  26.2 11.2 %collective-permute-start.8 = (f32[64,1152]{1,0:T(8,128)S(1)}, f32[64,1152]{1,0:T(8,128)S(1)}, u32[]{:S(2)}, u32[]{:S(2)}) collective-permute-start(f32[64,1152]{1,0:T(8,128)S(1)} %get-tuple-element.51), channel_id=1, source_target_pairs={{0,1},{1,0},{2,3},{3,2},{4,5},{5,4},{6,7},{7,6},{8,9},{9,8},{10,11... | collective-permute-start | bytes 884744 | tf_op jit(solution)/shard_map/ppermute | solution.py:296
  27.3 4.3 %collective-permute-start.9 = (f32[112,128]{1,0:T(8,128)S(1)}, f32[112,128]{1,0:T(8,128)S(1)}, u32[]{:S(2)}, u32[]{:S(2)}) collective-permute-start(f32[112,128]{1,0:T(8,128)S(1)} %sum_four.2.refs_0_), channel_id=1, source_target_pairs={{0,24},{4,28},{8,16},{12,20},{16,8},{20,12},{24,0},{28,4},{32,56},... | collective-permute-start | bytes 172040 | tf_op jit(solution)/shard_map/ppermute | solution.py:279
  31.6 8.7 %collective-permute-start.13 = (f32[112,128]{1,0:T(8,128)S(1)}, f32[112,128]{1,0:T(8,128)S(1)}, u32[]{:S(2)}, u32[]{:S(2)}) collective-permute-start(f32[112,128]{1,0:T(8,128)S(1)} %sum_two.1.refs_0_), channel_id=1, source_target_pairs={{0,160},{4,164},{8,168},{12,172},{16,176},{20,180},{24,184},{28,18... | collective-permute-start | bytes 172040 | tf_op jit(solution)/shard_map/ppermute | solution.py:279
  33.3 7.1 %collective-permute-start.12 = (f32[112,128]{1,0:T(8,128)S(1)}, f32[112,128]{1,0:T(8,128)S(1)}, u32[]{:S(2)}, u32[]{:S(2)}) collective-permute-start(f32[112,128]{1,0:T(8,128)S(1)} %sum_two.1.refs_0_), channel_id=1, source_target_pairs={{0,192},{4,196},{8,200},{12,204},{16,208},{20,212},{24,216},{28,22... | collective-permute-start | bytes 172040 | tf_op jit(solution)/shard_map/ppermute | solution.py:279
  33.7 6.7 %collective-permute-start.11 = (f32[112,128]{1,0:T(8,128)S(1)}, f32[112,128]{1,0:T(8,128)S(1)}, u32[]{:S(2)}, u32[]{:S(2)}) collective-permute-start(f32[112,128]{1,0:T(8,128)S(1)} %sum_two.1.refs_0_), channel_id=1, source_target_pairs={{0,96},{4,100},{8,104},{12,108},{16,112},{20,116},{24,120},{28,124... | collective-permute-start | bytes 172040 | tf_op jit(solution)/shard_map/ppermute | solution.py:279
  37.4 5.8 %collective-permute-start.10 = (f32[32,1536]{1,0:T(8,128)S(1)}, f32[32,1536]{1,0:T(8,128)S(1)}, u32[]{:S(2)}, u32[]{:S(2)}) collective-permute-start(f32[32,1536]{1,0:T(8,128)S(1)} %get-tuple-element.56), channel_id=1, source_target_pairs={{0,3},{1,2},{2,1},{3,0},{4,7},{5,6},{6,5},{7,4},{8,11},{9,10},{10,... | collective-permute-start | bytes 589832 | tf_op jit(solution)/shard_map/ppermute | solution.py:296
  40.4 4.3 %collective-permute-start.16 = (f32[112,128]{1,0:T(8,128)S(1)}, f32[112,128]{1,0:T(8,128)S(1)}, u32[]{:S(2)}, u32[]{:S(2)}) collective-permute-start(f32[112,128]{1,0:T(8,128)S(1)} %sum_four.3.refs_0_), channel_id=1, source_target_pairs={{0,40},{4,44},{8,32},{12,36},{16,56},{20,60},{24,48},{28,52},{32,8... | collective-permute-start | bytes 172040 | tf_op jit(solution)/shard_map/ppermute | solution.py:279
  40.5 4.2 %collective-permute-start.15 = (f32[112,128]{1,0:T(8,128)S(1)}, f32[112,128]{1,0:T(8,128)S(1)}, u32[]{:S(2)}, u32[]{:S(2)}) collective-permute-start(f32[112,128]{1,0:T(8,128)S(1)} %sum_four.3.refs_0_), channel_id=1, source_target_pairs={{0,32},{4,36},{8,40},{12,44},{16,48},{20,52},{24,56},{28,60},{32,0... | collective-permute-start | bytes 172040 | tf_op jit(solution)/shard_map/ppermute | solution.py:279
  41.2 4.2 %collective-permute-start.14 = (f32[112,128]{1,0:T(8,128)S(1)}, f32[112,128]{1,0:T(8,128)S(1)}, u32[]{:S(2)}, u32[]{:S(2)}) collective-permute-start(f32[112,128]{1,0:T(8,128)S(1)} %sum_four.3.refs_0_), channel_id=1, source_target_pairs={{0,8},{4,12},{8,0},{12,4},{16,24},{20,28},{24,16},{28,20},{32,40},... | collective-permute-start | bytes 172040 | tf_op jit(solution)/shard_map/ppermute | solution.py:279
  45.4 5.5 %collective-permute-start.17 = (f32[448,128]{1,0:T(8,128)S(1)}, f32[448,128]{1,0:T(8,128)S(1)}, u32[]{:S(2)}, u32[]{:S(2)}) collective-permute-start(f32[448,128]{1,0:T(8,128)S(1)} %join.3.even_ref), channel_id=1, source_target_pairs={{0,4},{4,0},{8,12},{12,8},{16,20},{20,16},{24,28},{28,24},{32,36},... | collective-permute-start | bytes 688136 | tf_op jit(solution)/shard_map/ppermute | solution.py:279

commit v18 on v17

--- a/solution.py
+++ b/solution.py
@@ -12,7 +12,7 @@
 LANES = 128
 PART = 112
 INNER = tuple(range(2, 8))
-EDGE = (0, 1)
+EDGE = (0, 1, 3)
 X1, X3, Z1, Z3, Z6 = 2, 6, 8, 24, 48
 ORDER = (0, 1, 3, 2)
 VMEM = pl.BlockSpec(memory_space=pltpu.VMEM)
@@ -342,7 +342,7 @@
     others = [swap(pieces[q], m) for q, m in ((3, X1 | Z1), (2, Z1), (1, X1))]
     first, = after((first,), *pieces)
     first = over_ch(first, 1)
-    inner = inner_part((2, 3))
+    inner = inner_part((2,))
     others = after(others, inner)
     total = call(sum_kernel, f32(PART, 128), (pieces[0], *others), name="sum_four")
     came = swap(total, X3)

time: 51.9 us -> 52 us (level)
  transfers between devices with their start and end apart: 18 -> 18, of which waited for: 5 -> 4; matrix products, arithmetic and copies ran while one was open for 0% -> 0% of each run, Pallas kernels for 26% -> 26%
where the time goes in v18:
time: 52 us; the launch traced here: 51.9 us
  starting transfers between devices  31.7 us (61%)
  Pallas kernels  15 us (29%)
  waiting for transfers between devices  4.3 us (8%)
  between operations  0.83 us (2%)
    ppermute x13, starting transfers between devices, swap(): return lax.ppermute(value, 'blk', [(i, i ^ mask) for i in range(count)])  24 us
    pallas_call x16, Pallas kernels, call(): pl.pallas_call(kernel, out_shape=outs, in_specs=[VMEM] * len(args), out_s...  13.6 us
    ppermute x4, starting transfers between devices, over_ch(): return lax.ppermute(value, 'ch', [(i, i ^ mask) for i in range(4)])  6.76 us
    ppermute x13, waiting for transfers between devices, swap(): return lax.ppermute(value, 'blk', [(i, i ^ mask) for i in range(count)])  4.21 us
    pallas_call x1, Pallas kernels, per_device(): pl.pallas_call(faces_kernel, out_shape=(bf16(64, FACE),) * 2, grid=(1,),...  1.37 us
  transfers between devices with their start and end apart: 18, of which 4 were waited for; matrix products, arithmetic and copies ran while one was open for 0% of the time, Pallas kernels for 26%

profile of v18, /device:TPU:1, one launch (start us, length us, event | category | flops | bytes accessed | tf_op | source)
XLA Modules:
  0.0 51.9 jit_solution(18001161798319056096)
XLA Ops:
  0.7 2.2 %collective-permute-start.2 = (bf16[32,1024]{1,0:T(8,128)(2,1)}, bf16[32,1024]{1,0:T(8,128)(2,1)S(1)}, u32[]{:S(2)}, u32[]{:S(2)}) collective-permute-start(bf16[32,1024]{1,0:T(8,128)(2,1)} %refs_0_.1), channel_id=1, source_target_pairs={{0,1},{1,0},{2,3},{3,2},{4,5},{5,4},{6,7},{7,6},{8,9},{9,8},{10,11... | collective-permute-start | bytes 196616 | tf_op jit(solution)/shard_map/ppermute | solution.py:296
  2.9 1.4 %faces.1 = (bf16[64,128]{1,0:T(8,128)(2,1)}, bf16[64,128]{1,0:T(8,128)(2,1)}) custom-call(bf16[32,1024]{1,0:T(8,128)(2,1)} %x_ref.3, bf16[32,1024]{1,0:T(8,128)(2,1)} %refs_0_.1), custom_call_target="tpu_custom_call" | custom-call | flops 1073741824 | bytes 65536 | tf_op jit(solution)/shard_map/faces/pallas_call | solution.py:301
  4.2 1.1 %collective-permute-start = (bf16[64,128]{1,0:T(8,128)(2,1)}, bf16[64,128]{1,0:T(8,128)(2,1)S(1)}, u32[]{:S(2)}, u32[]{:S(2)}) collective-permute-start(bf16[64,128]{1,0:T(8,128)(2,1)} %get-tuple-element.34), channel_id=1, source_target_pairs={{0,4},{4,0},{8,12},{12,8},{16,20},{20,16},{24,28},{28,24},{32,36},... | collective-permute-start | bytes 49160 | tf_op jit(solution)/shard_map/ppermute | solution.py:279
  5.4 0.9 %collective-permute-start.1 = (bf16[64,128]{1,0:T(8,128)(2,1)}, bf16[64,128]{1,0:T(8,128)(2,1)S(1)}, u32[]{:S(2)}, u32[]{:S(2)}) collective-permute-start(bf16[64,128]{1,0:T(8,128)(2,1)} %get-tuple-element.35), channel_id=1, source_target_pairs={{0,252},{4,8},{8,4},{12,16},{16,12},{20,24},{24,20},{28,32},{32,28... | collective-permute-start | bytes 49160 | tf_op jit(solution)/shard_map/ppermute | solution.py:285
  6.3 2.0 %collective-permute-start.3 = (bf16[64,1024]{1,0:T(8,128)(2,1)S(1)}, bf16[64,1024]{1,0:T(8,128)(2,1)S(1)}, u32[]{:S(2)}, u32[]{:S(2)}) collective-permute-start(bf16[64,1024]{1,0:T(8,128)(2,1)S(1)} %join.2.pair_ref), channel_id=1, source_target_pairs={{0,3},{1,2},{2,1},{3,0},{4,7},{5,6},{6,5},{7,4},{8,11},{9,10},{10,... | collective-permute-start | bytes 393224 | tf_op jit(solution)/shard_map/ppermute | solution.py:296
  8.3 3.9 %gather.1.dense_in = bf16[864,1024]{1,0:T(8,128)(2,1)S(1)} custom-call(bf16[32,1024]{1,0:T(8,128)(2,1)S(1)} %copy-done.3, s32[27,1024]{1,0:T(8,128)S(1)} %copy-done.2), custom_call_target="tpu_custom_call" | custom-call | flops 3221225472 | bytes 1945600 | tf_op jit(solution)/shard_map/gather/pallas_call | solution.py:256
  12.2 0.7 %weight_terms.1 = (bf16[864,1024]{1,0:T(8,128)(2,1)S(1)}, bf16[128,1024]{1,0:T(8,128)(2,1)S(1)}, f32[448,128]{1,0:T(8,128)S(1)}, f32[448,128]{1,0:T(8,128)S(1)}) custom-call(bf16[864,1024]{1,0:T(8,128)(2,1)S(1)} %gather.1.dense_in, s32[27,1024]{1,0:T(8,128)S(1)} %copy-done.2, ...), custom_call_target="tpu_custom_call", output_to_operand_aliasing={{0}: (0, {})} | custom-call | flops 1073741824 | bytes 4665344 | tf_op jit(solution)/shard_map/weight_terms/pallas_call | solution.py:256
  12.9 7.5 %collective-permute-start.4 = (f32[448,128]{1,0:T(8,128)S(1)}, f32[448,128]{1,0:T(8,128)S(1)}, u32[]{:S(2)}, u32[]{:S(2)}) collective-permute-start(f32[448,128]{1,0:T(8,128)S(1)} %get-tuple-element.38), channel_id=1, source_target_pairs={{0,4},{4,0},{8,12},{12,8},{16,20},{20,16},{24,28},{28,24},{32,36},... | collective-permute-start | bytes 688136 | tf_op jit(solution)/shard_map/ppermute | solution.py:279
  20.5 0.6 %back_terms.1.terms = f32[864,1024]{1,0:T(8,128)S(1)} custom-call(bf16[864,128]{1,0:T(8,128)(2,1)S(1)} %bitcast.2, bf16[128,1024]{1,0:T(8,128)(2,1)S(1)} %get-tuple-element.36.grad_ref), custom_call_target="tpu_custom_call" | custom-call | flops 1073741824 | bytes 4022272 | tf_op jit(solution)/shard_map/back_terms/pallas_call | solution.py:256
  21.1 0.5 forward.1
  21.6 0.1 collective-permute-start.5
  21.7 0.1 collective-permute-start.6
  21.8 2.5 %collective-permute-start.7 = (f32[112,128]{1,0:T(8,128)S(1)}, f32[112,128]{1,0:T(8,128)S(1)}, u32[]{:S(2)}, u32[]{:S(2)}) collective-permute-start(f32[112,128]{1,0:T(8,128)S(1)} %get-tuple-element.45), channel_id=1, source_target_pairs={{0,8},{4,12},{8,0},{12,4},{16,24},{20,28},{24,16},{28,20},{32,40},... | collective-permute-start | bytes 172040 | tf_op jit(solution)/shard_map/ppermute | solution.py:279
  24.4 1.0 %back_inner.3.refs_0_ = f32[32,1024]{1,0:T(8,128)S(1)} custom-call(f32[864,1024]{1,0:T(8,128)S(1)} %back_terms.1.terms, s32[27,1024]{1,0:T(8,128)S(1)} %copy-done.2), custom_call_target="tpu_custom_call" | custom-call | flops 2147483648 | bytes 3780608 | tf_op jit(solution)/shard_map/back_inner/pallas_call | solution.py:256
  25.3 0.4 collective-permute-start.8
  25.7 1.6 %collective-permute-done.7.refs_3_ = f32[112,128]{1,0:T(8,128)S(1)} collective-permute-done((f32[112,128]{1,0:T(8,128)S(1)}, f32[112,128]{1,0:T(8,128)S(1)}, u32[]{:S(2)}, u32[]{:S(2)}) %collective-permute-start.7) | collective-permute-done | bytes 57376 | tf_op jit(solution)/shard_map/ppermute | solution.py:279
  27.3 0.1 collective-permute-start.9
  27.4 2.7 %back_inner.4.refs_0_ = f32[32,1024]{1,0:T(8,128)S(1)} custom-call(f32[864,1024]{1,0:T(8,128)S(1)} %back_terms.1.terms, s32[27,1024]{1,0:T(8,128)S(1)} %copy-done.2, f32[32,1024]{1,0:T(8,128)S(1)} %back_inner.3.refs_0_), custom_call_target="tpu_custom_call", output_to_operand_aliasing={{}: (2, {})} | custom-call | flops 3221225472 | bytes 3911680 | tf_op jit(solution)/shard_map/back_inner/pallas_call | solution.py:256
  30.1 1.5 %collective-permute-done.9.refs_1_ = f32[112,128]{1,0:T(8,128)S(1)} collective-permute-done((f32[112,128]{1,0:T(8,128)S(1)}, f32[112,128]{1,0:T(8,128)S(1)}, u32[]{:S(2)}, u32[]{:S(2)}) %collective-permute-start.9) | collective-permute-done | bytes 57376 | tf_op jit(solution)/shard_map/ppermute | solution.py:279
  31.6 1.6 %collective-permute-start.13 = (f32[112,128]{1,0:T(8,128)S(1)}, f32[112,128]{1,0:T(8,128)S(1)}, u32[]{:S(2)}, u32[]{:S(2)}) collective-permute-start(f32[112,128]{1,0:T(8,128)S(1)} %sum_two.1.refs_0_), channel_id=1, source_target_pairs={{0,160},{4,164},{8,168},{12,172},{16,176},{20,180},{24,184},{28,18... | collective-permute-start | bytes 172040 | tf_op jit(solution)/shard_map/ppermute | solution.py:279
  33.3 0.5 collective-permute-start.12
  33.7 3.6 %collective-permute-start.11 = (f32[112,128]{1,0:T(8,128)S(1)}, f32[112,128]{1,0:T(8,128)S(1)}, u32[]{:S(2)}, u32[]{:S(2)}) collective-permute-start(f32[112,128]{1,0:T(8,128)S(1)} %sum_two.1.refs_0_), channel_id=1, source_target_pairs={{0,96},{4,100},{8,104},{12,108},{16,112},{20,116},{24,120},{28,124... | collective-permute-start | bytes 172040 | tf_op jit(solution)/shard_map/ppermute | solution.py:279
  37.4 2.2 %collective-permute-start.10 = (f32[32,1536]{1,0:T(8,128)S(1)}, f32[32,1536]{1,0:T(8,128)S(1)}, u32[]{:S(2)}, u32[]{:S(2)}) collective-permute-start(f32[32,1536]{1,0:T(8,128)S(1)} %get-tuple-element.56), channel_id=1, source_target_pairs={{0,3},{1,2},{2,1},{3,0},{4,7},{5,6},{6,5},{7,4},{8,11},{9,10},{10,... | collective-permute-start | bytes 589832 | tf_op jit(solution)/shard_map/ppermute | solution.py:296
  39.6 1.0 %back_inner.5.inner = f32[32,1024]{1,0:T(8,128)S(1)} custom-call(f32[864,1024]{1,0:T(8,128)S(1)} %back_terms.1.terms, s32[27,1024]{1,0:T(8,128)S(1)} %copy-done.2, f32[32,1024]{1,0:T(8,128)S(1)} %back_inner.4.refs_0_), custom_call_target="tpu_custom_call", output_to_operand_aliasing={{}: (2, {})} | custom-call | flops 2147483648 | bytes 3911680 | tf_op jit(solution)/shard_map/back_inner/pallas_call | solution.py:256
  40.6 0.1 collective-permute-start.16
  40.7 0.6 %collective-permute-start.15 = (f32[112,128]{1,0:T(8,128)S(1)}, f32[112,128]{1,0:T(8,128)S(1)}, u32[]{:S(2)}, u32[]{:S(2)}) collective-permute-start(f32[112,128]{1,0:T(8,128)S(1)} %sum_four.3.refs_0_), channel_id=1, source_target_pairs={{0,32},{4,36},{8,40},{12,44},{16,48},{20,52},{24,56},{28,60},{32,0... | collective-permute-start | bytes 172040 | tf_op jit(solution)/shard_map/ppermute | solution.py:279
  41.4 2.0 %collective-permute-start.14 = (f32[112,128]{1,0:T(8,128)S(1)}, f32[112,128]{1,0:T(8,128)S(1)}, u32[]{:S(2)}, u32[]{:S(2)}) collective-permute-start(f32[112,128]{1,0:T(8,128)S(1)} %sum_four.3.refs_0_), channel_id=1, source_target_pairs={{0,8},{4,12},{8,0},{12,4},{16,24},{20,28},{24,16},{28,20},{32,40},... | collective-permute-start | bytes 172040 | tf_op jit(solution)/shard_map/ppermute | solution.py:279
  43.4 0.1 collective-permute-done.10.second_ref
  43.4 2.4 %edge.1 = (bf16[32,1024]{1,0:T(8,128)(2,1)}, bf16[32,1024]{1,0:T(8,128)(2,1)}) custom-call(f32[864,1024]{1,0:T(8,128)S(1)} %back_terms.1.terms, s32[27,1024]{1,0:T(8,128)S(1)} %copy-done.2, bf16[864,128]{1,0:T(8,128)(2,1)S(1)} %bitcast.4, bf16[64,128]{1,0:T(8,128)(2,1)S(1)} %collective-permute-done.near_ref, ...), custom_call_target="tpu_custom_call" | custom-call | flops 2147483648 | bytes 4788224 | tf_op jit(solution)/shard_map/edge/pallas_call | solution.py:256
  45.8 4.1 %collective-permute-start.17 = (f32[448,128]{1,0:T(8,128)S(1)}, f32[448,128]{1,0:T(8,128)S(1)}, u32[]{:S(2)}, u32[]{:S(2)}) collective-permute-start(f32[448,128]{1,0:T(8,128)S(1)} %join.3.even_ref), channel_id=1, source_target_pairs={{0,4},{4,0},{8,12},{12,8},{16,20},{20,16},{24,28},{28,24},{32,36},... | collective-permute-start | bytes 688136 | tf_op jit(solution)/shard_map/ppermute | solution.py:279
  50.0 1.1 %collective-permute-done.17.odd_ref = f32[448,128]{1,0:T(8,128)S(1)} collective-permute-done((f32[448,128]{1,0:T(8,128)S(1)}, f32[448,128]{1,0:T(8,128)S(1)}, u32[]{:S(2)}, u32[]{:S(2)}) %collective-permute-start.17) | collective-permute-done | bytes 229408 | tf_op jit(solution)/shard_map/ppermute | solution.py:279
  51.1 0.8 %place.1 = f32[864,128]{1,0:T(8,128)} custom-call(f32[448,128]{1,0:T(8,128)S(1)} %join.3.even_ref, f32[448,128]{1,0:T(8,128)S(1)} %collective-permute-done.17.odd_ref), custom_call_target="tpu_custom_call" | custom-call | bytes 901120 | tf_op jit(solution)/shard_map/place/pallas_call | solution.py:256
  (29 shorter events, 0.2 us)
Async XLA Ops:
  0.6 5.7 %copy-start.1 = (bf16[32,1024]{1,0:T(8,128)(2,1)S(1)}, bf16[32,1024]{1,0:T(8,128)(2,1)}, u32[]{:S(2)}) copy-start(bf16[32,1024]{1,0:T(8,128)(2,1)} %refs_0_.1) | copy-start | bytes 196612
  0.6 7.7 %copy-start.3 = (bf16[32,1024]{1,0:T(8,128)(2,1)S(1)}, bf16[32,1024]{1,0:T(8,128)(2,1)}, u32[]{:S(2)}) copy-start(bf16[32,1024]{1,0:T(8,128)(2,1)} %x_ref.3) | copy-start | bytes 196612
  0.7 7.7 %copy-start.2 = (s32[27,1024]{1,0:T(8,128)S(1)}, s32[27,1024]{1,0:T(8,128)}, u32[]{:S(2)}) copy-start(s32[27,1024]{1,0:T(8,128)} %rule_ref.11) | copy-start | bytes 331780
  0.7 5.6 %collective-permute-start.2 = (bf16[32,1024]{1,0:T(8,128)(2,1)}, bf16[32,1024]{1,0:T(8,128)(2,1)S(1)}, u32[]{:S(2)}, u32[]{:S(2)}) collective-permute-start(bf16[32,1024]{1,0:T(8,128)(2,1)} %refs_0_.1), channel_id=1, source_target_pairs={{0,1},{1,0},{2,3},{3,2},{4,5},{5,4},{6,7},{7,6},{8,9},{9,8},{10,11... | collective-permute-start | bytes 196616 | tf_op jit(solution)/shard_map/ppermute | solution.py:296
  4.2 7.9 %collective-permute-start = (bf16[64,128]{1,0:T(8,128)(2,1)}, bf16[64,128]{1,0:T(8,128)(2,1)S(1)}, u32[]{:S(2)}, u32[]{:S(2)}) collective-permute-start(bf16[64,128]{1,0:T(8,128)(2,1)} %get-tuple-element.34), channel_id=1, source_target_pairs={{0,4},{4,0},{8,12},{12,8},{16,20},{20,16},{24,28},{28,24},{32,36},... | collective-permute-start | bytes 49160 | tf_op jit(solution)/shard_map/ppermute | solution.py:279
  5.4 6.8 %collective-permute-start.1 = (bf16[64,128]{1,0:T(8,128)(2,1)}, bf16[64,128]{1,0:T(8,128)(2,1)S(1)}, u32[]{:S(2)}, u32[]{:S(2)}) collective-permute-start(bf16[64,128]{1,0:T(8,128)(2,1)} %get-tuple-element.35), channel_id=1, source_target_pairs={{0,252},{4,8},{8,4},{12,16},{16,12},{20,24},{24,20},{28,32},{32,28... | collective-permute-start | bytes 49160 | tf_op jit(solution)/shard_map/ppermute | solution.py:285
  6.3 5.9 %collective-permute-start.3 = (bf16[64,1024]{1,0:T(8,128)(2,1)S(1)}, bf16[64,1024]{1,0:T(8,128)(2,1)S(1)}, u32[]{:S(2)}, u32[]{:S(2)}) collective-permute-start(bf16[64,1024]{1,0:T(8,128)(2,1)S(1)} %join.2.pair_ref), channel_id=1, source_target_pairs={{0,3},{1,2},{2,1},{3,0},{4,7},{5,6},{6,5},{7,4},{8,11},{9,10},{10,... | collective-permute-start | bytes 393224 | tf_op jit(solution)/shard_map/ppermute | solution.py:296
  12.2 8.3 %copy-start = (bf16[27,32,128]{2,1,0:T(8,128)(2,1)S(1)}, bf16[27,32,128]{2,1,0:T(8,128)(2,1)}, u32[]{:S(2)}) copy-start(bf16[27,32,128]{2,1,0:T(8,128)(2,1)} %param.5) | copy-start | bytes 663556
  12.9 8.6 %collective-permute-start.4 = (f32[448,128]{1,0:T(8,128)S(1)}, f32[448,128]{1,0:T(8,128)S(1)}, u32[]{:S(2)}, u32[]{:S(2)}) collective-permute-start(f32[448,128]{1,0:T(8,128)S(1)} %get-tuple-element.38), channel_id=1, source_target_pairs={{0,4},{4,0},{8,12},{12,8},{16,20},{20,16},{24,28},{28,24},{32,36},... | collective-permute-start | bytes 688136 | tf_op jit(solution)/shard_map/ppermute | solution.py:279
  21.6 4.1 %collective-permute-start.5 = (f32[112,128]{1,0:T(8,128)S(1)}, f32[112,128]{1,0:T(8,128)S(1)}, u32[]{:S(2)}, u32[]{:S(2)}) collective-permute-start(f32[112,128]{1,0:T(8,128)S(1)} %get-tuple-element.43), channel_id=1, source_target_pairs={{0,40},{4,44},{8,32},{12,36},{16,56},{20,60},{24,48},{28,52},{32,8... | collective-permute-start | bytes 172040 | tf_op jit(solution)/shard_map/ppermute | solution.py:279
  21.7 4.0 %collective-permute-start.6 = (f32[112,128]{1,0:T(8,128)S(1)}, f32[112,128]{1,0:T(8,128)S(1)}, u32[]{:S(2)}, u32[]{:S(2)}) collective-permute-start(f32[112,128]{1,0:T(8,128)S(1)} %get-tuple-element.44), channel_id=1, source_target_pairs={{0,32},{4,36},{8,40},{12,44},{16,48},{20,52},{24,56},{28,60},{32,0... | collective-permute-start | bytes 172040 | tf_op jit(solution)/shard_map/ppermute | solution.py:279
  21.8 5.5 %collective-permute-start.7 = (f32[112,128]{1,0:T(8,128)S(1)}, f32[112,128]{1,0:T(8,128)S(1)}, u32[]{:S(2)}, u32[]{:S(2)}) collective-permute-start(f32[112,128]{1,0:T(8,128)S(1)} %get-tuple-element.45), channel_id=1, source_target_pairs={{0,8},{4,12},{8,0},{12,4},{16,24},{20,28},{24,16},{28,20},{32,40},... | collective-permute-start | bytes 172040 | tf_op jit(solution)/shard_map/ppermute | solution.py:279
  25.3 12.1 %collective-permute-start.8 = (f32[64,1152]{1,0:T(8,128)S(1)}, f32[64,1152]{1,0:T(8,128)S(1)}, u32[]{:S(2)}, u32[]{:S(2)}) collective-permute-start(f32[64,1152]{1,0:T(8,128)S(1)} %get-tuple-element.51), channel_id=1, source_target_pairs={{0,1},{1,0},{2,3},{3,2},{4,5},{5,4},{6,7},{7,6},{8,9},{9,8},{10,11... | collective-permute-start | bytes 884744 | tf_op jit(solution)/shard_map/ppermute | solution.py:296
  27.3 4.3 %collective-permute-start.9 = (f32[112,128]{1,0:T(8,128)S(1)}, f32[112,128]{1,0:T(8,128)S(1)}, u32[]{:S(2)}, u32[]{:S(2)}) collective-permute-start(f32[112,128]{1,0:T(8,128)S(1)} %sum_four.2.refs_0_), channel_id=1, source_target_pairs={{0,24},{4,28},{8,16},{12,20},{16,8},{20,12},{24,0},{28,4},{32,56},... | collective-permute-start | bytes 172040 | tf_op jit(solution)/shard_map/ppermute | solution.py:279
  31.6 8.9 %collective-permute-start.13 = (f32[112,128]{1,0:T(8,128)S(1)}, f32[112,128]{1,0:T(8,128)S(1)}, u32[]{:S(2)}, u32[]{:S(2)}) collective-permute-start(f32[112,128]{1,0:T(8,128)S(1)} %sum_two.1.refs_0_), channel_id=1, source_target_pairs={{0,160},{4,164},{8,168},{12,172},{16,176},{20,180},{24,184},{28,18... | collective-permute-start | bytes 172040 | tf_op jit(solution)/shard_map/ppermute | solution.py:279
  33.3 7.3 %collective-permute-start.12 = (f32[112,128]{1,0:T(8,128)S(1)}, f32[112,128]{1,0:T(8,128)S(1)}, u32[]{:S(2)}, u32[]{:S(2)}) collective-permute-start(f32[112,128]{1,0:T(8,128)S(1)} %sum_two.1.refs_0_), channel_id=1, source_target_pairs={{0,192},{4,196},{8,200},{12,204},{16,208},{20,212},{24,216},{28,22... | collective-permute-start | bytes 172040 | tf_op jit(solution)/shard_map/ppermute | solution.py:279
  33.7 6.8 %collective-permute-start.11 = (f32[112,128]{1,0:T(8,128)S(1)}, f32[112,128]{1,0:T(8,128)S(1)}, u32[]{:S(2)}, u32[]{:S(2)}) collective-permute-start(f32[112,128]{1,0:T(8,128)S(1)} %sum_two.1.refs_0_), channel_id=1, source_target_pairs={{0,96},{4,100},{8,104},{12,108},{16,112},{20,116},{24,120},{28,124... | collective-permute-start | bytes 172040 | tf_op jit(solution)/shard_map/ppermute | solution.py:279
  37.4 6.0 %collective-permute-start.10 = (f32[32,1536]{1,0:T(8,128)S(1)}, f32[32,1536]{1,0:T(8,128)S(1)}, u32[]{:S(2)}, u32[]{:S(2)}) collective-permute-start(f32[32,1536]{1,0:T(8,128)S(1)} %get-tuple-element.56), channel_id=1, source_target_pairs={{0,3},{1,2},{2,1},{3,0},{4,7},{5,6},{6,5},{7,4},{8,11},{9,10},{10,... | collective-permute-start | bytes 589832 | tf_op jit(solution)/shard_map/ppermute | solution.py:296
  40.6 5.2 %collective-permute-start.16 = (f32[112,128]{1,0:T(8,128)S(1)}, f32[112,128]{1,0:T(8,128)S(1)}, u32[]{:S(2)}, u32[]{:S(2)}) collective-permute-start(f32[112,128]{1,0:T(8,128)S(1)} %sum_four.3.refs_0_), channel_id=1, source_target_pairs={{0,40},{4,44},{8,32},{12,36},{16,56},{20,60},{24,48},{28,52},{32,8... | collective-permute-start | bytes 172040 | tf_op jit(solution)/shard_map/ppermute | solution.py:279
  40.7 5.1 %collective-permute-start.15 = (f32[112,128]{1,0:T(8,128)S(1)}, f32[112,128]{1,0:T(8,128)S(1)}, u32[]{:S(2)}, u32[]{:S(2)}) collective-permute-start(f32[112,128]{1,0:T(8,128)S(1)} %sum_four.3.refs_0_), channel_id=1, source_target_pairs={{0,32},{4,36},{8,40},{12,44},{16,48},{20,52},{24,56},{28,60},{32,0... | collective-permute-start | bytes 172040 | tf_op jit(solution)/shard_map/ppermute | solution.py:279
  41.4 4.5 %collective-permute-start.14 = (f32[112,128]{1,0:T(8,128)S(1)}, f32[112,128]{1,0:T(8,128)S(1)}, u32[]{:S(2)}, u32[]{:S(2)}) collective-permute-start(f32[112,128]{1,0:T(8,128)S(1)} %sum_four.3.refs_0_), channel_id=1, source_target_pairs={{0,8},{4,12},{8,0},{12,4},{16,24},{20,28},{24,16},{28,20},{32,40},... | collective-permute-start | bytes 172040 | tf_op jit(solution)/shard_map/ppermute | solution.py:279
  45.8 5.2 %collective-permute-start.17 = (f32[448,128]{1,0:T(8,128)S(1)}, f32[448,128]{1,0:T(8,128)S(1)}, u32[]{:S(2)}, u32[]{:S(2)}) collective-permute-start(f32[448,128]{1,0:T(8,128)S(1)} %join.3.even_ref), channel_id=1, source_target_pairs={{0,4},{4,0},{8,12},{12,8},{16,20},{20,16},{24,28},{28,24},{32,36},... | collective-permute-start | bytes 688136 | tf_op jit(solution)/shard_map/ppermute | solution.py:279

commit v19 on v18

--- a/solution.py
+++ b/solution.py
@@ -350,7 +350,7 @@
     inner = inner_part((4, 5, 6), inner)
     came, = after((came,), inner)
     total = call(sum_kernel, f32(PART, 128), (total, came), name="sum_two")
-    others = [swap(total, m) for m in (Z3, Z6, Z3 ^ Z6)]
+    others = [swap(total, m) for m in (Z3, Z3 ^ Z6, Z6)]
     ours, first = after((ours, first), total)
     own, second = call(
         middle_kernel, (f32(32, VOX), f32(32, VOX + 4 * FACE)), (ours, first, near, far),

time: 52 us -> 52 us (level)
  no operation moved by 1% of the time
where the time goes in v19:
time: 52 us; the launch traced here: 51.9 us
  starting transfers between devices  31.7 us (61%)
  Pallas kernels  15 us (29%)
  waiting for transfers between devices  4.3 us (8%)
  between operations  0.83 us (2%)
    ppermute x13, starting transfers between devices, swap(): return lax.ppermute(value, 'blk', [(i, i ^ mask) for i in range(count)])  24 us
    pallas_call x16, Pallas kernels, call(): pl.pallas_call(kernel, out_shape=outs, in_specs=[VMEM] * len(args), out_s...  13.6 us
    ppermute x4, starting transfers between devices, over_ch(): return lax.ppermute(value, 'ch', [(i, i ^ mask) for i in range(4)])  6.76 us
    ppermute x13, waiting for transfers between devices, swap(): return lax.ppermute(value, 'blk', [(i, i ^ mask) for i in range(count)])  4.21 us
    pallas_call x1, Pallas kernels, per_device(): pl.pallas_call(faces_kernel, out_shape=(bf16(64, FACE),) * 2, grid=(1,),...  1.37 us
  transfers between devices with their start and end apart: 18, of which 4 were waited for; matrix products, arithmetic and copies ran while one was open for 0% of the time, Pallas kernels for 26%

profile of v19, /device:TPU:1, one launch (start us, length us, event | category | flops | bytes accessed | tf_op | source)
XLA Modules:
  0.0 51.9 jit_solution(13363453148173715843)
XLA Ops:
  0.7 2.2 %collective-permute-start.2 = (bf16[32,1024]{1,0:T(8,128)(2,1)}, bf16[32,1024]{1,0:T(8,128)(2,1)S(1)}, u32[]{:S(2)}, u32[]{:S(2)}) collective-permute-start(bf16[32,1024]{1,0:T(8,128)(2,1)} %refs_0_.1), channel_id=1, source_target_pairs={{0,1},{1,0},{2,3},{3,2},{4,5},{5,4},{6,7},{7,6},{8,9},{9,8},{10,11... | collective-permute-start | bytes 196616 | tf_op jit(solution)/shard_map/ppermute | solution.py:296
  2.9 1.4 %faces.1 = (bf16[64,128]{1,0:T(8,128)(2,1)}, bf16[64,128]{1,0:T(8,128)(2,1)}) custom-call(bf16[32,1024]{1,0:T(8,128)(2,1)} %x_ref.3, bf16[32,1024]{1,0:T(8,128)(2,1)} %refs_0_.1), custom_call_target="tpu_custom_call" | custom-call | flops 1073741824 | bytes 65536 | tf_op jit(solution)/shard_map/faces/pallas_call | solution.py:301
  4.2 1.1 %collective-permute-start = (bf16[64,128]{1,0:T(8,128)(2,1)}, bf16[64,128]{1,0:T(8,128)(2,1)S(1)}, u32[]{:S(2)}, u32[]{:S(2)}) collective-permute-start(bf16[64,128]{1,0:T(8,128)(2,1)} %get-tuple-element.34), channel_id=1, source_target_pairs={{0,4},{4,0},{8,12},{12,8},{16,20},{20,16},{24,28},{28,24},{32,36},... | collective-permute-start | bytes 49160 | tf_op jit(solution)/shard_map/ppermute | solution.py:279
  5.4 0.9 %collective-permute-start.1 = (bf16[64,128]{1,0:T(8,128)(2,1)}, bf16[64,128]{1,0:T(8,128)(2,1)S(1)}, u32[]{:S(2)}, u32[]{:S(2)}) collective-permute-start(bf16[64,128]{1,0:T(8,128)(2,1)} %get-tuple-element.35), channel_id=1, source_target_pairs={{0,252},{4,8},{8,4},{12,16},{16,12},{20,24},{24,20},{28,32},{32,28... | collective-permute-start | bytes 49160 | tf_op jit(solution)/shard_map/ppermute | solution.py:285
  6.3 2.0 %collective-permute-start.3 = (bf16[64,1024]{1,0:T(8,128)(2,1)S(1)}, bf16[64,1024]{1,0:T(8,128)(2,1)S(1)}, u32[]{:S(2)}, u32[]{:S(2)}) collective-permute-start(bf16[64,1024]{1,0:T(8,128)(2,1)S(1)} %join.2.pair_ref), channel_id=1, source_target_pairs={{0,3},{1,2},{2,1},{3,0},{4,7},{5,6},{6,5},{7,4},{8,11},{9,10},{10,... | collective-permute-start | bytes 393224 | tf_op jit(solution)/shard_map/ppermute | solution.py:296
  8.3 3.9 %gather.1.dense_in = bf16[864,1024]{1,0:T(8,128)(2,1)S(1)} custom-call(bf16[32,1024]{1,0:T(8,128)(2,1)S(1)} %copy-done.3, s32[27,1024]{1,0:T(8,128)S(1)} %copy-done.2), custom_call_target="tpu_custom_call" | custom-call | flops 3221225472 | bytes 1945600 | tf_op jit(solution)/shard_map/gather/pallas_call | solution.py:256
  12.2 0.7 %weight_terms.1 = (bf16[864,1024]{1,0:T(8,128)(2,1)S(1)}, bf16[128,1024]{1,0:T(8,128)(2,1)S(1)}, f32[448,128]{1,0:T(8,128)S(1)}, f32[448,128]{1,0:T(8,128)S(1)}) custom-call(bf16[864,1024]{1,0:T(8,128)(2,1)S(1)} %gather.1.dense_in, s32[27,1024]{1,0:T(8,128)S(1)} %copy-done.2, ...), custom_call_target="tpu_custom_call", output_to_operand_aliasing={{0}: (0, {})} | custom-call | flops 1073741824 | bytes 4665344 | tf_op jit(solution)/shard_map/weight_terms/pallas_call | solution.py:256
  12.9 7.5 %collective-permute-start.4 = (f32[448,128]{1,0:T(8,128)S(1)}, f32[448,128]{1,0:T(8,128)S(1)}, u32[]{:S(2)}, u32[]{:S(2)}) collective-permute-start(f32[448,128]{1,0:T(8,128)S(1)} %get-tuple-element.38), channel_id=1, source_target_pairs={{0,4},{4,0},{8,12},{12,8},{16,20},{20,16},{24,28},{28,24},{32,36},... | collective-permute-start | bytes 688136 | tf_op jit(solution)/shard_map/ppermute | solution.py:279
  20.5 0.6 %back_terms.1.terms = f32[864,1024]{1,0:T(8,128)S(1)} custom-call(bf16[864,128]{1,0:T(8,128)(2,1)S(1)} %bitcast.2, bf16[128,1024]{1,0:T(8,128)(2,1)S(1)} %get-tuple-element.36.grad_ref), custom_call_target="tpu_custom_call" | custom-call | flops 1073741824 | bytes 4022272 | tf_op jit(solution)/shard_map/back_terms/pallas_call | solution.py:256
  21.1 0.5 forward.1
  21.6 0.1 collective-permute-start.5
  21.7 0.1 collective-permute-start.6
  21.8 2.5 %collective-permute-start.7 = (f32[112,128]{1,0:T(8,128)S(1)}, f32[112,128]{1,0:T(8,128)S(1)}, u32[]{:S(2)}, u32[]{:S(2)}) collective-permute-start(f32[112,128]{1,0:T(8,128)S(1)} %get-tuple-element.45), channel_id=1, source_target_pairs={{0,8},{4,12},{8,0},{12,4},{16,24},{20,28},{24,16},{28,20},{32,40},... | collective-permute-start | bytes 172040 | tf_op jit(solution)/shard_map/ppermute | solution.py:279
  24.4 1.0 %back_inner.3.refs_0_ = f32[32,1024]{1,0:T(8,128)S(1)} custom-call(f32[864,1024]{1,0:T(8,128)S(1)} %back_terms.1.terms, s32[27,1024]{1,0:T(8,128)S(1)} %copy-done.2), custom_call_target="tpu_custom_call" | custom-call | flops 2147483648 | bytes 3780608 | tf_op jit(solution)/shard_map/back_inner/pallas_call | solution.py:256
  25.3 0.4 collective-permute-start.8
  25.7 1.6 %collective-permute-done.7.refs_3_ = f32[112,128]{1,0:T(8,128)S(1)} collective-permute-done((f32[112,128]{1,0:T(8,128)S(1)}, f32[112,128]{1,0:T(8,128)S(1)}, u32[]{:S(2)}, u32[]{:S(2)}) %collective-permute-start.7) | collective-permute-done | bytes 57376 | tf_op jit(solution)/shard_map/ppermute | solution.py:279
  27.3 0.1 collective-permute-start.9
  27.4 2.7 %back_inner.4.refs_0_ = f32[32,1024]{1,0:T(8,128)S(1)} custom-call(f32[864,1024]{1,0:T(8,128)S(1)} %back_terms.1.terms, s32[27,1024]{1,0:T(8,128)S(1)} %copy-done.2, f32[32,1024]{1,0:T(8,128)S(1)} %back_inner.3.refs_0_), custom_call_target="tpu_custom_call", output_to_operand_aliasing={{}: (2, {})} | custom-call | flops 3221225472 | bytes 3911680 | tf_op jit(solution)/shard_map/back_inner/pallas_call | solution.py:256
  30.1 1.5 %collective-permute-done.9.refs_1_ = f32[112,128]{1,0:T(8,128)S(1)} collective-permute-done((f32[112,128]{1,0:T(8,128)S(1)}, f32[112,128]{1,0:T(8,128)S(1)}, u32[]{:S(2)}, u32[]{:S(2)}) %collective-permute-start.9) | collective-permute-done | bytes 57376 | tf_op jit(solution)/shard_map/ppermute | solution.py:279
  31.6 1.2 %collective-permute-start.13 = (f32[112,128]{1,0:T(8,128)S(1)}, f32[112,128]{1,0:T(8,128)S(1)}, u32[]{:S(2)}, u32[]{:S(2)}) collective-permute-start(f32[112,128]{1,0:T(8,128)S(1)} %sum_two.1.refs_0_), channel_id=1, source_target_pairs={{0,192},{4,196},{8,200},{12,204},{16,208},{20,212},{24,216},{28,22... | collective-permute-start | bytes 172040 | tf_op jit(solution)/shard_map/ppermute | solution.py:279
  32.8 0.9 %collective-permute-start.12 = (f32[112,128]{1,0:T(8,128)S(1)}, f32[112,128]{1,0:T(8,128)S(1)}, u32[]{:S(2)}, u32[]{:S(2)}) collective-permute-start(f32[112,128]{1,0:T(8,128)S(1)} %sum_two.1.refs_0_), channel_id=1, source_target_pairs={{0,160},{4,164},{8,168},{12,172},{16,176},{20,180},{24,184},{28,18... | collective-permute-start | bytes 172040 | tf_op jit(solution)/shard_map/ppermute | solution.py:279
  33.7 3.6 %collective-permute-start.11 = (f32[112,128]{1,0:T(8,128)S(1)}, f32[112,128]{1,0:T(8,128)S(1)}, u32[]{:S(2)}, u32[]{:S(2)}) collective-permute-start(f32[112,128]{1,0:T(8,128)S(1)} %sum_two.1.refs_0_), channel_id=1, source_target_pairs={{0,96},{4,100},{8,104},{12,108},{16,112},{20,116},{24,120},{28,124... | collective-permute-start | bytes 172040 | tf_op jit(solution)/shard_map/ppermute | solution.py:279
  37.4 2.2 %collective-permute-start.10 = (f32[32,1536]{1,0:T(8,128)S(1)}, f32[32,1536]{1,0:T(8,128)S(1)}, u32[]{:S(2)}, u32[]{:S(2)}) collective-permute-start(f32[32,1536]{1,0:T(8,128)S(1)} %get-tuple-element.56), channel_id=1, source_target_pairs={{0,3},{1,2},{2,1},{3,0},{4,7},{5,6},{6,5},{7,4},{8,11},{9,10},{10,... | collective-permute-start | bytes 589832 | tf_op jit(solution)/shard_map/ppermute | solution.py:296
  39.6 1.0 %back_inner.5.inner = f32[32,1024]{1,0:T(8,128)S(1)} custom-call(f32[864,1024]{1,0:T(8,128)S(1)} %back_terms.1.terms, s32[27,1024]{1,0:T(8,128)S(1)} %copy-done.2, f32[32,1024]{1,0:T(8,128)S(1)} %back_inner.4.refs_0_), custom_call_target="tpu_custom_call", output_to_operand_aliasing={{}: (2, {})} | custom-call | flops 2147483648 | bytes 3911680 | tf_op jit(solution)/shard_map/back_inner/pallas_call | solution.py:256
  40.6 0.1 collective-permute-start.16
  40.7 0.6 %collective-permute-start.15 = (f32[112,128]{1,0:T(8,128)S(1)}, f32[112,128]{1,0:T(8,128)S(1)}, u32[]{:S(2)}, u32[]{:S(2)}) collective-permute-start(f32[112,128]{1,0:T(8,128)S(1)} %sum_four.3.refs_0_), channel_id=1, source_target_pairs={{0,32},{4,36},{8,40},{12,44},{16,48},{20,52},{24,56},{28,60},{32,0... | collective-permute-start | bytes 172040 | tf_op jit(solution)/shard_map/ppermute | solution.py:279
  41.4 2.0 %collective-permute-start.14 = (f32[112,128]{1,0:T(8,128)S(1)}, f32[112,128]{1,0:T(8,128)S(1)}, u32[]{:S(2)}, u32[]{:S(2)}) collective-permute-start(f32[112,128]{1,0:T(8,128)S(1)} %sum_four.3.refs_0_), channel_id=1, source_target_pairs={{0,8},{4,12},{8,0},{12,4},{16,24},{20,28},{24,16},{28,20},{32,40},... | collective-permute-start | bytes 172040 | tf_op jit(solution)/shard_map/ppermute | solution.py:279
  43.4 0.1 collective-permute-done.10.second_ref
  43.4 2.4 %edge.1 = (bf16[32,1024]{1,0:T(8,128)(2,1)}, bf16[32,1024]{1,0:T(8,128)(2,1)}) custom-call(f32[864,1024]{1,0:T(8,128)S(1)} %back_terms.1.terms, s32[27,1024]{1,0:T(8,128)S(1)} %copy-done.2, bf16[864,128]{1,0:T(8,128)(2,1)S(1)} %bitcast.4, bf16[64,128]{1,0:T(8,128)(2,1)S(1)} %collective-permute-done.near_ref, ...), custom_call_target="tpu_custom_call" | custom-call | flops 2147483648 | bytes 4788224 | tf_op jit(solution)/shard_map/edge/pallas_call | solution.py:256
  45.8 4.1 %collective-permute-start.17 = (f32[448,128]{1,0:T(8,128)S(1)}, f32[448,128]{1,0:T(8,128)S(1)}, u32[]{:S(2)}, u32[]{:S(2)}) collective-permute-start(f32[448,128]{1,0:T(8,128)S(1)} %join.3.even_ref), channel_id=1, source_target_pairs={{0,4},{4,0},{8,12},{12,8},{16,20},{20,16},{24,28},{28,24},{32,36},... | collective-permute-start | bytes 688136 | tf_op jit(solution)/shard_map/ppermute | solution.py:279
  50.0 1.1 %collective-permute-done.17.odd_ref = f32[448,128]{1,0:T(8,128)S(1)} collective-permute-done((f32[448,128]{1,0:T(8,128)S(1)}, f32[448,128]{1,0:T(8,128)S(1)}, u32[]{:S(2)}, u32[]{:S(2)}) %collective-permute-start.17) | collective-permute-done | bytes 229408 | tf_op jit(solution)/shard_map/ppermute | solution.py:279
  51.1 0.8 %place.1 = f32[864,128]{1,0:T(8,128)} custom-call(f32[448,128]{1,0:T(8,128)S(1)} %join.3.even_ref, f32[448,128]{1,0:T(8,128)S(1)} %collective-permute-done.17.odd_ref), custom_call_target="tpu_custom_call" | custom-call | bytes 901120 | tf_op jit(solution)/shard_map/place/pallas_call | solution.py:256
  (29 shorter events, 0.2 us)
Async XLA Ops:
  0.6 5.7 %copy-start.1 = (bf16[32,1024]{1,0:T(8,128)(2,1)S(1)}, bf16[32,1024]{1,0:T(8,128)(2,1)}, u32[]{:S(2)}) copy-start(bf16[32,1024]{1,0:T(8,128)(2,1)} %refs_0_.1) | copy-start | bytes 196612
  0.6 7.7 %copy-start.3 = (bf16[32,1024]{1,0:T(8,128)(2,1)S(1)}, bf16[32,1024]{1,0:T(8,128)(2,1)}, u32[]{:S(2)}) copy-start(bf16[32,1024]{1,0:T(8,128)(2,1)} %x_ref.3) | copy-start | bytes 196612
  0.7 7.7 %copy-start.2 = (s32[27,1024]{1,0:T(8,128)S(1)}, s32[27,1024]{1,0:T(8,128)}, u32[]{:S(2)}) copy-start(s32[27,1024]{1,0:T(8,128)} %rule_ref.11) | copy-start | bytes 331780
  0.7 5.6 %collective-permute-start.2 = (bf16[32,1024]{1,0:T(8,128)(2,1)}, bf16[32,1024]{1,0:T(8,128)(2,1)S(1)}, u32[]{:S(2)}, u32[]{:S(2)}) collective-permute-start(bf16[32,1024]{1,0:T(8,128)(2,1)} %refs_0_.1), channel_id=1, source_target_pairs={{0,1},{1,0},{2,3},{3,2},{4,5},{5,4},{6,7},{7,6},{8,9},{9,8},{10,11... | collective-permute-start | bytes 196616 | tf_op jit(solution)/shard_map/ppermute | solution.py:296
  4.2 7.9 %collective-permute-start = (bf16[64,128]{1,0:T(8,128)(2,1)}, bf16[64,128]{1,0:T(8,128)(2,1)S(1)}, u32[]{:S(2)}, u32[]{:S(2)}) collective-permute-start(bf16[64,128]{1,0:T(8,128)(2,1)} %get-tuple-element.34), channel_id=1, source_target_pairs={{0,4},{4,0},{8,12},{12,8},{16,20},{20,16},{24,28},{28,24},{32,36},... | collective-permute-start | bytes 49160 | tf_op jit(solution)/shard_map/ppermute | solution.py:279
  5.4 6.8 %collective-permute-start.1 = (bf16[64,128]{1,0:T(8,128)(2,1)}, bf16[64,128]{1,0:T(8,128)(2,1)S(1)}, u32[]{:S(2)}, u32[]{:S(2)}) collective-permute-start(bf16[64,128]{1,0:T(8,128)(2,1)} %get-tuple-element.35), channel_id=1, source_target_pairs={{0,252},{4,8},{8,4},{12,16},{16,12},{20,24},{24,20},{28,32},{32,28... | collective-permute-start | bytes 49160 | tf_op jit(solution)/shard_map/ppermute | solution.py:285
  6.3 5.9 %collective-permute-start.3 = (bf16[64,1024]{1,0:T(8,128)(2,1)S(1)}, bf16[64,1024]{1,0:T(8,128)(2,1)S(1)}, u32[]{:S(2)}, u32[]{:S(2)}) collective-permute-start(bf16[64,1024]{1,0:T(8,128)(2,1)S(1)} %join.2.pair_ref), channel_id=1, source_target_pairs={{0,3},{1,2},{2,1},{3,0},{4,7},{5,6},{6,5},{7,4},{8,11},{9,10},{10,... | collective-permute-start | bytes 393224 | tf_op jit(solution)/shard_map/ppermute | solution.py:296
  12.2 8.3 %copy-start = (bf16[27,32,128]{2,1,0:T(8,128)(2,1)S(1)}, bf16[27,32,128]{2,1,0:T(8,128)(2,1)}, u32[]{:S(2)}) copy-start(bf16[27,32,128]{2,1,0:T(8,128)(2,1)} %param.5) | copy-start | bytes 663556
  12.9 8.6 %collective-permute-start.4 = (f32[448,128]{1,0:T(8,128)S(1)}, f32[448,128]{1,0:T(8,128)S(1)}, u32[]{:S(2)}, u32[]{:S(2)}) collective-permute-start(f32[448,128]{1,0:T(8,128)S(1)} %get-tuple-element.38), channel_id=1, source_target_pairs={{0,4},{4,0},{8,12},{12,8},{16,20},{20,16},{24,28},{28,24},{32,36},... | collective-permute-start | bytes 688136 | tf_op jit(solution)/shard_map/ppermute | solution.py:279
  21.6 4.1 %collective-permute-start.5 = (f32[112,128]{1,0:T(8,128)S(1)}, f32[112,128]{1,0:T(8,128)S(1)}, u32[]{:S(2)}, u32[]{:S(2)}) collective-permute-start(f32[112,128]{1,0:T(8,128)S(1)} %get-tuple-element.43), channel_id=1, source_target_pairs={{0,40},{4,44},{8,32},{12,36},{16,56},{20,60},{24,48},{28,52},{32,8... | collective-permute-start | bytes 172040 | tf_op jit(solution)/shard_map/ppermute | solution.py:279
  21.7 4.0 %collective-permute-start.6 = (f32[112,128]{1,0:T(8,128)S(1)}, f32[112,128]{1,0:T(8,128)S(1)}, u32[]{:S(2)}, u32[]{:S(2)}) collective-permute-start(f32[112,128]{1,0:T(8,128)S(1)} %get-tuple-element.44), channel_id=1, source_target_pairs={{0,32},{4,36},{8,40},{12,44},{16,48},{20,52},{24,56},{28,60},{32,0... | collective-permute-start | bytes 172040 | tf_op jit(solution)/shard_map/ppermute | solution.py:279
  21.8 5.5 %collective-permute-start.7 = (f32[112,128]{1,0:T(8,128)S(1)}, f32[112,128]{1,0:T(8,128)S(1)}, u32[]{:S(2)}, u32[]{:S(2)}) collective-permute-start(f32[112,128]{1,0:T(8,128)S(1)} %get-tuple-element.45), channel_id=1, source_target_pairs={{0,8},{4,12},{8,0},{12,4},{16,24},{20,28},{24,16},{28,20},{32,40},... | collective-permute-start | bytes 172040 | tf_op jit(solution)/shard_map/ppermute | solution.py:279
  25.3 12.1 %collective-permute-start.8 = (f32[64,1152]{1,0:T(8,128)S(1)}, f32[64,1152]{1,0:T(8,128)S(1)}, u32[]{:S(2)}, u32[]{:S(2)}) collective-permute-start(f32[64,1152]{1,0:T(8,128)S(1)} %get-tuple-element.51), channel_id=1, source_target_pairs={{0,1},{1,0},{2,3},{3,2},{4,5},{5,4},{6,7},{7,6},{8,9},{9,8},{10,11... | collective-permute-start | bytes 884744 | tf_op jit(solution)/shard_map/ppermute | solution.py:296
  27.3 4.3 %collective-permute-start.9 = (f32[112,128]{1,0:T(8,128)S(1)}, f32[112,128]{1,0:T(8,128)S(1)}, u32[]{:S(2)}, u32[]{:S(2)}) collective-permute-start(f32[112,128]{1,0:T(8,128)S(1)} %sum_four.2.refs_0_), channel_id=1, source_target_pairs={{0,24},{4,28},{8,16},{12,20},{16,8},{20,12},{24,0},{28,4},{32,56},... | collective-permute-start | bytes 172040 | tf_op jit(solution)/shard_map/ppermute | solution.py:279
  31.6 8.9 %collective-permute-start.13 = (f32[112,128]{1,0:T(8,128)S(1)}, f32[112,128]{1,0:T(8,128)S(1)}, u32[]{:S(2)}, u32[]{:S(2)}) collective-permute-start(f32[112,128]{1,0:T(8,128)S(1)} %sum_two.1.refs_0_), channel_id=1, source_target_pairs={{0,192},{4,196},{8,200},{12,204},{16,208},{20,212},{24,216},{28,22... | collective-permute-start | bytes 172040 | tf_op jit(solution)/shard_map/ppermute | solution.py:279
  32.8 7.8 %collective-permute-start.12 = (f32[112,128]{1,0:T(8,128)S(1)}, f32[112,128]{1,0:T(8,128)S(1)}, u32[]{:S(2)}, u32[]{:S(2)}) collective-permute-start(f32[112,128]{1,0:T(8,128)S(1)} %sum_two.1.refs_0_), channel_id=1, source_target_pairs={{0,160},{4,164},{8,168},{12,172},{16,176},{20,180},{24,184},{28,18... | collective-permute-start | bytes 172040 | tf_op jit(solution)/shard_map/ppermute | solution.py:279
  33.7 6.8 %collective-permute-start.11 = (f32[112,128]{1,0:T(8,128)S(1)}, f32[112,128]{1,0:T(8,128)S(1)}, u32[]{:S(2)}, u32[]{:S(2)}) collective-permute-start(f32[112,128]{1,0:T(8,128)S(1)} %sum_two.1.refs_0_), channel_id=1, source_target_pairs={{0,96},{4,100},{8,104},{12,108},{16,112},{20,116},{24,120},{28,124... | collective-permute-start | bytes 172040 | tf_op jit(solution)/shard_map/ppermute | solution.py:279
  37.4 6.0 %collective-permute-start.10 = (f32[32,1536]{1,0:T(8,128)S(1)}, f32[32,1536]{1,0:T(8,128)S(1)}, u32[]{:S(2)}, u32[]{:S(2)}) collective-permute-start(f32[32,1536]{1,0:T(8,128)S(1)} %get-tuple-element.56), channel_id=1, source_target_pairs={{0,3},{1,2},{2,1},{3,0},{4,7},{5,6},{6,5},{7,4},{8,11},{9,10},{10,... | collective-permute-start | bytes 589832 | tf_op jit(solution)/shard_map/ppermute | solution.py:296
  40.6 5.2 %collective-permute-start.16 = (f32[112,128]{1,0:T(8,128)S(1)}, f32[112,128]{1,0:T(8,128)S(1)}, u32[]{:S(2)}, u32[]{:S(2)}) collective-permute-start(f32[112,128]{1,0:T(8,128)S(1)} %sum_four.3.refs_0_), channel_id=1, source_target_pairs={{0,40},{4,44},{8,32},{12,36},{16,56},{20,60},{24,48},{28,52},{32,8... | collective-permute-start | bytes 172040 | tf_op jit(solution)/shard_map/ppermute | solution.py:279
  40.7 5.1 %collective-permute-start.15 = (f32[112,128]{1,0:T(8,128)S(1)}, f32[112,128]{1,0:T(8,128)S(1)}, u32[]{:S(2)}, u32[]{:S(2)}) collective-permute-start(f32[112,128]{1,0:T(8,128)S(1)} %sum_four.3.refs_0_), channel_id=1, source_target_pairs={{0,32},{4,36},{8,40},{12,44},{16,48},{20,52},{24,56},{28,60},{32,0... | collective-permute-start | bytes 172040 | tf_op jit(solution)/shard_map/ppermute | solution.py:279
  41.4 4.5 %collective-permute-start.14 = (f32[112,128]{1,0:T(8,128)S(1)}, f32[112,128]{1,0:T(8,128)S(1)}, u32[]{:S(2)}, u32[]{:S(2)}) collective-permute-start(f32[112,128]{1,0:T(8,128)S(1)} %sum_four.3.refs_0_), channel_id=1, source_target_pairs={{0,8},{4,12},{8,0},{12,4},{16,24},{20,28},{24,16},{28,20},{32,40},... | collective-permute-start | bytes 172040 | tf_op jit(solution)/shard_map/ppermute | solution.py:279
  45.8 5.2 %collective-permute-start.17 = (f32[448,128]{1,0:T(8,128)S(1)}, f32[448,128]{1,0:T(8,128)S(1)}, u32[]{:S(2)}, u32[]{:S(2)}) collective-permute-start(f32[448,128]{1,0:T(8,128)S(1)} %join.3.even_ref), channel_id=1, source_target_pairs={{0,4},{4,0},{8,12},{12,8},{16,20},{20,16},{24,28},{28,24},{32,36},... | collective-permute-start | bytes 688136 | tf_op jit(solution)/shard_map/ppermute | solution.py:279

commit v20 on v18

--- a/solution.py
+++ b/solution.py
@@ -70,7 +70,7 @@
     for k in range(27):
         row = rule_ref[k : k + 1, :]
         for group in range(8):
-            tiles = source_tiles(group, k % 3 - 1)
+            tiles = (group,) if k == 13 else source_tiles(group, k % 3 - 1)
             if tiles[0] >= 8:
                 continue
             got = picked(row, group, tiles, lambda t: table[:, tile_span(t)])
@@ -177,7 +177,8 @@
         row = rule_ref[k : k + 1, :]
         rows = slice(32 * (26 - k), 32 * (26 - k) + 32)
         for group in groups:
-            got = picked(row, group, source_tiles(group, k % 3 - 1), lambda t: load(rows, t))
+            tiles = (group,) if k == 13 else source_tiles(group, k % 3 - 1)
+            got = picked(row, group, tiles, lambda t: load(rows, t))
             totals[group] = got if k == 0 else totals[group] + got
     return totals
 

time: 52 us -> 52 us (level)
  no operation moved by 1% of the time
where the time goes in v20:
time: 52 us; the launch traced here: 51.9 us
  starting transfers between devices  31.7 us (61%)
  Pallas kernels  14.8 us (28%)
  waiting for transfers between devices  4.44 us (9%)
  between operations  0.83 us (2%)
    ppermute x13, starting transfers between devices, swap(): return lax.ppermute(value, 'blk', [(i, i ^ mask) for i in range(count)])  24 us
    pallas_call x16, Pallas kernels, call(): pl.pallas_call(kernel, out_shape=outs, in_specs=[VMEM] * len(args), out_s...  13.5 us
    ppermute x4, starting transfers between devices, over_ch(): return lax.ppermute(value, 'ch', [(i, i ^ mask) for i in range(4)])  6.76 us
    ppermute x13, waiting for transfers between devices, swap(): return lax.ppermute(value, 'blk', [(i, i ^ mask) for i in range(count)])  4.31 us
    pallas_call x1, Pallas kernels, per_device(): pl.pallas_call(faces_kernel, out_shape=(bf16(64, FACE),) * 2, grid=(1,),...  1.37 us
  transfers between devices with their start and end apart: 18, of which 4 were waited for; matrix products, arithmetic and copies ran while one was open for 0% of the time, Pallas kernels for 26%

profile of v20, /device:TPU:1, one launch (start us, length us, event | category | flops | bytes accessed | tf_op | source)
XLA Modules:
  0.0 51.9 jit_solution(4666472688715012780)
XLA Ops:
  0.7 2.2 %collective-permute-start.2 = (bf16[32,1024]{1,0:T(8,128)(2,1)}, bf16[32,1024]{1,0:T(8,128)(2,1)S(1)}, u32[]{:S(2)}, u32[]{:S(2)}) collective-permute-start(bf16[32,1024]{1,0:T(8,128)(2,1)} %refs_0_.1), channel_id=1, source_target_pairs={{0,1},{1,0},{2,3},{3,2},{4,5},{5,4},{6,7},{7,6},{8,9},{9,8},{10,11... | collective-permute-start | bytes 196616 | tf_op jit(solution)/shard_map/ppermute | solution.py:297
  2.9 1.4 %faces.1 = (bf16[64,128]{1,0:T(8,128)(2,1)}, bf16[64,128]{1,0:T(8,128)(2,1)}) custom-call(bf16[32,1024]{1,0:T(8,128)(2,1)} %x_ref.3, bf16[32,1024]{1,0:T(8,128)(2,1)} %refs_0_.1), custom_call_target="tpu_custom_call" | custom-call | flops 1073741824 | bytes 65536 | tf_op jit(solution)/shard_map/faces/pallas_call | solution.py:302
  4.2 1.1 %collective-permute-start = (bf16[64,128]{1,0:T(8,128)(2,1)}, bf16[64,128]{1,0:T(8,128)(2,1)S(1)}, u32[]{:S(2)}, u32[]{:S(2)}) collective-permute-start(bf16[64,128]{1,0:T(8,128)(2,1)} %get-tuple-element.34), channel_id=1, source_target_pairs={{0,4},{4,0},{8,12},{12,8},{16,20},{20,16},{24,28},{28,24},{32,36},... | collective-permute-start | bytes 49160 | tf_op jit(solution)/shard_map/ppermute | solution.py:280
  5.4 0.9 %collective-permute-start.1 = (bf16[64,128]{1,0:T(8,128)(2,1)}, bf16[64,128]{1,0:T(8,128)(2,1)S(1)}, u32[]{:S(2)}, u32[]{:S(2)}) collective-permute-start(bf16[64,128]{1,0:T(8,128)(2,1)} %get-tuple-element.35), channel_id=1, source_target_pairs={{0,252},{4,8},{8,4},{12,16},{16,12},{20,24},{24,20},{28,32},{32,28... | collective-permute-start | bytes 49160 | tf_op jit(solution)/shard_map/ppermute | solution.py:286
  6.3 2.0 %collective-permute-start.3 = (bf16[64,1024]{1,0:T(8,128)(2,1)S(1)}, bf16[64,1024]{1,0:T(8,128)(2,1)S(1)}, u32[]{:S(2)}, u32[]{:S(2)}) collective-permute-start(bf16[64,1024]{1,0:T(8,128)(2,1)S(1)} %join.2.pair_ref), channel_id=1, source_target_pairs={{0,3},{1,2},{2,1},{3,0},{4,7},{5,6},{6,5},{7,4},{8,11},{9,10},{10,... | collective-permute-start | bytes 393224 | tf_op jit(solution)/shard_map/ppermute | solution.py:297
  8.3 3.9 %gather.1.dense_in = bf16[864,1024]{1,0:T(8,128)(2,1)S(1)} custom-call(bf16[32,1024]{1,0:T(8,128)(2,1)S(1)} %copy-done.3, s32[27,1024]{1,0:T(8,128)S(1)} %copy-done.2), custom_call_target="tpu_custom_call" | custom-call | flops 3221225472 | bytes 1945600 | tf_op jit(solution)/shard_map/gather/pallas_call | solution.py:257
  12.2 0.7 %weight_terms.1 = (bf16[864,1024]{1,0:T(8,128)(2,1)S(1)}, bf16[128,1024]{1,0:T(8,128)(2,1)S(1)}, f32[448,128]{1,0:T(8,128)S(1)}, f32[448,128]{1,0:T(8,128)S(1)}) custom-call(bf16[864,1024]{1,0:T(8,128)(2,1)S(1)} %gather.1.dense_in, s32[27,1024]{1,0:T(8,128)S(1)} %copy-done.2, ...), custom_call_target="tpu_custom_call", output_to_operand_aliasing={{0}: (0, {})} | custom-call | flops 1073741824 | bytes 4665344 | tf_op jit(solution)/shard_map/weight_terms/pallas_call | solution.py:257
  12.9 7.5 %collective-permute-start.4 = (f32[448,128]{1,0:T(8,128)S(1)}, f32[448,128]{1,0:T(8,128)S(1)}, u32[]{:S(2)}, u32[]{:S(2)}) collective-permute-start(f32[448,128]{1,0:T(8,128)S(1)} %get-tuple-element.38), channel_id=1, source_target_pairs={{0,4},{4,0},{8,12},{12,8},{16,20},{20,16},{24,28},{28,24},{32,36},... | collective-permute-start | bytes 688136 | tf_op jit(solution)/shard_map/ppermute | solution.py:280
  20.5 0.6 %back_terms.1.terms = f32[864,1024]{1,0:T(8,128)S(1)} custom-call(bf16[864,128]{1,0:T(8,128)(2,1)S(1)} %bitcast.2, bf16[128,1024]{1,0:T(8,128)(2,1)S(1)} %get-tuple-element.36.grad_ref), custom_call_target="tpu_custom_call" | custom-call | flops 1073741824 | bytes 4022272 | tf_op jit(solution)/shard_map/back_terms/pallas_call | solution.py:257
  21.1 0.5 forward.1
  21.6 0.1 collective-permute-start.5
  21.7 0.1 collective-permute-start.6
  21.8 2.5 %collective-permute-start.7 = (f32[112,128]{1,0:T(8,128)S(1)}, f32[112,128]{1,0:T(8,128)S(1)}, u32[]{:S(2)}, u32[]{:S(2)}) collective-permute-start(f32[112,128]{1,0:T(8,128)S(1)} %get-tuple-element.45), channel_id=1, source_target_pairs={{0,8},{4,12},{8,0},{12,4},{16,24},{20,28},{24,16},{28,20},{32,40},... | collective-permute-start | bytes 172040 | tf_op jit(solution)/shard_map/ppermute | solution.py:280
  24.4 0.9 %back_inner.3.refs_0_ = f32[32,1024]{1,0:T(8,128)S(1)} custom-call(f32[864,1024]{1,0:T(8,128)S(1)} %back_terms.1.terms, s32[27,1024]{1,0:T(8,128)S(1)} %copy-done.2), custom_call_target="tpu_custom_call" | custom-call | flops 2147483648 | bytes 3780608 | tf_op jit(solution)/shard_map/back_inner/pallas_call | solution.py:257
  25.3 0.4 collective-permute-start.8
  25.7 1.6 %collective-permute-done.7.refs_3_ = f32[112,128]{1,0:T(8,128)S(1)} collective-permute-done((f32[112,128]{1,0:T(8,128)S(1)}, f32[112,128]{1,0:T(8,128)S(1)}, u32[]{:S(2)}, u32[]{:S(2)}) %collective-permute-start.7) | collective-permute-done | bytes 57376 | tf_op jit(solution)/shard_map/ppermute | solution.py:280
  27.3 0.1 collective-permute-start.9
  27.4 2.7 %back_inner.4.refs_0_ = f32[32,1024]{1,0:T(8,128)S(1)} custom-call(f32[864,1024]{1,0:T(8,128)S(1)} %back_terms.1.terms, s32[27,1024]{1,0:T(8,128)S(1)} %copy-done.2, f32[32,1024]{1,0:T(8,128)S(1)} %back_inner.3.refs_0_), custom_call_target="tpu_custom_call", output_to_operand_aliasing={{}: (2, {})} | custom-call | flops 3221225472 | bytes 3911680 | tf_op jit(solution)/shard_map/back_inner/pallas_call | solution.py:257
  30.1 1.6 %collective-permute-done.9.refs_1_ = f32[112,128]{1,0:T(8,128)S(1)} collective-permute-done((f32[112,128]{1,0:T(8,128)S(1)}, f32[112,128]{1,0:T(8,128)S(1)}, u32[]{:S(2)}, u32[]{:S(2)}) %collective-permute-start.9) | collective-permute-done | bytes 57376 | tf_op jit(solution)/shard_map/ppermute | solution.py:280
  31.6 1.6 %collective-permute-start.13 = (f32[112,128]{1,0:T(8,128)S(1)}, f32[112,128]{1,0:T(8,128)S(1)}, u32[]{:S(2)}, u32[]{:S(2)}) collective-permute-start(f32[112,128]{1,0:T(8,128)S(1)} %sum_two.1.refs_0_), channel_id=1, source_target_pairs={{0,160},{4,164},{8,168},{12,172},{16,176},{20,180},{24,184},{28,18... | collective-permute-start | bytes 172040 | tf_op jit(solution)/shard_map/ppermute | solution.py:280
  33.2 0.5 collective-permute-start.12
  33.7 3.7 %collective-permute-start.11 = (f32[112,128]{1,0:T(8,128)S(1)}, f32[112,128]{1,0:T(8,128)S(1)}, u32[]{:S(2)}, u32[]{:S(2)}) collective-permute-start(f32[112,128]{1,0:T(8,128)S(1)} %sum_two.1.refs_0_), channel_id=1, source_target_pairs={{0,96},{4,100},{8,104},{12,108},{16,112},{20,116},{24,120},{28,124... | collective-permute-start | bytes 172040 | tf_op jit(solution)/shard_map/ppermute | solution.py:280
  37.4 2.2 %collective-permute-start.10 = (f32[32,1536]{1,0:T(8,128)S(1)}, f32[32,1536]{1,0:T(8,128)S(1)}, u32[]{:S(2)}, u32[]{:S(2)}) collective-permute-start(f32[32,1536]{1,0:T(8,128)S(1)} %get-tuple-element.56), channel_id=1, source_target_pairs={{0,3},{1,2},{2,1},{3,0},{4,7},{5,6},{6,5},{7,4},{8,11},{9,10},{10,... | collective-permute-start | bytes 589832 | tf_op jit(solution)/shard_map/ppermute | solution.py:297
  39.6 0.9 %back_inner.5.inner = f32[32,1024]{1,0:T(8,128)S(1)} custom-call(f32[864,1024]{1,0:T(8,128)S(1)} %back_terms.1.terms, s32[27,1024]{1,0:T(8,128)S(1)} %copy-done.2, f32[32,1024]{1,0:T(8,128)S(1)} %back_inner.4.refs_0_), custom_call_target="tpu_custom_call", output_to_operand_aliasing={{}: (2, {})} | custom-call | flops 2147483648 | bytes 3911680 | tf_op jit(solution)/shard_map/back_inner/pallas_call | solution.py:257
  40.6 0.1 collective-permute-start.16
  40.7 0.6 %collective-permute-start.15 = (f32[112,128]{1,0:T(8,128)S(1)}, f32[112,128]{1,0:T(8,128)S(1)}, u32[]{:S(2)}, u32[]{:S(2)}) collective-permute-start(f32[112,128]{1,0:T(8,128)S(1)} %sum_four.3.refs_0_), channel_id=1, source_target_pairs={{0,32},{4,36},{8,40},{12,44},{16,48},{20,52},{24,56},{28,60},{32,0... | collective-permute-start | bytes 172040 | tf_op jit(solution)/shard_map/ppermute | solution.py:280
  41.3 2.0 %collective-permute-start.14 = (f32[112,128]{1,0:T(8,128)S(1)}, f32[112,128]{1,0:T(8,128)S(1)}, u32[]{:S(2)}, u32[]{:S(2)}) collective-permute-start(f32[112,128]{1,0:T(8,128)S(1)} %sum_four.3.refs_0_), channel_id=1, source_target_pairs={{0,8},{4,12},{8,0},{12,4},{16,24},{20,28},{24,16},{28,20},{32,40},... | collective-permute-start | bytes 172040 | tf_op jit(solution)/shard_map/ppermute | solution.py:280
  43.3 0.1 collective-permute-done.10.second_ref
  43.4 2.4 %edge.1 = (bf16[32,1024]{1,0:T(8,128)(2,1)}, bf16[32,1024]{1,0:T(8,128)(2,1)}) custom-call(f32[864,1024]{1,0:T(8,128)S(1)} %back_terms.1.terms, s32[27,1024]{1,0:T(8,128)S(1)} %copy-done.2, bf16[864,128]{1,0:T(8,128)(2,1)S(1)} %bitcast.4, bf16[64,128]{1,0:T(8,128)(2,1)S(1)} %collective-permute-done.near_ref, ...), custom_call_target="tpu_custom_call" | custom-call | flops 2147483648 | bytes 4788224 | tf_op jit(solution)/shard_map/edge/pallas_call | solution.py:257
  45.8 4.1 %collective-permute-start.17 = (f32[448,128]{1,0:T(8,128)S(1)}, f32[448,128]{1,0:T(8,128)S(1)}, u32[]{:S(2)}, u32[]{:S(2)}) collective-permute-start(f32[448,128]{1,0:T(8,128)S(1)} %join.3.even_ref), channel_id=1, source_target_pairs={{0,4},{4,0},{8,12},{12,8},{16,20},{20,16},{24,28},{28,24},{32,36},... | collective-permute-start | bytes 688136 | tf_op jit(solution)/shard_map/ppermute | solution.py:280
  49.9 1.1 %collective-permute-done.17.odd_ref = f32[448,128]{1,0:T(8,128)S(1)} collective-permute-done((f32[448,128]{1,0:T(8,128)S(1)}, f32[448,128]{1,0:T(8,128)S(1)}, u32[]{:S(2)}, u32[]{:S(2)}) %collective-permute-start.17) | collective-permute-done | bytes 229408 | tf_op jit(solution)/shard_map/ppermute | solution.py:280
  51.1 0.8 %place.1 = f32[864,128]{1,0:T(8,128)} custom-call(f32[448,128]{1,0:T(8,128)S(1)} %join.3.even_ref, f32[448,128]{1,0:T(8,128)S(1)} %collective-permute-done.17.odd_ref), custom_call_target="tpu_custom_call" | custom-call | bytes 901120 | tf_op jit(solution)/shard_map/place/pallas_call | solution.py:257
  (29 shorter events, 0.2 us)
Async XLA Ops:
  0.6 5.7 %copy-start.1 = (bf16[32,1024]{1,0:T(8,128)(2,1)S(1)}, bf16[32,1024]{1,0:T(8,128)(2,1)}, u32[]{:S(2)}) copy-start(bf16[32,1024]{1,0:T(8,128)(2,1)} %refs_0_.1) | copy-start | bytes 196612
  0.6 7.7 %copy-start.3 = (bf16[32,1024]{1,0:T(8,128)(2,1)S(1)}, bf16[32,1024]{1,0:T(8,128)(2,1)}, u32[]{:S(2)}) copy-start(bf16[32,1024]{1,0:T(8,128)(2,1)} %x_ref.3) | copy-start | bytes 196612
  0.7 7.7 %copy-start.2 = (s32[27,1024]{1,0:T(8,128)S(1)}, s32[27,1024]{1,0:T(8,128)}, u32[]{:S(2)}) copy-start(s32[27,1024]{1,0:T(8,128)} %rule_ref.11) | copy-start | bytes 331780
  0.7 5.6 %collective-permute-start.2 = (bf16[32,1024]{1,0:T(8,128)(2,1)}, bf16[32,1024]{1,0:T(8,128)(2,1)S(1)}, u32[]{:S(2)}, u32[]{:S(2)}) collective-permute-start(bf16[32,1024]{1,0:T(8,128)(2,1)} %refs_0_.1), channel_id=1, source_target_pairs={{0,1},{1,0},{2,3},{3,2},{4,5},{5,4},{6,7},{7,6},{8,9},{9,8},{10,11... | collective-permute-start | bytes 196616 | tf_op jit(solution)/shard_map/ppermute | solution.py:297
  4.2 7.9 %collective-permute-start = (bf16[64,128]{1,0:T(8,128)(2,1)}, bf16[64,128]{1,0:T(8,128)(2,1)S(1)}, u32[]{:S(2)}, u32[]{:S(2)}) collective-permute-start(bf16[64,128]{1,0:T(8,128)(2,1)} %get-tuple-element.34), channel_id=1, source_target_pairs={{0,4},{4,0},{8,12},{12,8},{16,20},{20,16},{24,28},{28,24},{32,36},... | collective-permute-start | bytes 49160 | tf_op jit(solution)/shard_map/ppermute | solution.py:280
  5.4 6.8 %collective-permute-start.1 = (bf16[64,128]{1,0:T(8,128)(2,1)}, bf16[64,128]{1,0:T(8,128)(2,1)S(1)}, u32[]{:S(2)}, u32[]{:S(2)}) collective-permute-start(bf16[64,128]{1,0:T(8,128)(2,1)} %get-tuple-element.35), channel_id=1, source_target_pairs={{0,252},{4,8},{8,4},{12,16},{16,12},{20,24},{24,20},{28,32},{32,28... | collective-permute-start | bytes 49160 | tf_op jit(solution)/shard_map/ppermute | solution.py:286
  6.3 5.9 %collective-permute-start.3 = (bf16[64,1024]{1,0:T(8,128)(2,1)S(1)}, bf16[64,1024]{1,0:T(8,128)(2,1)S(1)}, u32[]{:S(2)}, u32[]{:S(2)}) collective-permute-start(bf16[64,1024]{1,0:T(8,128)(2,1)S(1)} %join.2.pair_ref), channel_id=1, source_target_pairs={{0,3},{1,2},{2,1},{3,0},{4,7},{5,6},{6,5},{7,4},{8,11},{9,10},{10,... | collective-permute-start | bytes 393224 | tf_op jit(solution)/shard_map/ppermute | solution.py:297
  12.2 8.3 %copy-start = (bf16[27,32,128]{2,1,0:T(8,128)(2,1)S(1)}, bf16[27,32,128]{2,1,0:T(8,128)(2,1)}, u32[]{:S(2)}) copy-start(bf16[27,32,128]{2,1,0:T(8,128)(2,1)} %param.5) | copy-start | bytes 663556
  12.9 8.6 %collective-permute-start.4 = (f32[448,128]{1,0:T(8,128)S(1)}, f32[448,128]{1,0:T(8,128)S(1)}, u32[]{:S(2)}, u32[]{:S(2)}) collective-permute-start(f32[448,128]{1,0:T(8,128)S(1)} %get-tuple-element.38), channel_id=1, source_target_pairs={{0,4},{4,0},{8,12},{12,8},{16,20},{20,16},{24,28},{28,24},{32,36},... | collective-permute-start | bytes 688136 | tf_op jit(solution)/shard_map/ppermute | solution.py:280
  21.6 4.0 %collective-permute-start.5 = (f32[112,128]{1,0:T(8,128)S(1)}, f32[112,128]{1,0:T(8,128)S(1)}, u32[]{:S(2)}, u32[]{:S(2)}) collective-permute-start(f32[112,128]{1,0:T(8,128)S(1)} %get-tuple-element.43), channel_id=1, source_target_pairs={{0,40},{4,44},{8,32},{12,36},{16,56},{20,60},{24,48},{28,52},{32,8... | collective-permute-start | bytes 172040 | tf_op jit(solution)/shard_map/ppermute | solution.py:280
  21.7 4.0 %collective-permute-start.6 = (f32[112,128]{1,0:T(8,128)S(1)}, f32[112,128]{1,0:T(8,128)S(1)}, u32[]{:S(2)}, u32[]{:S(2)}) collective-permute-start(f32[112,128]{1,0:T(8,128)S(1)} %get-tuple-element.44), channel_id=1, source_target_pairs={{0,32},{4,36},{8,40},{12,44},{16,48},{20,52},{24,56},{28,60},{32,0... | collective-permute-start | bytes 172040 | tf_op jit(solution)/shard_map/ppermute | solution.py:280
  21.8 5.5 %collective-permute-start.7 = (f32[112,128]{1,0:T(8,128)S(1)}, f32[112,128]{1,0:T(8,128)S(1)}, u32[]{:S(2)}, u32[]{:S(2)}) collective-permute-start(f32[112,128]{1,0:T(8,128)S(1)} %get-tuple-element.45), channel_id=1, source_target_pairs={{0,8},{4,12},{8,0},{12,4},{16,24},{20,28},{24,16},{28,20},{32,40},... | collective-permute-start | bytes 172040 | tf_op jit(solution)/shard_map/ppermute | solution.py:280
  25.3 12.1 %collective-permute-start.8 = (f32[64,1152]{1,0:T(8,128)S(1)}, f32[64,1152]{1,0:T(8,128)S(1)}, u32[]{:S(2)}, u32[]{:S(2)}) collective-permute-start(f32[64,1152]{1,0:T(8,128)S(1)} %get-tuple-element.51), channel_id=1, source_target_pairs={{0,1},{1,0},{2,3},{3,2},{4,5},{5,4},{6,7},{7,6},{8,9},{9,8},{10,11... | collective-permute-start | bytes 884744 | tf_op jit(solution)/shard_map/ppermute | solution.py:297
  27.3 4.3 %collective-permute-start.9 = (f32[112,128]{1,0:T(8,128)S(1)}, f32[112,128]{1,0:T(8,128)S(1)}, u32[]{:S(2)}, u32[]{:S(2)}) collective-permute-start(f32[112,128]{1,0:T(8,128)S(1)} %sum_four.2.refs_0_), channel_id=1, source_target_pairs={{0,24},{4,28},{8,16},{12,20},{16,8},{20,12},{24,0},{28,4},{32,56},... | collective-permute-start | bytes 172040 | tf_op jit(solution)/shard_map/ppermute | solution.py:280
  31.6 8.9 %collective-permute-start.13 = (f32[112,128]{1,0:T(8,128)S(1)}, f32[112,128]{1,0:T(8,128)S(1)}, u32[]{:S(2)}, u32[]{:S(2)}) collective-permute-start(f32[112,128]{1,0:T(8,128)S(1)} %sum_two.1.refs_0_), channel_id=1, source_target_pairs={{0,160},{4,164},{8,168},{12,172},{16,176},{20,180},{24,184},{28,18... | collective-permute-start | bytes 172040 | tf_op jit(solution)/shard_map/ppermute | solution.py:280
  33.2 7.3 %collective-permute-start.12 = (f32[112,128]{1,0:T(8,128)S(1)}, f32[112,128]{1,0:T(8,128)S(1)}, u32[]{:S(2)}, u32[]{:S(2)}) collective-permute-start(f32[112,128]{1,0:T(8,128)S(1)} %sum_two.1.refs_0_), channel_id=1, source_target_pairs={{0,192},{4,196},{8,200},{12,204},{16,208},{20,212},{24,216},{28,22... | collective-permute-start | bytes 172040 | tf_op jit(solution)/shard_map/ppermute | solution.py:280
  33.7 6.9 %collective-permute-start.11 = (f32[112,128]{1,0:T(8,128)S(1)}, f32[112,128]{1,0:T(8,128)S(1)}, u32[]{:S(2)}, u32[]{:S(2)}) collective-permute-start(f32[112,128]{1,0:T(8,128)S(1)} %sum_two.1.refs_0_), channel_id=1, source_target_pairs={{0,96},{4,100},{8,104},{12,108},{16,112},{20,116},{24,120},{28,124... | collective-permute-start | bytes 172040 | tf_op jit(solution)/shard_map/ppermute | solution.py:280
  37.4 6.0 %collective-permute-start.10 = (f32[32,1536]{1,0:T(8,128)S(1)}, f32[32,1536]{1,0:T(8,128)S(1)}, u32[]{:S(2)}, u32[]{:S(2)}) collective-permute-start(f32[32,1536]{1,0:T(8,128)S(1)} %get-tuple-element.56), channel_id=1, source_target_pairs={{0,3},{1,2},{2,1},{3,0},{4,7},{5,6},{6,5},{7,4},{8,11},{9,10},{10,... | collective-permute-start | bytes 589832 | tf_op jit(solution)/shard_map/ppermute | solution.py:297
  40.6 5.2 %collective-permute-start.16 = (f32[112,128]{1,0:T(8,128)S(1)}, f32[112,128]{1,0:T(8,128)S(1)}, u32[]{:S(2)}, u32[]{:S(2)}) collective-permute-start(f32[112,128]{1,0:T(8,128)S(1)} %sum_four.3.refs_0_), channel_id=1, source_target_pairs={{0,40},{4,44},{8,32},{12,36},{16,56},{20,60},{24,48},{28,52},{32,8... | collective-permute-start | bytes 172040 | tf_op jit(solution)/shard_map/ppermute | solution.py:280
  40.7 5.1 %collective-permute-start.15 = (f32[112,128]{1,0:T(8,128)S(1)}, f32[112,128]{1,0:T(8,128)S(1)}, u32[]{:S(2)}, u32[]{:S(2)}) collective-permute-start(f32[112,128]{1,0:T(8,128)S(1)} %sum_four.3.refs_0_), channel_id=1, source_target_pairs={{0,32},{4,36},{8,40},{12,44},{16,48},{20,52},{24,56},{28,60},{32,0... | collective-permute-start | bytes 172040 | tf_op jit(solution)/shard_map/ppermute | solution.py:280
  41.3 4.5 %collective-permute-start.14 = (f32[112,128]{1,0:T(8,128)S(1)}, f32[112,128]{1,0:T(8,128)S(1)}, u32[]{:S(2)}, u32[]{:S(2)}) collective-permute-start(f32[112,128]{1,0:T(8,128)S(1)} %sum_four.3.refs_0_), channel_id=1, source_target_pairs={{0,8},{4,12},{8,0},{12,4},{16,24},{20,28},{24,16},{28,20},{32,40},... | collective-permute-start | bytes 172040 | tf_op jit(solution)/shard_map/ppermute | solution.py:280
  45.8 5.2 %collective-permute-start.17 = (f32[448,128]{1,0:T(8,128)S(1)}, f32[448,128]{1,0:T(8,128)S(1)}, u32[]{:S(2)}, u32[]{:S(2)}) collective-permute-start(f32[448,128]{1,0:T(8,128)S(1)} %join.3.even_ref), channel_id=1, source_target_pairs={{0,4},{4,0},{8,12},{12,8},{16,20},{20,16},{24,28},{28,24},{32,36},... | collective-permute-start | bytes 688136 | tf_op jit(solution)/shard_map/ppermute | solution.py:280
